TPU v7x, 128 devices: a whole 4x4x4 slice. The times are simulated.
128 devices in a mesh: view: 2 (over y_hi), block: 64 (over y_lo, x, z, core).
Axes of the slice: x: 4, y: 4 (y_hi: 2, y_lo: 2; y = y_hi * 2 + y_lo), z: 4, core: 2. Of those that a mesh axis runs over, the one named last changes fastest.
Arguments:
- estimate: float32 [2048, 128, 128], P('block'), may hold values from 0.5 to 2
- view_tiles: bfloat16 [2, 1536, 4, 128, 128], P('view', 'block'), may hold values from 0.25 to 4
- tile_dest: int32 [2, 1536, 3], P('view', 'block'), may hold values from 0 to 63, as said below
- psf_taps: float32 [6, 3, 31], P('view'), may hold values from 0.05 to 1
Outputs:
- deblurred: float32 [2048, 128, 128], P('block')
Inputs may be any that keep to these rules, and one draw needn't show every extreme that they name: `tile_dest`: for each index of view, every triple of owner block, view within the index and tile position appears in exactly one row. The rows of block device s send exactly 2 tiles to each owner (s + d) mod 64 for d from -(6) to 5, and none elsewhere, in any order.
All inputs are finite; a program needn't handle non-finite values.
Results may differ from a plain program's by a relative error of at most 0.0003.
Values may be sent and summed in bfloat16 or wider, within the bound.
No kernel may reach another device: no remote copies, remote signals or barrier semaphores. Data moves between devices by JAX's collectives and lax.ppermute only.
A program may use at most 192 MiB of HBM per device.

v0:
```python
import jax
import jax.numpy as jnp
from jax import lax
from jax.sharding import PartitionSpec as P

TAPS = 31
BX = 32
VIEWS_DEV = 3
ITERS = 2
CAP = 2
SPAN = 12
TP = 4


def passed_along(shard, axis, by):
    length = lax.axis_size(axis)
    return lax.ppermute(shard, axis, [(i, (i + by) % length) for i in range(length)])


def extended(shard, sides, width):
    for axis, dim in sides:
        size, length = (lax.axis_size(axis), shard.shape[dim])
        up = [(i, (i + 1) % size) for i in range(size - 1)]
        down = [(j, i) for i, j in up]
        last = lax.slice_in_dim(shard, length - width, length, axis=dim)
        first = lax.slice_in_dim(shard, 0, width, axis=dim)
        before = lax.ppermute(last, axis, up)
        after = lax.ppermute(first, axis, down)
        shard = jnp.concatenate([before, shard, after], axis=dim)
    return shard


def banded(kernel, rows, cols, sign, offset):
    row_idx = jnp.arange(rows)[:, None]
    col_idx = jnp.arange(cols)[None, :]
    lag = sign * (col_idx - row_idx) + offset
    hits = (lag[:, :, None] == jnp.arange(kernel.shape[-1])[None, None, :]).astype(jnp.float32)
    return jnp.einsum("vt,ijt->vij", kernel, hits, precision=lax.Precision.HIGHEST)


def pass_yz(volume, along_y, along_z):
    volume = jnp.einsum("vij,vxjz->vxiz", along_y, volume, precision=lax.Precision.HIGHEST)
    return jnp.einsum("vxyj,vij->vxyi", volume, along_z, precision=lax.Precision.HIGHEST)


def pack_tiles(tiles, labels_in, target, groups):
    slots = tiles.shape[0]
    feature = tiles.shape[1] * tiles.shape[2] * tiles.shape[3]
    picker = jnp.arange(groups * CAP)[:, None] == target[None, :]
    packed = jnp.dot(
        picker.astype(jnp.bfloat16),
        tiles.reshape(slots, feature),
        preferred_element_type=jnp.float32,
    )
    packed = packed.astype(jnp.bfloat16).reshape(groups, CAP, feature)
    item_code = labels_in[:, 1] * (BX // TP) + labels_in[:, 2] + 1
    labels = jnp.sum(jnp.where(picker, item_code[None, :], 0), axis=1).reshape(groups, CAP)
    return (packed, labels)


def route_tiles(view_tiles, tile_dest):
    tiles = view_tiles[0]
    labels_in = tile_dest[0]
    slots = tiles.shape[0]
    blocks = lax.axis_size("block")
    feature = tiles.shape[1] * tiles.shape[2] * tiles.shape[3]
    owner_ids = labels_in[:, 0]
    slot_order = jnp.arange(slots)
    same_owner = owner_ids[:, None] == owner_ids[None, :]
    slot_rank = jnp.sum(same_owner & (slot_order[None, :] < slot_order[:, None]), axis=1)
    offset_ids = (owner_ids - lax.axis_index("block") + SPAN // 2) % blocks
    packed, labels = pack_tiles(tiles, labels_in, offset_ids * CAP + slot_rank, SPAN)
    got_list = []
    label_list = []
    for step in range(SPAN):
        moved_tiles, moved_labels = passed_along(
            (packed[step], labels[step]), "block", step - SPAN // 2
        )
        got_list.append(moved_tiles)
        label_list.append(moved_labels)
    got_tiles = jnp.stack(got_list, axis=0)
    got_labels = jnp.stack(label_list, axis=0)
    arrived = SPAN * CAP
    placed_rows = VIEWS_DEV * (BX // TP)
    placer = (jnp.arange(placed_rows)[:, None] + 1 == got_labels.reshape(-1)[None, :]).astype(
        jnp.bfloat16
    )
    measured = jnp.dot(
        placer, got_tiles.reshape(arrived, feature), preferred_element_type=jnp.float32
    )
    return measured.astype(jnp.bfloat16).reshape(VIEWS_DEV, BX, tiles.shape[2], tiles.shape[3])


def shards(estimate, view_tiles, tile_dest, psf_taps):
    kernels = psf_taps / jnp.sum(psf_taps, axis=-1, keepdims=True)
    half_width = TAPS // 2
    planes, size_y, size_z = estimate.shape
    view_count = kernels.shape[0] * lax.axis_size("view")
    measured = route_tiles(view_tiles, tile_dest)
    fwd_y = banded(kernels[:, 1], size_y, size_y, 1, half_width)
    back_y = banded(kernels[:, 1], size_y, size_y, -1, half_width)
    fwd_z = banded(kernels[:, 2], size_z, size_z, 1, half_width)
    back_z = banded(kernels[:, 2], size_z, size_z, -1, half_width)
    back_x = banded(kernels[:, 0], planes, planes + 2 * half_width, -1, 2 * half_width)
    fwd_x = banded(kernels[:, 0], planes, planes + 2 * half_width, 1, 0)
    for sweep in range(ITERS):
        padded = extended(estimate.astype(jnp.bfloat16), (("block", 0),), half_width).astype(
            estimate.dtype
        )
        blurred = jnp.einsum("vij,jyz->viyz", fwd_x, padded, precision=lax.Precision.HIGHEST)
        blurred = pass_yz(blurred, fwd_y, fwd_z)
        ratios = measured.astype(jnp.float32) / blurred
        ratio_pad = extended(ratios.astype(jnp.bfloat16), (("block", 1),), half_width).astype(
            ratios.dtype
        )
        backed = jnp.einsum("vij,vjyz->viyz", back_x, ratio_pad, precision=lax.Precision.HIGHEST)
        backed = pass_yz(backed, back_y, back_z)
        partial_sum = jnp.sum(backed, axis=0)
        total = lax.psum(partial_sum, "view")
        estimate = estimate * total / view_count
    return estimate


def solution(mesh):
    return jax.shard_map(
        shards,
        mesh=mesh,
        in_specs=(
            P("block", None, None),
            P("view", "block", None, None, None),
            P("view", "block", None),
            P("view", None, None),
        ),
        out_specs=P("block", None, None),
        check_vma=False,
    )
```

profile of v0, /device:TPU:1, one launch (start us, length us, event | category | flops | bytes accessed | tf_op | source)
XLA Modules:
  0.0 506.1 jit_solution(10347358304629241625)
XLA Ops:
  8.2 5.1 %collective-permute-start.11 = (s32[2]{0:T(128)}, s32[2]{0:T(128)S(1)}, u32[]{:S(2)}, u32[]{:S(2)}) collective-permute-start(s32[2]{0:T(128)} %get-tuple-element.30), channel_id=1, source_target_pairs={{0,5},{1,6},{2,7},{3,8},{4,9},{5,10},{6,11},{7,12},{8,13},{9,14},{... | collective-permute-start | bytes 32 | tf_op jit(solution)/shard_map/ppermute | solution.py:17
  14.0 3.1 collective-permute-start.9
  17.8 3.4 reshape_squeeze.3
  21.2 1.0 convolution_convert_fusion.1
  22.2 3.6 fusion.92
  25.8 2.1 collective-permute-start.12
  28.8 1.5 fusion.44
  30.3 1.2 copy.182
  32.5 1.1 fusion.94
  33.6 1.4 collective-permute-start.7
  35.2 4.0 collective-permute-start.4
  39.5 2.4 collective-permute-start.2
  41.9 1.5 collective-permute-start.1
  44.0 3.1 collective-permute-start.24
  47.2 2.0 collective-permute-start.25
  49.1 2.8 collective-permute-start.23
  51.9 4.3 collective-permute-start.22
  56.3 2.9 collective-permute-start.13
  59.3 1.8 bitcast_dynamic-update-slice_fusion.11
  61.1 5.8 %collective-permute-done.13 = bf16[2,65536]{1,0:T(2,128)(2,1)S(1)} collective-permute-done((bf16[2,65536]{1,0:T(2,128)(2,1)}, bf16[2,65536]{1,0:T(2,128)(2,1)S(1)}, u32[]{:S(2)}, u32[]{:S(2)}) %collective-permute-start.13) | collective-permute-done | bytes 262176 | tf_op jit(solution)/shard_map/ppermute | solution.py:17
  66.9 5.8 %collective-permute-start.14 = (bf16[2,65536]{1,0:T(2,128)(2,1)}, bf16[2,65536]{1,0:T(2,128)(2,1)S(1)}, u32[]{:S(2)}, u32[]{:S(2)}) collective-permute-start(bf16[2,65536]{1,0:T(2,128)(2,1)} %get-tuple-element.18), channel_id=1, source_target_pairs={{0,60},{1,61},{2,62},{3,63},{4,0},{5,1},{6,2},{7,3},{8,4},{9,5},{1... | collective-permute-start | bytes 786440 | tf_op jit(solution)/shard_map/ppermute | solution.py:17
  73.7 4.8 collective-permute-done.14
  78.5 8.0 %collective-permute-start.15 = (bf16[2,65536]{1,0:T(2,128)(2,1)S(1)}, bf16[2,65536]{1,0:T(2,128)(2,1)S(1)}, u32[]{:S(2)}, u32[]{:S(2)}) collective-permute-start(bf16[2,65536]{1,0:T(2,128)(2,1)S(1)} %copy-done.8), channel_id=1, source_target_pairs={{0,61},{1,62},{2,63},{3,0},{4,1},{5,2},{6,3},{7,4},{8,5},{9,6},{10... | collective-permute-start | bytes 786440 | tf_op jit(solution)/shard_map/ppermute | solution.py:17
  87.4 4.4 collective-permute-done.15
  91.8 5.7 %collective-permute-start.16 = (bf16[2,65536]{1,0:T(2,128)(2,1)S(1)}, bf16[2,65536]{1,0:T(2,128)(2,1)S(1)}, u32[]{:S(2)}, u32[]{:S(2)}) collective-permute-start(bf16[2,65536]{1,0:T(2,128)(2,1)S(1)} %copy-done.7), channel_id=1, source_target_pairs={{0,62},{1,63},{2,0},{3,1},{4,2},{5,3},{6,4},{7,5},{8,6},{9,7},{10,... | collective-permute-start | bytes 786440 | tf_op jit(solution)/shard_map/ppermute | solution.py:17
  98.3 2.8 collective-permute-done.16
  101.1 2.8 collective-permute-start.17
  104.9 2.1 collective-permute-done.17
  108.8 5.1 collective-permute-done.19
  114.7 10.9 %collective-permute-done.20 = bf16[2,65536]{1,0:T(2,128)(2,1)S(1)} collective-permute-done((bf16[2,65536]{1,0:T(2,128)(2,1)S(1)}, bf16[2,65536]{1,0:T(2,128)(2,1)S(1)}, u32[]{:S(2)}, u32[]{:S(2)}) %collective-permute-start.20) | collective-permute-done | bytes 262176 | tf_op jit(solution)/shard_map/ppermute | solution.py:17
  125.6 0.9 bitcast_dynamic-update-slice_fusion.3
  126.5 12.5 %collective-permute-done.21 = bf16[2,65536]{1,0:T(2,128)(2,1)S(1)} collective-permute-done((bf16[2,65536]{1,0:T(2,128)(2,1)S(1)}, bf16[2,65536]{1,0:T(2,128)(2,1)S(1)}, u32[]{:S(2)}, u32[]{:S(2)}) %collective-permute-start.21) | collective-permute-done | bytes 262176 | tf_op jit(solution)/shard_map/ppermute | solution.py:17
  141.7 3.3 reshape.148
  144.9 3.7 fusion
  148.7 7.2 %reshape.149 = f32[3,32,128,128]{3,2,1,0:T(8,128)} reshape(f32[24,65536]{1,0:T(8,128)} %fusion) | data formatting | bytes 12582912 | tf_op jit(solution)/shard_map/convert_element_type | solution.py:112
  155.9 4.0 fusion.25
  159.9 12.9 %fusion.19 = f32[3,32,128,128]{3,2,1,0:T(8,128)S(1)} fusion(f32[3,32,128,128]{3,1,2,0:T(8,128)S(1)} %fusion.25, f32[3,128,128,1]{2,0,1,3:T(4,128)S(1)} %fusion.43), kind=kOutput, calls=%fused_computation.21 | convolution fusion | flops 2415919104 | bytes 12779520 | tf_op jit(solution)/shard_map/vij,vxjz->vxiz/dot_general | solution.py:42
  172.8 10.4 %divide_convert_fusion.1 = bf16[3,32,128,128]{3,2,1,0:T(8,128)(2,1)S(1)} fusion(f32[3,32,128,128]{3,2,1,0:T(8,128)S(1)} %bitcast.121, f32[3,32,128,128]{3,2,1,0:T(8,128)S(1)} %fusion.19, f32[3,128,128,1]{2,0,1,3:T(4,128)S(1)} %copy-done.10), kind=kOutput, calls=%fused_computation.24 | convolution fusion | flops 2419064832 | bytes 15925248 | tf_op jit(solution)/shard_map/vxyj,vij->vxyi/dot_general | solution.py:43
  183.5 4.2 collective-permute-start.26
  187.7 4.0 collective-permute-start.27
  193.5 10.5 %collective-permute-done.26 = bf16[3,15,128,128]{3,2,1,0:T(8,128)(2,1)S(1)} collective-permute-done((bf16[3,15,128,128]{3,2,1,0:T(8,128)(2,1)S(1)}, bf16[3,15,128,128]{3,2,1,0:T(8,128)(2,1)S(1)}, u32[]{:S(2)}, u32[]{:S(2)}) %collective-permute-start.26) | collective-permute-done | bytes 1474592 | tf_op jit(solution)/shard_map/ppermute | solution.py:27
  204.0 4.4 collective-permute-done.27
  208.4 1.0 pad_maximum_fusion
  209.4 5.5 %fusion.17 = f32[3,32,128,128]{3,1,2,0:T(8,128)S(1)} fusion(bf16[3,62,128,128]{3,2,1,0:T(8,128)(2,1)S(1)} %pad_maximum_fusion, f32[3,32,62,1]{2,0,1,3:T(4,128)S(1)} %convolution_bitcast_fusion.1), kind=kOutput, calls=%fused_computation.19 | convolution fusion | flops 1170210816 | bytes 12410112 | tf_op jit(solution)/shard_map/vij,vjyz->viyz/dot_general | solution.py:116
  214.9 12.9 %fusion.15 = f32[3,32,128,128]{3,2,0,1:T(8,128)S(1)} fusion(f32[3,32,128,128]{3,1,2,0:T(8,128)S(1)} %fusion.17, f32[3,128,128]{2,0,1:T(4,128)S(1)} %fusion.34), kind=kOutput, calls=%fused_computation.17 | convolution fusion | flops 2415919104 | bytes 12779520 | tf_op jit(solution)/shard_map/vij,vxjz->vxiz/dot_general | solution.py:42
  227.8 11.5 %fusion.37 = f32[32,128,128]{2,1,0:T(8,128)} fusion(f32[3,32,128,128]{3,2,0,1:T(8,128)S(1)} %fusion.15, f32[3,128,128]{2,0,1:T(4,128)S(1)} %fusion.33), kind=kOutput, calls=%fused_computation.46 | convolution fusion | flops 2415919104 | bytes 8585216 | tf_op jit(solution)/shard_map/vxyj,vij->vxyi/dot_general | solution.py:43
  239.4 81.1 %all-reduce.3.cloned.1.call-done = f32[32,128,128]{2,1,0:T(8,128)} async-done(((f32[32,128,128]{2,1,0:T(8,128)}), f32[32,128,128]{2,1,0:T(8,128)}) %all-reduce.3.cloned.1.call-update) | async-done | bytes 2097168 | tf_op jit(solution)/shard_map/psum | solution.py:119
  320.5 1.9 fusion.49
  322.6 3.7 collective-permute-start.28
  326.3 1.9 collective-permute-start.29
  328.3 3.8 collective-permute-done.28
  332.1 4.4 collective-permute-done.29
  336.7 3.1 fusion.30
  339.9 13.1 %fusion.13 = f32[3,32,128,128]{3,2,1,0:T(8,128)S(1)} fusion(f32[3,32,128,128]{3,1,2,0:T(8,128)S(1)} %fusion.30, f32[3,128,128,1]{2,0,1,3:T(4,128)S(1)} %fusion.43), kind=kOutput, calls=%fused_computation.15 | convolution fusion | flops 2415919104 | bytes 12779520 | tf_op jit(solution)/shard_map/vij,vxjz->vxiz/dot_general | solution.py:42
  353.0 10.4 %divide_convert_fusion = bf16[3,32,128,128]{3,2,1,0:T(8,128)(2,1)S(1)} fusion(f32[3,32,128,128]{3,2,1,0:T(8,128)S(1)} %bitcast.123, f32[3,32,128,128]{3,2,1,0:T(8,128)S(1)} %fusion.13, f32[3,128,128,1]{2,0,1,3:T(4,128)S(1)} %copy-done.11), kind=kOutput, calls=%fused_computation.23 | convolution fusion | flops 2419064832 | bytes 15925248 | tf_op jit(solution)/shard_map/vxyj,vij->vxyi/dot_general | solution.py:43
  363.7 1.9 collective-permute-start.30
  365.7 2.5 collective-permute-start.31
  368.2 13.8 %collective-permute-done.30 = bf16[3,15,128,128]{3,2,1,0:T(8,128)(2,1)S(1)} collective-permute-done((bf16[3,15,128,128]{3,2,1,0:T(8,128)(2,1)S(1)}, bf16[3,15,128,128]{3,2,1,0:T(8,128)(2,1)S(1)}, u32[]{:S(2)}, u32[]{:S(2)}) %collective-permute-start.30) | collective-permute-done | bytes 1474592 | tf_op jit(solution)/shard_map/ppermute | solution.py:27
  381.9 4.4 collective-permute-done.31
  387.2 5.5 %fusion.11 = f32[3,32,128,128]{3,1,2,0:T(8,128)S(1)} fusion(bf16[3,62,128,128]{3,2,1,0:T(8,128)(2,1)S(1)} %pad_maximum_fusion.1, f32[3,32,62,1]{2,0,1,3:T(4,128)S(1)} %convolution_bitcast_fusion.1), kind=kOutput, calls=%fused_computation.13 | convolution fusion | flops 1170210816 | bytes 12410112 | tf_op jit(solution)/shard_map/vij,vjyz->viyz/dot_general | solution.py:116
  392.7 12.7 %fusion.9 = f32[3,32,128,128]{3,2,0,1:T(8,128)S(1)} fusion(f32[3,32,128,128]{3,1,2,0:T(8,128)S(1)} %fusion.11, f32[3,128,128]{2,0,1:T(4,128)S(1)} %fusion.34), kind=kOutput, calls=%fused_computation.11 | convolution fusion | flops 2415919104 | bytes 12779520 | tf_op jit(solution)/shard_map/vij,vxjz->vxiz/dot_general | solution.py:42
  405.4 11.6 %fusion.40 = f32[32,128,128]{2,1,0:T(8,128)} fusion(f32[3,32,128,128]{3,2,0,1:T(8,128)S(1)} %fusion.9, f32[3,128,128]{2,0,1:T(4,128)S(1)} %fusion.33), kind=kOutput, calls=%fused_computation.47 | convolution fusion | flops 2415919104 | bytes 8585216 | tf_op jit(solution)/shard_map/vxyj,vij->vxyi/dot_general | solution.py:43
  417.1 77.6 %all-reduce.5.cloned.1.call-done = f32[32,128,128]{2,1,0:T(8,128)} async-done(((f32[32,128,128]{2,1,0:T(8,128)}), f32[32,128,128]{2,1,0:T(8,128)}) %all-reduce.5.cloned.1.call-update) | async-done | bytes 2097168 | tf_op jit(solution)/shard_map/psum | solution.py:119
  494.7 4.1 multiply_multiply_fusion
  (102 shorter events, 18.6 us)
Async XLA Ops:
  6.5 314.0 %all-reduce.3.cloned.1.call-start = ((), (), s32[]{:S(2)}) async-start(), calls=%async_computation | async-start | bytes 4194304 | tf_op jit(solution)/shard_map/psum | solution.py:119
  8.2 25.4 %collective-permute-start.11 = (s32[2]{0:T(128)}, s32[2]{0:T(128)S(1)}, u32[]{:S(2)}, u32[]{:S(2)}) collective-permute-start(s32[2]{0:T(128)} %get-tuple-element.30), channel_id=1, source_target_pairs={{0,5},{1,6},{2,7},{3,8},{4,9},{5,10},{6,11},{7,12},{8,13},{9,14},{... | collective-permute-start | bytes 32 | tf_op jit(solution)/shard_map/ppermute | solution.py:17
  13.4 21.7 %collective-permute-start.10 = (s32[2]{0:T(128)}, s32[2]{0:T(128)S(1)}, u32[]{:S(2)}, u32[]{:S(2)}) collective-permute-start(s32[2]{0:T(128)} %get-tuple-element.31), channel_id=1, source_target_pairs={{0,4},{1,5},{2,6},{3,7},{4,8},{5,9},{6,10},{7,11},{8,12},{9,13},{1... | collective-permute-start | bytes 32 | tf_op jit(solution)/shard_map/ppermute | solution.py:17
  14.0 21.1 %collective-permute-start.9 = (s32[2]{0:T(128)}, s32[2]{0:T(128)S(1)}, u32[]{:S(2)}, u32[]{:S(2)}) collective-permute-start(s32[2]{0:T(128)} %get-tuple-element.32), channel_id=1, source_target_pairs={{0,3},{1,4},{2,5},{3,6},{4,7},{5,8},{6,9},{7,10},{8,11},{9,12},{10... | collective-permute-start | bytes 32 | tf_op jit(solution)/shard_map/ppermute | solution.py:17
  17.1 18.0 %collective-permute-start.8 = (s32[2]{0:T(128)}, s32[2]{0:T(128)S(1)}, u32[]{:S(2)}, u32[]{:S(2)}) collective-permute-start(s32[2]{0:T(128)} %get-tuple-element.33), channel_id=1, source_target_pairs={{0,2},{1,3},{2,4},{3,5},{4,6},{5,7},{6,8},{7,9},{8,10},{9,11},{10,... | collective-permute-start | bytes 32 | tf_op jit(solution)/shard_map/ppermute | solution.py:17
  22.2 5.7 %copy-start.9 = (f32[3,3,31]{2,1,0:T(4,128)S(1)}, f32[3,3,31]{2,1,0:T(4,128)}, u32[]{:S(2)}) copy-start(f32[3,3,31]{2,1,0:T(4,128)} %param.7) | copy-start | bytes 3352
  22.2 8.1 %copy-start = (f32[32,128,128]{2,1,0:T(8,128)S(1)}, f32[32,128,128]{2,1,0:T(8,128)}, u32[]{:S(2)}) copy-start(f32[32,128,128]{2,1,0:T(8,128)} %param.4) | copy-start | bytes 6291460
  25.8 30.6 %collective-permute-start.12 = (bf16[2,65536]{1,0:T(2,128)(2,1)}, bf16[2,65536]{1,0:T(2,128)(2,1)}, u32[]{:S(2)}, u32[]{:S(2)}) collective-permute-start(bf16[2,65536]{1,0:T(2,128)(2,1)} %get-tuple-element.20), channel_id=1, source_target_pairs={{0,58},{1,59},{2,60},{3,61},{4,62},{5,63},{6,0},{7,1},{8,2},{9,3},... | collective-permute-start | bytes 786440 | tf_op jit(solution)/shard_map/ppermute | solution.py:17
  31.5 1.0 copy-start.2
  31.5 46.9 %copy-start.8 = (bf16[2,65536]{1,0:T(2,128)(2,1)S(1)}, bf16[2,65536]{1,0:T(2,128)(2,1)}, u32[]{:S(2)}) copy-start(bf16[2,65536]{1,0:T(2,128)(2,1)} %get-tuple-element.17) | copy-start | bytes 786436
  31.5 60.2 %copy-start.7 = (bf16[2,65536]{1,0:T(2,128)(2,1)S(1)}, bf16[2,65536]{1,0:T(2,128)(2,1)}, u32[]{:S(2)}) copy-start(bf16[2,65536]{1,0:T(2,128)(2,1)} %get-tuple-element.16) | copy-start | bytes 786436
  31.6 69.6 %copy-start.6 = (bf16[2,65536]{1,0:T(2,128)(2,1)S(1)}, bf16[2,65536]{1,0:T(2,128)(2,1)}, u32[]{:S(2)}) copy-start(bf16[2,65536]{1,0:T(2,128)(2,1)} %get-tuple-element.15) | copy-start | bytes 786436
  31.6 75.4 %copy-start.5 = (bf16[2,65536]{1,0:T(2,128)(2,1)S(1)}, bf16[2,65536]{1,0:T(2,128)(2,1)}, u32[]{:S(2)}) copy-start(bf16[2,65536]{1,0:T(2,128)(2,1)} %get-tuple-element.14) | copy-start | bytes 786436
  31.6 76.3 %copy-start.4 = (bf16[2,65536]{1,0:T(2,128)(2,1)S(1)}, bf16[2,65536]{1,0:T(2,128)(2,1)}, u32[]{:S(2)}) copy-start(bf16[2,65536]{1,0:T(2,128)(2,1)} %get-tuple-element.13) | copy-start | bytes 786436
  33.6 5.5 %collective-permute-start.7 = (s32[2]{0:T(128)S(1)}, s32[2]{0:T(128)S(1)}, u32[]{:S(2)}, u32[]{:S(2)}) collective-permute-start(s32[2]{0:T(128)S(1)} %get-tuple-element.34), channel_id=1, source_target_pairs={{0,1},{1,2},{2,3},{3,4},{4,5},{5,6},{6,7},{7,8},{8,9},{9,10},{10,1... | collective-permute-start | bytes 32 | tf_op jit(solution)/shard_map/ppermute | solution.py:17
  35.0 4.4 collective-permute-start.6
  35.1 6.8 %collective-permute-start.5 = (s32[2]{0:T(128)S(1)}, s32[2]{0:T(128)S(1)}, u32[]{:S(2)}, u32[]{:S(2)}) collective-permute-start(s32[2]{0:T(128)S(1)} %get-tuple-element.36), channel_id=1, source_target_pairs={{0,63},{1,0},{2,1},{3,2},{4,3},{5,4},{6,5},{7,6},{8,7},{9,8},{10,9... | collective-permute-start | bytes 32 | tf_op jit(solution)/shard_map/ppermute | solution.py:17
  35.2 8.2 %collective-permute-start.4 = (s32[2]{0:T(128)S(1)}, s32[2]{0:T(128)S(1)}, u32[]{:S(2)}, u32[]{:S(2)}) collective-permute-start(s32[2]{0:T(128)S(1)} %get-tuple-element.37), channel_id=1, source_target_pairs={{0,62},{1,63},{2,0},{3,1},{4,2},{5,3},{6,4},{7,5},{8,6},{9,7},{10,... | collective-permute-start | bytes 32 | tf_op jit(solution)/shard_map/ppermute | solution.py:17
  39.1 4.9 collective-permute-start.3
  39.5 7.7 %collective-permute-start.2 = (s32[2]{0:T(128)S(1)}, s32[2]{0:T(128)S(1)}, u32[]{:S(2)}, u32[]{:S(2)}) collective-permute-start(s32[2]{0:T(128)S(1)} %get-tuple-element.39), channel_id=1, source_target_pairs={{0,60},{1,61},{2,62},{3,63},{4,0},{5,1},{6,2},{7,3},{8,4},{9,5},{1... | collective-permute-start | bytes 32 | tf_op jit(solution)/shard_map/ppermute | solution.py:17
  41.9 7.3 %collective-permute-start.1 = (s32[2]{0:T(128)S(1)}, s32[2]{0:T(128)S(1)}, u32[]{:S(2)}, u32[]{:S(2)}) collective-permute-start(s32[2]{0:T(128)S(1)} %get-tuple-element.40), channel_id=1, source_target_pairs={{0,59},{1,60},{2,61},{3,62},{4,63},{5,0},{6,1},{7,2},{8,3},{9,4},{... | collective-permute-start | bytes 32 | tf_op jit(solution)/shard_map/ppermute | solution.py:17
  43.4 8.5 %collective-permute-start = (s32[2]{0:T(128)S(1)}, s32[2]{0:T(128)S(1)}, u32[]{:S(2)}, u32[]{:S(2)}) collective-permute-start(s32[2]{0:T(128)S(1)} %get-tuple-element.41), channel_id=1, source_target_pairs={{0,58},{1,59},{2,60},{3,61},{4,62},{5,63},{6,0},{7,1},{8,2},{9,3},... | collective-permute-start | bytes 32 | tf_op jit(solution)/shard_map/ppermute | solution.py:17
  44.0 111.9 %collective-permute-start.24 = (bf16[15,128,128]{2,0,1:T(8,128)(2,1)}, bf16[15,128,128]{2,0,1:T(8,128)(2,1)}, u32[]{:S(2)}, u32[]{:S(2)}) collective-permute-start(bf16[15,128,128]{2,0,1:T(8,128)(2,1)} %get-tuple-element.23), channel_id=1, source_target_pairs={{0,1},{1,2},{2,3},{3,4},{4,5},{5,6},{6,7},{7,8},{8,9},{9,10},{10,1... | collective-permute-start | bytes 1474568 | tf_op jit(solution)/shard_map/ppermute | solution.py:27
  47.2 108.7 %collective-permute-start.25 = (bf16[15,128,128]{2,0,1:T(8,128)(2,1)}, bf16[15,128,128]{2,0,1:T(8,128)(2,1)}, u32[]{:S(2)}, u32[]{:S(2)}) collective-permute-start(bf16[15,128,128]{2,0,1:T(8,128)(2,1)} %get-tuple-element.24), channel_id=1, source_target_pairs={{1,0},{2,1},{3,2},{4,3},{5,4},{6,5},{7,6},{8,7},{9,8},{10,9},{11,1... | collective-permute-start | bytes 1474568 | tf_op jit(solution)/shard_map/ppermute | solution.py:28
  49.1 91.6 %collective-permute-start.23 = (bf16[2,65536]{1,0:T(2,128)(2,1)S(1)}, bf16[2,65536]{1,0:T(2,128)(2,1)S(1)}, u32[]{:S(2)}, u32[]{:S(2)}) collective-permute-start(bf16[2,65536]{1,0:T(2,128)(2,1)S(1)} %get-tuple-element.9), channel_id=1, source_target_pairs={{0,5},{1,6},{2,7},{3,8},{4,9},{5,10},{6,11},{7,12},{8,13},{9,14},{... | collective-permute-start | bytes 786440 | tf_op jit(solution)/shard_map/ppermute | solution.py:17
  51.9 87.9 %collective-permute-start.22 = (bf16[2,65536]{1,0:T(2,128)(2,1)S(1)}, bf16[2,65536]{1,0:T(2,128)(2,1)S(1)}, u32[]{:S(2)}, u32[]{:S(2)}) collective-permute-start(bf16[2,65536]{1,0:T(2,128)(2,1)S(1)} %get-tuple-element.10), channel_id=1, source_target_pairs={{0,4},{1,5},{2,6},{3,7},{4,8},{5,9},{6,10},{7,11},{8,12},{9,13},{1... | collective-permute-start | bytes 786440 | tf_op jit(solution)/shard_map/ppermute | solution.py:17
  56.3 10.6 %collective-permute-start.13 = (bf16[2,65536]{1,0:T(2,128)(2,1)}, bf16[2,65536]{1,0:T(2,128)(2,1)S(1)}, u32[]{:S(2)}, u32[]{:S(2)}) collective-permute-start(bf16[2,65536]{1,0:T(2,128)(2,1)} %get-tuple-element.19), channel_id=1, source_target_pairs={{0,59},{1,60},{2,61},{3,62},{4,63},{5,0},{6,1},{7,2},{8,3},{9,4},{... | collective-permute-start | bytes 786440 | tf_op jit(solution)/shard_map/ppermute | solution.py:17
  66.9 11.5 %collective-permute-start.14 = (bf16[2,65536]{1,0:T(2,128)(2,1)}, bf16[2,65536]{1,0:T(2,128)(2,1)S(1)}, u32[]{:S(2)}, u32[]{:S(2)}) collective-permute-start(bf16[2,65536]{1,0:T(2,128)(2,1)} %get-tuple-element.18), channel_id=1, source_target_pairs={{0,60},{1,61},{2,62},{3,63},{4,0},{5,1},{6,2},{7,3},{8,4},{9,5},{1... | collective-permute-start | bytes 786440 | tf_op jit(solution)/shard_map/ppermute | solution.py:17
  78.5 13.3 %collective-permute-start.15 = (bf16[2,65536]{1,0:T(2,128)(2,1)S(1)}, bf16[2,65536]{1,0:T(2,128)(2,1)S(1)}, u32[]{:S(2)}, u32[]{:S(2)}) collective-permute-start(bf16[2,65536]{1,0:T(2,128)(2,1)S(1)} %copy-done.8), channel_id=1, source_target_pairs={{0,61},{1,62},{2,63},{3,0},{4,1},{5,2},{6,3},{7,4},{8,5},{9,6},{10... | collective-permute-start | bytes 786440 | tf_op jit(solution)/shard_map/ppermute | solution.py:17
  91.8 9.4 %collective-permute-start.16 = (bf16[2,65536]{1,0:T(2,128)(2,1)S(1)}, bf16[2,65536]{1,0:T(2,128)(2,1)S(1)}, u32[]{:S(2)}, u32[]{:S(2)}) collective-permute-start(bf16[2,65536]{1,0:T(2,128)(2,1)S(1)} %copy-done.7), channel_id=1, source_target_pairs={{0,62},{1,63},{2,0},{3,1},{4,2},{5,3},{6,4},{7,5},{8,6},{9,7},{10,... | collective-permute-start | bytes 786440 | tf_op jit(solution)/shard_map/ppermute | solution.py:17
  101.1 5.8 %collective-permute-start.17 = (bf16[2,65536]{1,0:T(2,128)(2,1)S(1)}, bf16[2,65536]{1,0:T(2,128)(2,1)S(1)}, u32[]{:S(2)}, u32[]{:S(2)}) collective-permute-start(bf16[2,65536]{1,0:T(2,128)(2,1)S(1)} %copy-done.6), channel_id=1, source_target_pairs={{0,63},{1,0},{2,1},{3,2},{4,3},{5,4},{6,5},{7,6},{8,7},{9,8},{10,9... | collective-permute-start | bytes 786440 | tf_op jit(solution)/shard_map/ppermute | solution.py:17
  106.9 0.9 collective-permute-start.18
  107.9 5.9 %collective-permute-start.19 = (bf16[2,65536]{1,0:T(2,128)(2,1)S(1)}, bf16[2,65536]{1,0:T(2,128)(2,1)S(1)}, u32[]{:S(2)}, u32[]{:S(2)}) collective-permute-start(bf16[2,65536]{1,0:T(2,128)(2,1)S(1)} %copy-done.4), channel_id=1, source_target_pairs={{0,1},{1,2},{2,3},{3,4},{4,5},{5,6},{6,7},{7,8},{8,9},{9,10},{10,1... | collective-permute-start | bytes 786440 | tf_op jit(solution)/shard_map/ppermute | solution.py:17
  113.8 11.8 %collective-permute-start.20 = (bf16[2,65536]{1,0:T(2,128)(2,1)S(1)}, bf16[2,65536]{1,0:T(2,128)(2,1)S(1)}, u32[]{:S(2)}, u32[]{:S(2)}) collective-permute-start(bf16[2,65536]{1,0:T(2,128)(2,1)S(1)} %get-tuple-element.12), channel_id=1, source_target_pairs={{0,2},{1,3},{2,4},{3,5},{4,6},{5,7},{6,8},{7,9},{8,10},{9,11},{10,... | collective-permute-start | bytes 786440 | tf_op jit(solution)/shard_map/ppermute | solution.py:17
  125.6 13.4 %collective-permute-start.21 = (bf16[2,65536]{1,0:T(2,128)(2,1)S(1)}, bf16[2,65536]{1,0:T(2,128)(2,1)S(1)}, u32[]{:S(2)}, u32[]{:S(2)}) collective-permute-start(bf16[2,65536]{1,0:T(2,128)(2,1)S(1)} %get-tuple-element.11), channel_id=1, source_target_pairs={{0,3},{1,4},{2,5},{3,6},{4,7},{5,8},{6,9},{7,10},{8,11},{9,12},{10... | collective-permute-start | bytes 786440 | tf_op jit(solution)/shard_map/ppermute | solution.py:17
  148.7 7.3 %copy-start.3 = (bf16[32,128,128]{2,0,1:T(8,128)(2,1)S(1)}, bf16[32,128,128]{2,0,1:T(8,128)(2,1)}, u32[]{:S(2)}) copy-start(bf16[32,128,128]{2,0,1:T(8,128)(2,1)} %copy-done.2) | copy-start | bytes 3145732
  155.9 16.9 %slice-start = ((s8[6291456]{0:T(1024)(128)(4,1)}), s8[4194304]{0:T(1024)(128)(4,1)S(1)}, s32[]{:S(2)}) async-start(s8[6291456]{0:T(1024)(128)(4,1)} %bitcast.120), calls=%async_computation.2 | async-start | bytes 8388608
  159.9 12.9 %slice-start.1 = ((s8[6291456]{0:T(1024)(128)(4,1)}), s8[2097152]{0:T(1024)(128)(4,1)S(1)}, s32[]{:S(2)}) async-start(s8[6291456]{0:T(1024)(128)(4,1)} %bitcast.120), calls=%async_computation.3 | async-start | bytes 4194304
  159.9 12.9 %copy-start.10 = (f32[3,128,128,1]{2,0,1,3:T(4,128)S(1)}, f32[3,128,128,1]{2,0,1,3:T(4,128)}, u32[]{:S(2)}) copy-start(f32[3,128,128,1]{2,0,1,3:T(4,128)} %fusion.44) | copy-start | bytes 589828
  183.5 20.5 %collective-permute-start.26 = (bf16[3,15,128,128]{3,2,1,0:T(8,128)(2,1)S(1)}, bf16[3,15,128,128]{3,2,1,0:T(8,128)(2,1)S(1)}, u32[]{:S(2)}, u32[]{:S(2)}) collective-permute-start(bf16[3,15,128,128]{3,2,1,0:T(8,128)(2,1)S(1)} %get-tuple-element.7), channel_id=1, source_target_pairs={{0,1},{1,2},{2,3},{3,4},{4,5},{5,6},{6,7},{7,8},{8,9},{9,10},{10,1... | collective-permute-start | bytes 4423688 | tf_op jit(solution)/shard_map/ppermute | solution.py:27
  187.7 20.7 %collective-permute-start.27 = (bf16[3,15,128,128]{3,2,1,0:T(8,128)(2,1)S(1)}, bf16[3,15,128,128]{3,2,1,0:T(8,128)(2,1)S(1)}, u32[]{:S(2)}, u32[]{:S(2)}) collective-permute-start(bf16[3,15,128,128]{3,2,1,0:T(8,128)(2,1)S(1)} %get-tuple-element.8), channel_id=1, source_target_pairs={{1,0},{2,1},{3,2},{4,3},{5,4},{6,5},{7,6},{8,7},{9,8},{10,9},{11,1... | collective-permute-start | bytes 4423688 | tf_op jit(solution)/shard_map/ppermute | solution.py:28
  239.3 81.2 %copy-start.1 = (f32[32,128,128]{2,1,0:T(8,128)S(1)}, f32[32,128,128]{2,1,0:T(8,128)}, u32[]{:S(2)}) copy-start(f32[32,128,128]{2,1,0:T(8,128)} %param.4) | copy-start | bytes 6291460
  239.3 255.3 %all-reduce.5.cloned.1.call-start = ((), (), s32[]{:S(2)}) async-start(), calls=%async_computation.1 | async-start | bytes 4194304 | tf_op jit(solution)/shard_map/psum | solution.py:119
  322.6 9.5 %collective-permute-start.28 = (bf16[15,128,128]{2,1,0:T(8,128)(2,1)S(1)}, bf16[15,128,128]{2,1,0:T(8,128)(2,1)S(1)}, u32[]{:S(2)}, u32[]{:S(2)}) collective-permute-start(bf16[15,128,128]{2,1,0:T(8,128)(2,1)S(1)} %get-tuple-element.21), channel_id=1, source_target_pairs={{0,1},{1,2},{2,3},{3,4},{4,5},{5,6},{6,7},{7,8},{8,9},{9,10},{10,1... | collective-permute-start | bytes 1474568 | tf_op jit(solution)/shard_map/ppermute | solution.py:27
  326.3 10.1 %collective-permute-start.29 = (bf16[15,128,128]{2,1,0:T(8,128)(2,1)S(1)}, bf16[15,128,128]{2,1,0:T(8,128)(2,1)S(1)}, u32[]{:S(2)}, u32[]{:S(2)}) collective-permute-start(bf16[15,128,128]{2,1,0:T(8,128)(2,1)S(1)} %get-tuple-element.22), channel_id=1, source_target_pairs={{1,0},{2,1},{3,2},{4,3},{5,4},{6,5},{7,6},{8,7},{9,8},{10,9},{11,1... | collective-permute-start | bytes 1474568 | tf_op jit(solution)/shard_map/ppermute | solution.py:28
  336.7 16.3 %slice-start.2 = ((s8[6291456]{0:T(1024)(128)(4,1)}), s8[4194304]{0:T(1024)(128)(4,1)S(1)}, s32[]{:S(2)}) async-start(s8[6291456]{0:T(1024)(128)(4,1)} %bitcast.122), calls=%async_computation.4 | async-start | bytes 8388608
  339.9 13.1 %slice-start.3 = ((s8[6291456]{0:T(1024)(128)(4,1)}), s8[2097152]{0:T(1024)(128)(4,1)S(1)}, s32[]{:S(2)}) async-start(s8[6291456]{0:T(1024)(128)(4,1)} %bitcast.122), calls=%async_computation.5 | async-start | bytes 4194304
  339.9 13.1 %copy-start.11 = (f32[3,128,128,1]{2,0,1,3:T(4,128)S(1)}, f32[3,128,128,1]{2,0,1,3:T(4,128)}, u32[]{:S(2)}) copy-start(f32[3,128,128,1]{2,0,1,3:T(4,128)} %fusion.44) | copy-start | bytes 589828
  363.7 18.2 %collective-permute-start.30 = (bf16[3,15,128,128]{3,2,1,0:T(8,128)(2,1)S(1)}, bf16[3,15,128,128]{3,2,1,0:T(8,128)(2,1)S(1)}, u32[]{:S(2)}, u32[]{:S(2)}) collective-permute-start(bf16[3,15,128,128]{3,2,1,0:T(8,128)(2,1)S(1)} %get-tuple-element.5), channel_id=1, source_target_pairs={{0,1},{1,2},{2,3},{3,4},{4,5},{5,6},{6,7},{7,8},{8,9},{9,10},{10,1... | collective-permute-start | bytes 4423688 | tf_op jit(solution)/shard_map/ppermute | solution.py:27
  365.7 20.7 %collective-permute-start.31 = (bf16[3,15,128,128]{3,2,1,0:T(8,128)(2,1)S(1)}, bf16[3,15,128,128]{3,2,1,0:T(8,128)(2,1)S(1)}, u32[]{:S(2)}, u32[]{:S(2)}) collective-permute-start(bf16[3,15,128,128]{3,2,1,0:T(8,128)(2,1)S(1)} %get-tuple-element.6), channel_id=1, source_target_pairs={{1,0},{2,1},{3,2},{4,3},{5,4},{6,5},{7,6},{8,7},{9,8},{10,9},{11,1... | collective-permute-start | bytes 4423688 | tf_op jit(solution)/shard_map/ppermute | solution.py:28
Sparse Core Ops, SparseCore 0:
  239.5 81.0 all-reduce.2
  417.2 77.4 all-reduce.4
where the time goes:
time: 515 us; the launch traced here: 506 us
  waiting for transfers between devices  248 us (48%)
  matrix products  123 us (24%)
  starting transfers between devices  77.8 us (15%)
  local copies, waits for them, and re-layouts  34.2 us (7%)
  between operations  14.4 us (3%)
  other arithmetic  8.71 us (2%)
    psum x2, waiting for transfers between devices, shards(): total = lax.psum(partial_sum, 'view')  159 us
    ppermute x24, starting transfers between devices, passed_along(): lax.ppermute(shard, axis, [(i, (i + by) % length) for i in range(length)])  54.4 us
    dot_general x4, matrix products, pass_yz(): jnp.einsum('vij,vxjz->vxiz', along_y, volume, precision=lax.Precision.HIG...  51.6 us
    ppermute x24, waiting for transfers between devices, passed_along(): lax.ppermute(shard, axis, [(i, (i + by) % length) for i in range(length)])  48.4 us
    dot_general x4, matrix products, pass_yz(): jnp.einsum('vxyj,vij->vxyi', volume, along_z, precision=lax.Precision.HIG...  44 us
    ppermute x4, waiting for transfers between devices, extended(): before = lax.ppermute(last, axis, up)  28.1 us
    unnamed x45, local copies, waits for them, and re-layouts  13.3 us
    ppermute x4, waiting for transfers between devices, extended(): after = lax.ppermute(first, axis, down)  13.2 us
  transfers between devices with their start and end apart: 34, of which 16 were waited for; matrix products, arithmetic and copies ran while one was open for 8% of the time, Pallas kernels for 0%

commit v1 on v0

v1 whole, which is shorter than its diff:
```python
import functools

import jax
import jax.numpy as jnp
from jax import lax
from jax.experimental import pallas as pl
from jax.experimental.pallas import tpu as pltpu
from jax.sharding import PartitionSpec as P

TAPS = 31
HALF = TAPS // 2
BX = 32
HX = 16
EX = BX + 2 * HX
Y = 128
Z = 128
VIEWS_DEV = 3
ITERS = 2
CAP = 2
SPAN = 12
TP = 4
SLOTS = SPAN * CAP
TROWS = TP * Y
PROWS = CAP * TROWS + 16
SUB = 16
F32 = jnp.float32
BF16 = jnp.bfloat16
VMEM_LIMIT = 56 << 20


def banded(kernel, rows, cols, sign, offset):
    row_idx = jnp.arange(rows)[:, None]
    col_idx = jnp.arange(cols)[None, :]
    lag = sign * (col_idx - row_idx) + offset
    hits = (lag[:, :, None] == jnp.arange(kernel.shape[-1])[None, None, :]).astype(F32)
    return jnp.einsum("vt,ijt->vij", kernel, hits, precision=lax.Precision.HIGHEST)


def rounded(value):
    return lax.reduce_precision(value, 8, 7)


def two_terms(matrix, axis):
    high = rounded(matrix)
    return jnp.concatenate([high, matrix - high], axis=axis).astype(BF16)


def blur_matrices(kernels):
    taps_x = rounded(kernels[:, 0])
    taps_y = kernels[:, 1] * (jnp.sum(kernels[:, 0], -1) / jnp.sum(taps_x, -1))[:, None]
    taps_z = kernels[:, 2]
    small = banded(taps_x, BX, EX, 1, -1)
    eye = jnp.eye(SUB, dtype=F32)
    fwd_x = (small[:, :, None, :, None] * eye[None, None, :, None, :]).reshape(
        VIEWS_DEV * BX * SUB, EX * SUB
    )
    flipped = jnp.transpose(small, (2, 0, 1))
    back_x = (flipped[:, None, :, :, None] * eye[None, :, None, None, :]).reshape(
        EX * SUB, VIEWS_DEV * BX * SUB
    )
    y_fwd = banded(taps_y, Y, Y, 1, HALF)
    y_back = banded(taps_y, Y, Y, -1, HALF)
    z_fwd = banded(taps_z, Z, Z, -1, HALF)
    z_back = banded(taps_z, Z, Z, 1, HALF)
    return (
        (fwd_x.astype(BF16), two_terms(y_fwd, 2), two_terms(z_fwd, 1)),
        (back_x.astype(BF16), two_terms(y_back, 2), two_terms(z_back, 1)),
    )


def pack_kernel(me_ref, dest_ref, tiles_ref, *refs):
    outs, (order_ref, count_ref) = refs[:SPAN], refs[SPAN:]
    me = me_ref[0]
    for k in range(SPAN):
        count_ref[k] = 0
    for n in range(SLOTS):
        step = lax.rem(dest_ref[n, 0] - me + SPAN // 2 + 64, 64)
        rank = count_ref[step]
        count_ref[step] = rank + 1
        order_ref[step * CAP + rank] = n
    for k in range(SPAN):
        codes = []
        for c in range(CAP):
            n = order_ref[k * CAP + c]
            outs[k][c * TROWS : (c + 1) * TROWS, :] = tiles_ref[n]
            code = dest_ref[n, 1] * (BX // TP) + dest_ref[n, 2]
            codes.append(jnp.full((8, Z), code, jnp.int32).astype(F32))
        outs[k][CAP * TROWS :, :] = jnp.concatenate(codes, axis=0).astype(BF16)


def pack_tiles(view_tiles, tile_dest):
    me = lax.axis_index("block").astype(jnp.int32).reshape(1)
    return pl.pallas_call(
        pack_kernel,
        out_shape=[jax.ShapeDtypeStruct((PROWS, Z), BF16)] * SPAN,
        in_specs=[
            pl.BlockSpec(memory_space=pltpu.SMEM),
            pl.BlockSpec(memory_space=pltpu.SMEM),
            pl.BlockSpec(memory_space=pltpu.VMEM),
        ],
        out_specs=[pl.BlockSpec(memory_space=pltpu.VMEM)] * SPAN,
        scratch_shapes=[pltpu.SMEM((SLOTS,), jnp.int32), pltpu.SMEM((SPAN,), jnp.int32)],
        compiler_params=pltpu.CompilerParams(vmem_limit_bytes=VMEM_LIMIT),
        cost_estimate=pl.CostEstimate(flops=0, bytes_accessed=2 * SLOTS * TROWS * Z * 2, transcendentals=0),
        name="pack_tiles",
    )(me, tile_dest[0], view_tiles.reshape(SLOTS, TROWS, Z))


def side_by_side(ref, y0):
    planes = ref.shape[0]
    return jnp.concatenate(
        [ref[:, pl.ds(y0 + h * SUB, SUB), :].reshape(planes * SUB, Z) for h in range(2)], axis=1
    )


def blur_into(kx_ref, ky_ref, kz_ref, parts, half_ref, out_ref):
    def along_x(t, carry):
        y0 = pl.multiple_of(t * 2 * SUB, 2 * SUB)
        data = jnp.concatenate([side_by_side(ref, y0) for ref in parts], axis=0)
        for v in range(VIEWS_DEV):
            rows = slice(v * BX * SUB, (v + 1) * BX * SUB)
            got = jnp.dot(kx_ref[rows, :], data, preferred_element_type=F32).astype(BF16)
            for h in range(2):
                half_ref[v * BX : (v + 1) * BX, pl.ds(y0 + h * SUB, SUB), :] = got[
                    :, h * Z : (h + 1) * Z
                ].reshape(BX, SUB, Z)
        return carry

    lax.fori_loop(0, Y // (2 * SUB), along_x, 0)

    def along_yz(q, carry):
        v = q // (BX // TP)
        planes = [half_ref[q * TP + i] for i in range(TP)]
        outs = []
        for i in range(0, TP, 2):
            pair = jnp.concatenate(planes[i : i + 2], axis=1)
            got = jnp.dot(
                ky_ref[v], jnp.concatenate([pair, pair], axis=0), preferred_element_type=F32
            ).astype(BF16)
            outs += [got[:, :Z], got[:, Z:]]
        rows = jnp.concatenate(outs, axis=0)
        out_ref[q] = jnp.dot(
            jnp.concatenate([rows, rows], axis=1), kz_ref[v], preferred_element_type=F32
        )
        return carry

    lax.fori_loop(0, VIEWS_DEV * BX // TP, along_yz, 0)


def back_from(kx_ref, ky_ref, kz_ref, measured_ref, blurred_ref, half_ref, outs):
    def along_zy(q, carry):
        v = q // (BX // TP)
        ratio = (measured_ref[q].astype(F32) / blurred_ref[q]).astype(BF16)
        rows = jnp.dot(
            jnp.concatenate([ratio, ratio], axis=1), kz_ref[v], preferred_element_type=F32
        ).astype(BF16)
        for i in range(0, TP, 2):
            pair = jnp.concatenate([rows[(i + j) * Y : (i + j + 1) * Y] for j in range(2)], axis=1)
            got = jnp.dot(
                ky_ref[v], jnp.concatenate([pair, pair], axis=0), preferred_element_type=F32
            )
            high = got.astype(BF16)
            low = (got - high.astype(F32)).astype(BF16)
            for j in range(2):
                half_ref[0, q * TP + i + j] = high[:, j * Z : (j + 1) * Z]
                half_ref[1, q * TP + i + j] = low[:, j * Z : (j + 1) * Z]
        return carry

    lax.fori_loop(0, VIEWS_DEV * BX // TP, along_zy, 0)

    def along_x(t, carry):
        y0 = pl.multiple_of(t * 2 * SUB, 2 * SUB)
        high = side_by_side(half_ref.at[0], y0)
        low = side_by_side(half_ref.at[1], y0)
        first = 0
        for ref in outs:
            count = ref.shape[0]
            taps = kx_ref[first * SUB : (first + count) * SUB, :]
            got = jnp.dot(taps, high, preferred_element_type=F32)
            got += jnp.dot(taps, low, preferred_element_type=F32)
            for h in range(2):
                ref[:, pl.ds(y0 + h * SUB, SUB), :] = got[:, h * Z : (h + 1) * Z].reshape(
                    count, SUB, Z
                )
            first += count
        return carry

    lax.fori_loop(0, Y // (2 * SUB), along_x, 0)


def first_blur_kernel(kx_ref, ky_ref, kz_ref, left_ref, mid_ref, right_ref, out_ref, half_ref):
    blur_into(kx_ref, ky_ref, kz_ref, (left_ref, mid_ref, right_ref), half_ref, out_ref)


def first_back_kernel(kx_ref, ky_ref, kz_ref, blurred_ref, *refs):
    tiles = refs[:SPAN]
    left_ref, mid_ref, right_ref, measured_ref, half_ref = refs[SPAN:]
    for k in range(SPAN):
        for c in range(CAP):
            code = tiles[k][CAP * TROWS :, :].astype(F32)[8 * c, 0].astype(jnp.int32)
            measured_ref[code] = tiles[k][c * TROWS : (c + 1) * TROWS, :]
    back_from(
        kx_ref, ky_ref, kz_ref, measured_ref, blurred_ref, half_ref, (left_ref, mid_ref, right_ref)
    )


def sweep_kernel(*refs):
    fwd, back, parts = refs[0:3], refs[3:6], refs[6:9]
    measured_ref = refs[9]
    outs = refs[10:13]
    half_ref, back_half_ref, blurred_ref = refs[13:]
    blur_into(*fwd, parts, half_ref, blurred_ref)
    back_from(*back, measured_ref, blurred_ref, back_half_ref, outs)


VM = pl.BlockSpec(memory_space=pltpu.VMEM)
BLURRED = (VIEWS_DEV * BX // TP, TROWS, Z)
HALF_SHAPE = (VIEWS_DEV * BX, Y, Z)
CONTRIB = [jax.ShapeDtypeStruct((n, Y, Z), F32) for n in (HX, BX, HX)]


def call(kernel, name, operands, out_shape, scratch, flops):
    return pl.pallas_call(
        kernel,
        out_shape=out_shape,
        in_specs=[VM] * len(operands),
        out_specs=jax.tree.map(lambda _: VM, out_shape),
        scratch_shapes=scratch,
        compiler_params=pltpu.CompilerParams(vmem_limit_bytes=VMEM_LIMIT),
        cost_estimate=pl.CostEstimate(flops=flops, bytes_accessed=12 << 20, transcendentals=0),
        name=name,
    )(*operands)


def neighbours(low, high):
    size = lax.axis_size("block")
    up = [(i, i + 1) for i in range(size - 1)]
    down = [(j, i) for i, j in up]
    return lax.ppermute(high, "block", up), lax.ppermute(low, "block", down)


def with_halo(estimate):
    planes = estimate.astype(BF16)
    left, right = neighbours(planes[:HX], planes[HX:])
    return left, planes, right


def updated(estimate, contributions, view_count):
    left, mid, right = contributions
    from_left, from_right = neighbours(left, right)
    partial = mid + jnp.concatenate([from_left, from_right], axis=0)
    other = lax.ppermute(partial, "view", [(0, 1), (1, 0)])
    return estimate * (partial + other) / view_count


def shards(estimate, view_tiles, tile_dest, psf_taps):
    kernels = psf_taps / jnp.sum(psf_taps, axis=-1, keepdims=True)
    view_count = kernels.shape[0] * lax.axis_size("view")
    blocks = lax.axis_size("block")
    packed = pack_tiles(view_tiles, tile_dest)
    arrived = []
    for k in range(SPAN):
        by = k - SPAN // 2
        perm = [(i, (i + by) % blocks) for i in range(blocks)]
        arrived.append(lax.ppermute(packed[k], "block", perm) if by else packed[k])
    fwd, back = blur_matrices(kernels)
    blurred = call(
        first_blur_kernel,
        "first_blur",
        (*fwd, *with_halo(estimate)),
        jax.ShapeDtypeStruct(BLURRED, F32),
        [pltpu.VMEM(HALF_SHAPE, BF16)],
        6 << 30,
    )
    *contributions, measured = call(
        first_back_kernel,
        "first_back",
        (*back, blurred, *arrived),
        [*CONTRIB, jax.ShapeDtypeStruct((VIEWS_DEV * BX // TP, TROWS, Z), BF16)],
        [pltpu.VMEM((2, *HALF_SHAPE), BF16)],
        8 << 30,
    )
    estimate = updated(estimate, contributions, view_count)
    contributions = call(
        sweep_kernel,
        "sweep",
        (*fwd, *back, *with_halo(estimate), measured),
        CONTRIB,
        [
            pltpu.VMEM(HALF_SHAPE, BF16),
            pltpu.VMEM((2, *HALF_SHAPE), BF16),
            pltpu.VMEM(BLURRED, F32),
        ],
        14 << 30,
    )
    return updated(estimate, contributions, view_count)


def solution(mesh):
    return jax.shard_map(
        shards,
        mesh=mesh,
        in_specs=(
            P("block", None, None),
            P("view", "block", None, None, None),
            P("view", "block", None),
            P("view", None, None),
        ),
        out_specs=P("block", None, None),
        check_vma=False,
    )
```

time: 515 us -> 395 us (0.77)
  the two profiles are of different devices: /device:TPU:1 before, /device:TPU:97 now
where the time goes in v1:
time: 395 us
  waiting for transfers between devices  140 us (35%)
  local copies, waits for them, and re-layouts  89.1 us (23%)
  Pallas kernels  83.1 us (21%)
  starting transfers between devices  50.4 us (13%)
  other arithmetic  28.9 us (7%)
    ppermute x2, waiting for transfers between devices, updated(): other = lax.ppermute(partial, 'view', [(0, 1), (1, 0)])  94 us
    pallas_call x3, Pallas kernels, call(): pl.pallas_call(kernel, out_shape=out_shape, in_specs=[VM] * len(operands)...  79.2 us
    convert_element_type x1, local copies, waits for them, and re-layouts, blur_matrices(): fwd_x.astype(BF16)  43.7 us
    convert_element_type x1, local copies, waits for them, and re-layouts, blur_matrices(): back_x.astype(BF16)  42.2 us
    ppermute x8, waiting for transfers between devices, neighbours(): return (lax.ppermute(high, 'block', up), lax.ppermute(low, 'block', down))  32 us
    ppermute x8, starting transfers between devices, neighbours(): return (lax.ppermute(high, 'block', up), lax.ppermute(low, 'block', down))  26.6 us
    ppermute x11, starting transfers between devices, shards(): arrived.append(lax.ppermute(packed[k], 'block', perm) if by else packed[k])  18.9 us
    ppermute x11, waiting for transfers between devices, shards(): arrived.append(lax.ppermute(packed[k], 'block', perm) if by else packed[k])  13.7 us
  transfers between devices with their start and end apart: 21, of which 11 were waited for; matrix products, arithmetic and copies ran while one was open for 28% of the time, Pallas kernels for 6%

profile of v1, /device:TPU:97, one launch (start us, length us, event | category | flops | bytes accessed | tf_op | source)
XLA Modules:
  0.0 394.8 jit_solution(12667852028415571925)
XLA Ops:
  0.0 1.8 convert_element_type.43.mid_ref
  1.8 0.0 copy-start.1
  1.8 0.1 fusion.30
  1.9 0.0 copy-start.3
  1.9 2.4 collective-permute-start
  4.3 2.2 collective-permute-start.1
  6.5 0.7 copy.27
  7.2 3.9 pack_tiles.1
  11.1 0.5 collective-permute-start.2
  11.6 6.6 %collective-permute-start.3 = (bf16[1040,128]{1,0:T(8,128)(2,1)}, bf16[1040,128]{1,0:T(8,128)(2,1)}, u32[]{:S(2)}, u32[]{:S(2)}) collective-permute-start(bf16[1040,128]{1,0:T(8,128)(2,1)} %get-tuple-element.25), channel_id=1, source_target_pairs={{0,59},{1,60},{2,61},{3,62},{4,63},{5,0},{6,1},{7,2},{8,3},{9,4},{... | collective-permute-start | bytes 798728 | tf_op jit(solution)/shard_map/ppermute | solution.py:265
  18.2 2.1 collective-permute-start.4
  20.3 0.1 reduce_sum.27
  20.4 0.1 broadcast_divide_fusion
  20.5 0.1 fusion.31
  20.6 0.3 fusion.8
  20.9 0.8 fusion.3
  21.7 0.8 fusion
  22.5 0.8 fusion.1
  23.2 0.1 copy.16
  23.4 9.2 %multiply_convert_fusion = bf16[3,32,16,64,16]{4,3,2,1,0:T(8,128)(2,1)} fusion(f32[16,16]{1,0:T(8,128)S(1)} %fusion.15, f32[3,32,64]{2,1,0:T(8,128)S(1)} %copy.21), kind=kLoop, calls=%fused_computation | loop fusion | flops 3145728 | bytes 3171328 | tf_op jit(solution)/shard_map/convert_element_type | solution.py:66
  32.6 8.8 %multiply_convert_fusion.1 = bf16[64,16,3,32,16]{4,3,2,1,0:T(8,128)(2,1)} fusion(f32[16,16]{1,0:T(8,128)S(1)} %fusion.15, f32[64,3,32]{2,1,0:T(4,128)S(1)} %copy.16), kind=kLoop, calls=%fused_computation.1 | loop fusion | flops 3145728 | bytes 3171328 | tf_op jit(solution)/shard_map/convert_element_type | solution.py:67
  41.4 0.8 fusion.2
  42.2 0.1 collective-permute-start.5
  42.3 0.8 collective-permute-start.6
  43.1 1.0 collective-permute-start.7
  44.1 43.7 %convert_element_type.42.kx_ref.refs_0_ = bf16[1536,1024]{1,0:T(8,128)(2,1)} reshape(bf16[3,32,16,64,16]{4,3,2,1,0:T(8,128)(2,1)} %multiply_convert_fusion) | data formatting | bytes 6291456 | tf_op jit(solution)/shard_map/convert_element_type | solution.py:66
  87.9 42.2 %convert_element_type.40.kx_ref.refs_3_ = bf16[1024,1536]{1,0:T(8,128)(2,1)} reshape(bf16[64,16,3,32,16]{4,3,2,1,0:T(8,128)(2,1)} %multiply_convert_fusion.1) | data formatting | bytes 6291456 | tf_op jit(solution)/shard_map/convert_element_type | solution.py:67
  130.0 0.8 pad_maximum_fusion
  130.8 0.8 pad_maximum_fusion.1
  131.6 3.5 collective-permute-start.8
  135.1 0.7 collective-permute-start.9
  135.9 0.7 collective-permute-start.10
  136.5 3.0 collective-permute-start.11
  139.6 0.1 collective-permute-start.12
  139.7 0.7 copy-done.6
  140.3 18.0 %first_blur.1.blurred_ref = f32[24,512,128]{2,1,0:T(8,128)} custom-call(bf16[1536,1024]{1,0:T(8,128)(2,1)} %convert_element_type.42.kx_ref.refs_0_, bf16[3,128,256]{2,1,0:T(8,128)(2,1)} %get-tuple-element.63.ky_ref.refs_1_, bf16[3,256,128]{2,1,0:T(8,128)(2,1)} %get-tuple-element.65.kz_ref.refs_2_, bf16[16,128,128]{2,1,0:T(8,128)(2,1)} %copy-done.5, ...), custom_call_target="tpu_custom_call" | custom-call | flops 6442450944 | bytes 12582912 | tf_op jit(solution)/shard_map/first_blur/pallas_call | solution.py:223
  158.4 4.1 %collective-permute-done.10.refs_9_ = bf16[1040,128]{1,0:T(8,128)(2,1)S(1)} collective-permute-done((bf16[1040,128]{1,0:T(8,128)(2,1)}, bf16[1040,128]{1,0:T(8,128)(2,1)S(1)}, u32[]{:S(2)}, u32[]{:S(2)}) %collective-permute-start.10) | collective-permute-done | bytes 266272 | tf_op jit(solution)/shard_map/ppermute | solution.py:265
  162.5 5.7 %collective-permute-done.11.refs_10_ = bf16[1040,128]{1,0:T(8,128)(2,1)S(1)} collective-permute-done((bf16[1040,128]{1,0:T(8,128)(2,1)}, bf16[1040,128]{1,0:T(8,128)(2,1)S(1)}, u32[]{:S(2)}, u32[]{:S(2)}) %collective-permute-start.11) | collective-permute-done | bytes 266272 | tf_op jit(solution)/shard_map/ppermute | solution.py:265
  168.2 3.8 collective-permute-done.12.refs_11_
  172.1 0.7 copy-done.15
  172.8 24.4 %first_back.1 = (f32[16,128,128]{2,1,0:T(8,128)}, f32[32,128,128]{2,1,0:T(8,128)}, f32[16,128,128]{2,1,0:T(8,128)}, bf16[24,512,128]{2,1,0:T(8,128)(2,1)}) custom-call(bf16[1024,1536]{1,0:T(8,128)(2,1)} %convert_element_type.40.kx_ref.refs_3_, bf16[3,128,256]{2,1,0:T(8,128)(2,1)} %get-tuple-element.62.ky_ref.refs_4_, ...), custom_call_target="tpu_custom_call" | custom-call | flops 8589934592 | bytes 12582912 | tf_op jit(solution)/shard_map/first_back/pallas_call | solution.py:223
  197.1 1.9 collective-permute-start.14
  199.0 5.8 %collective-permute-start.13 = (f32[16,128,128]{2,1,0:T(8,128)}, f32[16,128,128]{2,1,0:T(8,128)S(1)}, u32[]{:S(2)}, u32[]{:S(2)}) collective-permute-start(f32[16,128,128]{2,1,0:T(8,128)} %get-tuple-element.37), channel_id=1, source_target_pairs={{0,1},{1,2},{2,3},{3,4},{4,5},{5,6},{6,7},{7,8},{8,9},{9,10},{10,1... | collective-permute-start | bytes 3145736 | tf_op jit(solution)/shard_map/ppermute | solution.py:239
  204.8 10.8 %collective-permute-done.14 = f32[16,128,128]{2,1,0:T(8,128)S(1)} collective-permute-done((f32[16,128,128]{2,1,0:T(8,128)}, f32[16,128,128]{2,1,0:T(8,128)S(1)}, u32[]{:S(2)}, u32[]{:S(2)}) %collective-permute-start.14) | collective-permute-done | bytes 1048608 | tf_op jit(solution)/shard_map/ppermute | solution.py:239
  215.5 1.3 collective-permute-done.13
  216.8 2.1 maximum_add_fusion
  218.9 2.7 collective-permute-start.15
  221.6 44.6 %collective-permute-done.15 = f32[32,128,128]{2,1,0:T(8,128)S(1)} collective-permute-done((f32[32,128,128]{2,1,0:T(8,128)S(1)}, f32[32,128,128]{2,1,0:T(8,128)S(1)}, u32[]{:S(2)}, u32[]{:S(2)}) %collective-permute-start.15) | collective-permute-done | bytes 2097184 | tf_op jit(solution)/shard_map/ppermute | solution.py:252
  266.3 0.6 fusion.27.refs_7_
  266.9 0.1 fusion.29
  267.0 1.9 collective-permute-start.16
  268.9 4.7 %collective-permute-start.17 = (bf16[16,128,128]{2,1,0:T(8,128)(2,1)S(1)}, bf16[16,128,128]{2,1,0:T(8,128)(2,1)S(1)}, u32[]{:S(2)}, u32[]{:S(2)}) collective-permute-start(bf16[16,128,128]{2,1,0:T(8,128)(2,1)S(1)} %get-tuple-element.45), channel_id=1, source_target_pairs={{1,0},{2,1},{3,2},{4,3},{5,4},{6,5},{7,6},{8,7},{9,8},{10,9},{11,1... | collective-permute-start | bytes 1572872 | tf_op jit(solution)/shard_map/ppermute | solution.py:239
  273.6 1.4 collective-permute-done.16.refs_6_
  275.0 6.5 %collective-permute-done.17.refs_8_ = bf16[16,128,128]{2,1,0:T(8,128)(2,1)S(1)} collective-permute-done((bf16[16,128,128]{2,1,0:T(8,128)(2,1)S(1)}, bf16[16,128,128]{2,1,0:T(8,128)(2,1)S(1)}, u32[]{:S(2)}, u32[]{:S(2)}) %collective-permute-start.17) | collective-permute-done | bytes 524320 | tf_op jit(solution)/shard_map/ppermute | solution.py:239
  281.5 0.8 copy-done.8
  282.4 36.9 %sweep.1 = (f32[16,128,128]{2,1,0:T(8,128)}, f32[32,128,128]{2,1,0:T(8,128)}, f32[16,128,128]{2,1,0:T(8,128)}) custom-call(bf16[1536,1024]{1,0:T(8,128)(2,1)} %convert_element_type.42.kx_ref.refs_0_, bf16[3,128,256]{2,1,0:T(8,128)(2,1)} %get-tuple-element.63.ky_ref.refs_1_, bf16[3,256,128]{2,1,0:T(8,128)(2,1)} %get-tuple-element.65.kz_ref.refs_2_, ...), custom_call_target="tpu_custom_call" | custom-call | flops 15032385536 | bytes 12582912 | tf_op jit(solution)/shard_map/sweep/pallas_call | solution.py:223
  319.2 2.2 collective-permute-start.19
  321.4 5.5 %collective-permute-start.18 = (f32[16,128,128]{2,1,0:T(8,128)}, f32[16,128,128]{2,1,0:T(8,128)S(1)}, u32[]{:S(2)}, u32[]{:S(2)}) collective-permute-start(f32[16,128,128]{2,1,0:T(8,128)} %get-tuple-element.41), channel_id=1, source_target_pairs={{0,1},{1,2},{2,3},{3,4},{4,5},{5,6},{6,7},{7,8},{8,9},{9,10},{10,1... | collective-permute-start | bytes 3145736 | tf_op jit(solution)/shard_map/ppermute | solution.py:239
  326.9 10.8 %collective-permute-done.19 = f32[16,128,128]{2,1,0:T(8,128)S(1)} collective-permute-done((f32[16,128,128]{2,1,0:T(8,128)}, f32[16,128,128]{2,1,0:T(8,128)S(1)}, u32[]{:S(2)}, u32[]{:S(2)}) %collective-permute-start.19) | collective-permute-done | bytes 1048608 | tf_op jit(solution)/shard_map/ppermute | solution.py:239
  337.6 1.3 collective-permute-done.18
  338.9 1.9 maximum_add_fusion.1
  340.8 2.2 collective-permute-start.20
  343.0 49.3 %collective-permute-done.20 = f32[32,128,128]{2,1,0:T(8,128)S(1)} collective-permute-done((f32[32,128,128]{2,1,0:T(8,128)S(1)}, f32[32,128,128]{2,1,0:T(8,128)S(1)}, u32[]{:S(2)}, u32[]{:S(2)}) %collective-permute-start.20) | collective-permute-done | bytes 2097184 | tf_op jit(solution)/shard_map/ppermute | solution.py:252
  392.3 2.4 multiply_multiply_fusion
  (47 shorter events, 0.3 us)
Async XLA Ops:
  0.0 6.5 %copy-start.4 = (s32[1,24,3]{1,0,2:T(1,128)S(1)}, s32[1,24,3]{1,0,2:T(1,128)}, u32[]{:S(2)}) copy-start(s32[1,24,3]{1,0,2:T(1,128)} %param.6) | copy-start | bytes 868
  1.8 9.3 %copy-start.1 = (bf16[32,128,128]{2,1,0:T(8,128)(2,1)}, bf16[32,128,128]{2,1,0:T(8,128)(2,1)S(1)}, u32[]{:S(2)}) copy-start(bf16[32,128,128]{2,1,0:T(8,128)(2,1)S(1)} %convert_element_type.43.mid_ref) | copy-start | bytes 3145732
  1.9 18.4 %copy-start.3 = (f32[3,3,31]{2,1,0:T(4,128)S(1)}, f32[3,3,31]{2,1,0:T(4,128)}, u32[]{:S(2)}) copy-start(f32[3,3,31]{2,1,0:T(4,128)} %param.7) | copy-start | bytes 3352
  1.9 134.7 %collective-permute-start = (bf16[16,128,128]{2,1,0:T(8,128)(2,1)S(1)}, bf16[16,128,128]{2,1,0:T(8,128)(2,1)S(1)}, u32[]{:S(2)}, u32[]{:S(2)}) collective-permute-start(bf16[16,128,128]{2,1,0:T(8,128)(2,1)S(1)} %get-tuple-element.48), channel_id=1, source_target_pairs={{0,1},{1,2},{2,3},{3,4},{4,5},{5,6},{6,7},{7,8},{8,9},{9,10},{10,1... | collective-permute-start | bytes 1572872 | tf_op jit(solution)/shard_map/ppermute | solution.py:239
  4.3 135.2 %collective-permute-start.1 = (bf16[16,128,128]{2,1,0:T(8,128)(2,1)S(1)}, bf16[16,128,128]{2,1,0:T(8,128)(2,1)S(1)}, u32[]{:S(2)}, u32[]{:S(2)}) collective-permute-start(bf16[16,128,128]{2,1,0:T(8,128)(2,1)S(1)} %get-tuple-element.47), channel_id=1, source_target_pairs={{1,0},{2,1},{3,2},{4,3},{5,4},{6,5},{7,6},{8,7},{9,8},{10,9},{11,1... | collective-permute-start | bytes 1572872 | tf_op jit(solution)/shard_map/ppermute | solution.py:239
  11.1 31.1 %collective-permute-start.2 = (bf16[1040,128]{1,0:T(8,128)(2,1)}, bf16[1040,128]{1,0:T(8,128)(2,1)S(1)}, u32[]{:S(2)}, u32[]{:S(2)}) collective-permute-start(bf16[1040,128]{1,0:T(8,128)(2,1)} %get-tuple-element.24), channel_id=1, source_target_pairs={{0,58},{1,59},{2,60},{3,61},{4,62},{5,63},{6,0},{7,1},{8,2},{9,3},... | collective-permute-start | bytes 798728 | tf_op jit(solution)/shard_map/ppermute | solution.py:265
  11.6 30.7 %collective-permute-start.3 = (bf16[1040,128]{1,0:T(8,128)(2,1)}, bf16[1040,128]{1,0:T(8,128)(2,1)}, u32[]{:S(2)}, u32[]{:S(2)}) collective-permute-start(bf16[1040,128]{1,0:T(8,128)(2,1)} %get-tuple-element.25), channel_id=1, source_target_pairs={{0,59},{1,60},{2,61},{3,62},{4,63},{5,0},{6,1},{7,2},{8,3},{9,4},{... | collective-permute-start | bytes 798728 | tf_op jit(solution)/shard_map/ppermute | solution.py:265
  18.2 24.9 %collective-permute-start.4 = (bf16[1040,128]{1,0:T(8,128)(2,1)}, bf16[1040,128]{1,0:T(8,128)(2,1)}, u32[]{:S(2)}, u32[]{:S(2)}) collective-permute-start(bf16[1040,128]{1,0:T(8,128)(2,1)} %get-tuple-element.26), channel_id=1, source_target_pairs={{0,60},{1,61},{2,62},{3,63},{4,0},{5,1},{6,2},{7,3},{8,4},{9,5},{1... | collective-permute-start | bytes 798728 | tf_op jit(solution)/shard_map/ppermute | solution.py:265
  42.2 45.6 %copy-start.9 = (bf16[1040,128]{1,0:T(8,128)(2,1)}, bf16[1040,128]{1,0:T(8,128)(2,1)S(1)}, u32[]{:S(2)}) copy-start(bf16[1040,128]{1,0:T(8,128)(2,1)S(1)} %collective-permute-done.2.refs_0_) | copy-start | bytes 798724
  42.2 89.4 %collective-permute-start.5 = (bf16[1040,128]{1,0:T(8,128)(2,1)}, bf16[1040,128]{1,0:T(8,128)(2,1)}, u32[]{:S(2)}, u32[]{:S(2)}) collective-permute-start(bf16[1040,128]{1,0:T(8,128)(2,1)} %get-tuple-element.27), channel_id=1, source_target_pairs={{0,61},{1,62},{2,63},{3,0},{4,1},{5,2},{6,3},{7,4},{8,5},{9,6},{10... | collective-permute-start | bytes 798728 | tf_op jit(solution)/shard_map/ppermute | solution.py:265
  42.3 92.8 %collective-permute-start.6 = (bf16[1040,128]{1,0:T(8,128)(2,1)}, bf16[1040,128]{1,0:T(8,128)(2,1)}, u32[]{:S(2)}, u32[]{:S(2)}) collective-permute-start(bf16[1040,128]{1,0:T(8,128)(2,1)} %get-tuple-element.28), channel_id=1, source_target_pairs={{0,62},{1,63},{2,0},{3,1},{4,2},{5,3},{6,4},{7,5},{8,6},{9,7},{10,... | collective-permute-start | bytes 798728 | tf_op jit(solution)/shard_map/ppermute | solution.py:265
  43.1 92.8 %collective-permute-start.7 = (bf16[1040,128]{1,0:T(8,128)(2,1)}, bf16[1040,128]{1,0:T(8,128)(2,1)}, u32[]{:S(2)}, u32[]{:S(2)}) collective-permute-start(bf16[1040,128]{1,0:T(8,128)(2,1)} %get-tuple-element.29), channel_id=1, source_target_pairs={{0,63},{1,0},{2,1},{3,2},{4,3},{5,4},{6,5},{7,6},{8,7},{9,8},{10,9... | collective-permute-start | bytes 798728 | tf_op jit(solution)/shard_map/ppermute | solution.py:265
  87.9 51.7 %copy-start.10 = (bf16[1040,128]{1,0:T(8,128)(2,1)S(1)}, bf16[1040,128]{1,0:T(8,128)(2,1)}, u32[]{:S(2)}) copy-start(bf16[1040,128]{1,0:T(8,128)(2,1)} %get-tuple-element.35) | copy-start | bytes 798724
  131.6 26.7 %collective-permute-start.8 = (bf16[1040,128]{1,0:T(8,128)(2,1)}, bf16[1040,128]{1,0:T(8,128)(2,1)S(1)}, u32[]{:S(2)}, u32[]{:S(2)}) collective-permute-start(bf16[1040,128]{1,0:T(8,128)(2,1)} %get-tuple-element.31), channel_id=1, source_target_pairs={{0,1},{1,2},{2,3},{3,4},{4,5},{5,6},{6,7},{7,8},{8,9},{9,10},{10,1... | collective-permute-start | bytes 798728 | tf_op jit(solution)/shard_map/ppermute | solution.py:265
  135.1 23.2 %collective-permute-start.9 = (bf16[1040,128]{1,0:T(8,128)(2,1)}, bf16[1040,128]{1,0:T(8,128)(2,1)S(1)}, u32[]{:S(2)}, u32[]{:S(2)}) collective-permute-start(bf16[1040,128]{1,0:T(8,128)(2,1)} %get-tuple-element.32), channel_id=1, source_target_pairs={{0,2},{1,3},{2,4},{3,5},{4,6},{5,7},{6,8},{7,9},{8,10},{9,11},{10,... | collective-permute-start | bytes 798728 | tf_op jit(solution)/shard_map/ppermute | solution.py:265
  135.9 26.6 %collective-permute-start.10 = (bf16[1040,128]{1,0:T(8,128)(2,1)}, bf16[1040,128]{1,0:T(8,128)(2,1)S(1)}, u32[]{:S(2)}, u32[]{:S(2)}) collective-permute-start(bf16[1040,128]{1,0:T(8,128)(2,1)} %get-tuple-element.33), channel_id=1, source_target_pairs={{0,3},{1,4},{2,5},{3,6},{4,7},{5,8},{6,9},{7,10},{8,11},{9,12},{10... | collective-permute-start | bytes 798728 | tf_op jit(solution)/shard_map/ppermute | solution.py:265
  136.5 3.1 copy-start.5
  136.5 31.7 %collective-permute-start.11 = (bf16[1040,128]{1,0:T(8,128)(2,1)}, bf16[1040,128]{1,0:T(8,128)(2,1)S(1)}, u32[]{:S(2)}, u32[]{:S(2)}) collective-permute-start(bf16[1040,128]{1,0:T(8,128)(2,1)} %get-tuple-element.34), channel_id=1, source_target_pairs={{0,4},{1,5},{2,6},{3,7},{4,8},{5,9},{6,10},{7,11},{8,12},{9,13},{1... | collective-permute-start | bytes 798728 | tf_op jit(solution)/shard_map/ppermute | solution.py:265
  139.6 0.8 copy-start.6
  139.6 32.5 %collective-permute-start.12 = (bf16[1040,128]{1,0:T(8,128)(2,1)S(1)}, bf16[1040,128]{1,0:T(8,128)(2,1)S(1)}, u32[]{:S(2)}, u32[]{:S(2)}) collective-permute-start(bf16[1040,128]{1,0:T(8,128)(2,1)S(1)} %copy-done.10), channel_id=1, source_target_pairs={{0,5},{1,6},{2,7},{3,8},{4,9},{5,10},{6,11},{7,12},{8,13},{9,14},{... | collective-permute-start | bytes 798728 | tf_op jit(solution)/shard_map/ppermute | solution.py:265
  158.4 13.7 %copy-start.11 = (bf16[1040,128]{1,0:T(8,128)(2,1)}, bf16[1040,128]{1,0:T(8,128)(2,1)S(1)}, u32[]{:S(2)}) copy-start(bf16[1040,128]{1,0:T(8,128)(2,1)S(1)} %collective-permute-done.8.refs_7_) | copy-start | bytes 798724
  158.4 13.7 %copy-start.12 = (bf16[1040,128]{1,0:T(8,128)(2,1)}, bf16[1040,128]{1,0:T(8,128)(2,1)S(1)}, u32[]{:S(2)}) copy-start(bf16[1040,128]{1,0:T(8,128)(2,1)S(1)} %collective-permute-done.9.refs_8_) | copy-start | bytes 798724
  162.5 9.6 %copy-start.13 = (bf16[1040,128]{1,0:T(8,128)(2,1)}, bf16[1040,128]{1,0:T(8,128)(2,1)S(1)}, u32[]{:S(2)}) copy-start(bf16[1040,128]{1,0:T(8,128)(2,1)S(1)} %collective-permute-done.10.refs_9_) | copy-start | bytes 798724
  168.2 3.9 copy-start.14
  172.0 0.7 copy-start.15
  197.1 18.4 %collective-permute-start.14 = (f32[16,128,128]{2,1,0:T(8,128)}, f32[16,128,128]{2,1,0:T(8,128)S(1)}, u32[]{:S(2)}, u32[]{:S(2)}) collective-permute-start(f32[16,128,128]{2,1,0:T(8,128)} %get-tuple-element.38), channel_id=1, source_target_pairs={{1,0},{2,1},{3,2},{4,3},{5,4},{6,5},{7,6},{8,7},{9,8},{10,9},{11,1... | collective-permute-start | bytes 3145736 | tf_op jit(solution)/shard_map/ppermute | solution.py:239
  199.0 17.8 %collective-permute-start.13 = (f32[16,128,128]{2,1,0:T(8,128)}, f32[16,128,128]{2,1,0:T(8,128)S(1)}, u32[]{:S(2)}, u32[]{:S(2)}) collective-permute-start(f32[16,128,128]{2,1,0:T(8,128)} %get-tuple-element.37), channel_id=1, source_target_pairs={{0,1},{1,2},{2,3},{3,4},{4,5},{5,6},{6,7},{7,8},{8,9},{9,10},{10,1... | collective-permute-start | bytes 3145736 | tf_op jit(solution)/shard_map/ppermute | solution.py:239
  216.8 49.4 %copy-start = (f32[32,128,128]{2,1,0:T(8,128)S(1)}, f32[32,128,128]{2,1,0:T(8,128)}, u32[]{:S(2)}) copy-start(f32[32,128,128]{2,1,0:T(8,128)} %param.4) | copy-start | bytes 6291460
  218.9 47.3 %collective-permute-start.15 = (f32[32,128,128]{2,1,0:T(8,128)S(1)}, f32[32,128,128]{2,1,0:T(8,128)S(1)}, u32[]{:S(2)}, u32[]{:S(2)}) collective-permute-start(f32[32,128,128]{2,1,0:T(8,128)S(1)} %maximum_add_fusion), channel_id=1, source_target_pairs={{0,64},{64,0},{1,65},{65,1},{2,66},{66,2},{3,67},{67,3},{4,68},{68... | collective-permute-start | bytes 6291464 | tf_op jit(solution)/shard_map/ppermute | solution.py:252
  266.9 15.4 %copy-start.2 = (bf16[32,128,128]{2,1,0:T(8,128)(2,1)}, bf16[32,128,128]{2,1,0:T(8,128)(2,1)S(1)}, u32[]{:S(2)}) copy-start(bf16[32,128,128]{2,1,0:T(8,128)(2,1)S(1)} %fusion.27.refs_7_) | copy-start | bytes 3145732
  267.0 8.0 %collective-permute-start.16 = (bf16[16,128,128]{2,1,0:T(8,128)(2,1)S(1)}, bf16[16,128,128]{2,1,0:T(8,128)(2,1)S(1)}, u32[]{:S(2)}, u32[]{:S(2)}) collective-permute-start(bf16[16,128,128]{2,1,0:T(8,128)(2,1)S(1)} %get-tuple-element.46), channel_id=1, source_target_pairs={{0,1},{1,2},{2,3},{3,4},{4,5},{5,6},{6,7},{7,8},{8,9},{9,10},{10,1... | collective-permute-start | bytes 1572872 | tf_op jit(solution)/shard_map/ppermute | solution.py:239
  268.9 12.6 %collective-permute-start.17 = (bf16[16,128,128]{2,1,0:T(8,128)(2,1)S(1)}, bf16[16,128,128]{2,1,0:T(8,128)(2,1)S(1)}, u32[]{:S(2)}, u32[]{:S(2)}) collective-permute-start(bf16[16,128,128]{2,1,0:T(8,128)(2,1)S(1)} %get-tuple-element.45), channel_id=1, source_target_pairs={{1,0},{2,1},{3,2},{4,3},{5,4},{6,5},{7,6},{8,7},{9,8},{10,9},{11,1... | collective-permute-start | bytes 1572872 | tf_op jit(solution)/shard_map/ppermute | solution.py:239
  275.0 7.3 %copy-start.7 = (bf16[16,128,128]{2,1,0:T(8,128)(2,1)}, bf16[16,128,128]{2,1,0:T(8,128)(2,1)S(1)}, u32[]{:S(2)}) copy-start(bf16[16,128,128]{2,1,0:T(8,128)(2,1)S(1)} %collective-permute-done.16.refs_6_) | copy-start | bytes 1572868
  281.5 0.8 copy-start.8
  319.2 18.4 %collective-permute-start.19 = (f32[16,128,128]{2,1,0:T(8,128)}, f32[16,128,128]{2,1,0:T(8,128)S(1)}, u32[]{:S(2)}, u32[]{:S(2)}) collective-permute-start(f32[16,128,128]{2,1,0:T(8,128)} %get-tuple-element.42), channel_id=1, source_target_pairs={{1,0},{2,1},{3,2},{4,3},{5,4},{6,5},{7,6},{8,7},{9,8},{10,9},{11,1... | collective-permute-start | bytes 3145736 | tf_op jit(solution)/shard_map/ppermute | solution.py:239
  321.4 17.5 %collective-permute-start.18 = (f32[16,128,128]{2,1,0:T(8,128)}, f32[16,128,128]{2,1,0:T(8,128)S(1)}, u32[]{:S(2)}, u32[]{:S(2)}) collective-permute-start(f32[16,128,128]{2,1,0:T(8,128)} %get-tuple-element.41), channel_id=1, source_target_pairs={{0,1},{1,2},{2,3},{3,4},{4,5},{5,6},{6,7},{7,8},{8,9},{9,10},{10,1... | collective-permute-start | bytes 3145736 | tf_op jit(solution)/shard_map/ppermute | solution.py:239
  340.8 51.5 %collective-permute-start.20 = (f32[32,128,128]{2,1,0:T(8,128)S(1)}, f32[32,128,128]{2,1,0:T(8,128)S(1)}, u32[]{:S(2)}, u32[]{:S(2)}) collective-permute-start(f32[32,128,128]{2,1,0:T(8,128)S(1)} %maximum_add_fusion.1), channel_id=1, source_target_pairs={{0,64},{64,0},{1,65},{65,1},{2,66},{66,2},{3,67},{67,3},{4,68},{68... | collective-permute-start | bytes 6291464 | tf_op jit(solution)/shard_map/ppermute | solution.py:252

commit v2 on v1

--- a/solution.py
+++ b/solution.py
@@ -26,6 +26,7 @@
 F32 = jnp.float32
 BF16 = jnp.bfloat16
 VMEM_LIMIT = 56 << 20
+UNROLL = 2
 
 
 def banded(kernel, rows, cols, sign, offset):
@@ -46,25 +47,19 @@
 
 
 def blur_matrices(kernels):
-    taps_x = rounded(kernels[:, 0])
-    taps_y = kernels[:, 1] * (jnp.sum(kernels[:, 0], -1) / jnp.sum(taps_x, -1))[:, None]
-    taps_z = kernels[:, 2]
-    small = banded(taps_x, BX, EX, 1, -1)
-    eye = jnp.eye(SUB, dtype=F32)
-    fwd_x = (small[:, :, None, :, None] * eye[None, None, :, None, :]).reshape(
-        VIEWS_DEV * BX * SUB, EX * SUB
-    )
-    flipped = jnp.transpose(small, (2, 0, 1))
-    back_x = (flipped[:, None, :, :, None] * eye[None, :, None, None, :]).reshape(
-        EX * SUB, VIEWS_DEV * BX * SUB
-    )
+    taps_x, taps_y, taps_z = kernels[:, 0], kernels[:, 1], kernels[:, 2]
+    near_x = rounded(taps_x)
+    back_y = taps_y * (jnp.sum(taps_x, -1) / jnp.sum(near_x, -1))[:, None]
+    fwd_x = banded(taps_x, BX, EX, 1, -1).reshape(VIEWS_DEV * BX, EX)
+    back_x = jnp.transpose(banded(near_x, BX, EX, 1, -1).reshape(VIEWS_DEV * BX, EX))
+    back_x = jnp.concatenate([back_x, back_x], axis=1).astype(BF16)
     y_fwd = banded(taps_y, Y, Y, 1, HALF)
-    y_back = banded(taps_y, Y, Y, -1, HALF)
+    y_back = banded(back_y, Y, Y, -1, HALF)
     z_fwd = banded(taps_z, Z, Z, -1, HALF)
     z_back = banded(taps_z, Z, Z, 1, HALF)
     return (
-        (fwd_x.astype(BF16), two_terms(y_fwd, 2), two_terms(z_fwd, 1)),
-        (back_x.astype(BF16), two_terms(y_back, 2), two_terms(z_back, 1)),
+        (two_terms(fwd_x, 1), two_terms(y_fwd, 2), two_terms(z_fwd, 1)),
+        (back_x, two_terms(y_back, 2), two_terms(z_back, 1)),
     )
 
 
@@ -106,34 +101,35 @@
     )(me, tile_dest[0], view_tiles.reshape(SLOTS, TROWS, Z))
 
 
-def side_by_side(ref, y0):
-    planes = ref.shape[0]
-    return jnp.concatenate(
-        [ref[:, pl.ds(y0 + h * SUB, SUB), :].reshape(planes * SUB, Z) for h in range(2)], axis=1
-    )
+def swapped(block):
+    return jnp.transpose(block, (1, 0, 2))
 
 
 def blur_into(kx_ref, ky_ref, kz_ref, parts, half_ref, out_ref):
     def along_x(t, carry):
-        y0 = pl.multiple_of(t * 2 * SUB, 2 * SUB)
-        data = jnp.concatenate([side_by_side(ref, y0) for ref in parts], axis=0)
-        for v in range(VIEWS_DEV):
-            rows = slice(v * BX * SUB, (v + 1) * BX * SUB)
-            got = jnp.dot(kx_ref[rows, :], data, preferred_element_type=F32).astype(BF16)
-            for h in range(2):
-                half_ref[v * BX : (v + 1) * BX, pl.ds(y0 + h * SUB, SUB), :] = got[
-                    :, h * Z : (h + 1) * Z
-                ].reshape(BX, SUB, Z)
+        y0 = pl.multiple_of(t * SUB, SUB)
+        data = jnp.concatenate([ref[:, pl.ds(y0, SUB), :] for ref in parts], axis=0).astype(F32)
+        for h in range(0, SUB, 8):
+            rows = swapped(data[:, h : h + 8]).astype(BF16)
+            outs = []
+            for j in range(0, 8, 2):
+                pair = jnp.concatenate([rows[j], rows[j + 1]], axis=1)
+                got = jnp.dot(
+                    kx_ref[...], jnp.concatenate([pair, pair], axis=0), preferred_element_type=F32
+                )
+                outs += [got[:, :Z], got[:, Z:]]
+            half_ref[:, pl.ds(y0 + h, 8), :] = swapped(jnp.stack(outs, axis=0))
         return carry
 
-    lax.fori_loop(0, Y // (2 * SUB), along_x, 0)
+    lax.fori_loop(0, Y // SUB, along_x, 0)
 
     def along_yz(q, carry):
         v = q // (BX // TP)
-        planes = [half_ref[q * TP + i] for i in range(TP)]
         outs = []
         for i in range(0, TP, 2):
-            pair = jnp.concatenate(planes[i : i + 2], axis=1)
+            pair = jnp.concatenate(
+                [half_ref[q * TP + i + j].astype(BF16) for j in range(2)], axis=1
+            )
             got = jnp.dot(
                 ky_ref[v], jnp.concatenate([pair, pair], axis=0), preferred_element_type=F32
             ).astype(BF16)
@@ -144,7 +140,7 @@
         )
         return carry
 
-    lax.fori_loop(0, VIEWS_DEV * BX // TP, along_yz, 0)
+    lax.fori_loop(0, VIEWS_DEV * BX // TP, along_yz, 0, unroll=UNROLL)
 
 
 def back_from(kx_ref, ky_ref, kz_ref, measured_ref, blurred_ref, half_ref, outs):
@@ -159,33 +155,33 @@
             got = jnp.dot(
                 ky_ref[v], jnp.concatenate([pair, pair], axis=0), preferred_element_type=F32
             )
-            high = got.astype(BF16)
-            low = (got - high.astype(F32)).astype(BF16)
             for j in range(2):
-                half_ref[0, q * TP + i + j] = high[:, j * Z : (j + 1) * Z]
-                half_ref[1, q * TP + i + j] = low[:, j * Z : (j + 1) * Z]
+                half_ref[q * TP + i + j] = got[:, j * Z : (j + 1) * Z]
         return carry
 
-    lax.fori_loop(0, VIEWS_DEV * BX // TP, along_zy, 0)
+    lax.fori_loop(0, VIEWS_DEV * BX // TP, along_zy, 0, unroll=UNROLL)
 
     def along_x(t, carry):
-        y0 = pl.multiple_of(t * 2 * SUB, 2 * SUB)
-        high = side_by_side(half_ref.at[0], y0)
-        low = side_by_side(half_ref.at[1], y0)
+        y0 = pl.multiple_of(t * 8, 8)
+        data = swapped(half_ref[:, pl.ds(y0, 8), :])
+        high = data.astype(BF16)
+        low = (data - high.astype(F32)).astype(BF16)
+        got = []
+        for j in range(0, 8, 2):
+            pair = [jnp.concatenate([part[j], part[j + 1]], axis=1) for part in (high, low)]
+            both = jnp.dot(
+                kx_ref[...], jnp.concatenate(pair, axis=0), preferred_element_type=F32
+            )
+            got += [both[:, :Z], both[:, Z:]]
+        planes = swapped(jnp.stack(got, axis=0))
         first = 0
         for ref in outs:
             count = ref.shape[0]
-            taps = kx_ref[first * SUB : (first + count) * SUB, :]
-            got = jnp.dot(taps, high, preferred_element_type=F32)
-            got += jnp.dot(taps, low, preferred_element_type=F32)
-            for h in range(2):
-                ref[:, pl.ds(y0 + h * SUB, SUB), :] = got[:, h * Z : (h + 1) * Z].reshape(
-                    count, SUB, Z
-                )
+            ref[:, pl.ds(y0, 8), :] = planes[first : first + count]
             first += count
         return carry
 
-    lax.fori_loop(0, Y // (2 * SUB), along_x, 0)
+    lax.fori_loop(0, Y // 8, along_x, 0, unroll=UNROLL)
 
 
 def first_blur_kernel(kx_ref, ky_ref, kz_ref, left_ref, mid_ref, right_ref, out_ref, half_ref):
@@ -269,7 +265,7 @@
         "first_blur",
         (*fwd, *with_halo(estimate)),
         jax.ShapeDtypeStruct(BLURRED, F32),
-        [pltpu.VMEM(HALF_SHAPE, BF16)],
+        [pltpu.VMEM(HALF_SHAPE, F32)],
         6 << 30,
     )
     *contributions, measured = call(
@@ -277,7 +273,7 @@
         "first_back",
         (*back, blurred, *arrived),
         [*CONTRIB, jax.ShapeDtypeStruct((VIEWS_DEV * BX // TP, TROWS, Z), BF16)],
-        [pltpu.VMEM((2, *HALF_SHAPE), BF16)],
+        [pltpu.VMEM(HALF_SHAPE, F32)],
         8 << 30,
     )
     estimate = updated(estimate, contributions, view_count)
@@ -287,8 +283,8 @@
         (*fwd, *back, *with_halo(estimate), measured),
         CONTRIB,
         [
-            pltpu.VMEM(HALF_SHAPE, BF16),
-            pltpu.VMEM((2, *HALF_SHAPE), BF16),
+            pltpu.VMEM(HALF_SHAPE, F32),
+            pltpu.VMEM(HALF_SHAPE, F32),
             pltpu.VMEM(BLURRED, F32),
         ],
         14 << 30,

time: 395 us -> 297 us (0.75); the launches traced: 395 us -> 291 us
  local copies, waits for them, and re-layouts: 89.1 us -> 2.52 us
  Pallas kernels: 83.1 us -> 62.2 us
  waiting for transfers between devices: 140 us -> 159 us
  other arithmetic: 28.9 us -> 12.4 us
    convert_element_type x2 -> x0, local copies, waits for them, and re-layouts: 85.9 us -> none  [the longest x1 43.7 us: blur_matrices(): fwd_x.astype(BF16)]
    pallas_call x3, Pallas kernels: 79.2 us -> 58.3 us  [call(): pl.pallas_call(kernel, out_shape=out_shape, in_specs=[VM] * len(operands)...]
    convert_element_type x3 -> x0, other arithmetic: 18 us -> none  [the longest x1 9.24 us: blur_matrices(): fwd_x.astype(BF16)]
    ppermute x11, waiting for transfers between devices: 13.7 us -> 22.9 us  [shards(): arrived.append(lax.ppermute(packed[k], 'block', perm) if by else packed[k])]
    ppermute x8, waiting for transfers between devices: 32 us -> 38.9 us  [neighbours(): return (lax.ppermute(high, 'block', up), lax.ppermute(low, 'block', down))]
  transfers between devices with their start and end apart: 21 -> 21, of which waited for: 11 -> 13; matrix products, arithmetic and copies ran while one was open for 28% -> 3% of each run, Pallas kernels for 6% -> 6%
where the time goes in v2:
time: 297 us; the launch traced here: 291 us
  waiting for transfers between devices  159 us (54%)
  Pallas kernels  62.2 us (21%)
  starting transfers between devices  50.8 us (17%)
  other arithmetic  12.4 us (4%)
  matrix products  3.57 us (1%)
    ppermute x2, waiting for transfers between devices, updated(): other = lax.ppermute(partial, 'view', [(0, 1), (1, 0)])  97.6 us
    pallas_call x3, Pallas kernels, call(): pl.pallas_call(kernel, out_shape=out_shape, in_specs=[VM] * len(operands)...  58.3 us
    ppermute x8, waiting for transfers between devices, neighbours(): return (lax.ppermute(high, 'block', up), lax.ppermute(low, 'block', down))  38.9 us
    ppermute x8, starting transfers between devices, neighbours(): return (lax.ppermute(high, 'block', up), lax.ppermute(low, 'block', down))  28.2 us
    ppermute x11, waiting for transfers between devices, shards(): arrived.append(lax.ppermute(packed[k], 'block', perm) if by else packed[k])  22.9 us
    ppermute x11, starting transfers between devices, shards(): arrived.append(lax.ppermute(packed[k], 'block', perm) if by else packed[k])  19.3 us
  transfers between devices with their start and end apart: 21, of which 13 were waited for; matrix products, arithmetic and copies ran while one was open for 3% of the time, Pallas kernels for 6%

profile of v2, /device:TPU:97, one launch (start us, length us, event | category | flops | bytes accessed | tf_op | source)
XLA Modules:
  0.0 291.2 jit_solution(13528686713282181177)
XLA Ops:
  0.0 1.8 convert_element_type.4.mid_ref
  1.8 0.0 copy-start.1
  1.8 0.1 fusion.31
  1.9 0.0 copy-start.3
  1.9 2.7 collective-permute-start.1
  4.6 5.1 %collective-permute-start = (bf16[16,128,128]{2,1,0:T(8,128)(2,1)S(1)}, bf16[16,128,128]{2,1,0:T(8,128)(2,1)S(1)}, u32[]{:S(2)}, u32[]{:S(2)}) collective-permute-start(bf16[16,128,128]{2,1,0:T(8,128)(2,1)S(1)} %get-tuple-element.46), channel_id=1, source_target_pairs={{0,1},{1,2},{2,3},{3,4},{4,5},{5,6},{6,7},{7,8},{8,9},{9,10},{10,1... | collective-permute-start | bytes 1572872 | tf_op jit(solution)/shard_map/ppermute | solution.py:235
  9.7 0.7 copy.28
  10.4 3.9 %pack_tiles.1 = (bf16[1040,128]{1,0:T(8,128)(2,1)}, bf16[1040,128]{1,0:T(8,128)(2,1)}, bf16[1040,128]{1,0:T(8,128)(2,1)}, bf16[1040,128]{1,0:T(8,128)(2,1)}, bf1...) custom-call(s32[1]{0:T(128)} %bitcast.5.me_ref, ...), custom_call_target="tpu_custom_call" | custom-call | bytes 6291456 | tf_op jit(solution)/shard_map/pack_tiles/pallas_call | solution.py:88
  14.3 0.0 collective-permute-start.2
  14.3 2.6 collective-permute-start.3
  16.9 3.2 %collective-permute-start.4 = (bf16[1040,128]{1,0:T(8,128)(2,1)}, bf16[1040,128]{1,0:T(8,128)(2,1)}, u32[]{:S(2)}, u32[]{:S(2)}) collective-permute-start(bf16[1040,128]{1,0:T(8,128)(2,1)} %get-tuple-element.26), channel_id=1, source_target_pairs={{0,60},{1,61},{2,62},{3,63},{4,0},{5,1},{6,2},{7,3},{8,4},{9,5},{1... | collective-permute-start | bytes 798728 | tf_op jit(solution)/shard_map/ppermute | solution.py:261
  20.2 0.1 reduce_sum.27
  20.3 0.1 broadcast_divide_fusion
  20.4 0.1 slice_reduce_fusion
  20.5 0.1 fusion.26
  20.6 0.3 fusion.8
  20.9 0.8 fusion.2
  21.7 0.8 fusion.1
  22.4 0.8 fusion
  23.2 0.8 fusion.3
  24.1 0.3 convolution_convert_fusion
  24.4 0.1 copy.17
  24.5 0.7 pad_maximum_fusion.4.kx_ref.refs_3_
  25.2 0.0 collective-permute-start.5
  25.3 4.2 %collective-permute-start.6 = (bf16[1040,128]{1,0:T(8,128)(2,1)}, bf16[1040,128]{1,0:T(8,128)(2,1)S(1)}, u32[]{:S(2)}, u32[]{:S(2)}) collective-permute-start(bf16[1040,128]{1,0:T(8,128)(2,1)} %get-tuple-element.28), channel_id=1, source_target_pairs={{0,62},{1,63},{2,0},{3,1},{4,2},{5,3},{6,4},{7,5},{8,6},{9,7},{10,... | collective-permute-start | bytes 798728 | tf_op jit(solution)/shard_map/ppermute | solution.py:261
  29.5 4.7 %collective-permute-done.4.refs_2_ = bf16[1040,128]{1,0:T(8,128)(2,1)} collective-permute-done((bf16[1040,128]{1,0:T(8,128)(2,1)}, bf16[1040,128]{1,0:T(8,128)(2,1)}, u32[]{:S(2)}, u32[]{:S(2)}) %collective-permute-start.4) | collective-permute-done | bytes 266272 | tf_op jit(solution)/shard_map/ppermute | solution.py:261
  34.2 0.0 collective-permute-start.7
  34.2 0.7 pad_maximum_fusion.5.kx_ref.refs_0_
  34.9 0.8 pad_maximum_fusion.1
  35.7 0.8 pad_maximum_fusion
  36.5 2.1 collective-permute-done.5.refs_3_
  38.6 3.8 %collective-permute-start.8 = (bf16[1040,128]{1,0:T(8,128)(2,1)}, bf16[1040,128]{1,0:T(8,128)(2,1)S(1)}, u32[]{:S(2)}, u32[]{:S(2)}) collective-permute-start(bf16[1040,128]{1,0:T(8,128)(2,1)} %get-tuple-element.31), channel_id=1, source_target_pairs={{0,1},{1,2},{2,3},{3,4},{4,5},{5,6},{6,7},{7,8},{8,9},{9,10},{10,1... | collective-permute-start | bytes 798728 | tf_op jit(solution)/shard_map/ppermute | solution.py:261
  42.4 4.5 %collective-permute-done.6.refs_4_ = bf16[1040,128]{1,0:T(8,128)(2,1)S(1)} collective-permute-done((bf16[1040,128]{1,0:T(8,128)(2,1)}, bf16[1040,128]{1,0:T(8,128)(2,1)S(1)}, u32[]{:S(2)}, u32[]{:S(2)}) %collective-permute-start.6) | collective-permute-done | bytes 266272 | tf_op jit(solution)/shard_map/ppermute | solution.py:261
  46.9 1.7 collective-permute-start.9
  48.6 2.7 collective-permute-start.11
  51.3 1.1 collective-permute-start.12
  52.4 12.8 %first_blur.1.blurred_ref = f32[24,512,128]{2,1,0:T(8,128)} custom-call(bf16[96,128]{1,0:T(8,128)(2,1)} %pad_maximum_fusion.5.kx_ref.refs_0_, bf16[3,128,256]{2,1,0:T(8,128)(2,1)} %get-tuple-element.62.ky_ref.refs_1_, bf16[3,256,128]{2,1,0:T(8,128)(2,1)} %get-tuple-element.64.kz_ref.refs_2_, bf16[16,128,128]{2,1,0:T(8,128)(2,1)} %copy-done.6, ...), custom_call_target="tpu_custom_call" | custom-call | flops 6442450944 | bytes 12582912 | tf_op jit(solution)/shard_map/first_blur/pallas_call | solution.py:219
  65.3 7.8 %collective-permute-done.11.refs_10_ = bf16[1040,128]{1,0:T(8,128)(2,1)S(1)} collective-permute-done((bf16[1040,128]{1,0:T(8,128)(2,1)}, bf16[1040,128]{1,0:T(8,128)(2,1)S(1)}, u32[]{:S(2)}, u32[]{:S(2)}) %collective-permute-start.11) | collective-permute-done | bytes 266272 | tf_op jit(solution)/shard_map/ppermute | solution.py:261
  73.0 3.7 %collective-permute-done.12.refs_11_ = bf16[1040,128]{1,0:T(8,128)(2,1)S(1)} collective-permute-done((bf16[1040,128]{1,0:T(8,128)(2,1)S(1)}, bf16[1040,128]{1,0:T(8,128)(2,1)S(1)}, u32[]{:S(2)}, u32[]{:S(2)}) %collective-permute-start.12) | collective-permute-done | bytes 266272 | tf_op jit(solution)/shard_map/ppermute | solution.py:261
  76.8 0.7 copy-done.18
  77.5 19.4 %first_back.1 = (f32[16,128,128]{2,1,0:T(8,128)}, f32[32,128,128]{2,1,0:T(8,128)}, f32[16,128,128]{2,1,0:T(8,128)}, bf16[24,512,128]{2,1,0:T(8,128)(2,1)}) custom-call(bf16[64,192]{1,0:T(8,128)(2,1)} %pad_maximum_fusion.4.kx_ref.refs_3_, bf16[3,128,256]{2,1,0:T(8,128)(2,1)} %get-tuple-element.61.ky_ref.refs_4_, ...), custom_call_target="tpu_custom_call" | custom-call | flops 8589934592 | bytes 12582912 | tf_op jit(solution)/shard_map/first_back/pallas_call | solution.py:219
  96.9 1.9 collective-permute-start.13
  98.8 2.4 collective-permute-start.14
  101.2 9.6 %collective-permute-done.13 = f32[16,128,128]{2,1,0:T(8,128)S(1)} collective-permute-done((f32[16,128,128]{2,1,0:T(8,128)}, f32[16,128,128]{2,1,0:T(8,128)S(1)}, u32[]{:S(2)}, u32[]{:S(2)}) %collective-permute-start.13) | collective-permute-done | bytes 1048608 | tf_op jit(solution)/shard_map/ppermute | solution.py:235
  110.8 6.4 %collective-permute-done.14 = f32[16,128,128]{2,1,0:T(8,128)S(1)} collective-permute-done((f32[16,128,128]{2,1,0:T(8,128)}, f32[16,128,128]{2,1,0:T(8,128)S(1)}, u32[]{:S(2)}, u32[]{:S(2)}) %collective-permute-start.14) | collective-permute-done | bytes 1048608 | tf_op jit(solution)/shard_map/ppermute | solution.py:235
  117.2 2.1 maximum_add_fusion
  119.3 3.2 %collective-permute-start.15 = (f32[32,128,128]{2,1,0:T(8,128)S(1)}, f32[32,128,128]{2,1,0:T(8,128)S(1)}, u32[]{:S(2)}, u32[]{:S(2)}) collective-permute-start(f32[32,128,128]{2,1,0:T(8,128)S(1)} %maximum_add_fusion), channel_id=1, source_target_pairs={{0,64},{64,0},{1,65},{65,1},{2,66},{66,2},{3,67},{67,3},{4,68},{68... | collective-permute-start | bytes 6291464 | tf_op jit(solution)/shard_map/ppermute | solution.py:248
  122.5 47.4 %collective-permute-done.15 = f32[32,128,128]{2,1,0:T(8,128)S(1)} collective-permute-done((f32[32,128,128]{2,1,0:T(8,128)S(1)}, f32[32,128,128]{2,1,0:T(8,128)S(1)}, u32[]{:S(2)}, u32[]{:S(2)}) %collective-permute-start.15) | collective-permute-done | bytes 2097184 | tf_op jit(solution)/shard_map/ppermute | solution.py:248
  169.9 0.6 fusion.29.refs_7_
  170.5 0.1 fusion.30
  170.6 2.3 collective-permute-start.17
  172.9 5.4 %collective-permute-start.16 = (bf16[16,128,128]{2,1,0:T(8,128)(2,1)S(1)}, bf16[16,128,128]{2,1,0:T(8,128)(2,1)S(1)}, u32[]{:S(2)}, u32[]{:S(2)}) collective-permute-start(bf16[16,128,128]{2,1,0:T(8,128)(2,1)S(1)} %get-tuple-element.44), channel_id=1, source_target_pairs={{0,1},{1,2},{2,3},{3,4},{4,5},{5,6},{6,7},{7,8},{8,9},{9,10},{10,1... | collective-permute-start | bytes 1572872 | tf_op jit(solution)/shard_map/ppermute | solution.py:235
  178.3 4.9 %collective-permute-done.17.refs_8_ = bf16[16,128,128]{2,1,0:T(8,128)(2,1)S(1)} collective-permute-done((bf16[16,128,128]{2,1,0:T(8,128)(2,1)S(1)}, bf16[16,128,128]{2,1,0:T(8,128)(2,1)S(1)}, u32[]{:S(2)}, u32[]{:S(2)}) %collective-permute-start.17) | collective-permute-done | bytes 524320 | tf_op jit(solution)/shard_map/ppermute | solution.py:235
  183.2 1.2 collective-permute-done.16.refs_6_
  184.4 0.8 copy-done.8
  185.2 26.1 %sweep.1 = (f32[16,128,128]{2,1,0:T(8,128)}, f32[32,128,128]{2,1,0:T(8,128)}, f32[16,128,128]{2,1,0:T(8,128)}) custom-call(bf16[96,128]{1,0:T(8,128)(2,1)} %pad_maximum_fusion.5.kx_ref.refs_0_, bf16[3,128,256]{2,1,0:T(8,128)(2,1)} %get-tuple-element.62.ky_ref.refs_1_, bf16[3,256,128]{2,1,0:T(8,128)(2,1)} %get-tuple-element.64.kz_ref.refs_2_, ...), custom_call_target="tpu_custom_call" | custom-call | flops 15032385536 | bytes 12582912 | tf_op jit(solution)/shard_map/sweep/pallas_call | solution.py:219
  211.3 6.5 %collective-permute-start.18 = (f32[16,128,128]{2,1,0:T(8,128)}, f32[16,128,128]{2,1,0:T(8,128)S(1)}, u32[]{:S(2)}, u32[]{:S(2)}) collective-permute-start(f32[16,128,128]{2,1,0:T(8,128)} %get-tuple-element.41), channel_id=1, source_target_pairs={{0,1},{1,2},{2,3},{3,4},{4,5},{5,6},{6,7},{7,8},{8,9},{9,10},{10,1... | collective-permute-start | bytes 3145736 | tf_op jit(solution)/shard_map/ppermute | solution.py:235
  217.8 1.9 collective-permute-start.19
  219.8 10.1 %collective-permute-done.18 = f32[16,128,128]{2,1,0:T(8,128)S(1)} collective-permute-done((f32[16,128,128]{2,1,0:T(8,128)}, f32[16,128,128]{2,1,0:T(8,128)S(1)}, u32[]{:S(2)}, u32[]{:S(2)}) %collective-permute-start.18) | collective-permute-done | bytes 1048608 | tf_op jit(solution)/shard_map/ppermute | solution.py:235
  229.9 6.7 %collective-permute-done.19 = f32[16,128,128]{2,1,0:T(8,128)S(1)} collective-permute-done((f32[16,128,128]{2,1,0:T(8,128)}, f32[16,128,128]{2,1,0:T(8,128)S(1)}, u32[]{:S(2)}, u32[]{:S(2)}) %collective-permute-start.19) | collective-permute-done | bytes 1048608 | tf_op jit(solution)/shard_map/ppermute | solution.py:235
  236.6 1.9 maximum_add_fusion.1
  238.5 0.1 collective-permute-start.20
  238.6 50.2 %collective-permute-done.20 = f32[32,128,128]{2,1,0:T(8,128)S(1)} collective-permute-done((f32[32,128,128]{2,1,0:T(8,128)S(1)}, f32[32,128,128]{2,1,0:T(8,128)S(1)}, u32[]{:S(2)}, u32[]{:S(2)}) %collective-permute-start.20) | collective-permute-done | bytes 2097184 | tf_op jit(solution)/shard_map/ppermute | solution.py:248
  288.8 2.4 multiply_multiply_fusion
  (54 shorter events, 0.3 us)
Async XLA Ops:
  0.0 9.7 %copy-start.4 = (s32[1,24,3]{1,0,2:T(1,128)S(1)}, s32[1,24,3]{1,0,2:T(1,128)}, u32[]{:S(2)}) copy-start(s32[1,24,3]{1,0,2:T(1,128)} %param.6) | copy-start | bytes 868
  1.8 12.5 %copy-start.1 = (bf16[32,128,128]{2,1,0:T(8,128)(2,1)}, bf16[32,128,128]{2,1,0:T(8,128)(2,1)S(1)}, u32[]{:S(2)}) copy-start(bf16[32,128,128]{2,1,0:T(8,128)(2,1)S(1)} %convert_element_type.4.mid_ref) | copy-start | bytes 3145732
  1.9 18.3 %copy-start.3 = (f32[3,3,31]{2,1,0:T(4,128)S(1)}, f32[3,3,31]{2,1,0:T(4,128)}, u32[]{:S(2)}) copy-start(f32[3,3,31]{2,1,0:T(4,128)} %param.7) | copy-start | bytes 3352
  1.9 46.7 %collective-permute-start.1 = (bf16[16,128,128]{2,1,0:T(8,128)(2,1)S(1)}, bf16[16,128,128]{2,1,0:T(8,128)(2,1)S(1)}, u32[]{:S(2)}, u32[]{:S(2)}) collective-permute-start(bf16[16,128,128]{2,1,0:T(8,128)(2,1)S(1)} %get-tuple-element.45), channel_id=1, source_target_pairs={{1,0},{2,1},{3,2},{4,3},{5,4},{6,5},{7,6},{8,7},{9,8},{10,9},{11,1... | collective-permute-start | bytes 1572872 | tf_op jit(solution)/shard_map/ppermute | solution.py:235
  4.6 46.7 %collective-permute-start = (bf16[16,128,128]{2,1,0:T(8,128)(2,1)S(1)}, bf16[16,128,128]{2,1,0:T(8,128)(2,1)S(1)}, u32[]{:S(2)}, u32[]{:S(2)}) collective-permute-start(bf16[16,128,128]{2,1,0:T(8,128)(2,1)S(1)} %get-tuple-element.46), channel_id=1, source_target_pairs={{0,1},{1,2},{2,3},{3,4},{4,5},{5,6},{6,7},{7,8},{8,9},{9,10},{10,1... | collective-permute-start | bytes 1572872 | tf_op jit(solution)/shard_map/ppermute | solution.py:235
  14.3 11.0 %collective-permute-start.2 = (bf16[1040,128]{1,0:T(8,128)(2,1)}, bf16[1040,128]{1,0:T(8,128)(2,1)S(1)}, u32[]{:S(2)}, u32[]{:S(2)}) collective-permute-start(bf16[1040,128]{1,0:T(8,128)(2,1)} %get-tuple-element.24), channel_id=1, source_target_pairs={{0,58},{1,59},{2,60},{3,61},{4,62},{5,63},{6,0},{7,1},{8,2},{9,3},... | collective-permute-start | bytes 798728 | tf_op jit(solution)/shard_map/ppermute | solution.py:261
  14.3 10.9 %collective-permute-start.3 = (bf16[1040,128]{1,0:T(8,128)(2,1)}, bf16[1040,128]{1,0:T(8,128)(2,1)}, u32[]{:S(2)}, u32[]{:S(2)}) collective-permute-start(bf16[1040,128]{1,0:T(8,128)(2,1)} %get-tuple-element.25), channel_id=1, source_target_pairs={{0,59},{1,60},{2,61},{3,62},{4,63},{5,0},{6,1},{7,2},{8,3},{9,4},{... | collective-permute-start | bytes 798728 | tf_op jit(solution)/shard_map/ppermute | solution.py:261
  16.9 17.3 %collective-permute-start.4 = (bf16[1040,128]{1,0:T(8,128)(2,1)}, bf16[1040,128]{1,0:T(8,128)(2,1)}, u32[]{:S(2)}, u32[]{:S(2)}) collective-permute-start(bf16[1040,128]{1,0:T(8,128)(2,1)} %get-tuple-element.26), channel_id=1, source_target_pairs={{0,60},{1,61},{2,62},{3,63},{4,0},{5,1},{6,2},{7,3},{8,4},{9,5},{1... | collective-permute-start | bytes 798728 | tf_op jit(solution)/shard_map/ppermute | solution.py:261
  23.2 28.1 %copy-start.10 = (bf16[1040,128]{1,0:T(8,128)(2,1)S(1)}, bf16[1040,128]{1,0:T(8,128)(2,1)}, u32[]{:S(2)}) copy-start(bf16[1040,128]{1,0:T(8,128)(2,1)} %get-tuple-element.35) | copy-start | bytes 798724
  25.2 39.9 %copy-start.9 = (bf16[1040,128]{1,0:T(8,128)(2,1)}, bf16[1040,128]{1,0:T(8,128)(2,1)S(1)}, u32[]{:S(2)}) copy-start(bf16[1040,128]{1,0:T(8,128)(2,1)S(1)} %collective-permute-done.2.refs_0_) | copy-start | bytes 798724
  25.2 13.4 %collective-permute-start.5 = (bf16[1040,128]{1,0:T(8,128)(2,1)}, bf16[1040,128]{1,0:T(8,128)(2,1)S(1)}, u32[]{:S(2)}, u32[]{:S(2)}) collective-permute-start(bf16[1040,128]{1,0:T(8,128)(2,1)} %get-tuple-element.27), channel_id=1, source_target_pairs={{0,61},{1,62},{2,63},{3,0},{4,1},{5,2},{6,3},{7,4},{8,5},{9,6},{10... | collective-permute-start | bytes 798728 | tf_op jit(solution)/shard_map/ppermute | solution.py:261
  25.3 21.6 %collective-permute-start.6 = (bf16[1040,128]{1,0:T(8,128)(2,1)}, bf16[1040,128]{1,0:T(8,128)(2,1)S(1)}, u32[]{:S(2)}, u32[]{:S(2)}) collective-permute-start(bf16[1040,128]{1,0:T(8,128)(2,1)} %get-tuple-element.28), channel_id=1, source_target_pairs={{0,62},{1,63},{2,0},{3,1},{4,2},{5,3},{6,4},{7,5},{8,6},{9,7},{10,... | collective-permute-start | bytes 798728 | tf_op jit(solution)/shard_map/ppermute | solution.py:261
  34.2 14.4 %collective-permute-start.7 = (bf16[1040,128]{1,0:T(8,128)(2,1)}, bf16[1040,128]{1,0:T(8,128)(2,1)S(1)}, u32[]{:S(2)}, u32[]{:S(2)}) collective-permute-start(bf16[1040,128]{1,0:T(8,128)(2,1)} %get-tuple-element.29), channel_id=1, source_target_pairs={{0,63},{1,0},{2,1},{3,2},{4,3},{5,4},{6,5},{7,6},{8,7},{9,8},{10,9... | collective-permute-start | bytes 798728 | tf_op jit(solution)/shard_map/ppermute | solution.py:261
  38.6 26.6 %copy-start.11 = (bf16[1040,128]{1,0:T(8,128)(2,1)}, bf16[1040,128]{1,0:T(8,128)(2,1)S(1)}, u32[]{:S(2)}) copy-start(bf16[1040,128]{1,0:T(8,128)(2,1)S(1)} %collective-permute-done.5.refs_3_) | copy-start | bytes 798724
  38.6 26.6 %collective-permute-start.8 = (bf16[1040,128]{1,0:T(8,128)(2,1)}, bf16[1040,128]{1,0:T(8,128)(2,1)S(1)}, u32[]{:S(2)}, u32[]{:S(2)}) collective-permute-start(bf16[1040,128]{1,0:T(8,128)(2,1)} %get-tuple-element.31), channel_id=1, source_target_pairs={{0,1},{1,2},{2,3},{3,4},{4,5},{5,6},{6,7},{7,8},{8,9},{9,10},{10,1... | collective-permute-start | bytes 798728 | tf_op jit(solution)/shard_map/ppermute | solution.py:261
  46.9 18.3 %copy-start.12 = (bf16[1040,128]{1,0:T(8,128)(2,1)}, bf16[1040,128]{1,0:T(8,128)(2,1)S(1)}, u32[]{:S(2)}) copy-start(bf16[1040,128]{1,0:T(8,128)(2,1)S(1)} %collective-permute-done.6.refs_4_) | copy-start | bytes 798724
  46.9 18.4 %collective-permute-start.9 = (bf16[1040,128]{1,0:T(8,128)(2,1)}, bf16[1040,128]{1,0:T(8,128)(2,1)S(1)}, u32[]{:S(2)}, u32[]{:S(2)}) collective-permute-start(bf16[1040,128]{1,0:T(8,128)(2,1)} %get-tuple-element.32), channel_id=1, source_target_pairs={{0,2},{1,3},{2,4},{3,5},{4,6},{5,7},{6,8},{7,9},{8,10},{9,11},{10,... | collective-permute-start | bytes 798728 | tf_op jit(solution)/shard_map/ppermute | solution.py:261
  48.6 16.6 %copy-start.13 = (bf16[1040,128]{1,0:T(8,128)(2,1)}, bf16[1040,128]{1,0:T(8,128)(2,1)S(1)}, u32[]{:S(2)}) copy-start(bf16[1040,128]{1,0:T(8,128)(2,1)S(1)} %collective-permute-done.7.refs_5_) | copy-start | bytes 798724
  48.6 16.7 %collective-permute-start.10 = (bf16[1040,128]{1,0:T(8,128)(2,1)}, bf16[1040,128]{1,0:T(8,128)(2,1)S(1)}, u32[]{:S(2)}, u32[]{:S(2)}) collective-permute-start(bf16[1040,128]{1,0:T(8,128)(2,1)} %get-tuple-element.33), channel_id=1, source_target_pairs={{0,3},{1,4},{2,5},{3,6},{4,7},{5,8},{6,9},{7,10},{8,11},{9,12},{10... | collective-permute-start | bytes 798728 | tf_op jit(solution)/shard_map/ppermute | solution.py:261
  48.6 3.8 %copy-start.5 = (bf16[16,128,128]{2,1,0:T(8,128)(2,1)}, bf16[16,128,128]{2,1,0:T(8,128)(2,1)S(1)}, u32[]{:S(2)}) copy-start(bf16[16,128,128]{2,1,0:T(8,128)(2,1)S(1)} %collective-permute-done.1.right_ref) | copy-start | bytes 1572868
  48.6 24.4 %collective-permute-start.11 = (bf16[1040,128]{1,0:T(8,128)(2,1)}, bf16[1040,128]{1,0:T(8,128)(2,1)S(1)}, u32[]{:S(2)}, u32[]{:S(2)}) collective-permute-start(bf16[1040,128]{1,0:T(8,128)(2,1)} %get-tuple-element.34), channel_id=1, source_target_pairs={{0,4},{1,5},{2,6},{3,7},{4,8},{5,9},{6,10},{7,11},{8,12},{9,13},{1... | collective-permute-start | bytes 798728 | tf_op jit(solution)/shard_map/ppermute | solution.py:261
  51.3 1.1 copy-start.6
  51.3 25.4 %collective-permute-start.12 = (bf16[1040,128]{1,0:T(8,128)(2,1)S(1)}, bf16[1040,128]{1,0:T(8,128)(2,1)S(1)}, u32[]{:S(2)}, u32[]{:S(2)}) collective-permute-start(bf16[1040,128]{1,0:T(8,128)(2,1)S(1)} %copy-done.10), channel_id=1, source_target_pairs={{0,5},{1,6},{2,7},{3,8},{4,9},{5,10},{6,11},{7,12},{8,13},{9,14},{... | collective-permute-start | bytes 798728 | tf_op jit(solution)/shard_map/ppermute | solution.py:261
  65.2 11.5 %copy-start.14 = (bf16[1040,128]{1,0:T(8,128)(2,1)}, bf16[1040,128]{1,0:T(8,128)(2,1)S(1)}, u32[]{:S(2)}) copy-start(bf16[1040,128]{1,0:T(8,128)(2,1)S(1)} %collective-permute-done.8.refs_7_) | copy-start | bytes 798724
  65.2 11.5 %copy-start.15 = (bf16[1040,128]{1,0:T(8,128)(2,1)}, bf16[1040,128]{1,0:T(8,128)(2,1)S(1)}, u32[]{:S(2)}) copy-start(bf16[1040,128]{1,0:T(8,128)(2,1)S(1)} %collective-permute-done.9.refs_8_) | copy-start | bytes 798724
  65.3 11.5 %copy-start.16 = (bf16[1040,128]{1,0:T(8,128)(2,1)}, bf16[1040,128]{1,0:T(8,128)(2,1)S(1)}, u32[]{:S(2)}) copy-start(bf16[1040,128]{1,0:T(8,128)(2,1)S(1)} %collective-permute-done.10.refs_9_) | copy-start | bytes 798724
  73.0 3.7 %copy-start.17 = (bf16[1040,128]{1,0:T(8,128)(2,1)}, bf16[1040,128]{1,0:T(8,128)(2,1)S(1)}, u32[]{:S(2)}) copy-start(bf16[1040,128]{1,0:T(8,128)(2,1)S(1)} %collective-permute-done.11.refs_10_) | copy-start | bytes 798724
  76.7 0.7 copy-start.18
  96.9 14.0 %collective-permute-start.13 = (f32[16,128,128]{2,1,0:T(8,128)}, f32[16,128,128]{2,1,0:T(8,128)S(1)}, u32[]{:S(2)}, u32[]{:S(2)}) collective-permute-start(f32[16,128,128]{2,1,0:T(8,128)} %get-tuple-element.37), channel_id=1, source_target_pairs={{0,1},{1,2},{2,3},{3,4},{4,5},{5,6},{6,7},{7,8},{8,9},{9,10},{10,1... | collective-permute-start | bytes 3145736 | tf_op jit(solution)/shard_map/ppermute | solution.py:235
  98.8 18.4 %collective-permute-start.14 = (f32[16,128,128]{2,1,0:T(8,128)}, f32[16,128,128]{2,1,0:T(8,128)S(1)}, u32[]{:S(2)}, u32[]{:S(2)}) collective-permute-start(f32[16,128,128]{2,1,0:T(8,128)} %get-tuple-element.38), channel_id=1, source_target_pairs={{1,0},{2,1},{3,2},{4,3},{5,4},{6,5},{7,6},{8,7},{9,8},{10,9},{11,1... | collective-permute-start | bytes 3145736 | tf_op jit(solution)/shard_map/ppermute | solution.py:235
  117.2 52.7 %copy-start = (f32[32,128,128]{2,1,0:T(8,128)S(1)}, f32[32,128,128]{2,1,0:T(8,128)}, u32[]{:S(2)}) copy-start(f32[32,128,128]{2,1,0:T(8,128)} %param.4) | copy-start | bytes 6291460
  119.3 50.6 %collective-permute-start.15 = (f32[32,128,128]{2,1,0:T(8,128)S(1)}, f32[32,128,128]{2,1,0:T(8,128)S(1)}, u32[]{:S(2)}, u32[]{:S(2)}) collective-permute-start(f32[32,128,128]{2,1,0:T(8,128)S(1)} %maximum_add_fusion), channel_id=1, source_target_pairs={{0,64},{64,0},{1,65},{65,1},{2,66},{66,2},{3,67},{67,3},{4,68},{68... | collective-permute-start | bytes 6291464 | tf_op jit(solution)/shard_map/ppermute | solution.py:248
  170.5 14.7 %copy-start.2 = (bf16[32,128,128]{2,1,0:T(8,128)(2,1)}, bf16[32,128,128]{2,1,0:T(8,128)(2,1)S(1)}, u32[]{:S(2)}) copy-start(bf16[32,128,128]{2,1,0:T(8,128)(2,1)S(1)} %fusion.29.refs_7_) | copy-start | bytes 3145732
  170.6 12.6 %collective-permute-start.17 = (bf16[16,128,128]{2,1,0:T(8,128)(2,1)S(1)}, bf16[16,128,128]{2,1,0:T(8,128)(2,1)S(1)}, u32[]{:S(2)}, u32[]{:S(2)}) collective-permute-start(bf16[16,128,128]{2,1,0:T(8,128)(2,1)S(1)} %get-tuple-element.43), channel_id=1, source_target_pairs={{1,0},{2,1},{3,2},{4,3},{5,4},{6,5},{7,6},{8,7},{9,8},{10,9},{11,1... | collective-permute-start | bytes 1572872 | tf_op jit(solution)/shard_map/ppermute | solution.py:235
  172.9 11.5 %collective-permute-start.16 = (bf16[16,128,128]{2,1,0:T(8,128)(2,1)S(1)}, bf16[16,128,128]{2,1,0:T(8,128)(2,1)S(1)}, u32[]{:S(2)}, u32[]{:S(2)}) collective-permute-start(bf16[16,128,128]{2,1,0:T(8,128)(2,1)S(1)} %get-tuple-element.44), channel_id=1, source_target_pairs={{0,1},{1,2},{2,3},{3,4},{4,5},{5,6},{6,7},{7,8},{8,9},{9,10},{10,1... | collective-permute-start | bytes 1572872 | tf_op jit(solution)/shard_map/ppermute | solution.py:235
  183.2 2.0 copy-start.7
  184.4 0.8 copy-start.8
  211.3 18.5 %collective-permute-start.18 = (f32[16,128,128]{2,1,0:T(8,128)}, f32[16,128,128]{2,1,0:T(8,128)S(1)}, u32[]{:S(2)}, u32[]{:S(2)}) collective-permute-start(f32[16,128,128]{2,1,0:T(8,128)} %get-tuple-element.41), channel_id=1, source_target_pairs={{0,1},{1,2},{2,3},{3,4},{4,5},{5,6},{6,7},{7,8},{8,9},{9,10},{10,1... | collective-permute-start | bytes 3145736 | tf_op jit(solution)/shard_map/ppermute | solution.py:235
  217.8 18.7 %collective-permute-start.19 = (f32[16,128,128]{2,1,0:T(8,128)}, f32[16,128,128]{2,1,0:T(8,128)S(1)}, u32[]{:S(2)}, u32[]{:S(2)}) collective-permute-start(f32[16,128,128]{2,1,0:T(8,128)} %get-tuple-element.42), channel_id=1, source_target_pairs={{1,0},{2,1},{3,2},{4,3},{5,4},{6,5},{7,6},{8,7},{9,8},{10,9},{11,1... | collective-permute-start | bytes 3145736 | tf_op jit(solution)/shard_map/ppermute | solution.py:235
  238.5 50.3 %collective-permute-start.20 = (f32[32,128,128]{2,1,0:T(8,128)S(1)}, f32[32,128,128]{2,1,0:T(8,128)S(1)}, u32[]{:S(2)}, u32[]{:S(2)}) collective-permute-start(f32[32,128,128]{2,1,0:T(8,128)S(1)} %maximum_add_fusion.1), channel_id=1, source_target_pairs={{0,64},{64,0},{1,65},{65,1},{2,66},{66,2},{3,67},{67,3},{4,68},{68... | collective-permute-start | bytes 6291464 | tf_op jit(solution)/shard_map/ppermute | solution.py:248

commit v3 on v2

--- a/solution.py
+++ b/solution.py
@@ -25,8 +25,10 @@
 SUB = 16
 F32 = jnp.float32
 BF16 = jnp.bfloat16
+F16 = jnp.float16
 VMEM_LIMIT = 56 << 20
 UNROLL = 2
+LEVELS = 7
 
 
 def banded(kernel, rows, cols, sign, offset):
@@ -101,6 +103,21 @@
     )(me, tile_dest[0], view_tiles.reshape(SLOTS, TROWS, Z))
 
 
+def level_of(peak):
+    level = jnp.full(peak.shape, -LEVELS, F32)
+    for j in range(-LEVELS, LEVELS):
+        level = jnp.where(peak > 2.0 ** (14 + 16 * j), j + 1.0, level)
+    return level
+
+
+def scale_of(level):
+    scale = jnp.ones(level.shape, F32)
+    for j in range(-LEVELS, LEVELS + 1):
+        if j:
+            scale = jnp.where(level == j, 2.0 ** (16 * j), scale)
+    return scale
+
+
 def swapped(block):
     return jnp.transpose(block, (1, 0, 2))
 
@@ -143,7 +160,9 @@
     lax.fori_loop(0, VIEWS_DEV * BX // TP, along_yz, 0, unroll=UNROLL)
 
 
-def back_from(kx_ref, ky_ref, kz_ref, measured_ref, blurred_ref, half_ref, outs):
+def back_from(kx_ref, ky_ref, kz_ref, measured_ref, blurred_ref, half_ref, edge_ref, outs):
+    left_ref, mid_ref, right_ref = outs
+
     def along_zy(q, carry):
         v = q // (BX // TP)
         ratio = (measured_ref[q].astype(F32) / blurred_ref[q]).astype(BF16)
@@ -161,7 +180,7 @@
 
     lax.fori_loop(0, VIEWS_DEV * BX // TP, along_zy, 0, unroll=UNROLL)
 
-    def along_x(t, carry):
+    def along_x(t, peak):
         y0 = pl.multiple_of(t * 8, 8)
         data = swapped(half_ref[:, pl.ds(y0, 8), :])
         high = data.astype(BF16)
@@ -174,14 +193,18 @@
             )
             got += [both[:, :Z], both[:, Z:]]
         planes = swapped(jnp.stack(got, axis=0))
-        first = 0
-        for ref in outs:
-            count = ref.shape[0]
-            ref[:, pl.ds(y0, 8), :] = planes[first : first + count]
-            first += count
-        return carry
-
-    lax.fori_loop(0, Y // 8, along_x, 0, unroll=UNROLL)
+        edge_ref[0, :, pl.ds(y0, 8), :] = planes[:HX]
+        mid_ref[:, pl.ds(y0, 8), :] = planes[HX : HX + BX]
+        edge_ref[1, :, pl.ds(y0, 8), :] = planes[HX + BX :]
+        return jnp.maximum(peak, jnp.max(planes, axis=0))
+
+    peak = lax.fori_loop(0, Y // 8, along_x, jnp.zeros((8, Z), F32), unroll=UNROLL)
+    level = level_of(jnp.full((8, Z), jnp.max(peak), F32))
+    shrink = scale_of(-level)[0:1]
+    for i, ref in enumerate((left_ref, right_ref)):
+        for p in range(HX):
+            ref[p * Y : (p + 1) * Y, :] = edge_ref[i, p] * shrink
+        ref[HX * Y :, :] = jnp.concatenate([level, level], axis=0)
 
 
 def first_blur_kernel(kx_ref, ky_ref, kz_ref, left_ref, mid_ref, right_ref, out_ref, half_ref):
@@ -190,29 +213,31 @@
 
 def first_back_kernel(kx_ref, ky_ref, kz_ref, blurred_ref, *refs):
     tiles = refs[:SPAN]
-    left_ref, mid_ref, right_ref, measured_ref, half_ref = refs[SPAN:]
+    left_ref, mid_ref, right_ref, measured_ref, half_ref, edge_ref = refs[SPAN:]
     for k in range(SPAN):
         for c in range(CAP):
             code = tiles[k][CAP * TROWS :, :].astype(F32)[8 * c, 0].astype(jnp.int32)
             measured_ref[code] = tiles[k][c * TROWS : (c + 1) * TROWS, :]
-    back_from(
-        kx_ref, ky_ref, kz_ref, measured_ref, blurred_ref, half_ref, (left_ref, mid_ref, right_ref)
-    )
+    outs = (left_ref, mid_ref, right_ref)
+    back_from(kx_ref, ky_ref, kz_ref, measured_ref, blurred_ref, half_ref, edge_ref, outs)
 
 
 def sweep_kernel(*refs):
     fwd, back, parts = refs[0:3], refs[3:6], refs[6:9]
     measured_ref = refs[9]
     outs = refs[10:13]
-    half_ref, back_half_ref, blurred_ref = refs[13:]
+    half_ref, back_half_ref, edge_ref, blurred_ref = refs[13:]
     blur_into(*fwd, parts, half_ref, blurred_ref)
-    back_from(*back, measured_ref, blurred_ref, back_half_ref, outs)
+    back_from(*back, measured_ref, blurred_ref, back_half_ref, edge_ref, outs)
 
 
 VM = pl.BlockSpec(memory_space=pltpu.VMEM)
 BLURRED = (VIEWS_DEV * BX // TP, TROWS, Z)
 HALF_SHAPE = (VIEWS_DEV * BX, Y, Z)
-CONTRIB = [jax.ShapeDtypeStruct((n, Y, Z), F32) for n in (HX, BX, HX)]
+EDGE_ROWS = HX * Y + SUB
+EDGE = jax.ShapeDtypeStruct((EDGE_ROWS, Z), F32)
+CONTRIB = [EDGE, jax.ShapeDtypeStruct((BX, Y, Z), F32), EDGE]
+EDGE_SCRATCH = pltpu.VMEM((2, HX, Y, Z), F32)
 
 
 def call(kernel, name, operands, out_shape, scratch, flops):
@@ -243,10 +268,27 @@
 
 def updated(estimate, contributions, view_count):
     left, mid, right = contributions
-    from_left, from_right = neighbours(left, right)
-    partial = mid + jnp.concatenate([from_left, from_right], axis=0)
-    other = lax.ppermute(partial, "view", [(0, 1), (1, 0)])
-    return estimate * (partial + other) / view_count
+    arrived = neighbours(*lax.optimization_barrier((left.astype(F16), right.astype(F16))))
+    level = left[HX * Y :]
+    added = []
+    for edge in arrived:
+        edge_level = edge[HX * Y :].astype(F32)
+        level = jnp.maximum(level, edge_level)
+        added.append((edge[: HX * Y].reshape(HX, Y, Z).astype(F32), scale_of(edge_level)[0, 0]))
+    scales, shrink, level = lax.optimization_barrier(
+        ([scale for _, scale in added], scale_of(-level)[0, 0], level)
+    )
+    partial = mid + jnp.concatenate(
+        [planes * scale for (planes, _), scale in zip(added, scales)], axis=0
+    )
+    own = lax.optimization_barrier((partial * shrink).astype(F16))
+    swap = [(0, 1), (1, 0)]
+    other, other_level = lax.ppermute((own, level), "view", swap)
+    own_scale, other_scale = lax.optimization_barrier(
+        (scale_of(level)[0, 0], scale_of(other_level)[0, 0])
+    )
+    total = own.astype(F32) * own_scale + other.astype(F32) * other_scale
+    return estimate * total / view_count
 
 
 def shards(estimate, view_tiles, tile_dest, psf_taps):
@@ -273,7 +315,7 @@
         "first_back",
         (*back, blurred, *arrived),
         [*CONTRIB, jax.ShapeDtypeStruct((VIEWS_DEV * BX // TP, TROWS, Z), BF16)],
-        [pltpu.VMEM(HALF_SHAPE, F32)],
+        [pltpu.VMEM(HALF_SHAPE, F32), EDGE_SCRATCH],
         8 << 30,
     )
     estimate = updated(estimate, contributions, view_count)
@@ -285,6 +327,7 @@
         [
             pltpu.VMEM(HALF_SHAPE, F32),
             pltpu.VMEM(HALF_SHAPE, F32),
+            EDGE_SCRATCH,
             pltpu.VMEM(BLURRED, F32),
         ],
         14 << 30,

time: 297 us -> 282 us (0.949)
  the two profiles are of different devices: /device:TPU:97 before, /device:TPU:24 now
where the time goes in v3:
time: 282 us; the launch traced here: 281 us
  waiting for transfers between devices  72 us (26%)
  starting transfers between devices  63.5 us (23%)
  Pallas kernels  62.9 us (22%)
  between operations  45.8 us (16%)
  local copies, waits for them, and re-layouts  19.7 us (7%)
  other arithmetic  13.7 us (5%)
  matrix products  3.57 us (1%)
    pallas_call x3, Pallas kernels, call(): pl.pallas_call(kernel, out_shape=out_shape, in_specs=[VM] * len(operands)...  58.9 us
    ppermute x8, starting transfers between devices, neighbours(): return (lax.ppermute(high, 'block', up), lax.ppermute(low, 'block', down))  42.3 us
    ppermute x11, waiting for transfers between devices, shards(): arrived.append(lax.ppermute(packed[k], 'block', perm) if by else packed[k])  24.5 us
    ppermute x8, waiting for transfers between devices, neighbours(): return (lax.ppermute(high, 'block', up), lax.ppermute(low, 'block', down))  24.3 us
    ppermute x4, waiting for transfers between devices, updated(): other, other_level = lax.ppermute((own, level), 'view', swap)  23.2 us
    ppermute x11, starting transfers between devices, shards(): arrived.append(lax.ppermute(packed[k], 'block', perm) if by else packed[k])  13.9 us
    ppermute x4, starting transfers between devices, updated(): other, other_level = lax.ppermute((own, level), 'view', swap)  7.22 us
    slice x12, local copies, waits for them, and re-layouts, updated(): scale_of(edge_level)[0, 0]  6.37 us
  transfers between devices with their start and end apart: 23, of which 12 were waited for; matrix products, arithmetic and copies ran while one was open for 6% of the time, Pallas kernels for 6%

profile of v3, /device:TPU:24, one launch (start us, length us, event | category | flops | bytes accessed | tf_op | source)
XLA Modules:
  0.0 281.1 jit_solution(16839069163146119924)
XLA Ops:
  0.0 1.8 convert_element_type.76.mid_ref
  1.9 7.9 %collective-permute-start.1 = (bf16[16,128,128]{2,1,0:T(8,128)(2,1)S(1)}, bf16[16,128,128]{2,1,0:T(8,128)(2,1)S(1)}, u32[]{:S(2)}, u32[]{:S(2)}) collective-permute-start(bf16[16,128,128]{2,1,0:T(8,128)(2,1)S(1)} %get-tuple-element.81), channel_id=1, source_target_pairs={{1,0},{2,1},{3,2},{4,3},{5,4},{6,5},{7,6},{8,7},{9,8},{10,9},{11,1... | collective-permute-start | bytes 1572872 | tf_op jit(solution)/shard_map/ppermute | solution.py:260
  9.8 1.9 collective-permute-start
  11.8 0.7 copy.28
  12.4 3.9 %pack_tiles.1 = (bf16[1040,128]{1,0:T(8,128)(2,1)}, bf16[1040,128]{1,0:T(8,128)(2,1)}, bf16[1040,128]{1,0:T(8,128)(2,1)}, bf16[1040,128]{1,0:T(8,128)(2,1)}, bf1...) custom-call(s32[1]{0:T(128)} %bitcast.5.me_ref, ...), custom_call_target="tpu_custom_call" | custom-call | bytes 6291456 | tf_op jit(solution)/shard_map/pack_tiles/pallas_call | solution.py:90
  16.4 1.7 collective-permute-start.3
  18.1 4.0 %collective-permute-start.4 = (bf16[1040,128]{1,0:T(8,128)(2,1)}, bf16[1040,128]{1,0:T(8,128)(2,1)}, u32[]{:S(2)}, u32[]{:S(2)}) collective-permute-start(bf16[1040,128]{1,0:T(8,128)(2,1)} %get-tuple-element.42), channel_id=1, source_target_pairs={{0,60},{1,61},{2,62},{3,63},{4,0},{5,1},{6,2},{7,3},{8,4},{9,5},{1... | collective-permute-start | bytes 798728 | tf_op jit(solution)/shard_map/ppermute | solution.py:303
  23.1 0.8 fusion.6
  23.9 0.8 fusion.5
  24.7 0.8 fusion.4
  25.5 0.8 fusion.7
  26.4 0.7 pad_maximum_fusion.ky_ref.refs_4_
  27.1 0.7 pad_maximum_fusion.3.kz_ref.refs_2_
  27.8 0.7 pad_maximum_fusion.4.kx_ref.refs_3_
  28.5 10.3 %collective-permute-done.2.refs_0_ = bf16[1040,128]{1,0:T(8,128)(2,1)S(1)} collective-permute-done((bf16[1040,128]{1,0:T(8,128)(2,1)}, bf16[1040,128]{1,0:T(8,128)(2,1)S(1)}, u32[]{:S(2)}, u32[]{:S(2)}) %collective-permute-start.2) | collective-permute-done | bytes 266272 | tf_op jit(solution)/shard_map/ppermute | solution.py:303
  38.9 2.8 collective-permute-start.7
  41.7 0.7 pad_maximum_fusion.5.kx_ref.refs_0_
  42.4 0.7 pad_maximum_fusion.1.kz_ref.refs_5_
  43.1 0.7 pad_maximum_fusion.2.ky_ref.refs_1_
  43.8 6.1 %collective-permute-done.5.refs_3_ = bf16[1040,128]{1,0:T(8,128)(2,1)S(1)} collective-permute-done((bf16[1040,128]{1,0:T(8,128)(2,1)S(1)}, bf16[1040,128]{1,0:T(8,128)(2,1)S(1)}, u32[]{:S(2)}, u32[]{:S(2)}) %collective-permute-start.5) | collective-permute-done | bytes 266272 | tf_op jit(solution)/shard_map/ppermute | solution.py:303
  49.9 0.8 collective-permute-done.6.refs_4_
  50.7 2.8 collective-permute-done.7.refs_5_
  53.5 1.5 collective-permute-start.10
  54.9 3.8 %collective-permute-start.11 = (bf16[1040,128]{1,0:T(8,128)(2,1)S(1)}, bf16[1040,128]{1,0:T(8,128)(2,1)S(1)}, u32[]{:S(2)}, u32[]{:S(2)}) collective-permute-start(bf16[1040,128]{1,0:T(8,128)(2,1)S(1)} %copy-done.16), channel_id=1, source_target_pairs={{0,4},{1,5},{2,6},{3,7},{4,8},{5,9},{6,10},{7,11},{8,12},{9,13},{1... | collective-permute-start | bytes 798728 | tf_op jit(solution)/shard_map/ppermute | solution.py:303
  58.9 0.7 copy-done.10
  59.6 12.8 %first_blur.1.blurred_ref = f32[24,512,128]{2,1,0:T(8,128)} custom-call(bf16[96,128]{1,0:T(8,128)(2,1)} %pad_maximum_fusion.5.kx_ref.refs_0_, bf16[3,128,256]{2,1,0:T(8,128)(2,1)} %pad_maximum_fusion.2.ky_ref.refs_1_, bf16[3,256,128]{2,1,0:T(8,128)(2,1)} %pad_maximum_fusion.3.kz_ref.refs_2_, bf16[16,128,128]{2,1,0:T(8,128)(2,1)} %copy-done.10, ...), custom_call_target="tpu_custom_call" | custom-call | flops 6442450944 | bytes 12582912 | tf_op jit(solution)/shard_map/first_blur/pallas_call | solution.py:244
  72.4 4.6 %collective-permute-done.11.refs_10_ = bf16[1040,128]{1,0:T(8,128)(2,1)S(1)} collective-permute-done((bf16[1040,128]{1,0:T(8,128)(2,1)S(1)}, bf16[1040,128]{1,0:T(8,128)(2,1)S(1)}, u32[]{:S(2)}, u32[]{:S(2)}) %collective-permute-start.11) | collective-permute-done | bytes 266272 | tf_op jit(solution)/shard_map/ppermute | solution.py:303
  77.1 0.7 copy-done.29
  77.9 19.9 %first_back.1 = (f32[2064,128]{1,0:T(8,128)}, f32[32,128,128]{2,1,0:T(8,128)}, f32[2064,128]{1,0:T(8,128)}, bf16[24,512,128]{2,1,0:T(8,128)(2,1)}) custom-call(bf16[64,192]{1,0:T(8,128)(2,1)} %pad_maximum_fusion.4.kx_ref.refs_3_, bf16[3,128,256]{2,1,0:T(8,128)(2,1)} %pad_maximum_fusion.ky_ref.refs_4_, bf16[3,256,128]{2,1,0:T(8,128)(2,1)} %pad_maximum_fusion.1.kz_ref.refs_5_, ...), custom_call_target="tpu_custom_call" | custom-call | flops 8589934592 | bytes 12582912 | tf_op jit(solution)/shard_map/first_back/pallas_call | solution.py:244
  97.8 1.4 convert_element_type.78
  99.4 5.7 %collective-permute-start.13 = (f16[2064,128]{1,0:T(8,128)(2,1)S(1)}, f16[2064,128]{1,0:T(8,128)(2,1)S(1)}, u32[]{:S(2)}, u32[]{:S(2)}) collective-permute-start(f16[2064,128]{1,0:T(8,128)(2,1)S(1)} %convert_element_type.78), channel_id=1, source_target_pairs={{0,1},{1,2},{2,3},{3,4},{4,5},{5,6},{6,7},{7,8},{8,9},{9,10},{10,1... | collective-permute-start | bytes 1585160 | tf_op jit(solution)/shard_map/ppermute | solution.py:260
  105.2 11.7 %collective-permute-start.14 = (f16[2064,128]{1,0:T(8,128)(2,1)S(1)}, f16[2064,128]{1,0:T(8,128)(2,1)S(1)}, u32[]{:S(2)}, u32[]{:S(2)}) collective-permute-start(f16[2064,128]{1,0:T(8,128)(2,1)S(1)} %convert_element_type.77), channel_id=1, source_target_pairs={{1,0},{2,1},{3,2},{4,3},{5,4},{6,5},{7,6},{8,7},{9,8},{10,9},{11,1... | collective-permute-start | bytes 1585160 | tf_op jit(solution)/shard_map/ppermute | solution.py:260
  116.9 4.8 %collective-permute-done.13 = f16[2064,128]{1,0:T(8,128)(2,1)S(1)} collective-permute-done((f16[2064,128]{1,0:T(8,128)(2,1)S(1)}, f16[2064,128]{1,0:T(8,128)(2,1)S(1)}, u32[]{:S(2)}, u32[]{:S(2)}) %collective-permute-start.13) | collective-permute-done | bytes 528416 | tf_op jit(solution)/shard_map/ppermute | solution.py:260
  121.7 1.8 collective-permute-done.14
  123.5 0.5 slice.115
  125.2 0.6 slice.122
  136.4 0.6 slice.123
  137.0 0.6 slice.120
  141.9 1.0 collective-permute-start.16
  142.9 2.6 collective-permute-start.15
  151.6 16.6 %collective-permute-done.15 = f32[16,128]{1,0:T(8,128)S(1)} collective-permute-done((f32[16,128]{1,0:T(8,128)S(1)}, f32[16,128]{1,0:T(8,128)S(1)}, u32[]{:S(2)}, u32[]{:S(2)}) %collective-permute-start.15) | collective-permute-done | bytes 8224 | tf_op jit(solution)/shard_map/ppermute | solution.py:286
  172.4 0.6 slice.131
  174.3 0.7 fusion.13.refs_7_
  175.1 3.2 %collective-permute-start.18 = (bf16[16,128,128]{2,1,0:T(8,128)(2,1)S(1)}, bf16[16,128,128]{2,1,0:T(8,128)(2,1)S(1)}, u32[]{:S(2)}, u32[]{:S(2)}) collective-permute-start(bf16[16,128,128]{2,1,0:T(8,128)(2,1)S(1)} %get-tuple-element.79), channel_id=1, source_target_pairs={{1,0},{2,1},{3,2},{4,3},{5,4},{6,5},{7,6},{8,7},{9,8},{10,9},{11,1... | collective-permute-start | bytes 1572872 | tf_op jit(solution)/shard_map/ppermute | solution.py:260
  178.3 1.9 collective-permute-start.17
  180.3 4.7 %collective-permute-done.18.refs_8_ = bf16[16,128,128]{2,1,0:T(8,128)(2,1)S(1)} collective-permute-done((bf16[16,128,128]{2,1,0:T(8,128)(2,1)S(1)}, bf16[16,128,128]{2,1,0:T(8,128)(2,1)S(1)}, u32[]{:S(2)}, u32[]{:S(2)}) %collective-permute-start.18) | collective-permute-done | bytes 524320 | tf_op jit(solution)/shard_map/ppermute | solution.py:260
  185.0 8.0 %collective-permute-done.17.refs_6_ = bf16[16,128,128]{2,1,0:T(8,128)(2,1)S(1)} collective-permute-done((bf16[16,128,128]{2,1,0:T(8,128)(2,1)S(1)}, bf16[16,128,128]{2,1,0:T(8,128)(2,1)S(1)}, u32[]{:S(2)}, u32[]{:S(2)}) %collective-permute-start.17) | collective-permute-done | bytes 524320 | tf_op jit(solution)/shard_map/ppermute | solution.py:260
  193.1 0.8 copy-done.12
  193.9 26.2 %sweep.1 = (f32[2064,128]{1,0:T(8,128)}, f32[32,128,128]{2,1,0:T(8,128)}, f32[2064,128]{1,0:T(8,128)}) custom-call(bf16[96,128]{1,0:T(8,128)(2,1)} %pad_maximum_fusion.5.kx_ref.refs_0_, bf16[3,128,256]{2,1,0:T(8,128)(2,1)} %pad_maximum_fusion.2.ky_ref.refs_1_, bf16[3,256,128]{2,1,0:T(8,128)(2,1)} %pad_maximum_fusion.3.kz_ref.refs_2_, ...), custom_call_target="tpu_custom_call" | custom-call | flops 15032385536 | bytes 12582912 | tf_op jit(solution)/shard_map/sweep/pallas_call | solution.py:244
  220.1 1.4 convert_element_type.88
  221.7 2.1 collective-permute-start.19
  223.8 7.9 %collective-permute-start.20 = (f16[2064,128]{1,0:T(8,128)(2,1)S(1)}, f16[2064,128]{1,0:T(8,128)(2,1)S(1)}, u32[]{:S(2)}, u32[]{:S(2)}) collective-permute-start(f16[2064,128]{1,0:T(8,128)(2,1)S(1)} %convert_element_type.87), channel_id=1, source_target_pairs={{1,0},{2,1},{3,2},{4,3},{5,4},{6,5},{7,6},{8,7},{9,8},{10,9},{11,1... | collective-permute-start | bytes 1585160 | tf_op jit(solution)/shard_map/ppermute | solution.py:260
  231.7 5.0 %collective-permute-done.19 = f16[2064,128]{1,0:T(8,128)(2,1)S(1)} collective-permute-done((f16[2064,128]{1,0:T(8,128)(2,1)S(1)}, f16[2064,128]{1,0:T(8,128)(2,1)S(1)}, u32[]{:S(2)}, u32[]{:S(2)}) %collective-permute-start.19) | collective-permute-done | bytes 528416 | tf_op jit(solution)/shard_map/ppermute | solution.py:260
  236.6 0.6 slice.136
  240.7 0.6 slice.143
  244.6 0.6 slice.140
  249.1 0.6 slice.142
  250.2 0.6 slice.145
  250.8 0.6 slice.144
  256.2 1.0 collective-permute-start.22
  257.3 2.6 collective-permute-start.21
  264.1 0.6 slice.149
  266.1 6.6 %collective-permute-done.21 = f32[16,128]{1,0:T(8,128)S(1)} collective-permute-done((f32[16,128]{1,0:T(8,128)S(1)}, f32[16,128]{1,0:T(8,128)S(1)}, u32[]{:S(2)}, u32[]{:S(2)}) %collective-permute-start.21) | collective-permute-done | bytes 8224 | tf_op jit(solution)/shard_map/ppermute | solution.py:286
  278.7 2.4 multiply_multiply_fusion
  (143 shorter events, 12.7 us)
Async XLA Ops:
  0.0 11.7 %copy-start.8 = (s32[1,24,3]{1,0,2:T(1,128)S(1)}, s32[1,24,3]{1,0,2:T(1,128)}, u32[]{:S(2)}) copy-start(s32[1,24,3]{1,0,2:T(1,128)} %param.6) | copy-start | bytes 868
  1.8 14.6 %copy-start.1 = (bf16[32,128,128]{2,1,0:T(8,128)(2,1)}, bf16[32,128,128]{2,1,0:T(8,128)(2,1)S(1)}, u32[]{:S(2)}) copy-start(bf16[32,128,128]{2,1,0:T(8,128)(2,1)S(1)} %convert_element_type.76.mid_ref) | copy-start | bytes 3145732
  1.9 20.1 %copy-start.7 = (f32[3,3,31]{2,1,0:T(4,128)S(1)}, f32[3,3,31]{2,1,0:T(4,128)}, u32[]{:S(2)}) copy-start(f32[3,3,31]{2,1,0:T(4,128)} %param.7) | copy-start | bytes 3352
  1.9 53.0 %collective-permute-start.1 = (bf16[16,128,128]{2,1,0:T(8,128)(2,1)S(1)}, bf16[16,128,128]{2,1,0:T(8,128)(2,1)S(1)}, u32[]{:S(2)}, u32[]{:S(2)}) collective-permute-start(bf16[16,128,128]{2,1,0:T(8,128)(2,1)S(1)} %get-tuple-element.81), channel_id=1, source_target_pairs={{1,0},{2,1},{3,2},{4,3},{5,4},{6,5},{7,6},{8,7},{9,8},{10,9},{11,1... | collective-permute-start | bytes 1572872 | tf_op jit(solution)/shard_map/ppermute | solution.py:260
  9.8 49.0 %collective-permute-start = (bf16[16,128,128]{2,1,0:T(8,128)(2,1)S(1)}, bf16[16,128,128]{2,1,0:T(8,128)(2,1)S(1)}, u32[]{:S(2)}, u32[]{:S(2)}) collective-permute-start(bf16[16,128,128]{2,1,0:T(8,128)(2,1)S(1)} %get-tuple-element.82), channel_id=1, source_target_pairs={{0,1},{1,2},{2,3},{3,4},{4,5},{5,6},{6,7},{7,8},{8,9},{9,10},{10,1... | collective-permute-start | bytes 1572872 | tf_op jit(solution)/shard_map/ppermute | solution.py:260
  16.4 22.4 %collective-permute-start.2 = (bf16[1040,128]{1,0:T(8,128)(2,1)}, bf16[1040,128]{1,0:T(8,128)(2,1)S(1)}, u32[]{:S(2)}, u32[]{:S(2)}) collective-permute-start(bf16[1040,128]{1,0:T(8,128)(2,1)} %get-tuple-element.40), channel_id=1, source_target_pairs={{0,58},{1,59},{2,60},{3,61},{4,62},{5,63},{6,0},{7,1},{8,2},{9,3},... | collective-permute-start | bytes 798728 | tf_op jit(solution)/shard_map/ppermute | solution.py:303
  16.4 22.4 %collective-permute-start.3 = (bf16[1040,128]{1,0:T(8,128)(2,1)}, bf16[1040,128]{1,0:T(8,128)(2,1)S(1)}, u32[]{:S(2)}, u32[]{:S(2)}) collective-permute-start(bf16[1040,128]{1,0:T(8,128)(2,1)} %get-tuple-element.41), channel_id=1, source_target_pairs={{0,59},{1,60},{2,61},{3,62},{4,63},{5,0},{6,1},{7,2},{8,3},{9,4},{... | collective-permute-start | bytes 798728 | tf_op jit(solution)/shard_map/ppermute | solution.py:303
  18.1 20.9 %collective-permute-start.4 = (bf16[1040,128]{1,0:T(8,128)(2,1)}, bf16[1040,128]{1,0:T(8,128)(2,1)}, u32[]{:S(2)}, u32[]{:S(2)}) collective-permute-start(bf16[1040,128]{1,0:T(8,128)(2,1)} %get-tuple-element.42), channel_id=1, source_target_pairs={{0,60},{1,61},{2,62},{3,63},{4,0},{5,1},{6,2},{7,3},{8,4},{9,5},{1... | collective-permute-start | bytes 798728 | tf_op jit(solution)/shard_map/ppermute | solution.py:303
  23.9 14.9 %copy-start.22 = (bf16[1040,128]{1,0:T(8,128)(2,1)S(1)}, bf16[1040,128]{1,0:T(8,128)(2,1)}, u32[]{:S(2)}) copy-start(bf16[1040,128]{1,0:T(8,128)(2,1)} %get-tuple-element.43) | copy-start | bytes 798724
  23.9 14.9 %copy-start.21 = (bf16[1040,128]{1,0:T(8,128)(2,1)S(1)}, bf16[1040,128]{1,0:T(8,128)(2,1)}, u32[]{:S(2)}) copy-start(bf16[1040,128]{1,0:T(8,128)(2,1)} %get-tuple-element.44) | copy-start | bytes 798724
  23.9 15.0 %copy-start.20 = (bf16[1040,128]{1,0:T(8,128)(2,1)S(1)}, bf16[1040,128]{1,0:T(8,128)(2,1)}, u32[]{:S(2)}) copy-start(bf16[1040,128]{1,0:T(8,128)(2,1)} %get-tuple-element.45) | copy-start | bytes 798724
  25.5 24.4 %copy-start.19 = (bf16[1040,128]{1,0:T(8,128)(2,1)S(1)}, bf16[1040,128]{1,0:T(8,128)(2,1)}, u32[]{:S(2)}) copy-start(bf16[1040,128]{1,0:T(8,128)(2,1)} %get-tuple-element.47) | copy-start | bytes 798724
  25.5 25.1 %copy-start.18 = (bf16[1040,128]{1,0:T(8,128)(2,1)S(1)}, bf16[1040,128]{1,0:T(8,128)(2,1)}, u32[]{:S(2)}) copy-start(bf16[1040,128]{1,0:T(8,128)(2,1)} %get-tuple-element.48) | copy-start | bytes 798724
  25.5 28.0 %copy-start.17 = (bf16[1040,128]{1,0:T(8,128)(2,1)S(1)}, bf16[1040,128]{1,0:T(8,128)(2,1)}, u32[]{:S(2)}) copy-start(bf16[1040,128]{1,0:T(8,128)(2,1)} %get-tuple-element.49) | copy-start | bytes 798724
  25.5 29.4 %copy-start.16 = (bf16[1040,128]{1,0:T(8,128)(2,1)S(1)}, bf16[1040,128]{1,0:T(8,128)(2,1)}, u32[]{:S(2)}) copy-start(bf16[1040,128]{1,0:T(8,128)(2,1)} %get-tuple-element.50) | copy-start | bytes 798724
  25.5 33.3 %copy-start.14 = (bf16[1040,128]{1,0:T(8,128)(2,1)S(1)}, bf16[1040,128]{1,0:T(8,128)(2,1)}, u32[]{:S(2)}) copy-start(bf16[1040,128]{1,0:T(8,128)(2,1)} %get-tuple-element.51) | copy-start | bytes 798724
  38.8 33.6 %copy-start.13 = (bf16[1040,128]{1,0:T(8,128)(2,1)}, bf16[1040,128]{1,0:T(8,128)(2,1)S(1)}, u32[]{:S(2)}) copy-start(bf16[1040,128]{1,0:T(8,128)(2,1)S(1)} %collective-permute-done.2.refs_0_) | copy-start | bytes 798724
  38.8 11.1 %collective-permute-start.5 = (bf16[1040,128]{1,0:T(8,128)(2,1)S(1)}, bf16[1040,128]{1,0:T(8,128)(2,1)S(1)}, u32[]{:S(2)}, u32[]{:S(2)}) collective-permute-start(bf16[1040,128]{1,0:T(8,128)(2,1)S(1)} %copy-done.22), channel_id=1, source_target_pairs={{0,61},{1,62},{2,63},{3,0},{4,1},{5,2},{6,3},{7,4},{8,5},{9,6},{10... | collective-permute-start | bytes 798728 | tf_op jit(solution)/shard_map/ppermute | solution.py:303
  38.8 33.5 %copy-start.15 = (bf16[1040,128]{1,0:T(8,128)(2,1)}, bf16[1040,128]{1,0:T(8,128)(2,1)S(1)}, u32[]{:S(2)}) copy-start(bf16[1040,128]{1,0:T(8,128)(2,1)S(1)} %collective-permute-done.3.refs_1_) | copy-start | bytes 798724
  38.8 11.8 %collective-permute-start.6 = (bf16[1040,128]{1,0:T(8,128)(2,1)S(1)}, bf16[1040,128]{1,0:T(8,128)(2,1)S(1)}, u32[]{:S(2)}, u32[]{:S(2)}) collective-permute-start(bf16[1040,128]{1,0:T(8,128)(2,1)S(1)} %copy-done.21), channel_id=1, source_target_pairs={{0,62},{1,63},{2,0},{3,1},{4,2},{5,3},{6,4},{7,5},{8,6},{9,7},{10,... | collective-permute-start | bytes 798728 | tf_op jit(solution)/shard_map/ppermute | solution.py:303
  38.9 14.5 %collective-permute-start.7 = (bf16[1040,128]{1,0:T(8,128)(2,1)S(1)}, bf16[1040,128]{1,0:T(8,128)(2,1)S(1)}, u32[]{:S(2)}, u32[]{:S(2)}) collective-permute-start(bf16[1040,128]{1,0:T(8,128)(2,1)S(1)} %copy-done.20), channel_id=1, source_target_pairs={{0,63},{1,0},{2,1},{3,2},{4,3},{5,4},{6,5},{7,6},{8,7},{9,8},{10,9... | collective-permute-start | bytes 798728 | tf_op jit(solution)/shard_map/ppermute | solution.py:303
  49.9 22.5 %copy-start.23 = (bf16[1040,128]{1,0:T(8,128)(2,1)}, bf16[1040,128]{1,0:T(8,128)(2,1)S(1)}, u32[]{:S(2)}) copy-start(bf16[1040,128]{1,0:T(8,128)(2,1)S(1)} %collective-permute-done.5.refs_3_) | copy-start | bytes 798724
  49.9 22.5 %collective-permute-start.8 = (bf16[1040,128]{1,0:T(8,128)(2,1)S(1)}, bf16[1040,128]{1,0:T(8,128)(2,1)S(1)}, u32[]{:S(2)}, u32[]{:S(2)}) collective-permute-start(bf16[1040,128]{1,0:T(8,128)(2,1)S(1)} %copy-done.19), channel_id=1, source_target_pairs={{0,1},{1,2},{2,3},{3,4},{4,5},{5,6},{6,7},{7,8},{8,9},{9,10},{10,1... | collective-permute-start | bytes 798728 | tf_op jit(solution)/shard_map/ppermute | solution.py:303
  50.6 21.8 %copy-start.24 = (bf16[1040,128]{1,0:T(8,128)(2,1)}, bf16[1040,128]{1,0:T(8,128)(2,1)S(1)}, u32[]{:S(2)}) copy-start(bf16[1040,128]{1,0:T(8,128)(2,1)S(1)} %collective-permute-done.6.refs_4_) | copy-start | bytes 798724
  50.6 21.8 %collective-permute-start.9 = (bf16[1040,128]{1,0:T(8,128)(2,1)S(1)}, bf16[1040,128]{1,0:T(8,128)(2,1)S(1)}, u32[]{:S(2)}, u32[]{:S(2)}) collective-permute-start(bf16[1040,128]{1,0:T(8,128)(2,1)S(1)} %copy-done.18), channel_id=1, source_target_pairs={{0,2},{1,3},{2,4},{3,5},{4,6},{5,7},{6,8},{7,9},{8,10},{9,11},{10,... | collective-permute-start | bytes 798728 | tf_op jit(solution)/shard_map/ppermute | solution.py:303
  53.5 18.9 %copy-start.25 = (bf16[1040,128]{1,0:T(8,128)(2,1)}, bf16[1040,128]{1,0:T(8,128)(2,1)S(1)}, u32[]{:S(2)}) copy-start(bf16[1040,128]{1,0:T(8,128)(2,1)S(1)} %collective-permute-done.7.refs_5_) | copy-start | bytes 798724
  53.5 19.0 %collective-permute-start.10 = (bf16[1040,128]{1,0:T(8,128)(2,1)S(1)}, bf16[1040,128]{1,0:T(8,128)(2,1)S(1)}, u32[]{:S(2)}, u32[]{:S(2)}) collective-permute-start(bf16[1040,128]{1,0:T(8,128)(2,1)S(1)} %copy-done.17), channel_id=1, source_target_pairs={{0,3},{1,4},{2,5},{3,6},{4,7},{5,8},{6,9},{7,10},{8,11},{9,12},{10... | collective-permute-start | bytes 798728 | tf_op jit(solution)/shard_map/ppermute | solution.py:303
  54.9 3.9 %copy-start.9 = (bf16[16,128,128]{2,1,0:T(8,128)(2,1)}, bf16[16,128,128]{2,1,0:T(8,128)(2,1)S(1)}, u32[]{:S(2)}) copy-start(bf16[16,128,128]{2,1,0:T(8,128)(2,1)S(1)} %collective-permute-done.1.right_ref) | copy-start | bytes 1572868
  54.9 22.1 %collective-permute-start.11 = (bf16[1040,128]{1,0:T(8,128)(2,1)S(1)}, bf16[1040,128]{1,0:T(8,128)(2,1)S(1)}, u32[]{:S(2)}, u32[]{:S(2)}) collective-permute-start(bf16[1040,128]{1,0:T(8,128)(2,1)S(1)} %copy-done.16), channel_id=1, source_target_pairs={{0,4},{1,5},{2,6},{3,7},{4,8},{5,9},{6,10},{7,11},{8,12},{9,13},{1... | collective-permute-start | bytes 798728 | tf_op jit(solution)/shard_map/ppermute | solution.py:303
  58.8 0.8 copy-start.10
  58.8 18.3 %collective-permute-start.12 = (bf16[1040,128]{1,0:T(8,128)(2,1)S(1)}, bf16[1040,128]{1,0:T(8,128)(2,1)S(1)}, u32[]{:S(2)}, u32[]{:S(2)}) collective-permute-start(bf16[1040,128]{1,0:T(8,128)(2,1)S(1)} %copy-done.14), channel_id=1, source_target_pairs={{0,5},{1,6},{2,7},{3,8},{4,9},{5,10},{6,11},{7,12},{8,13},{9,14},{... | collective-permute-start | bytes 798728 | tf_op jit(solution)/shard_map/ppermute | solution.py:303
  72.4 4.6 %copy-start.26 = (bf16[1040,128]{1,0:T(8,128)(2,1)}, bf16[1040,128]{1,0:T(8,128)(2,1)S(1)}, u32[]{:S(2)}) copy-start(bf16[1040,128]{1,0:T(8,128)(2,1)S(1)} %collective-permute-done.8.refs_7_) | copy-start | bytes 798724
  72.4 4.6 %copy-start.27 = (bf16[1040,128]{1,0:T(8,128)(2,1)}, bf16[1040,128]{1,0:T(8,128)(2,1)S(1)}, u32[]{:S(2)}) copy-start(bf16[1040,128]{1,0:T(8,128)(2,1)S(1)} %collective-permute-done.9.refs_8_) | copy-start | bytes 798724
  72.4 4.6 %copy-start.28 = (bf16[1040,128]{1,0:T(8,128)(2,1)}, bf16[1040,128]{1,0:T(8,128)(2,1)S(1)}, u32[]{:S(2)}) copy-start(bf16[1040,128]{1,0:T(8,128)(2,1)S(1)} %collective-permute-done.10.refs_9_) | copy-start | bytes 798724
  77.0 0.7 copy-start.29
  77.0 0.8 copy-start.30
  97.8 1.5 copy-start.6
  99.3 42.1 %copy-start.3 = (f32[32,128,128]{2,1,0:T(8,128)S(1)}, f32[32,128,128]{2,1,0:T(8,128)}, u32[]{:S(2)}) copy-start(f32[32,128,128]{2,1,0:T(8,128)} %get-tuple-element.52) | copy-start | bytes 6291460
  99.4 22.3 %collective-permute-start.13 = (f16[2064,128]{1,0:T(8,128)(2,1)S(1)}, f16[2064,128]{1,0:T(8,128)(2,1)S(1)}, u32[]{:S(2)}, u32[]{:S(2)}) collective-permute-start(f16[2064,128]{1,0:T(8,128)(2,1)S(1)} %convert_element_type.78), channel_id=1, source_target_pairs={{0,1},{1,2},{2,3},{3,4},{4,5},{5,6},{6,7},{7,8},{8,9},{9,10},{10,1... | collective-permute-start | bytes 1585160 | tf_op jit(solution)/shard_map/ppermute | solution.py:260
  105.2 18.3 %collective-permute-start.14 = (f16[2064,128]{1,0:T(8,128)(2,1)S(1)}, f16[2064,128]{1,0:T(8,128)(2,1)S(1)}, u32[]{:S(2)}, u32[]{:S(2)}) collective-permute-start(f16[2064,128]{1,0:T(8,128)(2,1)S(1)} %convert_element_type.77), channel_id=1, source_target_pairs={{1,0},{2,1},{3,2},{4,3},{5,4},{6,5},{7,6},{8,7},{9,8},{10,9},{11,1... | collective-permute-start | bytes 1585160 | tf_op jit(solution)/shard_map/ppermute | solution.py:260
  141.4 32.9 %copy-start = (f32[32,128,128]{2,1,0:T(8,128)S(1)}, f32[32,128,128]{2,1,0:T(8,128)}, u32[]{:S(2)}) copy-start(f32[32,128,128]{2,1,0:T(8,128)} %param.4) | copy-start | bytes 6291460
  141.9 32.4 %collective-permute-start.16 = (f16[32,128,128]{2,1,0:T(8,128)(2,1)S(1)}, f16[32,128,128]{2,1,0:T(8,128)(2,1)S(1)}, u32[]{:S(2)}, u32[]{:S(2)}) collective-permute-start(f16[32,128,128]{2,1,0:T(8,128)(2,1)S(1)} %fusion.1), channel_id=1, source_target_pairs={{0,64},{64,0},{1,65},{65,1},{2,66},{66,2},{3,67},{67,3},{4,68},{68... | collective-permute-start | bytes 3145736 | tf_op jit(solution)/shard_map/ppermute | solution.py:286
  142.9 25.3 %collective-permute-start.15 = (f32[16,128]{1,0:T(8,128)S(1)}, f32[16,128]{1,0:T(8,128)S(1)}, u32[]{:S(2)}, u32[]{:S(2)}) collective-permute-start(f32[16,128]{1,0:T(8,128)S(1)} %get-tuple-element.60), channel_id=1, source_target_pairs={{0,64},{64,0},{1,65},{65,1},{2,66},{66,2},{3,67},{67,3},{4,68},{68... | collective-permute-start | bytes 24584 | tf_op jit(solution)/shard_map/ppermute | solution.py:286
  175.0 18.1 %copy-start.2 = (bf16[32,128,128]{2,1,0:T(8,128)(2,1)}, bf16[32,128,128]{2,1,0:T(8,128)(2,1)S(1)}, u32[]{:S(2)}) copy-start(bf16[32,128,128]{2,1,0:T(8,128)(2,1)S(1)} %fusion.13.refs_7_) | copy-start | bytes 3145732
  175.1 9.9 %collective-permute-start.18 = (bf16[16,128,128]{2,1,0:T(8,128)(2,1)S(1)}, bf16[16,128,128]{2,1,0:T(8,128)(2,1)S(1)}, u32[]{:S(2)}, u32[]{:S(2)}) collective-permute-start(bf16[16,128,128]{2,1,0:T(8,128)(2,1)S(1)} %get-tuple-element.79), channel_id=1, source_target_pairs={{1,0},{2,1},{3,2},{4,3},{5,4},{6,5},{7,6},{8,7},{9,8},{10,9},{11,1... | collective-permute-start | bytes 1572872 | tf_op jit(solution)/shard_map/ppermute | solution.py:260
  178.3 14.7 %collective-permute-start.17 = (bf16[16,128,128]{2,1,0:T(8,128)(2,1)S(1)}, bf16[16,128,128]{2,1,0:T(8,128)(2,1)S(1)}, u32[]{:S(2)}, u32[]{:S(2)}) collective-permute-start(bf16[16,128,128]{2,1,0:T(8,128)(2,1)S(1)} %get-tuple-element.80), channel_id=1, source_target_pairs={{0,1},{1,2},{2,3},{3,4},{4,5},{5,6},{6,7},{7,8},{8,9},{9,10},{10,1... | collective-permute-start | bytes 1572872 | tf_op jit(solution)/shard_map/ppermute | solution.py:260
  185.0 8.0 %copy-start.11 = (bf16[16,128,128]{2,1,0:T(8,128)(2,1)}, bf16[16,128,128]{2,1,0:T(8,128)(2,1)S(1)}, u32[]{:S(2)}) copy-start(bf16[16,128,128]{2,1,0:T(8,128)(2,1)S(1)} %collective-permute-done.18.refs_8_) | copy-start | bytes 1572868
  193.1 0.8 copy-start.12
  220.1 1.5 copy-start.5
  221.7 34.2 %copy-start.4 = (f32[32,128,128]{2,1,0:T(8,128)S(1)}, f32[32,128,128]{2,1,0:T(8,128)}, u32[]{:S(2)}) copy-start(f32[32,128,128]{2,1,0:T(8,128)} %get-tuple-element.64) | copy-start | bytes 6291460
  221.7 14.9 %collective-permute-start.19 = (f16[2064,128]{1,0:T(8,128)(2,1)S(1)}, f16[2064,128]{1,0:T(8,128)(2,1)S(1)}, u32[]{:S(2)}, u32[]{:S(2)}) collective-permute-start(f16[2064,128]{1,0:T(8,128)(2,1)S(1)} %convert_element_type.88), channel_id=1, source_target_pairs={{0,1},{1,2},{2,3},{3,4},{4,5},{5,6},{6,7},{7,8},{8,9},{9,10},{10,1... | collective-permute-start | bytes 1585160 | tf_op jit(solution)/shard_map/ppermute | solution.py:260
  223.8 16.8 %collective-permute-start.20 = (f16[2064,128]{1,0:T(8,128)(2,1)S(1)}, f16[2064,128]{1,0:T(8,128)(2,1)S(1)}, u32[]{:S(2)}, u32[]{:S(2)}) collective-permute-start(f16[2064,128]{1,0:T(8,128)(2,1)S(1)} %convert_element_type.87), channel_id=1, source_target_pairs={{1,0},{2,1},{3,2},{4,3},{5,4},{6,5},{7,6},{8,7},{9,8},{10,9},{11,1... | collective-permute-start | bytes 1585160 | tf_op jit(solution)/shard_map/ppermute | solution.py:260
  256.2 22.5 %collective-permute-start.22 = (f16[32,128,128]{2,1,0:T(8,128)(2,1)S(1)}, f16[32,128,128]{2,1,0:T(8,128)(2,1)S(1)}, u32[]{:S(2)}, u32[]{:S(2)}) collective-permute-start(f16[32,128,128]{2,1,0:T(8,128)(2,1)S(1)} %fusion.3), channel_id=1, source_target_pairs={{0,64},{64,0},{1,65},{65,1},{2,66},{66,2},{3,67},{67,3},{4,68},{68... | collective-permute-start | bytes 3145736 | tf_op jit(solution)/shard_map/ppermute | solution.py:286
  257.3 15.5 %collective-permute-start.21 = (f32[16,128]{1,0:T(8,128)S(1)}, f32[16,128]{1,0:T(8,128)S(1)}, u32[]{:S(2)}, u32[]{:S(2)}) collective-permute-start(f32[16,128]{1,0:T(8,128)S(1)} %get-tuple-element.72), channel_id=1, source_target_pairs={{0,64},{64,0},{1,65},{65,1},{2,66},{66,2},{3,67},{67,3},{4,68},{68... | collective-permute-start | bytes 24584 | tf_op jit(solution)/shard_map/ppermute | solution.py:286

commit v4 on v2

--- a/solution.py
+++ b/solution.py
@@ -25,6 +25,7 @@
 SUB = 16
 F32 = jnp.float32
 BF16 = jnp.bfloat16
+I16 = jnp.int16
 VMEM_LIMIT = 56 << 20
 UNROLL = 2
 
@@ -101,6 +102,56 @@
     )(me, tile_dest[0], view_tiles.reshape(SLOTS, TROWS, Z))
 
 
+STEPS = (64, 32, 16, 8, 4, 2, 1)
+OFFSET = 64
+
+
+def column_codes(peak):
+    bound = peak * (2.0**-15 * (1 + 2.0**-12))
+    scale = jnp.full(peak.shape, 2.0 ** (1 - OFFSET), F32)
+    shrink = jnp.full(peak.shape, 2.0 ** (OFFSET - 1), F32)
+    power = jnp.full(peak.shape, 1.0 - OFFSET, F32)
+    for step in STEPS:
+        larger = scale * 2.0 ** (step - 1) <= bound
+        scale = jnp.where(larger, scale * 2.0**step, scale)
+        shrink = jnp.where(larger, shrink * 2.0**-step, shrink)
+        power = jnp.where(larger, power + step, power)
+    return shrink, power
+
+
+def column_scales(power):
+    left = power + OFFSET
+    scale = jnp.full(power.shape, 2.0**-OFFSET, F32)
+    for step in STEPS:
+        larger = left >= step
+        scale = jnp.where(larger, scale * 2.0**step, scale)
+        left = jnp.where(larger, left - step, left)
+    return scale
+
+
+def to_codes(values):
+    return jnp.round(values).astype(jnp.int32).astype(I16)
+
+
+def from_codes(codes):
+    return codes.astype(jnp.int32).astype(F32)
+
+
+def write_payload(ref, planes, peak):
+    shrink, power = column_codes(peak)
+    for p in range(HX):
+        ref[p * Y : (p + 1) * Y, :] = to_codes(planes[p] * shrink[p : p + 1])
+    ref[HX * Y :, :] = power.astype(jnp.int32).astype(I16)
+
+
+def payload_scales(ref):
+    return column_scales(from_codes(ref[HX * Y :, :]))
+
+
+def payload_plane(ref, scales, p):
+    return from_codes(ref[p * Y : (p + 1) * Y, :]) * scales[p : p + 1]
+
+
 def swapped(block):
     return jnp.transpose(block, (1, 0, 2))
 
@@ -143,7 +194,9 @@
     lax.fori_loop(0, VIEWS_DEV * BX // TP, along_yz, 0, unroll=UNROLL)
 
 
-def back_from(kx_ref, ky_ref, kz_ref, measured_ref, blurred_ref, half_ref, outs):
+def back_from(kx_ref, ky_ref, kz_ref, measured_ref, blurred_ref, half_ref, edge_ref, peak_ref, outs):
+    left_ref, low_ref, high_ref, right_ref = outs
+
     def along_zy(q, carry):
         v = q // (BX // TP)
         ratio = (measured_ref[q].astype(F32) / blurred_ref[q]).astype(BF16)
@@ -174,45 +227,84 @@
             )
             got += [both[:, :Z], both[:, Z:]]
         planes = swapped(jnp.stack(got, axis=0))
-        first = 0
-        for ref in outs:
-            count = ref.shape[0]
-            ref[:, pl.ds(y0, 8), :] = planes[first : first + count]
-            first += count
+        for i, ref in enumerate((edge_ref.at[0], low_ref, high_ref, edge_ref.at[1])):
+            ref[:, pl.ds(y0, 8), :] = planes[i * HX : (i + 1) * HX]
+        for i, part in enumerate((planes[:HX], planes[HX + BX :])):
+            peak_ref[i] = jnp.maximum(peak_ref[i], part)
         return carry
 
+    peak_ref[...] = jnp.zeros(peak_ref.shape, F32)
     lax.fori_loop(0, Y // 8, along_x, 0, unroll=UNROLL)
-
-
-def first_blur_kernel(kx_ref, ky_ref, kz_ref, left_ref, mid_ref, right_ref, out_ref, half_ref):
-    blur_into(kx_ref, ky_ref, kz_ref, (left_ref, mid_ref, right_ref), half_ref, out_ref)
+    for i, ref in enumerate((left_ref, right_ref)):
+        write_payload(ref, edge_ref.at[i], jnp.max(peak_ref[i], axis=1))
+
+
+def first_blur_kernel(kx_ref, ky_ref, kz_ref, *refs):
+    *parts, out_ref, half_ref = refs
+    blur_into(kx_ref, ky_ref, kz_ref, parts, half_ref, out_ref)
 
 
 def first_back_kernel(kx_ref, ky_ref, kz_ref, blurred_ref, *refs):
     tiles = refs[:SPAN]
-    left_ref, mid_ref, right_ref, measured_ref, half_ref = refs[SPAN:]
+    *outs, measured_ref, half_ref, edge_ref, peak_ref = refs[SPAN:]
     for k in range(SPAN):
         for c in range(CAP):
             code = tiles[k][CAP * TROWS :, :].astype(F32)[8 * c, 0].astype(jnp.int32)
             measured_ref[code] = tiles[k][c * TROWS : (c + 1) * TROWS, :]
-    back_from(
-        kx_ref, ky_ref, kz_ref, measured_ref, blurred_ref, half_ref, (left_ref, mid_ref, right_ref)
-    )
+    back_from(kx_ref, ky_ref, kz_ref, measured_ref, blurred_ref, half_ref, edge_ref, peak_ref, outs)
 
 
 def sweep_kernel(*refs):
-    fwd, back, parts = refs[0:3], refs[3:6], refs[6:9]
-    measured_ref = refs[9]
-    outs = refs[10:13]
-    half_ref, back_half_ref, blurred_ref = refs[13:]
+    fwd, back, parts = refs[0:3], refs[3:6], refs[6:10]
+    measured_ref = refs[10]
+    outs = refs[11:15]
+    half_ref, back_half_ref, edge_ref, peak_ref, blurred_ref = refs[15:]
     blur_into(*fwd, parts, half_ref, blurred_ref)
-    back_from(*back, measured_ref, blurred_ref, back_half_ref, outs)
+    back_from(*back, measured_ref, blurred_ref, back_half_ref, edge_ref, peak_ref, outs)
+
+
+def join_kernel(own_ref, edge_ref, out_ref, sum_ref):
+    scales = payload_scales(edge_ref)
+    peaks = []
+    for p in range(HX):
+        plane = own_ref[p] + payload_plane(edge_ref, scales, p)
+        sum_ref[p] = plane
+        peaks.append(jnp.max(plane, axis=0, keepdims=True))
+    write_payload(out_ref, sum_ref, jnp.concatenate(peaks, axis=0))
+
+
+def update_planes(view_count, before_ref, own_ref, other_ref, out_refs):
+    own, other = payload_scales(own_ref), payload_scales(other_ref)
+    for p in range(HX):
+        total = payload_plane(own_ref, own, p) + payload_plane(other_ref, other, p)
+        plane = before_ref[p] * total * (1.0 / view_count)
+        for ref in out_refs:
+            ref[p] = plane.astype(ref.dtype)
+
+
+def update_kernel(view_count, before_ref, own_ref, other_ref, *out_refs):
+    update_planes(view_count, before_ref, own_ref, other_ref, out_refs)
+
+
+def last_kernel(view_count, low_ref, high_ref, *refs):
+    *payloads, out_ref = refs
+    for i, before_ref in enumerate((low_ref, high_ref)):
+        own_ref, other_ref = payloads[2 * i : 2 * i + 2]
+        update_planes(view_count, before_ref, own_ref, other_ref, (out_ref.at[pl.ds(i * HX, HX)],))
 
 
 VM = pl.BlockSpec(memory_space=pltpu.VMEM)
 BLURRED = (VIEWS_DEV * BX // TP, TROWS, Z)
 HALF_SHAPE = (VIEWS_DEV * BX, Y, Z)
-CONTRIB = [jax.ShapeDtypeStruct((n, Y, Z), F32) for n in (HX, BX, HX)]
+PAYLOAD = jax.ShapeDtypeStruct((HX * Y + HX, Z), I16)
+OWN = jax.ShapeDtypeStruct((HX, Y, Z), F32)
+CONTRIB = [PAYLOAD, OWN, OWN, PAYLOAD]
+BLUR_SCRATCH = [pltpu.VMEM(HALF_SHAPE, F32)]
+BACK_SCRATCH = [
+    pltpu.VMEM(HALF_SHAPE, F32),
+    pltpu.VMEM((2, HX, Y, Z), F32),
+    pltpu.VMEM((2, HX, 8, Z), F32),
+]
 
 
 def call(kernel, name, operands, out_shape, scratch, flops):
@@ -235,18 +327,13 @@
     return lax.ppermute(high, "block", up), lax.ppermute(low, "block", down)
 
 
-def with_halo(estimate):
-    planes = estimate.astype(BF16)
-    left, right = neighbours(planes[:HX], planes[HX:])
-    return left, planes, right
-
-
-def updated(estimate, contributions, view_count):
-    left, mid, right = contributions
-    from_left, from_right = neighbours(left, right)
-    partial = mid + jnp.concatenate([from_left, from_right], axis=0)
-    other = lax.ppermute(partial, "view", [(0, 1), (1, 0)])
-    return estimate * (partial + other) / view_count
+def exchanged(contributions):
+    left, low, high, right = contributions
+    pairs = []
+    for own, edge in zip((low, high), neighbours(left, right)):
+        payload = call(join_kernel, "join", (own, edge), PAYLOAD, [pltpu.VMEM(OWN.shape, F32)], 1 << 20)
+        pairs.append((payload, lax.ppermute(payload, "view", [(0, 1), (1, 0)])))
+    return pairs
 
 
 def shards(estimate, view_tiles, tile_dest, psf_taps):
@@ -260,12 +347,15 @@
         perm = [(i, (i + by) % blocks) for i in range(blocks)]
         arrived.append(lax.ppermute(packed[k], "block", perm) if by else packed[k])
     fwd, back = blur_matrices(kernels)
+    planes = estimate.astype(BF16)
+    low, high = planes[:HX], planes[HX:]
+    left, right = neighbours(low, high)
     blurred = call(
         first_blur_kernel,
         "first_blur",
-        (*fwd, *with_halo(estimate)),
+        (*fwd, left, low, high, right),
         jax.ShapeDtypeStruct(BLURRED, F32),
-        [pltpu.VMEM(HALF_SHAPE, F32)],
+        BLUR_SCRATCH,
         6 << 30,
     )
     *contributions, measured = call(
@@ -273,23 +363,40 @@
         "first_back",
         (*back, blurred, *arrived),
         [*CONTRIB, jax.ShapeDtypeStruct((VIEWS_DEV * BX // TP, TROWS, Z), BF16)],
-        [pltpu.VMEM(HALF_SHAPE, F32)],
+        BACK_SCRATCH,
         8 << 30,
     )
-    estimate = updated(estimate, contributions, view_count)
+    halves = []
+    for i, (own, other) in enumerate(exchanged(contributions)):
+        halves.append(
+            call(
+                functools.partial(update_kernel, view_count),
+                "update",
+                (estimate[i * HX : (i + 1) * HX], own, other),
+                [OWN, jax.ShapeDtypeStruct(OWN.shape, BF16)],
+                [],
+                1 << 20,
+            )
+        )
+    (low, low_planes), (high, high_planes) = halves
+    left, right = neighbours(low_planes, high_planes)
     contributions = call(
         sweep_kernel,
         "sweep",
-        (*fwd, *back, *with_halo(estimate), measured),
+        (*fwd, *back, left, low_planes, high_planes, right, measured),
         CONTRIB,
-        [
-            pltpu.VMEM(HALF_SHAPE, F32),
-            pltpu.VMEM(HALF_SHAPE, F32),
-            pltpu.VMEM(BLURRED, F32),
-        ],
+        [*BLUR_SCRATCH, *BACK_SCRATCH, pltpu.VMEM(BLURRED, F32)],
         14 << 30,
     )
-    return updated(estimate, contributions, view_count)
+    payloads = [payload for pair in exchanged(contributions) for payload in pair]
+    return call(
+        functools.partial(last_kernel, view_count),
+        "last_update",
+        (low, high, *payloads),
+        jax.ShapeDtypeStruct(estimate.shape, F32),
+        [],
+        1 << 20,
+    )
 
 
 def solution(mesh):

time: 297 us -> 226 us (0.76); the launches traced: 291 us -> 225 us
  waiting for transfers between devices: 159 us -> 59.9 us
  Pallas kernels: 62.2 us -> 82.5 us
  starting transfers between devices: 50.8 us -> 63 us
  local copies, waits for them, and re-layouts: 2.52 us -> 9.95 us
  other arithmetic: 12.4 us -> 5.36 us
    ppermute x2 -> x4, waiting for transfers between devices: 97.6 us -> 35.9 us  [exchanged(): pairs.append((payload, lax.ppermute(payload, 'view', [(0, 1), (1, 0)])))]
    pallas_call x3 -> x10, Pallas kernels: 58.3 us -> 78.6 us  [call(): pl.pallas_call(kernel, out_shape=out_shape, in_specs=[VM] * len(operands)...]
    ppermute x11, waiting for transfers between devices: 22.9 us -> 3.02 us  [shards(): arrived.append(lax.ppermute(packed[k], 'block', perm) if by else packed[k])]
    ppermute x8, waiting for transfers between devices: 38.9 us -> 21.1 us  [neighbours(): return (lax.ppermute(high, 'block', up), lax.ppermute(low, 'block', down))]
    ppermute x11, starting transfers between devices: 19.3 us -> 33.1 us  [shards(): arrived.append(lax.ppermute(packed[k], 'block', perm) if by else packed[k])]
    unnamed x38 -> x54, local copies, waits for them, and re-layouts: 1.6 us -> 7.43 us
    ppermute x8, starting transfers between devices: 28.2 us -> 24 us  [neighbours(): return (lax.ppermute(high, 'block', up), lax.ppermute(low, 'block', down))]
    add x2 -> x0, other arithmetic: 3.99 us -> none  [updated(): partial = mid + jnp.concatenate([from_left, from_right], axis=0)]
  transfers between devices with their start and end apart: 21 -> 23, of which waited for: 13 -> 8; matrix products, arithmetic and copies ran while one was open for 3% -> 4% of each run, Pallas kernels for 6% -> 15%
where the time goes in v4:
time: 226 us; the launch traced here: 225 us
  Pallas kernels  82.5 us (37%)
  starting transfers between devices  63 us (28%)
  waiting for transfers between devices  59.9 us (27%)
  local copies, waits for them, and re-layouts  9.95 us (4%)
  other arithmetic  5.36 us (2%)
  matrix products  3.57 us (2%)
    pallas_call x10, Pallas kernels, call(): pl.pallas_call(kernel, out_shape=out_shape, in_specs=[VM] * len(operands)...  78.6 us
    ppermute x4, waiting for transfers between devices, exchanged(): pairs.append((payload, lax.ppermute(payload, 'view', [(0, 1), (1, 0)])))  35.9 us
    ppermute x11, starting transfers between devices, shards(): arrived.append(lax.ppermute(packed[k], 'block', perm) if by else packed[k])  33.1 us
    ppermute x8, starting transfers between devices, neighbours(): return (lax.ppermute(high, 'block', up), lax.ppermute(low, 'block', down))  24 us
    ppermute x8, waiting for transfers between devices, neighbours(): return (lax.ppermute(high, 'block', up), lax.ppermute(low, 'block', down))  21.1 us
    unnamed x54, local copies, waits for them, and re-layouts  7.43 us
    ppermute x4, starting transfers between devices, exchanged(): pairs.append((payload, lax.ppermute(payload, 'view', [(0, 1), (1, 0)])))  5.94 us
  transfers between devices with their start and end apart: 23, of which 8 were waited for; matrix products, arithmetic and copies ran while one was open for 4% of the time, Pallas kernels for 15%

profile of v4, /device:TPU:97, one launch (start us, length us, event | category | flops | bytes accessed | tf_op | source)
XLA Modules:
  0.0 224.8 jit_solution(17382617146731527137)
XLA Ops:
  0.0 1.8 convert_element_type.2
  1.9 2.4 %collective-permute-start = (bf16[16,128,128]{2,1,0:T(8,128)(2,1)S(1)}, bf16[16,128,128]{2,1,0:T(8,128)(2,1)S(1)}, u32[]{:S(2)}, u32[]{:S(2)}) collective-permute-start(bf16[16,128,128]{2,1,0:T(8,128)(2,1)S(1)} %get-tuple-element.58.refs_2_), channel_id=1, source_target_pairs={{0,1},{1,2},{2,3},{3,4},{4,5},{5,6},{6,7},{7,8},{8,9},{9,10},{10,1... | collective-permute-start | bytes 1572872 | tf_op jit(solution)/shard_map/ppermute | solution.py:327
  4.4 2.2 collective-permute-start.1
  6.6 0.7 copy.28
  7.3 3.9 %pack_tiles.1 = (bf16[1040,128]{1,0:T(8,128)(2,1)}, bf16[1040,128]{1,0:T(8,128)(2,1)}, bf16[1040,128]{1,0:T(8,128)(2,1)}, bf16[1040,128]{1,0:T(8,128)(2,1)}, bf1...) custom-call(s32[1]{0:T(128)} %bitcast.5.me_ref, ...), custom_call_target="tpu_custom_call" | custom-call | bytes 6291456 | tf_op jit(solution)/shard_map/pack_tiles/pallas_call | solution.py:89
  11.2 2.8 %collective-permute-start.10 = (bf16[1040,128]{1,0:T(8,128)(2,1)}, bf16[1040,128]{1,0:T(8,128)(2,1)S(1)}, u32[]{:S(2)}, u32[]{:S(2)}) collective-permute-start(bf16[1040,128]{1,0:T(8,128)(2,1)} %get-tuple-element.39), channel_id=1, source_target_pairs={{0,3},{1,4},{2,5},{3,6},{4,7},{5,8},{6,9},{7,10},{8,11},{9,12},{10... | collective-permute-start | bytes 798728 | tf_op jit(solution)/shard_map/ppermute | solution.py:348
  14.0 2.7 %collective-permute-start.11 = (bf16[1040,128]{1,0:T(8,128)(2,1)}, bf16[1040,128]{1,0:T(8,128)(2,1)S(1)}, u32[]{:S(2)}, u32[]{:S(2)}) collective-permute-start(bf16[1040,128]{1,0:T(8,128)(2,1)} %get-tuple-element.40), channel_id=1, source_target_pairs={{0,4},{1,5},{2,6},{3,7},{4,8},{5,9},{6,10},{7,11},{8,12},{9,13},{1... | collective-permute-start | bytes 798728 | tf_op jit(solution)/shard_map/ppermute | solution.py:348
  16.9 0.1 fusion.31
  17.0 0.1 fusion.26
  17.1 0.8 fusion
  17.9 0.8 fusion.1
  18.7 0.8 fusion.2
  19.4 0.8 fusion.3
  20.4 0.3 fusion.8
  20.7 0.3 convolution_convert_fusion
  21.1 0.7 pad_maximum_fusion.4.kx_ref.refs_3_
  21.8 5.9 %collective-permute-start.2 = (bf16[1040,128]{1,0:T(8,128)(2,1)}, bf16[1040,128]{1,0:T(8,128)(2,1)S(1)}, u32[]{:S(2)}, u32[]{:S(2)}) collective-permute-start(bf16[1040,128]{1,0:T(8,128)(2,1)} %get-tuple-element.30), channel_id=1, source_target_pairs={{0,58},{1,59},{2,60},{3,61},{4,62},{5,63},{6,0},{7,1},{8,2},{9,3},... | collective-permute-start | bytes 798728 | tf_op jit(solution)/shard_map/ppermute | solution.py:348
  27.7 3.0 %collective-permute-done.11.refs_10_ = bf16[1040,128]{1,0:T(8,128)(2,1)S(1)} collective-permute-done((bf16[1040,128]{1,0:T(8,128)(2,1)}, bf16[1040,128]{1,0:T(8,128)(2,1)S(1)}, u32[]{:S(2)}, u32[]{:S(2)}) %collective-permute-start.11) | collective-permute-done | bytes 266272 | tf_op jit(solution)/shard_map/ppermute | solution.py:348
  30.7 2.0 collective-permute-start.3
  32.7 5.3 %collective-permute-start.4 = (bf16[1040,128]{1,0:T(8,128)(2,1)}, bf16[1040,128]{1,0:T(8,128)(2,1)S(1)}, u32[]{:S(2)}, u32[]{:S(2)}) collective-permute-start(bf16[1040,128]{1,0:T(8,128)(2,1)} %get-tuple-element.32), channel_id=1, source_target_pairs={{0,60},{1,61},{2,62},{3,63},{4,0},{5,1},{6,2},{7,3},{8,4},{9,5},{1... | collective-permute-start | bytes 798728 | tf_op jit(solution)/shard_map/ppermute | solution.py:348
  38.0 0.7 pad_maximum_fusion.5.kx_ref.refs_0_
  38.7 0.8 pad_maximum_fusion
  39.6 0.8 pad_maximum_fusion.1
  40.4 4.6 %collective-permute-start.5 = (bf16[1040,128]{1,0:T(8,128)(2,1)}, bf16[1040,128]{1,0:T(8,128)(2,1)S(1)}, u32[]{:S(2)}, u32[]{:S(2)}) collective-permute-start(bf16[1040,128]{1,0:T(8,128)(2,1)} %get-tuple-element.33), channel_id=1, source_target_pairs={{0,61},{1,62},{2,63},{3,0},{4,1},{5,2},{6,3},{7,4},{8,5},{9,6},{10... | collective-permute-start | bytes 798728 | tf_op jit(solution)/shard_map/ppermute | solution.py:348
  45.0 1.0 collective-permute-start.6
  46.0 6.5 %collective-permute-start.7 = (bf16[1040,128]{1,0:T(8,128)(2,1)}, bf16[1040,128]{1,0:T(8,128)(2,1)S(1)}, u32[]{:S(2)}, u32[]{:S(2)}) collective-permute-start(bf16[1040,128]{1,0:T(8,128)(2,1)} %get-tuple-element.35), channel_id=1, source_target_pairs={{0,63},{1,0},{2,1},{3,2},{4,3},{5,4},{6,5},{7,6},{8,7},{9,8},{10,9... | collective-permute-start | bytes 798728 | tf_op jit(solution)/shard_map/ppermute | solution.py:348
  52.5 0.5 collective-permute-start.8
  53.0 1.7 collective-permute-start.9
  54.8 12.8 %first_blur.1.blurred_ref = f32[24,512,128]{2,1,0:T(8,128)} custom-call(bf16[96,128]{1,0:T(8,128)(2,1)} %pad_maximum_fusion.5.kx_ref.refs_0_, bf16[3,128,256]{2,1,0:T(8,128)(2,1)} %get-tuple-element.74.ky_ref.refs_1_, bf16[3,256,128]{2,1,0:T(8,128)(2,1)} %get-tuple-element.76.kz_ref.refs_2_, bf16[16,128,128]{2,1,0:T(8,128)(2,1)} %copy-done.13, ...), custom_call_target="tpu_custom_call" | custom-call | flops 6442450944 | bytes 12582912 | tf_op jit(solution)/shard_map/first_blur/pallas_call | solution.py:311
  67.7 0.6 copy-done.22
  68.7 19.6 %first_back.1 = (s16[2064,128]{1,0:T(8,128)(2,1)}, f32[16,128,128]{2,1,0:T(8,128)}, f32[16,128,128]{2,1,0:T(8,128)}, s16[2064,128]{1,0:T(8,128)(2,1)}, bf16[24,512,128]{2,1,0:T(8,128)(2,1)}) custom-call(bf16[64,192]{1,0:T(8,128)(2,1)} %pad_maximum_fusion.4.kx_ref.refs_3_, bf16[3,128,256]{2,1,0:T(8,128)(2,1)} %get-tuple-element.73.ky_ref.refs_4_, ...), custom_call_target="tpu_custom_call" | custom-call | flops 8589934592 | bytes 12582912 | tf_op jit(solution)/shard_map/first_back/pallas_call | solution.py:311
  88.3 1.9 collective-permute-start.15
  90.2 5.9 %collective-permute-start.13 = (s16[2064,128]{1,0:T(8,128)(2,1)}, s16[2064,128]{1,0:T(8,128)(2,1)S(1)}, u32[]{:S(2)}, u32[]{:S(2)}) collective-permute-start(s16[2064,128]{1,0:T(8,128)(2,1)} %get-tuple-element.43), channel_id=1, source_target_pairs={{0,1},{1,2},{2,3},{3,4},{4,5},{5,6},{6,7},{7,8},{8,9},{9,10},{10,1... | collective-permute-start | bytes 1585160 | tf_op jit(solution)/shard_map/ppermute | solution.py:327
  96.2 5.0 %collective-permute-done.15.edge_ref = s16[2064,128]{1,0:T(8,128)(2,1)S(1)} collective-permute-done((s16[2064,128]{1,0:T(8,128)(2,1)}, s16[2064,128]{1,0:T(8,128)(2,1)S(1)}, u32[]{:S(2)}, u32[]{:S(2)}) %collective-permute-start.15) | collective-permute-done | bytes 528416 | tf_op jit(solution)/shard_map/ppermute | solution.py:327
  101.2 0.8 copy-done.7
  101.9 2.6 %join.5.own_ref = s16[2064,128]{1,0:T(8,128)(2,1)} custom-call(f32[16,128,128]{2,1,0:T(8,128)} %get-tuple-element.45.own_ref, s16[2064,128]{1,0:T(8,128)(2,1)} %copy-done.7), custom_call_target="tpu_custom_call" | custom-call | flops 1048576 | bytes 12582912 | tf_op jit(solution)/shard_map/join/pallas_call | solution.py:311
  104.6 2.9 %collective-permute-start.16 = (s16[2064,128]{1,0:T(8,128)(2,1)}, s16[2064,128]{1,0:T(8,128)(2,1)S(1)}, u32[]{:S(2)}, u32[]{:S(2)}) collective-permute-start(s16[2064,128]{1,0:T(8,128)(2,1)} %join.5.own_ref), channel_id=1, source_target_pairs={{0,64},{64,0},{1,65},{65,1},{2,66},{66,2},{3,67},{67,3},{4,68},{68... | collective-permute-start | bytes 1585160 | tf_op jit(solution)/shard_map/ppermute | solution.py:335
  107.5 0.8 copy-done.6
  108.3 2.5 %join.4.own_ref = s16[2064,128]{1,0:T(8,128)(2,1)} custom-call(f32[16,128,128]{2,1,0:T(8,128)} %get-tuple-element.42.own_ref, s16[2064,128]{1,0:T(8,128)(2,1)} %copy-done.6), custom_call_target="tpu_custom_call" | custom-call | flops 1048576 | bytes 12582912 | tf_op jit(solution)/shard_map/join/pallas_call | solution.py:311
  110.9 1.6 fusion.29
  112.5 13.1 %collective-permute-done.16.other_ref = s16[2064,128]{1,0:T(8,128)(2,1)S(1)} collective-permute-done((s16[2064,128]{1,0:T(8,128)(2,1)}, s16[2064,128]{1,0:T(8,128)(2,1)S(1)}, u32[]{:S(2)}, u32[]{:S(2)}) %collective-permute-start.16) | collective-permute-done | bytes 528416 | tf_op jit(solution)/shard_map/ppermute | solution.py:335
  125.6 0.8 copy-done.4
  126.4 3.0 %update.3 = (f32[16,128,128]{2,1,0:T(8,128)}, bf16[16,128,128]{2,1,0:T(8,128)(2,1)}) custom-call(f32[16,128,128]{2,1,0:T(8,128)} %get-tuple-element.55.before_ref, s16[2064,128]{1,0:T(8,128)(2,1)} %join.5.own_ref, s16[2064,128]{1,0:T(8,128)(2,1)} %copy-done.4), custom_call_target="tpu_custom_call" | custom-call | flops 1048576 | bytes 12582912 | tf_op jit(solution)/shard_map/update/pallas_call | solution.py:311
  129.5 1.9 collective-permute-start.17
  131.4 2.6 %collective-permute-done.14.other_ref = s16[2064,128]{1,0:T(8,128)(2,1)S(1)} collective-permute-done((s16[2064,128]{1,0:T(8,128)(2,1)}, s16[2064,128]{1,0:T(8,128)(2,1)S(1)}, u32[]{:S(2)}, u32[]{:S(2)}) %collective-permute-start.14) | collective-permute-done | bytes 528416 | tf_op jit(solution)/shard_map/ppermute | solution.py:335
  133.9 0.8 copy-done.3
  134.7 3.1 %update.2 = (f32[16,128,128]{2,1,0:T(8,128)}, bf16[16,128,128]{2,1,0:T(8,128)(2,1)}) custom-call(f32[16,128,128]{2,1,0:T(8,128)} %get-tuple-element.56.before_ref, s16[2064,128]{1,0:T(8,128)(2,1)} %join.4.own_ref, s16[2064,128]{1,0:T(8,128)(2,1)} %copy-done.3), custom_call_target="tpu_custom_call" | custom-call | flops 1048576 | bytes 12582912 | tf_op jit(solution)/shard_map/update/pallas_call | solution.py:311
  137.8 1.9 collective-permute-start.18
  139.8 10.9 %collective-permute-done.18.refs_9_ = bf16[16,128,128]{2,1,0:T(8,128)(2,1)S(1)} collective-permute-done((bf16[16,128,128]{2,1,0:T(8,128)(2,1)}, bf16[16,128,128]{2,1,0:T(8,128)(2,1)S(1)}, u32[]{:S(2)}, u32[]{:S(2)}) %collective-permute-start.18) | collective-permute-done | bytes 524320 | tf_op jit(solution)/shard_map/ppermute | solution.py:327
  150.7 0.8 copy-done.16
  151.4 25.8 %sweep.1 = (s16[2064,128]{1,0:T(8,128)(2,1)}, f32[16,128,128]{2,1,0:T(8,128)}, f32[16,128,128]{2,1,0:T(8,128)}, s16[2064,128]{1,0:T(8,128)(2,1)}) custom-call(bf16[96,128]{1,0:T(8,128)(2,1)} %pad_maximum_fusion.5.kx_ref.refs_0_, bf16[3,128,256]{2,1,0:T(8,128)(2,1)} %get-tuple-element.74.ky_ref.refs_1_, ...), custom_call_target="tpu_custom_call" | custom-call | flops 15032385536 | bytes 12582912 | tf_op jit(solution)/shard_map/sweep/pallas_call | solution.py:311
  177.3 1.9 collective-permute-start.21
  179.2 5.8 %collective-permute-start.19 = (s16[2064,128]{1,0:T(8,128)(2,1)}, s16[2064,128]{1,0:T(8,128)(2,1)S(1)}, u32[]{:S(2)}, u32[]{:S(2)}) collective-permute-start(s16[2064,128]{1,0:T(8,128)(2,1)} %get-tuple-element.52), channel_id=1, source_target_pairs={{0,1},{1,2},{2,3},{3,4},{4,5},{5,6},{6,7},{7,8},{8,9},{9,10},{10,1... | collective-permute-start | bytes 1585160 | tf_op jit(solution)/shard_map/ppermute | solution.py:327
  185.0 5.2 %collective-permute-done.21.edge_ref = s16[2064,128]{1,0:T(8,128)(2,1)S(1)} collective-permute-done((s16[2064,128]{1,0:T(8,128)(2,1)}, s16[2064,128]{1,0:T(8,128)(2,1)S(1)}, u32[]{:S(2)}, u32[]{:S(2)}) %collective-permute-start.21) | collective-permute-done | bytes 528416 | tf_op jit(solution)/shard_map/ppermute | solution.py:327
  190.1 0.8 copy-done.8
  190.9 2.5 %join.7.refs_2_ = s16[2064,128]{1,0:T(8,128)(2,1)} custom-call(f32[16,128,128]{2,1,0:T(8,128)} %get-tuple-element.53.own_ref, s16[2064,128]{1,0:T(8,128)(2,1)} %copy-done.8), custom_call_target="tpu_custom_call" | custom-call | flops 1048576 | bytes 12582912 | tf_op jit(solution)/shard_map/join/pallas_call | solution.py:311
  193.4 2.7 %collective-permute-start.22 = (s16[2064,128]{1,0:T(8,128)(2,1)}, s16[2064,128]{1,0:T(8,128)(2,1)S(1)}, u32[]{:S(2)}, u32[]{:S(2)}) collective-permute-start(s16[2064,128]{1,0:T(8,128)(2,1)} %join.7.refs_2_), channel_id=1, source_target_pairs={{0,64},{64,0},{1,65},{65,1},{2,66},{66,2},{3,67},{67,3},{4,68},{68... | collective-permute-start | bytes 1585160 | tf_op jit(solution)/shard_map/ppermute | solution.py:335
  196.1 0.8 copy-done.5
  196.9 2.5 %join.6.refs_0_ = s16[2064,128]{1,0:T(8,128)(2,1)} custom-call(f32[16,128,128]{2,1,0:T(8,128)} %get-tuple-element.51.own_ref, s16[2064,128]{1,0:T(8,128)(2,1)} %copy-done.5), custom_call_target="tpu_custom_call" | custom-call | flops 1048576 | bytes 12582912 | tf_op jit(solution)/shard_map/join/pallas_call | solution.py:311
  199.4 0.3 collective-permute-start.20
  199.7 11.9 %collective-permute-done.22.refs_3_ = s16[2064,128]{1,0:T(8,128)(2,1)S(1)} collective-permute-done((s16[2064,128]{1,0:T(8,128)(2,1)}, s16[2064,128]{1,0:T(8,128)(2,1)S(1)}, u32[]{:S(2)}, u32[]{:S(2)}) %collective-permute-start.22) | collective-permute-done | bytes 528416 | tf_op jit(solution)/shard_map/ppermute | solution.py:335
  211.7 8.2 %collective-permute-done.20.refs_1_ = s16[2064,128]{1,0:T(8,128)(2,1)S(1)} collective-permute-done((s16[2064,128]{1,0:T(8,128)(2,1)}, s16[2064,128]{1,0:T(8,128)(2,1)S(1)}, u32[]{:S(2)}, u32[]{:S(2)}) %collective-permute-start.20) | collective-permute-done | bytes 528416 | tf_op jit(solution)/shard_map/ppermute | solution.py:335
  219.9 0.8 copy-done.2
  220.7 4.1 %last_update.1 = f32[32,128,128]{2,1,0:T(8,128)} custom-call(f32[16,128,128]{2,1,0:T(8,128)} %get-tuple-element.44.low_ref, f32[16,128,128]{2,1,0:T(8,128)} %get-tuple-element.47.high_ref, s16[2064,128]{1,0:T(8,128)(2,1)} %join.6.refs_0_, s16[2064,128]{1,0:T(8,128)(2,1)} %copy-done.2, s16[2064,128]{1,0:T(8,128)(2,1)} %join.7.refs_2_, s16[2064,128]{1,0:T(8,128)(2,1)} %copy-done.1), custom_call_target="tpu_custom_call" | custom-call | flops 1048576 | bytes 12582912 | tf_op jit(solution)/shard_map/last_update/pallas_call | solution.py:311
  (77 shorter events, 1.1 us)
Async XLA Ops:
  0.0 6.6 %copy-start.12 = (s32[1,24,3]{1,0,2:T(1,128)S(1)}, s32[1,24,3]{1,0,2:T(1,128)}, u32[]{:S(2)}) copy-start(s32[1,24,3]{1,0,2:T(1,128)} %param.6) | copy-start | bytes 868
  1.9 16.8 %copy-start.9 = (bf16[16,128,128]{2,1,0:T(8,128)(2,1)}, bf16[16,128,128]{2,1,0:T(8,128)(2,1)S(1)}, u32[]{:S(2)}) copy-start(bf16[16,128,128]{2,1,0:T(8,128)(2,1)S(1)} %get-tuple-element.57.refs_1_) | copy-start | bytes 1572868
  1.9 16.8 %copy-start.10 = (bf16[16,128,128]{2,1,0:T(8,128)(2,1)}, bf16[16,128,128]{2,1,0:T(8,128)(2,1)S(1)}, u32[]{:S(2)}) copy-start(bf16[16,128,128]{2,1,0:T(8,128)(2,1)S(1)} %get-tuple-element.58.refs_2_) | copy-start | bytes 1572868
  1.9 14.8 %copy-start.11 = (f32[3,3,31]{2,1,0:T(4,128)S(1)}, f32[3,3,31]{2,1,0:T(4,128)}, u32[]{:S(2)}) copy-start(f32[3,3,31]{2,1,0:T(4,128)} %param.7) | copy-start | bytes 3352
  1.9 50.6 %collective-permute-start = (bf16[16,128,128]{2,1,0:T(8,128)(2,1)S(1)}, bf16[16,128,128]{2,1,0:T(8,128)(2,1)S(1)}, u32[]{:S(2)}, u32[]{:S(2)}) collective-permute-start(bf16[16,128,128]{2,1,0:T(8,128)(2,1)S(1)} %get-tuple-element.58.refs_2_), channel_id=1, source_target_pairs={{0,1},{1,2},{2,3},{3,4},{4,5},{5,6},{6,7},{7,8},{8,9},{9,10},{10,1... | collective-permute-start | bytes 1572872 | tf_op jit(solution)/shard_map/ppermute | solution.py:327
  4.4 48.7 %collective-permute-start.1 = (bf16[16,128,128]{2,1,0:T(8,128)(2,1)S(1)}, bf16[16,128,128]{2,1,0:T(8,128)(2,1)S(1)}, u32[]{:S(2)}, u32[]{:S(2)}) collective-permute-start(bf16[16,128,128]{2,1,0:T(8,128)(2,1)S(1)} %get-tuple-element.57.refs_1_), channel_id=1, source_target_pairs={{1,0},{2,1},{3,2},{4,3},{5,4},{6,5},{7,6},{8,7},{9,8},{10,9},{11,1... | collective-permute-start | bytes 1572872 | tf_op jit(solution)/shard_map/ppermute | solution.py:327
  11.2 10.6 %collective-permute-start.10 = (bf16[1040,128]{1,0:T(8,128)(2,1)}, bf16[1040,128]{1,0:T(8,128)(2,1)S(1)}, u32[]{:S(2)}, u32[]{:S(2)}) collective-permute-start(bf16[1040,128]{1,0:T(8,128)(2,1)} %get-tuple-element.39), channel_id=1, source_target_pairs={{0,3},{1,4},{2,5},{3,6},{4,7},{5,8},{6,9},{7,10},{8,11},{9,12},{10... | collective-permute-start | bytes 798728 | tf_op jit(solution)/shard_map/ppermute | solution.py:348
  14.0 16.7 %collective-permute-start.11 = (bf16[1040,128]{1,0:T(8,128)(2,1)}, bf16[1040,128]{1,0:T(8,128)(2,1)S(1)}, u32[]{:S(2)}, u32[]{:S(2)}) collective-permute-start(bf16[1040,128]{1,0:T(8,128)(2,1)} %get-tuple-element.40), channel_id=1, source_target_pairs={{0,4},{1,5},{2,6},{3,7},{4,8},{5,9},{6,10},{7,11},{8,12},{9,13},{1... | collective-permute-start | bytes 798728 | tf_op jit(solution)/shard_map/ppermute | solution.py:348
  16.7 16.1 %collective-permute-start.12 = (bf16[1040,128]{1,0:T(8,128)(2,1)}, bf16[1040,128]{1,0:T(8,128)(2,1)}, u32[]{:S(2)}, u32[]{:S(2)}) collective-permute-start(bf16[1040,128]{1,0:T(8,128)(2,1)} %get-tuple-element.41), channel_id=1, source_target_pairs={{0,5},{1,6},{2,7},{3,8},{4,9},{5,10},{6,11},{7,12},{8,13},{9,14},{... | collective-permute-start | bytes 798728 | tf_op jit(solution)/shard_map/ppermute | solution.py:348
  21.8 45.8 %copy-start.17 = (bf16[1040,128]{1,0:T(8,128)(2,1)}, bf16[1040,128]{1,0:T(8,128)(2,1)S(1)}, u32[]{:S(2)}) copy-start(bf16[1040,128]{1,0:T(8,128)(2,1)S(1)} %collective-permute-done.10.refs_9_) | copy-start | bytes 798724
  21.8 18.6 %collective-permute-start.2 = (bf16[1040,128]{1,0:T(8,128)(2,1)}, bf16[1040,128]{1,0:T(8,128)(2,1)S(1)}, u32[]{:S(2)}, u32[]{:S(2)}) collective-permute-start(bf16[1040,128]{1,0:T(8,128)(2,1)} %get-tuple-element.30), channel_id=1, source_target_pairs={{0,58},{1,59},{2,60},{3,61},{4,62},{5,63},{6,0},{7,1},{8,2},{9,3},... | collective-permute-start | bytes 798728 | tf_op jit(solution)/shard_map/ppermute | solution.py:348
  30.7 36.9 %copy-start.18 = (bf16[1040,128]{1,0:T(8,128)(2,1)}, bf16[1040,128]{1,0:T(8,128)(2,1)S(1)}, u32[]{:S(2)}) copy-start(bf16[1040,128]{1,0:T(8,128)(2,1)S(1)} %collective-permute-done.11.refs_10_) | copy-start | bytes 798724
  30.7 14.3 %collective-permute-start.3 = (bf16[1040,128]{1,0:T(8,128)(2,1)}, bf16[1040,128]{1,0:T(8,128)(2,1)S(1)}, u32[]{:S(2)}, u32[]{:S(2)}) collective-permute-start(bf16[1040,128]{1,0:T(8,128)(2,1)} %get-tuple-element.31), channel_id=1, source_target_pairs={{0,59},{1,60},{2,61},{3,62},{4,63},{5,0},{6,1},{7,2},{8,3},{9,4},{... | collective-permute-start | bytes 798728 | tf_op jit(solution)/shard_map/ppermute | solution.py:348
  32.7 13.3 %collective-permute-start.4 = (bf16[1040,128]{1,0:T(8,128)(2,1)}, bf16[1040,128]{1,0:T(8,128)(2,1)S(1)}, u32[]{:S(2)}, u32[]{:S(2)}) collective-permute-start(bf16[1040,128]{1,0:T(8,128)(2,1)} %get-tuple-element.32), channel_id=1, source_target_pairs={{0,60},{1,61},{2,62},{3,63},{4,0},{5,1},{6,2},{7,3},{8,4},{9,5},{1... | collective-permute-start | bytes 798728 | tf_op jit(solution)/shard_map/ppermute | solution.py:348
  40.4 27.2 %copy-start.19 = (bf16[1040,128]{1,0:T(8,128)(2,1)}, bf16[1040,128]{1,0:T(8,128)(2,1)S(1)}, u32[]{:S(2)}) copy-start(bf16[1040,128]{1,0:T(8,128)(2,1)S(1)} %collective-permute-done.2.refs_0_) | copy-start | bytes 798724
  40.4 27.2 %collective-permute-start.5 = (bf16[1040,128]{1,0:T(8,128)(2,1)}, bf16[1040,128]{1,0:T(8,128)(2,1)S(1)}, u32[]{:S(2)}, u32[]{:S(2)}) collective-permute-start(bf16[1040,128]{1,0:T(8,128)(2,1)} %get-tuple-element.33), channel_id=1, source_target_pairs={{0,61},{1,62},{2,63},{3,0},{4,1},{5,2},{6,3},{7,4},{8,5},{9,6},{10... | collective-permute-start | bytes 798728 | tf_op jit(solution)/shard_map/ppermute | solution.py:348
  45.0 22.6 %copy-start.20 = (bf16[1040,128]{1,0:T(8,128)(2,1)}, bf16[1040,128]{1,0:T(8,128)(2,1)S(1)}, u32[]{:S(2)}) copy-start(bf16[1040,128]{1,0:T(8,128)(2,1)S(1)} %collective-permute-done.3.refs_1_) | copy-start | bytes 798724
  45.0 22.6 %collective-permute-start.6 = (bf16[1040,128]{1,0:T(8,128)(2,1)}, bf16[1040,128]{1,0:T(8,128)(2,1)S(1)}, u32[]{:S(2)}, u32[]{:S(2)}) collective-permute-start(bf16[1040,128]{1,0:T(8,128)(2,1)} %get-tuple-element.34), channel_id=1, source_target_pairs={{0,62},{1,63},{2,0},{3,1},{4,2},{5,3},{6,4},{7,5},{8,6},{9,7},{10,... | collective-permute-start | bytes 798728 | tf_op jit(solution)/shard_map/ppermute | solution.py:348
  46.0 21.6 %copy-start.21 = (bf16[1040,128]{1,0:T(8,128)(2,1)}, bf16[1040,128]{1,0:T(8,128)(2,1)S(1)}, u32[]{:S(2)}) copy-start(bf16[1040,128]{1,0:T(8,128)(2,1)S(1)} %collective-permute-done.4.refs_2_) | copy-start | bytes 798724
  46.0 21.7 %collective-permute-start.7 = (bf16[1040,128]{1,0:T(8,128)(2,1)}, bf16[1040,128]{1,0:T(8,128)(2,1)S(1)}, u32[]{:S(2)}, u32[]{:S(2)}) collective-permute-start(bf16[1040,128]{1,0:T(8,128)(2,1)} %get-tuple-element.35), channel_id=1, source_target_pairs={{0,63},{1,0},{2,1},{3,2},{4,3},{5,4},{6,5},{7,6},{8,7},{9,8},{10,9... | collective-permute-start | bytes 798728 | tf_op jit(solution)/shard_map/ppermute | solution.py:348
  52.5 2.3 %copy-start.13 = (bf16[16,128,128]{2,1,0:T(8,128)(2,1)}, bf16[16,128,128]{2,1,0:T(8,128)(2,1)S(1)}, u32[]{:S(2)}) copy-start(bf16[16,128,128]{2,1,0:T(8,128)(2,1)S(1)} %collective-permute-done.refs_0_) | copy-start | bytes 1572868
  52.5 15.2 %collective-permute-start.8 = (bf16[1040,128]{1,0:T(8,128)(2,1)}, bf16[1040,128]{1,0:T(8,128)(2,1)S(1)}, u32[]{:S(2)}, u32[]{:S(2)}) collective-permute-start(bf16[1040,128]{1,0:T(8,128)(2,1)} %get-tuple-element.37), channel_id=1, source_target_pairs={{0,1},{1,2},{2,3},{3,4},{4,5},{5,6},{6,7},{7,8},{8,9},{9,10},{10,1... | collective-permute-start | bytes 798728 | tf_op jit(solution)/shard_map/ppermute | solution.py:348
  53.0 1.7 copy-start.14
  53.0 14.7 %collective-permute-start.9 = (bf16[1040,128]{1,0:T(8,128)(2,1)}, bf16[1040,128]{1,0:T(8,128)(2,1)S(1)}, u32[]{:S(2)}, u32[]{:S(2)}) collective-permute-start(bf16[1040,128]{1,0:T(8,128)(2,1)} %get-tuple-element.38), channel_id=1, source_target_pairs={{0,2},{1,3},{2,4},{3,5},{4,6},{5,7},{6,8},{7,9},{8,10},{9,11},{10,... | collective-permute-start | bytes 798728 | tf_op jit(solution)/shard_map/ppermute | solution.py:348
  67.6 0.7 copy-start.22
  67.6 0.8 copy-start.23
  67.7 0.8 copy-start.24
  67.7 0.9 copy-start.25
  67.7 1.0 copy-start.26
  88.3 12.9 %collective-permute-start.15 = (s16[2064,128]{1,0:T(8,128)(2,1)}, s16[2064,128]{1,0:T(8,128)(2,1)S(1)}, u32[]{:S(2)}, u32[]{:S(2)}) collective-permute-start(s16[2064,128]{1,0:T(8,128)(2,1)} %get-tuple-element.46), channel_id=1, source_target_pairs={{1,0},{2,1},{3,2},{4,3},{5,4},{6,5},{7,6},{8,7},{9,8},{10,9},{11,1... | collective-permute-start | bytes 1585160 | tf_op jit(solution)/shard_map/ppermute | solution.py:327
  90.2 17.3 %collective-permute-start.13 = (s16[2064,128]{1,0:T(8,128)(2,1)}, s16[2064,128]{1,0:T(8,128)(2,1)S(1)}, u32[]{:S(2)}, u32[]{:S(2)}) collective-permute-start(s16[2064,128]{1,0:T(8,128)(2,1)} %get-tuple-element.43), channel_id=1, source_target_pairs={{0,1},{1,2},{2,3},{3,4},{4,5},{5,6},{6,7},{7,8},{8,9},{9,10},{10,1... | collective-permute-start | bytes 1585160 | tf_op jit(solution)/shard_map/ppermute | solution.py:327
  101.2 0.8 copy-start.7
  101.9 8.9 %copy-start = (f32[32,128,128]{2,1,0:T(8,128)S(1)}, f32[32,128,128]{2,1,0:T(8,128)}, u32[]{:S(2)}) copy-start(f32[32,128,128]{2,1,0:T(8,128)} %param.4) | copy-start | bytes 6291460
  104.6 21.0 %collective-permute-start.16 = (s16[2064,128]{1,0:T(8,128)(2,1)}, s16[2064,128]{1,0:T(8,128)(2,1)S(1)}, u32[]{:S(2)}, u32[]{:S(2)}) collective-permute-start(s16[2064,128]{1,0:T(8,128)(2,1)} %join.5.own_ref), channel_id=1, source_target_pairs={{0,64},{64,0},{1,65},{65,1},{2,66},{66,2},{3,67},{67,3},{4,68},{68... | collective-permute-start | bytes 1585160 | tf_op jit(solution)/shard_map/ppermute | solution.py:335
  107.5 0.8 copy-start.6
  110.8 23.1 %collective-permute-start.14 = (s16[2064,128]{1,0:T(8,128)(2,1)}, s16[2064,128]{1,0:T(8,128)(2,1)S(1)}, u32[]{:S(2)}, u32[]{:S(2)}) collective-permute-start(s16[2064,128]{1,0:T(8,128)(2,1)} %join.4.own_ref), channel_id=1, source_target_pairs={{0,64},{64,0},{1,65},{65,1},{2,66},{66,2},{3,67},{67,3},{4,68},{68... | collective-permute-start | bytes 1585160 | tf_op jit(solution)/shard_map/ppermute | solution.py:335
  125.6 0.8 copy-start.4
  129.5 10.3 %collective-permute-start.17 = (bf16[16,128,128]{2,1,0:T(8,128)(2,1)}, bf16[16,128,128]{2,1,0:T(8,128)(2,1)S(1)}, u32[]{:S(2)}, u32[]{:S(2)}) collective-permute-start(bf16[16,128,128]{2,1,0:T(8,128)(2,1)} %get-tuple-element.48.refs_8_), channel_id=1, source_target_pairs={{0,1},{1,2},{2,3},{3,4},{4,5},{5,6},{6,7},{7,8},{8,9},{9,10},{10,1... | collective-permute-start | bytes 1572872 | tf_op jit(solution)/shard_map/ppermute | solution.py:327
  133.9 0.8 copy-start.3
  137.8 12.8 %collective-permute-start.18 = (bf16[16,128,128]{2,1,0:T(8,128)(2,1)}, bf16[16,128,128]{2,1,0:T(8,128)(2,1)S(1)}, u32[]{:S(2)}, u32[]{:S(2)}) collective-permute-start(bf16[16,128,128]{2,1,0:T(8,128)(2,1)} %get-tuple-element.49.refs_7_), channel_id=1, source_target_pairs={{1,0},{2,1},{3,2},{4,3},{5,4},{6,5},{7,6},{8,7},{9,8},{10,9},{11,1... | collective-permute-start | bytes 1572872 | tf_op jit(solution)/shard_map/ppermute | solution.py:327
  139.8 10.9 %copy-start.15 = (bf16[16,128,128]{2,1,0:T(8,128)(2,1)}, bf16[16,128,128]{2,1,0:T(8,128)(2,1)S(1)}, u32[]{:S(2)}) copy-start(bf16[16,128,128]{2,1,0:T(8,128)(2,1)S(1)} %collective-permute-done.17.refs_6_) | copy-start | bytes 1572868
  150.6 0.8 copy-start.16
  177.3 12.9 %collective-permute-start.21 = (s16[2064,128]{1,0:T(8,128)(2,1)}, s16[2064,128]{1,0:T(8,128)(2,1)S(1)}, u32[]{:S(2)}, u32[]{:S(2)}) collective-permute-start(s16[2064,128]{1,0:T(8,128)(2,1)} %get-tuple-element.54), channel_id=1, source_target_pairs={{1,0},{2,1},{3,2},{4,3},{5,4},{6,5},{7,6},{8,7},{9,8},{10,9},{11,1... | collective-permute-start | bytes 1585160 | tf_op jit(solution)/shard_map/ppermute | solution.py:327
  179.2 16.9 %collective-permute-start.19 = (s16[2064,128]{1,0:T(8,128)(2,1)}, s16[2064,128]{1,0:T(8,128)(2,1)S(1)}, u32[]{:S(2)}, u32[]{:S(2)}) collective-permute-start(s16[2064,128]{1,0:T(8,128)(2,1)} %get-tuple-element.52), channel_id=1, source_target_pairs={{0,1},{1,2},{2,3},{3,4},{4,5},{5,6},{6,7},{7,8},{8,9},{9,10},{10,1... | collective-permute-start | bytes 1585160 | tf_op jit(solution)/shard_map/ppermute | solution.py:327
  190.1 0.8 copy-start.8
  193.4 18.2 %collective-permute-start.22 = (s16[2064,128]{1,0:T(8,128)(2,1)}, s16[2064,128]{1,0:T(8,128)(2,1)S(1)}, u32[]{:S(2)}, u32[]{:S(2)}) collective-permute-start(s16[2064,128]{1,0:T(8,128)(2,1)} %join.7.refs_2_), channel_id=1, source_target_pairs={{0,64},{64,0},{1,65},{65,1},{2,66},{66,2},{3,67},{67,3},{4,68},{68... | collective-permute-start | bytes 1585160 | tf_op jit(solution)/shard_map/ppermute | solution.py:335
  196.1 0.8 copy-start.5
  199.4 20.5 %collective-permute-start.20 = (s16[2064,128]{1,0:T(8,128)(2,1)}, s16[2064,128]{1,0:T(8,128)(2,1)S(1)}, u32[]{:S(2)}, u32[]{:S(2)}) collective-permute-start(s16[2064,128]{1,0:T(8,128)(2,1)} %join.6.refs_0_), channel_id=1, source_target_pairs={{0,64},{64,0},{1,65},{65,1},{2,66},{66,2},{3,67},{67,3},{4,68},{68... | collective-permute-start | bytes 1585160 | tf_op jit(solution)/shard_map/ppermute | solution.py:335
  211.7 8.2 %copy-start.1 = (s16[2064,128]{1,0:T(8,128)(2,1)}, s16[2064,128]{1,0:T(8,128)(2,1)S(1)}, u32[]{:S(2)}) copy-start(s16[2064,128]{1,0:T(8,128)(2,1)S(1)} %collective-permute-done.22.refs_3_) | copy-start | bytes 1585156
  219.9 0.8 copy-start.2

commit v5 on v4

--- a/solution.py
+++ b/solution.py
@@ -14,6 +14,7 @@
 EX = BX + 2 * HX
 Y = 128
 Z = 128
+LANES = 128
 VIEWS_DEV = 3
 ITERS = 2
 CAP = 2
@@ -27,41 +28,74 @@
 BF16 = jnp.bfloat16
 I16 = jnp.int16
 VMEM_LIMIT = 56 << 20
-UNROLL = 2
-
-
-def banded(kernel, rows, cols, sign, offset):
-    row_idx = jnp.arange(rows)[:, None]
-    col_idx = jnp.arange(cols)[None, :]
-    lag = sign * (col_idx - row_idx) + offset
-    hits = (lag[:, :, None] == jnp.arange(kernel.shape[-1])[None, None, :]).astype(F32)
-    return jnp.einsum("vt,ijt->vij", kernel, hits, precision=lax.Precision.HIGHEST)
-
-
-def rounded(value):
-    return lax.reduce_precision(value, 8, 7)
-
-
-def two_terms(matrix, axis):
-    high = rounded(matrix)
-    return jnp.concatenate([high, matrix - high], axis=axis).astype(BF16)
-
-
-def blur_matrices(kernels):
-    taps_x, taps_y, taps_z = kernels[:, 0], kernels[:, 1], kernels[:, 2]
-    near_x = rounded(taps_x)
-    back_y = taps_y * (jnp.sum(taps_x, -1) / jnp.sum(near_x, -1))[:, None]
-    fwd_x = banded(taps_x, BX, EX, 1, -1).reshape(VIEWS_DEV * BX, EX)
-    back_x = jnp.transpose(banded(near_x, BX, EX, 1, -1).reshape(VIEWS_DEV * BX, EX))
-    back_x = jnp.concatenate([back_x, back_x], axis=1).astype(BF16)
-    y_fwd = banded(taps_y, Y, Y, 1, HALF)
-    y_back = banded(back_y, Y, Y, -1, HALF)
-    z_fwd = banded(taps_z, Z, Z, -1, HALF)
-    z_back = banded(taps_z, Z, Z, 1, HALF)
-    return (
-        (two_terms(fwd_x, 1), two_terms(y_fwd, 2), two_terms(z_fwd, 1)),
-        (back_x, two_terms(y_back, 2), two_terms(z_back, 1)),
-    )
+UNROLL = 4
+EARLY = (-6, 5, -5, 4, -4, 3, -3)
+LATE = (2, -2, 1, -1)
+
+
+def toeplitz(row, rows, shift, low, high):
+    turned = pltpu.roll(
+        jnp.broadcast_to(row, (rows, LANES)), shift % LANES, 1, stride=1, stride_axis=0
+    )
+    lag = lax.broadcasted_iota(jnp.int32, (rows, LANES), 1) - lax.broadcasted_iota(
+        jnp.int32, (rows, LANES), 0
+    )
+    return jnp.where((lag >= low) & (lag <= high), turned, 0.0)
+
+
+def prepare_kernel(psf_ref, *refs):
+    *outs, taps_ref, turned_ref = refs
+    fwd_x_ref, fwd_y_ref, fwd_z_ref, back_x_ref, back_y_ref, back_z_ref = outs
+    dims = psf_ref.shape[1]
+    taps_ref[...] = jnp.zeros(taps_ref.shape, F32)
+    for v in range(VIEWS_DEV):
+        taps = psf_ref[v]
+        taps_ref[v * dims : (v + 1) * dims, :TAPS] = taps / jnp.sum(taps, axis=1, keepdims=True)
+    turned_ref[...] = jnp.transpose(taps_ref[...])
+    left_over = jnp.zeros((1, LANES), F32)
+    for a in range(TAPS):
+        wanted = turned_ref[a : a + 1, :] + left_over
+        near = wanted.astype(BF16).astype(F32)
+        left_over = wanted - near
+        turned_ref[a : a + 1, :] = near
+    taps_ref[...] = jnp.transpose(turned_ref[...])
+    for a in range(TAPS):
+        turned_ref[TAPS + 1 + a : TAPS + 2 + a, :] = turned_ref[TAPS - 1 - a : TAPS - a, :]
+    turned_ref[:TAPS, :] = turned_ref[TAPS + 1 : 2 * TAPS + 1, :]
+    turned_ref[TAPS:, :] = jnp.zeros((LANES - TAPS, LANES), F32)
+    turned_ref[...] = jnp.transpose(turned_ref[...])
+    wide = []
+    for v in range(VIEWS_DEV):
+        ahead = [taps_ref[v * dims + d : v * dims + d + 1, :] for d in range(dims)]
+        behind = [turned_ref[v * dims + d : v * dims + d + 1, :] for d in range(dims)]
+        wide.append(toeplitz(ahead[0], BX, 1, 1, TAPS))
+        for ref, row in (
+            (fwd_y_ref, ahead[1]),
+            (back_y_ref, behind[1]),
+            (fwd_z_ref, behind[2]),
+            (back_z_ref, ahead[2]),
+        ):
+            ref[v] = toeplitz(row, LANES, -HALF, -HALF, HALF).astype(BF16)
+    along = jnp.concatenate(wide, axis=0)
+    fwd_x_ref[...] = along[:, :EX].astype(BF16)
+    full = jnp.concatenate([along, jnp.zeros((LANES - VIEWS_DEV * BX, LANES), F32)], axis=0)
+    across = jnp.transpose(full)[:EX, : VIEWS_DEV * BX].astype(BF16)
+    back_x_ref[...] = jnp.concatenate([across, across], axis=1)
+
+
+def blur_matrices(psf_taps):
+    square = jax.ShapeDtypeStruct((VIEWS_DEV, LANES, LANES), BF16)
+    shapes = [
+        jax.ShapeDtypeStruct((VIEWS_DEV * BX, EX), BF16),
+        square,
+        square,
+        jax.ShapeDtypeStruct((EX, 2 * VIEWS_DEV * BX), BF16),
+        square,
+        square,
+    ]
+    scratch = [pltpu.VMEM((LANES, LANES), F32)] * 2
+    matrices = call(prepare_kernel, "prepare", (psf_taps,), shapes, scratch, 1 << 20)
+    return matrices[:3], matrices[3:]
 
 
 def pack_kernel(me_ref, dest_ref, tiles_ref, *refs):
@@ -165,14 +199,12 @@
             outs = []
             for j in range(0, 8, 2):
                 pair = jnp.concatenate([rows[j], rows[j + 1]], axis=1)
-                got = jnp.dot(
-                    kx_ref[...], jnp.concatenate([pair, pair], axis=0), preferred_element_type=F32
-                )
+                got = jnp.dot(kx_ref[...], pair, preferred_element_type=F32)
                 outs += [got[:, :Z], got[:, Z:]]
             half_ref[:, pl.ds(y0 + h, 8), :] = swapped(jnp.stack(outs, axis=0))
         return carry
 
-    lax.fori_loop(0, Y // SUB, along_x, 0)
+    lax.fori_loop(0, Y // SUB, along_x, 0, unroll=2)
 
     def along_yz(q, carry):
         v = q // (BX // TP)
@@ -181,14 +213,10 @@
             pair = jnp.concatenate(
                 [half_ref[q * TP + i + j].astype(BF16) for j in range(2)], axis=1
             )
-            got = jnp.dot(
-                ky_ref[v], jnp.concatenate([pair, pair], axis=0), preferred_element_type=F32
-            ).astype(BF16)
+            got = jnp.dot(ky_ref[v], pair, preferred_element_type=F32).astype(BF16)
             outs += [got[:, :Z], got[:, Z:]]
         rows = jnp.concatenate(outs, axis=0)
-        out_ref[q] = jnp.dot(
-            jnp.concatenate([rows, rows], axis=1), kz_ref[v], preferred_element_type=F32
-        )
+        out_ref[q] = jnp.dot(rows, kz_ref[v], preferred_element_type=F32)
         return carry
 
     lax.fori_loop(0, VIEWS_DEV * BX // TP, along_yz, 0, unroll=UNROLL)
@@ -200,14 +228,10 @@
     def along_zy(q, carry):
         v = q // (BX // TP)
         ratio = (measured_ref[q].astype(F32) / blurred_ref[q]).astype(BF16)
-        rows = jnp.dot(
-            jnp.concatenate([ratio, ratio], axis=1), kz_ref[v], preferred_element_type=F32
-        ).astype(BF16)
+        rows = jnp.dot(ratio, kz_ref[v], preferred_element_type=F32).astype(BF16)
         for i in range(0, TP, 2):
             pair = jnp.concatenate([rows[(i + j) * Y : (i + j + 1) * Y] for j in range(2)], axis=1)
-            got = jnp.dot(
-                ky_ref[v], jnp.concatenate([pair, pair], axis=0), preferred_element_type=F32
-            )
+            got = jnp.dot(ky_ref[v], pair, preferred_element_type=F32)
             for j in range(2):
                 half_ref[q * TP + i + j] = got[:, j * Z : (j + 1) * Z]
         return carry
@@ -337,19 +361,22 @@
 
 
 def shards(estimate, view_tiles, tile_dest, psf_taps):
-    kernels = psf_taps / jnp.sum(psf_taps, axis=-1, keepdims=True)
-    view_count = kernels.shape[0] * lax.axis_size("view")
+    view_count = psf_taps.shape[0] * lax.axis_size("view")
     blocks = lax.axis_size("block")
     packed = pack_tiles(view_tiles, tile_dest)
-    arrived = []
-    for k in range(SPAN):
-        by = k - SPAN // 2
-        perm = [(i, (i + by) % blocks) for i in range(blocks)]
-        arrived.append(lax.ppermute(packed[k], "block", perm) if by else packed[k])
-    fwd, back = blur_matrices(kernels)
+    estimate, psf_taps, packed = lax.optimization_barrier((estimate, psf_taps, packed))
+    arrived = list(packed)
+
+    def route(steps):
+        for by in steps:
+            perm = [(i, (i + by) % blocks) for i in range(blocks)]
+            arrived[by + SPAN // 2] = lax.ppermute(packed[by + SPAN // 2], "block", perm)
+
     planes = estimate.astype(BF16)
     low, high = planes[:HX], planes[HX:]
     left, right = neighbours(low, high)
+    route(EARLY)
+    fwd, back = blur_matrices(psf_taps)
     blurred = call(
         first_blur_kernel,
         "first_blur",
@@ -358,6 +385,8 @@
         BLUR_SCRATCH,
         6 << 30,
     )
+    packed, blurred = lax.optimization_barrier((packed, blurred))
+    route(LATE)
     *contributions, measured = call(
         first_back_kernel,
         "first_back",

time: 226 us -> 207 us (0.916)
  waiting for transfers between devices: 59.9 us -> 77.2 us
  Pallas kernels: 82.5 us -> 67.6 us
  starting transfers between devices: 63 us -> 50.4 us
  other arithmetic: 5.36 us -> 0.16 us
  matrix products: 3.57 us -> 0 us
    ppermute x11, waiting for transfers between devices: 3.02 us -> 24.1 us  [route(): lax.ppermute(packed[by + SPAN // 2], 'block', perm)]
    pallas_call x10 -> x11, Pallas kernels: 78.6 us -> 63.7 us  [call(): pl.pallas_call(kernel, out_shape=out_shape, in_specs=[VM] * len(operands)...]
    ppermute x11, starting transfers between devices: 33.1 us -> 20.5 us  [route(): lax.ppermute(packed[by + SPAN // 2], 'block', perm)]
    ppermute x4, waiting for transfers between devices: 35.9 us -> 32 us  [exchanged(): pairs.append((payload, lax.ppermute(payload, 'view', [(0, 1), (1, 0)])))]
    dot_general x6 -> x0, matrix products: 3.57 us -> none  [banded(): jnp.einsum('vt,ijt->vij', kernel, hits, precision=lax.Precision.HIGHEST)]
    concatenate x4 -> x0, other arithmetic: 3.02 us -> none  [the longest x3 2.31 us: two_terms(): return jnp.concatenate([high, matrix - high], axis=axis).astype(BF16)]
    unnamed x54 -> x72, local copies, waits for them, and re-layouts: 7.43 us -> 7.35 us
  transfers between devices with their start and end apart: 23 -> 23, of which waited for: 8 -> 11; matrix products, arithmetic and copies ran while one was open for 4% -> 1% of each run, Pallas kernels for 15% -> 14%
where the time goes in v5:
time: 207 us; the launch traced here: 206 us
  waiting for transfers between devices  77.2 us (37%)
  Pallas kernels  67.6 us (33%)
  starting transfers between devices  50.4 us (24%)
  local copies, waits for them, and re-layouts  10.6 us (5%)
    pallas_call x11, Pallas kernels, call(): pl.pallas_call(kernel, out_shape=out_shape, in_specs=[VM] * len(operands)...  63.7 us
    ppermute x4, waiting for transfers between devices, exchanged(): pairs.append((payload, lax.ppermute(payload, 'view', [(0, 1), (1, 0)])))  32 us
    ppermute x11, waiting for transfers between devices, route(): lax.ppermute(packed[by + SPAN // 2], 'block', perm)  24.1 us
    ppermute x8, starting transfers between devices, neighbours(): return (lax.ppermute(high, 'block', up), lax.ppermute(low, 'block', down))  24 us
    ppermute x8, waiting for transfers between devices, neighbours(): return (lax.ppermute(high, 'block', up), lax.ppermute(low, 'block', down))  21.1 us
    ppermute x11, starting transfers between devices, route(): lax.ppermute(packed[by + SPAN // 2], 'block', perm)  20.5 us
    unnamed x72, local copies, waits for them, and re-layouts  7.35 us
    ppermute x4, starting transfers between devices, exchanged(): pairs.append((payload, lax.ppermute(payload, 'view', [(0, 1), (1, 0)])))  5.94 us
  transfers between devices with their start and end apart: 23, of which 11 were waited for; matrix products, arithmetic and copies ran while one was open for 1% of the time, Pallas kernels for 14%

profile of v5, /device:TPU:97, one launch (start us, length us, event | category | flops | bytes accessed | tf_op | source)
XLA Modules:
  0.0 206.3 jit_solution(13595579523445603898)
XLA Ops:
  0.0 1.5 copy.6
  1.5 3.9 %pack_tiles.1 = (bf16[1040,128]{1,0:T(8,128)(2,1)}, bf16[1040,128]{1,0:T(8,128)(2,1)}, bf16[1040,128]{1,0:T(8,128)(2,1)}, bf16[1040,128]{1,0:T(8,128)(2,1)}, bf1...) custom-call(s32[1]{0:T(128)} %bitcast.me_ref, ...), custom_call_target="tpu_custom_call" | custom-call | bytes 6291456 | tf_op jit(solution)/shard_map/pack_tiles/pallas_call | solution.py:123
  5.4 0.0 copy-start.26
  5.5 0.2 convert_element_type.3
  5.6 0.1 fusion.1
  5.7 2.4 %collective-permute-start = (bf16[16,128,128]{2,1,0:T(8,128)(2,1)S(1)}, bf16[16,128,128]{2,1,0:T(8,128)(2,1)S(1)}, u32[]{:S(2)}, u32[]{:S(2)}) collective-permute-start(bf16[16,128,128]{2,1,0:T(8,128)(2,1)S(1)} %get-tuple-element.108.refs_2_), channel_id=1, source_target_pairs={{0,1},{1,2},{2,3},{3,4},{4,5},{5,6},{6,7},{7,8},{8,9},{9,10},{10,1... | collective-permute-start | bytes 1572872 | tf_op jit(solution)/shard_map/ppermute | solution.py:351
  8.2 2.2 %collective-permute-start.1 = (bf16[16,128,128]{2,1,0:T(8,128)(2,1)S(1)}, bf16[16,128,128]{2,1,0:T(8,128)(2,1)S(1)}, u32[]{:S(2)}, u32[]{:S(2)}) collective-permute-start(bf16[16,128,128]{2,1,0:T(8,128)(2,1)S(1)} %get-tuple-element.107.refs_1_), channel_id=1, source_target_pairs={{1,0},{2,1},{3,2},{4,3},{5,4},{6,5},{7,6},{8,7},{9,8},{10,9},{11,1... | collective-permute-start | bytes 1572872 | tf_op jit(solution)/shard_map/ppermute | solution.py:351
  10.4 2.9 %collective-permute-start.10 = (bf16[1040,128]{1,0:T(8,128)(2,1)S(1)}, bf16[1040,128]{1,0:T(8,128)(2,1)S(1)}, u32[]{:S(2)}, u32[]{:S(2)}) collective-permute-start(bf16[1040,128]{1,0:T(8,128)(2,1)S(1)} %copy-done.33), channel_id=1, source_target_pairs={{0,3},{1,4},{2,5},{3,6},{4,7},{5,8},{6,9},{7,10},{8,11},{9,12},{10... | collective-permute-start | bytes 798728 | tf_op jit(solution)/shard_map/ppermute | solution.py:373
  13.3 2.7 %collective-permute-start.11 = (bf16[1040,128]{1,0:T(8,128)(2,1)}, bf16[1040,128]{1,0:T(8,128)(2,1)S(1)}, u32[]{:S(2)}, u32[]{:S(2)}) collective-permute-start(bf16[1040,128]{1,0:T(8,128)(2,1)} %get-tuple-element.82), channel_id=1, source_target_pairs={{0,4},{1,5},{2,6},{3,7},{4,8},{5,9},{6,10},{7,11},{8,12},{9,13},{1... | collective-permute-start | bytes 798728 | tf_op jit(solution)/shard_map/ppermute | solution.py:373
  16.0 2.1 %prepare.1 = (bf16[96,64]{1,0:T(8,128)(2,1)}, bf16[3,128,128]{2,1,0:T(8,128)(2,1)}, bf16[3,128,128]{2,1,0:T(8,128)(2,1)}, bf16[64,192]{1,0:T(8,128)(2,1)}, bf16[...) custom-call(f32[3,3,31]{2,1,0:T(4,128)} %psf_ref), custom_call_target="tpu_custom_call" | custom-call | flops 1048576 | bytes 12582912 | tf_op jit(solution)/shard_map/prepare/pallas_call | solution.py:335
  18.1 11.0 %collective-permute-done.10.refs_9_ = bf16[1040,128]{1,0:T(8,128)(2,1)S(1)} collective-permute-done((bf16[1040,128]{1,0:T(8,128)(2,1)S(1)}, bf16[1040,128]{1,0:T(8,128)(2,1)S(1)}, u32[]{:S(2)}, u32[]{:S(2)}) %collective-permute-start.10) | collective-permute-done | bytes 266272 | tf_op jit(solution)/shard_map/ppermute | solution.py:373
  29.1 0.0 collective-permute-start.2
  29.1 0.0 collective-permute-done.refs_0_
  29.1 0.0 copy-start.11
  29.1 6.7 %collective-permute-start.3 = (bf16[1040,128]{1,0:T(8,128)(2,1)S(1)}, bf16[1040,128]{1,0:T(8,128)(2,1)S(1)}, u32[]{:S(2)}, u32[]{:S(2)}) collective-permute-start(bf16[1040,128]{1,0:T(8,128)(2,1)S(1)} %copy-done.24), channel_id=1, source_target_pairs={{0,59},{1,60},{2,61},{3,62},{4,63},{5,0},{6,1},{7,2},{8,3},{9,4},{... | collective-permute-start | bytes 798728 | tf_op jit(solution)/shard_map/ppermute | solution.py:373
  35.8 0.0 collective-permute-done.1.refs_3_
  35.8 1.6 collective-permute-start.4
  37.4 10.6 %first_blur.1.blurred_ref = f32[24,512,128]{2,1,0:T(8,128)} custom-call(bf16[96,64]{1,0:T(8,128)(2,1)} %get-tuple-element.84.kx_ref.refs_0_, bf16[3,128,128]{2,1,0:T(8,128)(2,1)} %get-tuple-element.85.ky_ref.refs_1_, bf16[3,128,128]{2,1,0:T(8,128)(2,1)} %get-tuple-element.86.kz_ref.refs_2_, bf16[16,128,128]{2,1,0:T(8,128)(2,1)} %copy-done.11, ...), custom_call_target="tpu_custom_call" | custom-call | flops 6442450944 | bytes 12582912 | tf_op jit(solution)/shard_map/first_blur/pallas_call | solution.py:335
  48.1 0.1 collective-permute-start.5
  48.2 2.1 %collective-permute-start.6 = (bf16[1040,128]{1,0:T(8,128)(2,1)S(1)}, bf16[1040,128]{1,0:T(8,128)(2,1)S(1)}, u32[]{:S(2)}, u32[]{:S(2)}) collective-permute-start(bf16[1040,128]{1,0:T(8,128)(2,1)S(1)} %copy-done.18), channel_id=1, source_target_pairs={{0,62},{1,63},{2,0},{3,1},{4,2},{5,3},{6,4},{7,5},{8,6},{9,7},{10,... | collective-permute-start | bytes 798728 | tf_op jit(solution)/shard_map/ppermute | solution.py:373
  50.3 2.0 collective-permute-start.7
  52.3 2.0 collective-permute-start.8
  54.3 0.4 collective-permute-start.9
  54.8 3.6 %collective-permute-done.5.refs_3_ = bf16[1040,128]{1,0:T(8,128)(2,1)S(1)} collective-permute-done((bf16[1040,128]{1,0:T(8,128)(2,1)S(1)}, bf16[1040,128]{1,0:T(8,128)(2,1)S(1)}, u32[]{:S(2)}, u32[]{:S(2)}) %collective-permute-start.5) | collective-permute-done | bytes 266272 | tf_op jit(solution)/shard_map/ppermute | solution.py:373
  58.4 7.9 %collective-permute-done.6.refs_4_ = bf16[1040,128]{1,0:T(8,128)(2,1)S(1)} collective-permute-done((bf16[1040,128]{1,0:T(8,128)(2,1)S(1)}, bf16[1040,128]{1,0:T(8,128)(2,1)S(1)}, u32[]{:S(2)}, u32[]{:S(2)}) %collective-permute-start.6) | collective-permute-done | bytes 266272 | tf_op jit(solution)/shard_map/ppermute | solution.py:373
  66.3 1.6 collective-permute-done.7.refs_5_
  68.0 0.6 copy-done.32
  68.6 0.1 copy-done.34
  68.7 0.1 copy-done.35
  68.9 13.4 %first_back.1 = (s16[2064,128]{1,0:T(8,128)(2,1)}, f32[16,128,128]{2,1,0:T(8,128)}, f32[16,128,128]{2,1,0:T(8,128)}, s16[2064,128]{1,0:T(8,128)(2,1)}, bf16[24,512,128]{2,1,0:T(8,128)(2,1)}) custom-call(bf16[64,192]{1,0:T(8,128)(2,1)} %get-tuple-element.69.kx_ref.refs_3_, bf16[3,128,128]{2,1,0:T(8,128)(2,1)} %get-tuple-element.70.ky_ref.refs_4_, ...), custom_call_target="tpu_custom_call" | custom-call | flops 8589934592 | bytes 12582912 | tf_op jit(solution)/shard_map/first_back/pallas_call | solution.py:335
  82.3 1.9 collective-permute-start.15
  84.2 5.8 %collective-permute-start.13 = (s16[2064,128]{1,0:T(8,128)(2,1)}, s16[2064,128]{1,0:T(8,128)(2,1)S(1)}, u32[]{:S(2)}, u32[]{:S(2)}) collective-permute-start(s16[2064,128]{1,0:T(8,128)(2,1)} %get-tuple-element.93), channel_id=1, source_target_pairs={{0,1},{1,2},{2,3},{3,4},{4,5},{5,6},{6,7},{7,8},{8,9},{9,10},{10,1... | collective-permute-start | bytes 1585160 | tf_op jit(solution)/shard_map/ppermute | solution.py:351
  89.9 5.2 %collective-permute-done.15.edge_ref = s16[2064,128]{1,0:T(8,128)(2,1)S(1)} collective-permute-done((s16[2064,128]{1,0:T(8,128)(2,1)}, s16[2064,128]{1,0:T(8,128)(2,1)S(1)}, u32[]{:S(2)}, u32[]{:S(2)}) %collective-permute-start.15) | collective-permute-done | bytes 528416 | tf_op jit(solution)/shard_map/ppermute | solution.py:351
  95.1 0.8 copy-done.7
  95.9 2.5 %join.5.own_ref = s16[2064,128]{1,0:T(8,128)(2,1)} custom-call(f32[16,128,128]{2,1,0:T(8,128)} %get-tuple-element.95.own_ref, s16[2064,128]{1,0:T(8,128)(2,1)} %copy-done.7), custom_call_target="tpu_custom_call" | custom-call | flops 1048576 | bytes 12582912 | tf_op jit(solution)/shard_map/join/pallas_call | solution.py:335
  98.4 2.6 %collective-permute-start.16 = (s16[2064,128]{1,0:T(8,128)(2,1)}, s16[2064,128]{1,0:T(8,128)(2,1)S(1)}, u32[]{:S(2)}, u32[]{:S(2)}) collective-permute-start(s16[2064,128]{1,0:T(8,128)(2,1)} %join.5.own_ref), channel_id=1, source_target_pairs={{0,64},{64,0},{1,65},{65,1},{2,66},{66,2},{3,67},{67,3},{4,68},{68... | collective-permute-start | bytes 1585160 | tf_op jit(solution)/shard_map/ppermute | solution.py:359
  101.0 0.8 copy-done.6
  101.9 2.5 %join.4.own_ref = s16[2064,128]{1,0:T(8,128)(2,1)} custom-call(f32[16,128,128]{2,1,0:T(8,128)} %get-tuple-element.92.own_ref, s16[2064,128]{1,0:T(8,128)(2,1)} %copy-done.6), custom_call_target="tpu_custom_call" | custom-call | flops 1048576 | bytes 12582912 | tf_op jit(solution)/shard_map/join/pallas_call | solution.py:335
  104.3 0.4 collective-permute-start.14
  104.7 1.6 fusion
  106.4 9.3 %collective-permute-done.16.other_ref = s16[2064,128]{1,0:T(8,128)(2,1)S(1)} collective-permute-done((s16[2064,128]{1,0:T(8,128)(2,1)}, s16[2064,128]{1,0:T(8,128)(2,1)S(1)}, u32[]{:S(2)}, u32[]{:S(2)}) %collective-permute-start.16) | collective-permute-done | bytes 528416 | tf_op jit(solution)/shard_map/ppermute | solution.py:359
  115.7 0.8 copy-done.4
  116.5 3.0 %update.3 = (f32[16,128,128]{2,1,0:T(8,128)}, bf16[16,128,128]{2,1,0:T(8,128)(2,1)}) custom-call(f32[16,128,128]{2,1,0:T(8,128)} %get-tuple-element.105.before_ref, s16[2064,128]{1,0:T(8,128)(2,1)} %join.5.own_ref, s16[2064,128]{1,0:T(8,128)(2,1)} %copy-done.4), custom_call_target="tpu_custom_call" | custom-call | flops 1048576 | bytes 12582912 | tf_op jit(solution)/shard_map/update/pallas_call | solution.py:335
  119.5 1.9 collective-permute-start.17
  121.4 3.3 %collective-permute-done.14.other_ref = s16[2064,128]{1,0:T(8,128)(2,1)S(1)} collective-permute-done((s16[2064,128]{1,0:T(8,128)(2,1)}, s16[2064,128]{1,0:T(8,128)(2,1)S(1)}, u32[]{:S(2)}, u32[]{:S(2)}) %collective-permute-start.14) | collective-permute-done | bytes 528416 | tf_op jit(solution)/shard_map/ppermute | solution.py:359
  124.8 0.8 copy-done.3
  125.6 3.0 %update.2 = (f32[16,128,128]{2,1,0:T(8,128)}, bf16[16,128,128]{2,1,0:T(8,128)(2,1)}) custom-call(f32[16,128,128]{2,1,0:T(8,128)} %get-tuple-element.106.before_ref, s16[2064,128]{1,0:T(8,128)(2,1)} %join.4.own_ref, s16[2064,128]{1,0:T(8,128)(2,1)} %copy-done.3), custom_call_target="tpu_custom_call" | custom-call | flops 1048576 | bytes 12582912 | tf_op jit(solution)/shard_map/update/pallas_call | solution.py:335
  128.6 2.1 %collective-permute-start.18 = (bf16[16,128,128]{2,1,0:T(8,128)(2,1)}, bf16[16,128,128]{2,1,0:T(8,128)(2,1)S(1)}, u32[]{:S(2)}, u32[]{:S(2)}) collective-permute-start(bf16[16,128,128]{2,1,0:T(8,128)(2,1)} %get-tuple-element.99.refs_7_), channel_id=1, source_target_pairs={{1,0},{2,1},{3,2},{4,3},{5,4},{6,5},{7,6},{8,7},{9,8},{10,9},{11,1... | collective-permute-start | bytes 1572872 | tf_op jit(solution)/shard_map/ppermute | solution.py:351
  130.7 10.7 %collective-permute-done.18.refs_9_ = bf16[16,128,128]{2,1,0:T(8,128)(2,1)S(1)} collective-permute-done((bf16[16,128,128]{2,1,0:T(8,128)(2,1)}, bf16[16,128,128]{2,1,0:T(8,128)(2,1)S(1)}, u32[]{:S(2)}, u32[]{:S(2)}) %collective-permute-start.18) | collective-permute-done | bytes 524320 | tf_op jit(solution)/shard_map/ppermute | solution.py:351
  141.4 0.8 copy-done.14
  142.2 17.4 %sweep.1 = (s16[2064,128]{1,0:T(8,128)(2,1)}, f32[16,128,128]{2,1,0:T(8,128)}, f32[16,128,128]{2,1,0:T(8,128)}, s16[2064,128]{1,0:T(8,128)(2,1)}) custom-call(bf16[96,64]{1,0:T(8,128)(2,1)} %get-tuple-element.84.kx_ref.refs_0_, bf16[3,128,128]{2,1,0:T(8,128)(2,1)} %get-tuple-element.85.ky_ref.refs_1_, bf16[3,128,128]{2,1,0:T(8,128)(2,1)} %get-tuple-element.86.kz_ref.refs_2_, ...), custom_call_target="tpu_custom_call" | custom-call | flops 15032385536 | bytes 12582912 | tf_op jit(solution)/shard_map/sweep/pallas_call | solution.py:335
  159.6 1.9 collective-permute-start.21
  161.5 5.8 %collective-permute-start.19 = (s16[2064,128]{1,0:T(8,128)(2,1)}, s16[2064,128]{1,0:T(8,128)(2,1)S(1)}, u32[]{:S(2)}, u32[]{:S(2)}) collective-permute-start(s16[2064,128]{1,0:T(8,128)(2,1)} %get-tuple-element.102), channel_id=1, source_target_pairs={{0,1},{1,2},{2,3},{3,4},{4,5},{5,6},{6,7},{7,8},{8,9},{9,10},{10,1... | collective-permute-start | bytes 1585160 | tf_op jit(solution)/shard_map/ppermute | solution.py:351
  167.3 5.2 %collective-permute-done.21.edge_ref = s16[2064,128]{1,0:T(8,128)(2,1)S(1)} collective-permute-done((s16[2064,128]{1,0:T(8,128)(2,1)}, s16[2064,128]{1,0:T(8,128)(2,1)S(1)}, u32[]{:S(2)}, u32[]{:S(2)}) %collective-permute-start.21) | collective-permute-done | bytes 528416 | tf_op jit(solution)/shard_map/ppermute | solution.py:351
  172.4 0.8 copy-done.8
  173.2 2.5 %join.7.refs_2_ = s16[2064,128]{1,0:T(8,128)(2,1)} custom-call(f32[16,128,128]{2,1,0:T(8,128)} %get-tuple-element.103.own_ref, s16[2064,128]{1,0:T(8,128)(2,1)} %copy-done.8), custom_call_target="tpu_custom_call" | custom-call | flops 1048576 | bytes 12582912 | tf_op jit(solution)/shard_map/join/pallas_call | solution.py:335
  175.7 1.9 collective-permute-start.22
  177.6 0.8 copy-done.5
  178.4 2.5 %join.6.refs_0_ = s16[2064,128]{1,0:T(8,128)(2,1)} custom-call(f32[16,128,128]{2,1,0:T(8,128)} %get-tuple-element.101.own_ref, s16[2064,128]{1,0:T(8,128)(2,1)} %copy-done.5), custom_call_target="tpu_custom_call" | custom-call | flops 1048576 | bytes 12582912 | tf_op jit(solution)/shard_map/join/pallas_call | solution.py:335
  180.9 1.1 collective-permute-start.20
  182.0 11.3 %collective-permute-done.22.refs_3_ = s16[2064,128]{1,0:T(8,128)(2,1)S(1)} collective-permute-done((s16[2064,128]{1,0:T(8,128)(2,1)}, s16[2064,128]{1,0:T(8,128)(2,1)S(1)}, u32[]{:S(2)}, u32[]{:S(2)}) %collective-permute-start.22) | collective-permute-done | bytes 528416 | tf_op jit(solution)/shard_map/ppermute | solution.py:359
  193.3 8.1 %collective-permute-done.20.refs_1_ = s16[2064,128]{1,0:T(8,128)(2,1)S(1)} collective-permute-done((s16[2064,128]{1,0:T(8,128)(2,1)}, s16[2064,128]{1,0:T(8,128)(2,1)S(1)}, u32[]{:S(2)}, u32[]{:S(2)}) %collective-permute-start.20) | collective-permute-done | bytes 528416 | tf_op jit(solution)/shard_map/ppermute | solution.py:359
  201.3 0.8 copy-done.2
  202.1 4.1 %last_update.1 = f32[32,128,128]{2,1,0:T(8,128)} custom-call(f32[16,128,128]{2,1,0:T(8,128)} %get-tuple-element.94.low_ref, f32[16,128,128]{2,1,0:T(8,128)} %get-tuple-element.97.high_ref, s16[2064,128]{1,0:T(8,128)(2,1)} %join.6.refs_0_, s16[2064,128]{1,0:T(8,128)(2,1)} %copy-done.2, s16[2064,128]{1,0:T(8,128)(2,1)} %join.7.refs_2_, s16[2064,128]{1,0:T(8,128)(2,1)} %copy-done.1), custom_call_target="tpu_custom_call" | custom-call | flops 1048576 | bytes 12582912 | tf_op jit(solution)/shard_map/last_update/pallas_call | solution.py:335
  (70 shorter events, 0.1 us)
Async XLA Ops:
  0.0 5.4 %copy-start = (f32[32,128,128]{2,1,0:T(8,128)S(1)}, f32[32,128,128]{2,1,0:T(8,128)}, u32[]{:S(2)}) copy-start(f32[32,128,128]{2,1,0:T(8,128)} %param.4) | copy-start | bytes 6291460
  5.4 5.0 %copy-start.33 = (bf16[1040,128]{1,0:T(8,128)(2,1)S(1)}, bf16[1040,128]{1,0:T(8,128)(2,1)}, u32[]{:S(2)}) copy-start(bf16[1040,128]{1,0:T(8,128)(2,1)} %get-tuple-element.81) | copy-start | bytes 798724
  5.4 10.6 %copy-start.28 = (bf16[1040,128]{1,0:T(8,128)(2,1)S(1)}, bf16[1040,128]{1,0:T(8,128)(2,1)}, u32[]{:S(2)}) copy-start(bf16[1040,128]{1,0:T(8,128)(2,1)} %get-tuple-element.83) | copy-start | bytes 798724
  5.4 23.6 %copy-start.26 = (bf16[1040,128]{1,0:T(8,128)(2,1)S(1)}, bf16[1040,128]{1,0:T(8,128)(2,1)}, u32[]{:S(2)}) copy-start(bf16[1040,128]{1,0:T(8,128)(2,1)} %get-tuple-element.72) | copy-start | bytes 798724
  5.4 23.6 %copy-start.24 = (bf16[1040,128]{1,0:T(8,128)(2,1)S(1)}, bf16[1040,128]{1,0:T(8,128)(2,1)}, u32[]{:S(2)}) copy-start(bf16[1040,128]{1,0:T(8,128)(2,1)} %get-tuple-element.73) | copy-start | bytes 798724
  5.4 30.4 %copy-start.23 = (bf16[1040,128]{1,0:T(8,128)(2,1)S(1)}, bf16[1040,128]{1,0:T(8,128)(2,1)}, u32[]{:S(2)}) copy-start(bf16[1040,128]{1,0:T(8,128)(2,1)} %get-tuple-element.74) | copy-start | bytes 798724
  5.7 31.7 %copy-start.9 = (bf16[16,128,128]{2,1,0:T(8,128)(2,1)}, bf16[16,128,128]{2,1,0:T(8,128)(2,1)S(1)}, u32[]{:S(2)}) copy-start(bf16[16,128,128]{2,1,0:T(8,128)(2,1)S(1)} %get-tuple-element.107.refs_1_) | copy-start | bytes 1572868
  5.7 31.7 %copy-start.10 = (bf16[16,128,128]{2,1,0:T(8,128)(2,1)}, bf16[16,128,128]{2,1,0:T(8,128)(2,1)S(1)}, u32[]{:S(2)}) copy-start(bf16[16,128,128]{2,1,0:T(8,128)(2,1)S(1)} %get-tuple-element.108.refs_2_) | copy-start | bytes 1572868
  5.7 23.3 %collective-permute-start = (bf16[16,128,128]{2,1,0:T(8,128)(2,1)S(1)}, bf16[16,128,128]{2,1,0:T(8,128)(2,1)S(1)}, u32[]{:S(2)}, u32[]{:S(2)}) collective-permute-start(bf16[16,128,128]{2,1,0:T(8,128)(2,1)S(1)} %get-tuple-element.108.refs_2_), channel_id=1, source_target_pairs={{0,1},{1,2},{2,3},{3,4},{4,5},{5,6},{6,7},{7,8},{8,9},{9,10},{10,1... | collective-permute-start | bytes 1572872 | tf_op jit(solution)/shard_map/ppermute | solution.py:351
  8.2 27.6 %collective-permute-start.1 = (bf16[16,128,128]{2,1,0:T(8,128)(2,1)S(1)}, bf16[16,128,128]{2,1,0:T(8,128)(2,1)S(1)}, u32[]{:S(2)}, u32[]{:S(2)}) collective-permute-start(bf16[16,128,128]{2,1,0:T(8,128)(2,1)S(1)} %get-tuple-element.107.refs_1_), channel_id=1, source_target_pairs={{1,0},{2,1},{3,2},{4,3},{5,4},{6,5},{7,6},{8,7},{9,8},{10,9},{11,1... | collective-permute-start | bytes 1572872 | tf_op jit(solution)/shard_map/ppermute | solution.py:351
  10.4 18.7 %collective-permute-start.10 = (bf16[1040,128]{1,0:T(8,128)(2,1)S(1)}, bf16[1040,128]{1,0:T(8,128)(2,1)S(1)}, u32[]{:S(2)}, u32[]{:S(2)}) collective-permute-start(bf16[1040,128]{1,0:T(8,128)(2,1)S(1)} %copy-done.33), channel_id=1, source_target_pairs={{0,3},{1,4},{2,5},{3,6},{4,7},{5,8},{6,9},{7,10},{8,11},{9,12},{10... | collective-permute-start | bytes 798728 | tf_op jit(solution)/shard_map/ppermute | solution.py:373
  13.3 34.8 %collective-permute-start.11 = (bf16[1040,128]{1,0:T(8,128)(2,1)}, bf16[1040,128]{1,0:T(8,128)(2,1)S(1)}, u32[]{:S(2)}, u32[]{:S(2)}) collective-permute-start(bf16[1040,128]{1,0:T(8,128)(2,1)} %get-tuple-element.82), channel_id=1, source_target_pairs={{0,4},{1,5},{2,6},{3,7},{4,8},{5,9},{6,10},{7,11},{8,12},{9,13},{1... | collective-permute-start | bytes 798728 | tf_op jit(solution)/shard_map/ppermute | solution.py:373
  16.0 32.2 %collective-permute-start.12 = (bf16[1040,128]{1,0:T(8,128)(2,1)S(1)}, bf16[1040,128]{1,0:T(8,128)(2,1)S(1)}, u32[]{:S(2)}, u32[]{:S(2)}) collective-permute-start(bf16[1040,128]{1,0:T(8,128)(2,1)S(1)} %copy-done.28), channel_id=1, source_target_pairs={{0,5},{1,6},{2,7},{3,8},{4,9},{5,10},{6,11},{7,12},{8,13},{9,14},{... | collective-permute-start | bytes 798728 | tf_op jit(solution)/shard_map/ppermute | solution.py:373
  29.1 19.0 %copy-start.19 = (bf16[1040,128]{1,0:T(8,128)(2,1)}, bf16[1040,128]{1,0:T(8,128)(2,1)S(1)}, u32[]{:S(2)}) copy-start(bf16[1040,128]{1,0:T(8,128)(2,1)S(1)} %collective-permute-done.10.refs_9_) | copy-start | bytes 798724
  29.1 21.2 %collective-permute-start.2 = (bf16[1040,128]{1,0:T(8,128)(2,1)S(1)}, bf16[1040,128]{1,0:T(8,128)(2,1)S(1)}, u32[]{:S(2)}, u32[]{:S(2)}) collective-permute-start(bf16[1040,128]{1,0:T(8,128)(2,1)S(1)} %copy-done.26), channel_id=1, source_target_pairs={{0,58},{1,59},{2,60},{3,61},{4,62},{5,63},{6,0},{7,1},{8,2},{9,3},... | collective-permute-start | bytes 798728 | tf_op jit(solution)/shard_map/ppermute | solution.py:373
  29.1 8.3 %copy-start.11 = (bf16[16,128,128]{2,1,0:T(8,128)(2,1)}, bf16[16,128,128]{2,1,0:T(8,128)(2,1)S(1)}, u32[]{:S(2)}) copy-start(bf16[16,128,128]{2,1,0:T(8,128)(2,1)S(1)} %collective-permute-done.refs_0_) | copy-start | bytes 1572868
  29.1 23.2 %collective-permute-start.3 = (bf16[1040,128]{1,0:T(8,128)(2,1)S(1)}, bf16[1040,128]{1,0:T(8,128)(2,1)S(1)}, u32[]{:S(2)}, u32[]{:S(2)}) collective-permute-start(bf16[1040,128]{1,0:T(8,128)(2,1)S(1)} %copy-done.24), channel_id=1, source_target_pairs={{0,59},{1,60},{2,61},{3,62},{4,63},{5,0},{6,1},{7,2},{8,3},{9,4},{... | collective-permute-start | bytes 798728 | tf_op jit(solution)/shard_map/ppermute | solution.py:373
  35.8 1.6 copy-start.12
  35.8 18.5 %collective-permute-start.4 = (bf16[1040,128]{1,0:T(8,128)(2,1)S(1)}, bf16[1040,128]{1,0:T(8,128)(2,1)S(1)}, u32[]{:S(2)}, u32[]{:S(2)}) collective-permute-start(bf16[1040,128]{1,0:T(8,128)(2,1)S(1)} %copy-done.23), channel_id=1, source_target_pairs={{0,60},{1,61},{2,62},{3,63},{4,0},{5,1},{6,2},{7,3},{8,4},{9,5},{1... | collective-permute-start | bytes 798728 | tf_op jit(solution)/shard_map/ppermute | solution.py:373
  37.4 10.7 %copy-start.20 = (bf16[1040,128]{1,0:T(8,128)(2,1)S(1)}, bf16[1040,128]{1,0:T(8,128)(2,1)}, u32[]{:S(2)}) copy-start(bf16[1040,128]{1,0:T(8,128)(2,1)} %get-tuple-element.75) | copy-start | bytes 798724
  37.4 10.8 %copy-start.18 = (bf16[1040,128]{1,0:T(8,128)(2,1)S(1)}, bf16[1040,128]{1,0:T(8,128)(2,1)}, u32[]{:S(2)}) copy-start(bf16[1040,128]{1,0:T(8,128)(2,1)} %get-tuple-element.88) | copy-start | bytes 798724
  37.4 12.9 %copy-start.17 = (bf16[1040,128]{1,0:T(8,128)(2,1)S(1)}, bf16[1040,128]{1,0:T(8,128)(2,1)}, u32[]{:S(2)}) copy-start(bf16[1040,128]{1,0:T(8,128)(2,1)} %get-tuple-element.89) | copy-start | bytes 798724
  37.4 14.9 %copy-start.16 = (bf16[1040,128]{1,0:T(8,128)(2,1)S(1)}, bf16[1040,128]{1,0:T(8,128)(2,1)}, u32[]{:S(2)}) copy-start(bf16[1040,128]{1,0:T(8,128)(2,1)} %get-tuple-element.90) | copy-start | bytes 798724
  37.4 16.9 %copy-start.15 = (bf16[1040,128]{1,0:T(8,128)(2,1)S(1)}, bf16[1040,128]{1,0:T(8,128)(2,1)}, u32[]{:S(2)}) copy-start(bf16[1040,128]{1,0:T(8,128)(2,1)} %get-tuple-element.91) | copy-start | bytes 798724
  48.1 19.9 %copy-start.21 = (bf16[1040,128]{1,0:T(8,128)(2,1)}, bf16[1040,128]{1,0:T(8,128)(2,1)S(1)}, u32[]{:S(2)}) copy-start(bf16[1040,128]{1,0:T(8,128)(2,1)S(1)} %collective-permute-done.11.refs_10_) | copy-start | bytes 798724
  48.1 10.3 %collective-permute-start.5 = (bf16[1040,128]{1,0:T(8,128)(2,1)S(1)}, bf16[1040,128]{1,0:T(8,128)(2,1)S(1)}, u32[]{:S(2)}, u32[]{:S(2)}) collective-permute-start(bf16[1040,128]{1,0:T(8,128)(2,1)S(1)} %copy-done.20), channel_id=1, source_target_pairs={{0,61},{1,62},{2,63},{3,0},{4,1},{5,2},{6,3},{7,4},{8,5},{9,6},{10... | collective-permute-start | bytes 798728 | tf_op jit(solution)/shard_map/ppermute | solution.py:373
  48.2 19.7 %copy-start.22 = (bf16[1040,128]{1,0:T(8,128)(2,1)}, bf16[1040,128]{1,0:T(8,128)(2,1)S(1)}, u32[]{:S(2)}) copy-start(bf16[1040,128]{1,0:T(8,128)(2,1)S(1)} %collective-permute-done.12.refs_11_) | copy-start | bytes 798724
  48.2 18.1 %collective-permute-start.6 = (bf16[1040,128]{1,0:T(8,128)(2,1)S(1)}, bf16[1040,128]{1,0:T(8,128)(2,1)S(1)}, u32[]{:S(2)}, u32[]{:S(2)}) collective-permute-start(bf16[1040,128]{1,0:T(8,128)(2,1)S(1)} %copy-done.18), channel_id=1, source_target_pairs={{0,62},{1,63},{2,0},{3,1},{4,2},{5,3},{6,4},{7,5},{8,6},{9,7},{10,... | collective-permute-start | bytes 798728 | tf_op jit(solution)/shard_map/ppermute | solution.py:373
  50.3 17.7 %copy-start.25 = (bf16[1040,128]{1,0:T(8,128)(2,1)}, bf16[1040,128]{1,0:T(8,128)(2,1)S(1)}, u32[]{:S(2)}) copy-start(bf16[1040,128]{1,0:T(8,128)(2,1)S(1)} %collective-permute-done.2.refs_0_) | copy-start | bytes 798724
  50.3 17.6 %collective-permute-start.7 = (bf16[1040,128]{1,0:T(8,128)(2,1)S(1)}, bf16[1040,128]{1,0:T(8,128)(2,1)S(1)}, u32[]{:S(2)}, u32[]{:S(2)}) collective-permute-start(bf16[1040,128]{1,0:T(8,128)(2,1)S(1)} %copy-done.17), channel_id=1, source_target_pairs={{0,63},{1,0},{2,1},{3,2},{4,3},{5,4},{6,5},{7,6},{8,7},{9,8},{10,9... | collective-permute-start | bytes 798728 | tf_op jit(solution)/shard_map/ppermute | solution.py:373
  52.3 15.6 %copy-start.27 = (bf16[1040,128]{1,0:T(8,128)(2,1)}, bf16[1040,128]{1,0:T(8,128)(2,1)S(1)}, u32[]{:S(2)}) copy-start(bf16[1040,128]{1,0:T(8,128)(2,1)S(1)} %collective-permute-done.3.refs_1_) | copy-start | bytes 798724
  52.3 15.6 %collective-permute-start.8 = (bf16[1040,128]{1,0:T(8,128)(2,1)S(1)}, bf16[1040,128]{1,0:T(8,128)(2,1)S(1)}, u32[]{:S(2)}, u32[]{:S(2)}) collective-permute-start(bf16[1040,128]{1,0:T(8,128)(2,1)S(1)} %copy-done.16), channel_id=1, source_target_pairs={{0,1},{1,2},{2,3},{3,4},{4,5},{5,6},{6,7},{7,8},{8,9},{9,10},{10,1... | collective-permute-start | bytes 798728 | tf_op jit(solution)/shard_map/ppermute | solution.py:373
  54.3 13.7 %copy-start.29 = (bf16[1040,128]{1,0:T(8,128)(2,1)}, bf16[1040,128]{1,0:T(8,128)(2,1)S(1)}, u32[]{:S(2)}) copy-start(bf16[1040,128]{1,0:T(8,128)(2,1)S(1)} %collective-permute-done.4.refs_2_) | copy-start | bytes 798724
  54.3 13.6 %collective-permute-start.9 = (bf16[1040,128]{1,0:T(8,128)(2,1)S(1)}, bf16[1040,128]{1,0:T(8,128)(2,1)S(1)}, u32[]{:S(2)}, u32[]{:S(2)}) collective-permute-start(bf16[1040,128]{1,0:T(8,128)(2,1)S(1)} %copy-done.15), channel_id=1, source_target_pairs={{0,2},{1,3},{2,4},{3,5},{4,6},{5,7},{6,8},{7,9},{8,10},{9,11},{10,... | collective-permute-start | bytes 798728 | tf_op jit(solution)/shard_map/ppermute | solution.py:373
  58.4 9.6 %copy-start.30 = (bf16[1040,128]{1,0:T(8,128)(2,1)}, bf16[1040,128]{1,0:T(8,128)(2,1)S(1)}, u32[]{:S(2)}) copy-start(bf16[1040,128]{1,0:T(8,128)(2,1)S(1)} %collective-permute-done.5.refs_3_) | copy-start | bytes 798724
  66.3 1.7 copy-start.31
  67.9 0.7 copy-start.32
  67.9 0.8 copy-start.34
  67.9 0.9 copy-start.35
  82.3 12.9 %collective-permute-start.15 = (s16[2064,128]{1,0:T(8,128)(2,1)}, s16[2064,128]{1,0:T(8,128)(2,1)S(1)}, u32[]{:S(2)}, u32[]{:S(2)}) collective-permute-start(s16[2064,128]{1,0:T(8,128)(2,1)} %get-tuple-element.96), channel_id=1, source_target_pairs={{1,0},{2,1},{3,2},{4,3},{5,4},{6,5},{7,6},{8,7},{9,8},{10,9},{11,1... | collective-permute-start | bytes 1585160 | tf_op jit(solution)/shard_map/ppermute | solution.py:351
  84.2 16.9 %collective-permute-start.13 = (s16[2064,128]{1,0:T(8,128)(2,1)}, s16[2064,128]{1,0:T(8,128)(2,1)S(1)}, u32[]{:S(2)}, u32[]{:S(2)}) collective-permute-start(s16[2064,128]{1,0:T(8,128)(2,1)} %get-tuple-element.93), channel_id=1, source_target_pairs={{0,1},{1,2},{2,3},{3,4},{4,5},{5,6},{6,7},{7,8},{8,9},{9,10},{10,1... | collective-permute-start | bytes 1585160 | tf_op jit(solution)/shard_map/ppermute | solution.py:351
  95.1 0.8 copy-start.7
  98.4 17.3 %collective-permute-start.16 = (s16[2064,128]{1,0:T(8,128)(2,1)}, s16[2064,128]{1,0:T(8,128)(2,1)S(1)}, u32[]{:S(2)}, u32[]{:S(2)}) collective-permute-start(s16[2064,128]{1,0:T(8,128)(2,1)} %join.5.own_ref), channel_id=1, source_target_pairs={{0,64},{64,0},{1,65},{65,1},{2,66},{66,2},{3,67},{67,3},{4,68},{68... | collective-permute-start | bytes 1585160 | tf_op jit(solution)/shard_map/ppermute | solution.py:359
  101.0 0.8 copy-start.6
  104.3 20.4 %collective-permute-start.14 = (s16[2064,128]{1,0:T(8,128)(2,1)}, s16[2064,128]{1,0:T(8,128)(2,1)S(1)}, u32[]{:S(2)}, u32[]{:S(2)}) collective-permute-start(s16[2064,128]{1,0:T(8,128)(2,1)} %join.4.own_ref), channel_id=1, source_target_pairs={{0,64},{64,0},{1,65},{65,1},{2,66},{66,2},{3,67},{67,3},{4,68},{68... | collective-permute-start | bytes 1585160 | tf_op jit(solution)/shard_map/ppermute | solution.py:359
  115.7 0.8 copy-start.4
  119.5 11.2 %collective-permute-start.17 = (bf16[16,128,128]{2,1,0:T(8,128)(2,1)}, bf16[16,128,128]{2,1,0:T(8,128)(2,1)S(1)}, u32[]{:S(2)}, u32[]{:S(2)}) collective-permute-start(bf16[16,128,128]{2,1,0:T(8,128)(2,1)} %get-tuple-element.98.refs_8_), channel_id=1, source_target_pairs={{0,1},{1,2},{2,3},{3,4},{4,5},{5,6},{6,7},{7,8},{8,9},{9,10},{10,1... | collective-permute-start | bytes 1572872 | tf_op jit(solution)/shard_map/ppermute | solution.py:351
  124.8 0.8 copy-start.3
  128.6 12.8 %collective-permute-start.18 = (bf16[16,128,128]{2,1,0:T(8,128)(2,1)}, bf16[16,128,128]{2,1,0:T(8,128)(2,1)S(1)}, u32[]{:S(2)}, u32[]{:S(2)}) collective-permute-start(bf16[16,128,128]{2,1,0:T(8,128)(2,1)} %get-tuple-element.99.refs_7_), channel_id=1, source_target_pairs={{1,0},{2,1},{3,2},{4,3},{5,4},{6,5},{7,6},{8,7},{9,8},{10,9},{11,1... | collective-permute-start | bytes 1572872 | tf_op jit(solution)/shard_map/ppermute | solution.py:351
  130.7 10.7 %copy-start.13 = (bf16[16,128,128]{2,1,0:T(8,128)(2,1)}, bf16[16,128,128]{2,1,0:T(8,128)(2,1)S(1)}, u32[]{:S(2)}) copy-start(bf16[16,128,128]{2,1,0:T(8,128)(2,1)S(1)} %collective-permute-done.17.refs_6_) | copy-start | bytes 1572868
  141.4 0.8 copy-start.14
  159.6 12.9 %collective-permute-start.21 = (s16[2064,128]{1,0:T(8,128)(2,1)}, s16[2064,128]{1,0:T(8,128)(2,1)S(1)}, u32[]{:S(2)}, u32[]{:S(2)}) collective-permute-start(s16[2064,128]{1,0:T(8,128)(2,1)} %get-tuple-element.104), channel_id=1, source_target_pairs={{1,0},{2,1},{3,2},{4,3},{5,4},{6,5},{7,6},{8,7},{9,8},{10,9},{11,1... | collective-permute-start | bytes 1585160 | tf_op jit(solution)/shard_map/ppermute | solution.py:351
  161.5 16.1 %collective-permute-start.19 = (s16[2064,128]{1,0:T(8,128)(2,1)}, s16[2064,128]{1,0:T(8,128)(2,1)S(1)}, u32[]{:S(2)}, u32[]{:S(2)}) collective-permute-start(s16[2064,128]{1,0:T(8,128)(2,1)} %get-tuple-element.102), channel_id=1, source_target_pairs={{0,1},{1,2},{2,3},{3,4},{4,5},{5,6},{6,7},{7,8},{8,9},{9,10},{10,1... | collective-permute-start | bytes 1585160 | tf_op jit(solution)/shard_map/ppermute | solution.py:351
  172.4 0.8 copy-start.8
  175.7 17.6 %collective-permute-start.22 = (s16[2064,128]{1,0:T(8,128)(2,1)}, s16[2064,128]{1,0:T(8,128)(2,1)S(1)}, u32[]{:S(2)}, u32[]{:S(2)}) collective-permute-start(s16[2064,128]{1,0:T(8,128)(2,1)} %join.7.refs_2_), channel_id=1, source_target_pairs={{0,64},{64,0},{1,65},{65,1},{2,66},{66,2},{3,67},{67,3},{4,68},{68... | collective-permute-start | bytes 1585160 | tf_op jit(solution)/shard_map/ppermute | solution.py:359
  177.6 0.8 copy-start.5
  180.9 20.5 %collective-permute-start.20 = (s16[2064,128]{1,0:T(8,128)(2,1)}, s16[2064,128]{1,0:T(8,128)(2,1)S(1)}, u32[]{:S(2)}, u32[]{:S(2)}) collective-permute-start(s16[2064,128]{1,0:T(8,128)(2,1)} %join.6.refs_0_), channel_id=1, source_target_pairs={{0,64},{64,0},{1,65},{65,1},{2,66},{66,2},{3,67},{67,3},{4,68},{68... | collective-permute-start | bytes 1585160 | tf_op jit(solution)/shard_map/ppermute | solution.py:359
  193.3 8.1 %copy-start.1 = (s16[2064,128]{1,0:T(8,128)(2,1)}, s16[2064,128]{1,0:T(8,128)(2,1)S(1)}, u32[]{:S(2)}) copy-start(s16[2064,128]{1,0:T(8,128)(2,1)S(1)} %collective-permute-done.22.refs_3_) | copy-start | bytes 1585156
  201.3 0.8 copy-start.2

commit v6 on v5

--- a/solution.py
+++ b/solution.py
@@ -27,7 +27,7 @@
 F32 = jnp.float32
 BF16 = jnp.bfloat16
 I16 = jnp.int16
-VMEM_LIMIT = 56 << 20
+MIB = 1 << 20
 UNROLL = 4
 EARLY = (-6, 5, -5, 4, -4, 3, -3)
 LATE = (2, -2, 1, -1)
@@ -130,7 +130,7 @@
         ],
         out_specs=[pl.BlockSpec(memory_space=pltpu.VMEM)] * SPAN,
         scratch_shapes=[pltpu.SMEM((SLOTS,), jnp.int32), pltpu.SMEM((SPAN,), jnp.int32)],
-        compiler_params=pltpu.CompilerParams(vmem_limit_bytes=VMEM_LIMIT),
+        compiler_params=pltpu.CompilerParams(vmem_limit_bytes=8 * MIB),
         cost_estimate=pl.CostEstimate(flops=0, bytes_accessed=2 * SLOTS * TROWS * Z * 2, transcendentals=0),
         name="pack_tiles",
     )(me, tile_dest[0], view_tiles.reshape(SLOTS, TROWS, Z))
@@ -282,9 +282,9 @@
     fwd, back, parts = refs[0:3], refs[3:6], refs[6:10]
     measured_ref = refs[10]
     outs = refs[11:15]
-    half_ref, back_half_ref, edge_ref, peak_ref, blurred_ref = refs[15:]
+    half_ref, edge_ref, peak_ref, blurred_ref = refs[15:]
     blur_into(*fwd, parts, half_ref, blurred_ref)
-    back_from(*back, measured_ref, blurred_ref, back_half_ref, edge_ref, peak_ref, outs)
+    back_from(*back, measured_ref, blurred_ref, half_ref, edge_ref, peak_ref, outs)
 
 
 def join_kernel(own_ref, edge_ref, out_ref, sum_ref):
@@ -331,14 +331,14 @@
 ]
 
 
-def call(kernel, name, operands, out_shape, scratch, flops):
+def call(kernel, name, operands, out_shape, scratch, flops, vmem=6):
     return pl.pallas_call(
         kernel,
         out_shape=out_shape,
         in_specs=[VM] * len(operands),
         out_specs=jax.tree.map(lambda _: VM, out_shape),
         scratch_shapes=scratch,
-        compiler_params=pltpu.CompilerParams(vmem_limit_bytes=VMEM_LIMIT),
+        compiler_params=pltpu.CompilerParams(vmem_limit_bytes=vmem * MIB),
         cost_estimate=pl.CostEstimate(flops=flops, bytes_accessed=12 << 20, transcendentals=0),
         name=name,
     )(*operands)
@@ -384,6 +384,7 @@
         jax.ShapeDtypeStruct(BLURRED, F32),
         BLUR_SCRATCH,
         6 << 30,
+        18,
     )
     packed, blurred = lax.optimization_barrier((packed, blurred))
     route(LATE)
@@ -394,6 +395,7 @@
         [*CONTRIB, jax.ShapeDtypeStruct((VIEWS_DEV * BX // TP, TROWS, Z), BF16)],
         BACK_SCRATCH,
         8 << 30,
+        28,
     )
     halves = []
     for i, (own, other) in enumerate(exchanged(contributions)):
@@ -414,8 +416,9 @@
         "sweep",
         (*fwd, *back, left, low_planes, high_planes, right, measured),
         CONTRIB,
-        [*BLUR_SCRATCH, *BACK_SCRATCH, pltpu.VMEM(BLURRED, F32)],
+        [*BACK_SCRATCH, pltpu.VMEM(BLURRED, F32)],
         14 << 30,
+        28,
     )
     payloads = [payload for pair in exchanged(contributions) for payload in pair]
     return call(
@@ -425,6 +428,7 @@
         jax.ShapeDtypeStruct(estimate.shape, F32),
         [],
         1 << 20,
+        10,
     )
 
 

time: 207 us -> 183 us (0.88)
  Pallas kernels: 67.6 us -> 33.1 us
  waiting for transfers between devices: 77.2 us -> 87.5 us
  starting transfers between devices: 50.4 us -> 58.4 us
  local copies, waits for them, and re-layouts: 10.6 us -> 3.47 us
    pallas_call x11, Pallas kernels: 63.7 us -> 32 us  [call(): pl.pallas_call(kernel, out_shape=out_shape, in_specs=[VM] * len(operands)...]
    ppermute x4, waiting for transfers between devices: 32 us -> 44.8 us  [exchanged(): pairs.append((payload, lax.ppermute(payload, 'view', [(0, 1), (1, 0)])))]
    ppermute x11, starting transfers between devices: 20.5 us -> 26.6 us  [route(): lax.ppermute(packed[by + SPAN // 2], 'block', perm)]
    unnamed x72 -> x6, local copies, waits for them, and re-layouts: 7.35 us -> 2.4 us
    pallas_call x1, Pallas kernels: 3.9 us -> 1.07 us  [pack_tiles(): pl.pallas_call(pack_kernel, out_shape=[jax.ShapeDtypeStruct((PROWS, Z), B...]
    ppermute x11, waiting for transfers between devices: 24.1 us -> 21.7 us  [route(): lax.ppermute(packed[by + SPAN // 2], 'block', perm)]
  transfers between devices with their start and end apart: 23 -> 23, of which waited for: 11 -> 11; matrix products, arithmetic and copies ran while one was open for 1% -> 0% of each run, Pallas kernels for 14% -> 5%
where the time goes in v6:
time: 183 us
  waiting for transfers between devices  87.5 us (48%)
  starting transfers between devices  58.4 us (32%)
  Pallas kernels  33.1 us (18%)
  local copies, waits for them, and re-layouts  3.47 us (2%)
    ppermute x4, waiting for transfers between devices, exchanged(): pairs.append((payload, lax.ppermute(payload, 'view', [(0, 1), (1, 0)])))  44.8 us
    pallas_call x11, Pallas kernels, call(): pl.pallas_call(kernel, out_shape=out_shape, in_specs=[VM] * len(operands)...  32 us
    ppermute x11, starting transfers between devices, route(): lax.ppermute(packed[by + SPAN // 2], 'block', perm)  26.6 us
    ppermute x8, starting transfers between devices, neighbours(): return (lax.ppermute(high, 'block', up), lax.ppermute(low, 'block', down))  23.9 us
    ppermute x11, waiting for transfers between devices, route(): lax.ppermute(packed[by + SPAN // 2], 'block', perm)  21.7 us
    ppermute x8, waiting for transfers between devices, neighbours(): return (lax.ppermute(high, 'block', up), lax.ppermute(low, 'block', down))  21 us
    ppermute x4, starting transfers between devices, exchanged(): pairs.append((payload, lax.ppermute(payload, 'view', [(0, 1), (1, 0)])))  7.95 us
  transfers between devices with their start and end apart: 23, of which 11 were waited for; matrix products, arithmetic and copies ran while one was open for 0% of the time, Pallas kernels for 5%

profile of v6, /device:TPU:97, one launch (start us, length us, event | category | flops | bytes accessed | tf_op | source)
XLA Modules:
  0.0 182.9 jit_solution(15237043226653060360)
XLA Ops:
  0.0 0.8 copy.6
  0.8 1.9 %copy-done = bf16[1,24,4,128,128]{4,3,2,1,0:T(8,128)(2,1)S(1)} copy-done((bf16[1,24,4,128,128]{4,3,2,1,0:T(8,128)(2,1)S(1)}, bf16[1,24,4,128,128]{4,3,2,1,0:T(8,128)(2,1)}, u32[]{:S(2)}) %copy-start) | copy-done | bytes 3145752
  2.7 1.1 pack_tiles.1
  3.7 0.0 copy-start.1
  3.7 0.5 copy-done.2
  4.2 0.2 convert_element_type.3
  4.4 0.1 fusion.1
  4.5 2.3 %collective-permute-start = (bf16[16,128,128]{2,1,0:T(8,128)(2,1)S(1)}, bf16[16,128,128]{2,1,0:T(8,128)(2,1)S(1)}, u32[]{:S(2)}, u32[]{:S(2)}) collective-permute-start(bf16[16,128,128]{2,1,0:T(8,128)(2,1)S(1)} %get-tuple-element.108.refs_2_), channel_id=1, source_target_pairs={{0,1},{1,2},{2,3},{3,4},{4,5},{5,6},{6,7},{7,8},{8,9},{9,10},{10,1... | collective-permute-start | bytes 1572872 | tf_op jit(solution)/shard_map/ppermute | solution.py:351
  6.8 2.2 %collective-permute-start.1 = (bf16[16,128,128]{2,1,0:T(8,128)(2,1)S(1)}, bf16[16,128,128]{2,1,0:T(8,128)(2,1)S(1)}, u32[]{:S(2)}, u32[]{:S(2)}) collective-permute-start(bf16[16,128,128]{2,1,0:T(8,128)(2,1)S(1)} %get-tuple-element.107.refs_1_), channel_id=1, source_target_pairs={{1,0},{2,1},{3,2},{4,3},{5,4},{6,5},{7,6},{8,7},{9,8},{10,9},{11,1... | collective-permute-start | bytes 1572872 | tf_op jit(solution)/shard_map/ppermute | solution.py:351
  9.0 2.9 %collective-permute-start.10 = (bf16[1040,128]{1,0:T(8,128)(2,1)S(1)}, bf16[1040,128]{1,0:T(8,128)(2,1)S(1)}, u32[]{:S(2)}, u32[]{:S(2)}) collective-permute-start(bf16[1040,128]{1,0:T(8,128)(2,1)S(1)} %get-tuple-element.81), channel_id=1, source_target_pairs={{0,3},{1,4},{2,5},{3,6},{4,7},{5,8},{6,9},{7,10},{8,11},{9,12},{10... | collective-permute-start | bytes 798728 | tf_op jit(solution)/shard_map/ppermute | solution.py:373
  11.9 2.7 %collective-permute-start.11 = (bf16[1040,128]{1,0:T(8,128)(2,1)S(1)}, bf16[1040,128]{1,0:T(8,128)(2,1)S(1)}, u32[]{:S(2)}, u32[]{:S(2)}) collective-permute-start(bf16[1040,128]{1,0:T(8,128)(2,1)S(1)} %get-tuple-element.82), channel_id=1, source_target_pairs={{0,4},{1,5},{2,6},{3,7},{4,8},{5,9},{6,10},{7,11},{8,12},{9,13},{1... | collective-permute-start | bytes 798728 | tf_op jit(solution)/shard_map/ppermute | solution.py:373
  14.6 0.0 collective-permute-start.12
  14.6 0.7 prepare.1
  15.3 12.6 %collective-permute-done.10.refs_9_ = bf16[1040,128]{1,0:T(8,128)(2,1)S(1)} collective-permute-done((bf16[1040,128]{1,0:T(8,128)(2,1)S(1)}, bf16[1040,128]{1,0:T(8,128)(2,1)S(1)}, u32[]{:S(2)}, u32[]{:S(2)}) %collective-permute-start.10) | collective-permute-done | bytes 266272 | tf_op jit(solution)/shard_map/ppermute | solution.py:373
  27.9 0.0 collective-permute-start.2
  27.9 0.0 collective-permute-done.refs_0_
  27.9 6.5 %collective-permute-start.3 = (bf16[1040,128]{1,0:T(8,128)(2,1)S(1)}, bf16[1040,128]{1,0:T(8,128)(2,1)S(1)}, u32[]{:S(2)}, u32[]{:S(2)}) collective-permute-start(bf16[1040,128]{1,0:T(8,128)(2,1)S(1)} %get-tuple-element.73), channel_id=1, source_target_pairs={{0,59},{1,60},{2,61},{3,62},{4,63},{5,0},{6,1},{7,2},{8,3},{9,4},{... | collective-permute-start | bytes 798728 | tf_op jit(solution)/shard_map/ppermute | solution.py:373
  34.4 0.0 collective-permute-done.1.refs_3_
  34.4 1.6 collective-permute-start.4
  36.0 6.2 %first_blur.1.blurred_ref = f32[24,512,128]{2,1,0:T(8,128)S(1)} custom-call(bf16[96,64]{1,0:T(8,128)(2,1)S(1)} %get-tuple-element.84.kx_ref.refs_0_, bf16[3,128,128]{2,1,0:T(8,128)(2,1)S(1)} %get-tuple-element.85.ky_ref.refs_1_, bf16[3,128,128]{2,1,0:T(8,128)(2,1)S(1)} %get-tuple-element.86.kz_ref.refs_2_, ...), custom_call_target="tpu_custom_call" | custom-call | flops 6442450944 | bytes 12582912 | tf_op jit(solution)/shard_map/first_blur/pallas_call | solution.py:335
  42.1 0.0 collective-permute-done.11.refs_10_
  42.1 0.1 collective-permute-start.5
  42.2 0.0 collective-permute-done.12.refs_11_
  42.2 9.0 %collective-permute-start.6 = (bf16[1040,128]{1,0:T(8,128)(2,1)S(1)}, bf16[1040,128]{1,0:T(8,128)(2,1)S(1)}, u32[]{:S(2)}, u32[]{:S(2)}) collective-permute-start(bf16[1040,128]{1,0:T(8,128)(2,1)S(1)} %get-tuple-element.88), channel_id=1, source_target_pairs={{0,62},{1,63},{2,0},{3,1},{4,2},{5,3},{6,4},{7,5},{8,6},{9,7},{10,... | collective-permute-start | bytes 798728 | tf_op jit(solution)/shard_map/ppermute | solution.py:373
  51.3 0.0 collective-permute-done.2.refs_0_
  51.3 0.0 collective-permute-start.7
  51.3 0.0 collective-permute-done.3.refs_1_
  51.3 3.9 %collective-permute-start.8 = (bf16[1040,128]{1,0:T(8,128)(2,1)S(1)}, bf16[1040,128]{1,0:T(8,128)(2,1)S(1)}, u32[]{:S(2)}, u32[]{:S(2)}) collective-permute-start(bf16[1040,128]{1,0:T(8,128)(2,1)S(1)} %get-tuple-element.90), channel_id=1, source_target_pairs={{0,1},{1,2},{2,3},{3,4},{4,5},{5,6},{6,7},{7,8},{8,9},{9,10},{10,1... | collective-permute-start | bytes 798728 | tf_op jit(solution)/shard_map/ppermute | solution.py:373
  55.1 0.0 collective-permute-done.4.refs_2_
  55.1 0.0 collective-permute-start.9
  55.1 0.0 collective-permute-done.5.refs_3_
  55.1 5.1 %collective-permute-done.6.refs_4_ = bf16[1040,128]{1,0:T(8,128)(2,1)S(1)} collective-permute-done((bf16[1040,128]{1,0:T(8,128)(2,1)S(1)}, bf16[1040,128]{1,0:T(8,128)(2,1)S(1)}, u32[]{:S(2)}, u32[]{:S(2)}) %collective-permute-start.6) | collective-permute-done | bytes 266272 | tf_op jit(solution)/shard_map/ppermute | solution.py:373
  60.3 1.7 collective-permute-done.7.refs_5_
  61.9 0.0 collective-permute-done.8.refs_7_
  61.9 2.3 %collective-permute-done.9.refs_8_ = bf16[1040,128]{1,0:T(8,128)(2,1)S(1)} collective-permute-done((bf16[1040,128]{1,0:T(8,128)(2,1)S(1)}, bf16[1040,128]{1,0:T(8,128)(2,1)S(1)}, u32[]{:S(2)}, u32[]{:S(2)}) %collective-permute-start.9) | collective-permute-done | bytes 266272 | tf_op jit(solution)/shard_map/ppermute | solution.py:373
  64.2 7.6 %first_back.1 = (s16[2064,128]{1,0:T(8,128)(2,1)S(1)}, f32[16,128,128]{2,1,0:T(8,128)S(1)}, f32[16,128,128]{2,1,0:T(8,128)S(1)}, s16[2064,128]{1,0:T(8,128)(2,1)S(1)}, bf16[24,512,128]{2,1,0:T(8,128)(2,1)S(1)}) custom-call(bf16[64,192]{1,0:T(8,128)(2,1)S(1)} %get-tuple-element.69.kx_ref.refs_3_, bf16[3,128,128]{2,1,0:T(8,128)(2,1)S(1)} %get-tuple-element.70.ky_ref.refs_4_, ...), custom_call_target="tpu_custom_call" | custom-call | flops 8589934592 | bytes 12582912 | tf_op jit(solution)/shard_map/first_back/pallas_call | solution.py:335
  71.8 1.9 %collective-permute-start.15 = (s16[2064,128]{1,0:T(8,128)(2,1)S(1)}, s16[2064,128]{1,0:T(8,128)(2,1)S(1)}, u32[]{:S(2)}, u32[]{:S(2)}) collective-permute-start(s16[2064,128]{1,0:T(8,128)(2,1)S(1)} %get-tuple-element.96), channel_id=1, source_target_pairs={{1,0},{2,1},{3,2},{4,3},{5,4},{6,5},{7,6},{8,7},{9,8},{10,9},{11,1... | collective-permute-start | bytes 1585160 | tf_op jit(solution)/shard_map/ppermute | solution.py:351
  73.7 5.8 %collective-permute-start.13 = (s16[2064,128]{1,0:T(8,128)(2,1)S(1)}, s16[2064,128]{1,0:T(8,128)(2,1)S(1)}, u32[]{:S(2)}, u32[]{:S(2)}) collective-permute-start(s16[2064,128]{1,0:T(8,128)(2,1)S(1)} %get-tuple-element.93), channel_id=1, source_target_pairs={{0,1},{1,2},{2,3},{3,4},{4,5},{5,6},{6,7},{7,8},{8,9},{9,10},{10,1... | collective-permute-start | bytes 1585160 | tf_op jit(solution)/shard_map/ppermute | solution.py:351
  79.5 5.3 %collective-permute-done.15.edge_ref = s16[2064,128]{1,0:T(8,128)(2,1)S(1)} collective-permute-done((s16[2064,128]{1,0:T(8,128)(2,1)S(1)}, s16[2064,128]{1,0:T(8,128)(2,1)S(1)}, u32[]{:S(2)}, u32[]{:S(2)}) %collective-permute-start.15) | collective-permute-done | bytes 528416 | tf_op jit(solution)/shard_map/ppermute | solution.py:351
  84.8 0.3 join.5.own_ref
  85.1 3.1 %collective-permute-start.16 = (s16[2064,128]{1,0:T(8,128)(2,1)S(1)}, s16[2064,128]{1,0:T(8,128)(2,1)S(1)}, u32[]{:S(2)}, u32[]{:S(2)}) collective-permute-start(s16[2064,128]{1,0:T(8,128)(2,1)S(1)} %join.5.own_ref), channel_id=1, source_target_pairs={{0,64},{64,0},{1,65},{65,1},{2,66},{66,2},{3,67},{67,3},{4,68},{68... | collective-permute-start | bytes 1585160 | tf_op jit(solution)/shard_map/ppermute | solution.py:359
  88.2 0.0 collective-permute-done.13.edge_ref
  88.2 0.3 join.4.own_ref
  88.5 0.8 collective-permute-start.14
  89.4 0.2 fusion
  89.6 16.9 %collective-permute-done.16.other_ref = s16[2064,128]{1,0:T(8,128)(2,1)S(1)} collective-permute-done((s16[2064,128]{1,0:T(8,128)(2,1)S(1)}, s16[2064,128]{1,0:T(8,128)(2,1)S(1)}, u32[]{:S(2)}, u32[]{:S(2)}) %collective-permute-start.16) | collective-permute-done | bytes 528416 | tf_op jit(solution)/shard_map/ppermute | solution.py:359
  106.5 0.4 update.3
  106.9 1.9 %collective-permute-start.17 = (bf16[16,128,128]{2,1,0:T(8,128)(2,1)S(1)}, bf16[16,128,128]{2,1,0:T(8,128)(2,1)S(1)}, u32[]{:S(2)}, u32[]{:S(2)}) collective-permute-start(bf16[16,128,128]{2,1,0:T(8,128)(2,1)S(1)} %get-tuple-element.98.refs_8_), channel_id=1, source_target_pairs={{0,1},{1,2},{2,3},{3,4},{4,5},{5,6},{6,7},{7,8},{8,9},{9,10},{10,1... | collective-permute-start | bytes 1572872 | tf_op jit(solution)/shard_map/ppermute | solution.py:351
  108.8 8.6 %collective-permute-done.14.other_ref = s16[2064,128]{1,0:T(8,128)(2,1)S(1)} collective-permute-done((s16[2064,128]{1,0:T(8,128)(2,1)S(1)}, s16[2064,128]{1,0:T(8,128)(2,1)S(1)}, u32[]{:S(2)}, u32[]{:S(2)}) %collective-permute-start.14) | collective-permute-done | bytes 528416 | tf_op jit(solution)/shard_map/ppermute | solution.py:359
  117.4 0.4 update.2
  117.7 2.1 %collective-permute-start.18 = (bf16[16,128,128]{2,1,0:T(8,128)(2,1)S(1)}, bf16[16,128,128]{2,1,0:T(8,128)(2,1)S(1)}, u32[]{:S(2)}, u32[]{:S(2)}) collective-permute-start(bf16[16,128,128]{2,1,0:T(8,128)(2,1)S(1)} %get-tuple-element.99.refs_7_), channel_id=1, source_target_pairs={{1,0},{2,1},{3,2},{4,3},{5,4},{6,5},{7,6},{8,7},{9,8},{10,9},{11,1... | collective-permute-start | bytes 1572872 | tf_op jit(solution)/shard_map/ppermute | solution.py:351
  119.9 10.5 %collective-permute-done.18.refs_9_ = bf16[16,128,128]{2,1,0:T(8,128)(2,1)S(1)} collective-permute-done((bf16[16,128,128]{2,1,0:T(8,128)(2,1)S(1)}, bf16[16,128,128]{2,1,0:T(8,128)(2,1)S(1)}, u32[]{:S(2)}, u32[]{:S(2)}) %collective-permute-start.18) | collective-permute-done | bytes 524320 | tf_op jit(solution)/shard_map/ppermute | solution.py:351
  130.4 13.5 %sweep.1 = (s16[2064,128]{1,0:T(8,128)(2,1)S(1)}, f32[16,128,128]{2,1,0:T(8,128)S(1)}, f32[16,128,128]{2,1,0:T(8,128)S(1)}, s16[2064,128]{1,0:T(8,128)(2,1)S(1)}) custom-call(bf16[96,64]{1,0:T(8,128)(2,1)S(1)} %get-tuple-element.84.kx_ref.refs_0_, bf16[3,128,128]{2,1,0:T(8,128)(2,1)S(1)} %get-tuple-element.85.ky_ref.refs_1_, ...), custom_call_target="tpu_custom_call" | custom-call | flops 15032385536 | bytes 12582912 | tf_op jit(solution)/shard_map/sweep/pallas_call | solution.py:335
  143.9 1.9 %collective-permute-start.21 = (s16[2064,128]{1,0:T(8,128)(2,1)S(1)}, s16[2064,128]{1,0:T(8,128)(2,1)S(1)}, u32[]{:S(2)}, u32[]{:S(2)}) collective-permute-start(s16[2064,128]{1,0:T(8,128)(2,1)S(1)} %get-tuple-element.104), channel_id=1, source_target_pairs={{1,0},{2,1},{3,2},{4,3},{5,4},{6,5},{7,6},{8,7},{9,8},{10,9},{11,1... | collective-permute-start | bytes 1585160 | tf_op jit(solution)/shard_map/ppermute | solution.py:351
  145.8 5.8 %collective-permute-start.19 = (s16[2064,128]{1,0:T(8,128)(2,1)S(1)}, s16[2064,128]{1,0:T(8,128)(2,1)S(1)}, u32[]{:S(2)}, u32[]{:S(2)}) collective-permute-start(s16[2064,128]{1,0:T(8,128)(2,1)S(1)} %get-tuple-element.102), channel_id=1, source_target_pairs={{0,1},{1,2},{2,3},{3,4},{4,5},{5,6},{6,7},{7,8},{8,9},{9,10},{10,1... | collective-permute-start | bytes 1585160 | tf_op jit(solution)/shard_map/ppermute | solution.py:351
  151.5 5.3 %collective-permute-done.21.edge_ref = s16[2064,128]{1,0:T(8,128)(2,1)S(1)} collective-permute-done((s16[2064,128]{1,0:T(8,128)(2,1)S(1)}, s16[2064,128]{1,0:T(8,128)(2,1)S(1)}, u32[]{:S(2)}, u32[]{:S(2)}) %collective-permute-start.21) | collective-permute-done | bytes 528416 | tf_op jit(solution)/shard_map/ppermute | solution.py:351
  156.8 0.3 join.7.refs_2_
  157.2 3.2 %collective-permute-start.22 = (s16[2064,128]{1,0:T(8,128)(2,1)S(1)}, s16[2064,128]{1,0:T(8,128)(2,1)S(1)}, u32[]{:S(2)}, u32[]{:S(2)}) collective-permute-start(s16[2064,128]{1,0:T(8,128)(2,1)S(1)} %join.7.refs_2_), channel_id=1, source_target_pairs={{0,64},{64,0},{1,65},{65,1},{2,66},{66,2},{3,67},{67,3},{4,68},{68... | collective-permute-start | bytes 1585160 | tf_op jit(solution)/shard_map/ppermute | solution.py:359
  160.3 0.0 collective-permute-done.19.edge_ref
  160.4 0.3 join.6.refs_0_
  160.7 0.8 collective-permute-start.20
  161.5 11.5 %collective-permute-done.22.refs_3_ = s16[2064,128]{1,0:T(8,128)(2,1)S(1)} collective-permute-done((s16[2064,128]{1,0:T(8,128)(2,1)S(1)}, s16[2064,128]{1,0:T(8,128)(2,1)S(1)}, u32[]{:S(2)}, u32[]{:S(2)}) %collective-permute-start.22) | collective-permute-done | bytes 528416 | tf_op jit(solution)/shard_map/ppermute | solution.py:359
  173.0 7.9 %collective-permute-done.20.refs_1_ = s16[2064,128]{1,0:T(8,128)(2,1)S(1)} collective-permute-done((s16[2064,128]{1,0:T(8,128)(2,1)S(1)}, s16[2064,128]{1,0:T(8,128)(2,1)S(1)}, u32[]{:S(2)}, u32[]{:S(2)}) %collective-permute-start.20) | collective-permute-done | bytes 528416 | tf_op jit(solution)/shard_map/ppermute | solution.py:359
  180.9 2.0 %last_update.1 = f32[32,128,128]{2,1,0:T(8,128)} custom-call(f32[16,128,128]{2,1,0:T(8,128)S(1)} %get-tuple-element.94.low_ref, f32[16,128,128]{2,1,0:T(8,128)S(1)} %get-tuple-element.97.high_ref, s16[2064,128]{1,0:T(8,128)(2,1)S(1)} %join.6.refs_0_, s16[2064,128]{1,0:T(8,128)(2,1)S(1)} %collective-permute-done.20.refs_1_, ...), custom_call_target="tpu_custom_call" | custom-call | flops 1048576 | bytes 12582912 | tf_op jit(solution)/shard_map/last_update/pallas_call | solution.py:335
  (4 shorter events, 0.0 us)
Async XLA Ops:
  0.8 1.9 %copy-start = (bf16[1,24,4,128,128]{4,3,2,1,0:T(8,128)(2,1)S(1)}, bf16[1,24,4,128,128]{4,3,2,1,0:T(8,128)(2,1)}, u32[]{:S(2)}) copy-start(bf16[1,24,4,128,128]{4,3,2,1,0:T(8,128)(2,1)} %param.5) | copy-start | bytes 9437188
  2.6 1.6 copy-start.2
  3.7 10.9 %copy-start.1 = (f32[3,3,31]{2,1,0:T(4,128)S(1)}, f32[3,3,31]{2,1,0:T(4,128)}, u32[]{:S(2)}) copy-start(f32[3,3,31]{2,1,0:T(4,128)} %psf_ref) | copy-start | bytes 3352
  4.5 23.4 %collective-permute-start = (bf16[16,128,128]{2,1,0:T(8,128)(2,1)S(1)}, bf16[16,128,128]{2,1,0:T(8,128)(2,1)S(1)}, u32[]{:S(2)}, u32[]{:S(2)}) collective-permute-start(bf16[16,128,128]{2,1,0:T(8,128)(2,1)S(1)} %get-tuple-element.108.refs_2_), channel_id=1, source_target_pairs={{0,1},{1,2},{2,3},{3,4},{4,5},{5,6},{6,7},{7,8},{8,9},{9,10},{10,1... | collective-permute-start | bytes 1572872 | tf_op jit(solution)/shard_map/ppermute | solution.py:351
  6.8 27.6 %collective-permute-start.1 = (bf16[16,128,128]{2,1,0:T(8,128)(2,1)S(1)}, bf16[16,128,128]{2,1,0:T(8,128)(2,1)S(1)}, u32[]{:S(2)}, u32[]{:S(2)}) collective-permute-start(bf16[16,128,128]{2,1,0:T(8,128)(2,1)S(1)} %get-tuple-element.107.refs_1_), channel_id=1, source_target_pairs={{1,0},{2,1},{3,2},{4,3},{5,4},{6,5},{7,6},{8,7},{9,8},{10,9},{11,1... | collective-permute-start | bytes 1572872 | tf_op jit(solution)/shard_map/ppermute | solution.py:351
  9.0 18.9 %collective-permute-start.10 = (bf16[1040,128]{1,0:T(8,128)(2,1)S(1)}, bf16[1040,128]{1,0:T(8,128)(2,1)S(1)}, u32[]{:S(2)}, u32[]{:S(2)}) collective-permute-start(bf16[1040,128]{1,0:T(8,128)(2,1)S(1)} %get-tuple-element.81), channel_id=1, source_target_pairs={{0,3},{1,4},{2,5},{3,6},{4,7},{5,8},{6,9},{7,10},{8,11},{9,12},{10... | collective-permute-start | bytes 798728 | tf_op jit(solution)/shard_map/ppermute | solution.py:373
  11.9 30.2 %collective-permute-start.11 = (bf16[1040,128]{1,0:T(8,128)(2,1)S(1)}, bf16[1040,128]{1,0:T(8,128)(2,1)S(1)}, u32[]{:S(2)}, u32[]{:S(2)}) collective-permute-start(bf16[1040,128]{1,0:T(8,128)(2,1)S(1)} %get-tuple-element.82), channel_id=1, source_target_pairs={{0,4},{1,5},{2,6},{3,7},{4,8},{5,9},{6,10},{7,11},{8,12},{9,13},{1... | collective-permute-start | bytes 798728 | tf_op jit(solution)/shard_map/ppermute | solution.py:373
  14.6 27.6 %collective-permute-start.12 = (bf16[1040,128]{1,0:T(8,128)(2,1)S(1)}, bf16[1040,128]{1,0:T(8,128)(2,1)S(1)}, u32[]{:S(2)}, u32[]{:S(2)}) collective-permute-start(bf16[1040,128]{1,0:T(8,128)(2,1)S(1)} %get-tuple-element.83), channel_id=1, source_target_pairs={{0,5},{1,6},{2,7},{3,8},{4,9},{5,10},{6,11},{7,12},{8,13},{9,14},{... | collective-permute-start | bytes 798728 | tf_op jit(solution)/shard_map/ppermute | solution.py:373
  27.9 23.3 %collective-permute-start.2 = (bf16[1040,128]{1,0:T(8,128)(2,1)S(1)}, bf16[1040,128]{1,0:T(8,128)(2,1)S(1)}, u32[]{:S(2)}, u32[]{:S(2)}) collective-permute-start(bf16[1040,128]{1,0:T(8,128)(2,1)S(1)} %get-tuple-element.72), channel_id=1, source_target_pairs={{0,58},{1,59},{2,60},{3,61},{4,62},{5,63},{6,0},{7,1},{8,2},{9,3},... | collective-permute-start | bytes 798728 | tf_op jit(solution)/shard_map/ppermute | solution.py:373
  27.9 23.3 %collective-permute-start.3 = (bf16[1040,128]{1,0:T(8,128)(2,1)S(1)}, bf16[1040,128]{1,0:T(8,128)(2,1)S(1)}, u32[]{:S(2)}, u32[]{:S(2)}) collective-permute-start(bf16[1040,128]{1,0:T(8,128)(2,1)S(1)} %get-tuple-element.73), channel_id=1, source_target_pairs={{0,59},{1,60},{2,61},{3,62},{4,63},{5,0},{6,1},{7,2},{8,3},{9,4},{... | collective-permute-start | bytes 798728 | tf_op jit(solution)/shard_map/ppermute | solution.py:373
  34.4 20.7 %collective-permute-start.4 = (bf16[1040,128]{1,0:T(8,128)(2,1)S(1)}, bf16[1040,128]{1,0:T(8,128)(2,1)S(1)}, u32[]{:S(2)}, u32[]{:S(2)}) collective-permute-start(bf16[1040,128]{1,0:T(8,128)(2,1)S(1)} %get-tuple-element.74), channel_id=1, source_target_pairs={{0,60},{1,61},{2,62},{3,63},{4,0},{5,1},{6,2},{7,3},{8,4},{9,5},{1... | collective-permute-start | bytes 798728 | tf_op jit(solution)/shard_map/ppermute | solution.py:373
  42.1 13.0 %collective-permute-start.5 = (bf16[1040,128]{1,0:T(8,128)(2,1)S(1)}, bf16[1040,128]{1,0:T(8,128)(2,1)S(1)}, u32[]{:S(2)}, u32[]{:S(2)}) collective-permute-start(bf16[1040,128]{1,0:T(8,128)(2,1)S(1)} %get-tuple-element.75), channel_id=1, source_target_pairs={{0,61},{1,62},{2,63},{3,0},{4,1},{5,2},{6,3},{7,4},{8,5},{9,6},{10... | collective-permute-start | bytes 798728 | tf_op jit(solution)/shard_map/ppermute | solution.py:373
  42.2 18.0 %collective-permute-start.6 = (bf16[1040,128]{1,0:T(8,128)(2,1)S(1)}, bf16[1040,128]{1,0:T(8,128)(2,1)S(1)}, u32[]{:S(2)}, u32[]{:S(2)}) collective-permute-start(bf16[1040,128]{1,0:T(8,128)(2,1)S(1)} %get-tuple-element.88), channel_id=1, source_target_pairs={{0,62},{1,63},{2,0},{3,1},{4,2},{5,3},{6,4},{7,5},{8,6},{9,7},{10,... | collective-permute-start | bytes 798728 | tf_op jit(solution)/shard_map/ppermute | solution.py:373
  51.3 10.7 %collective-permute-start.7 = (bf16[1040,128]{1,0:T(8,128)(2,1)S(1)}, bf16[1040,128]{1,0:T(8,128)(2,1)S(1)}, u32[]{:S(2)}, u32[]{:S(2)}) collective-permute-start(bf16[1040,128]{1,0:T(8,128)(2,1)S(1)} %get-tuple-element.89), channel_id=1, source_target_pairs={{0,63},{1,0},{2,1},{3,2},{4,3},{5,4},{6,5},{7,6},{8,7},{9,8},{10,9... | collective-permute-start | bytes 798728 | tf_op jit(solution)/shard_map/ppermute | solution.py:373
  51.3 10.7 %collective-permute-start.8 = (bf16[1040,128]{1,0:T(8,128)(2,1)S(1)}, bf16[1040,128]{1,0:T(8,128)(2,1)S(1)}, u32[]{:S(2)}, u32[]{:S(2)}) collective-permute-start(bf16[1040,128]{1,0:T(8,128)(2,1)S(1)} %get-tuple-element.90), channel_id=1, source_target_pairs={{0,1},{1,2},{2,3},{3,4},{4,5},{5,6},{6,7},{7,8},{8,9},{9,10},{10,1... | collective-permute-start | bytes 798728 | tf_op jit(solution)/shard_map/ppermute | solution.py:373
  55.1 9.1 %collective-permute-start.9 = (bf16[1040,128]{1,0:T(8,128)(2,1)S(1)}, bf16[1040,128]{1,0:T(8,128)(2,1)S(1)}, u32[]{:S(2)}, u32[]{:S(2)}) collective-permute-start(bf16[1040,128]{1,0:T(8,128)(2,1)S(1)} %get-tuple-element.91), channel_id=1, source_target_pairs={{0,2},{1,3},{2,4},{3,5},{4,6},{5,7},{6,8},{7,9},{8,10},{9,11},{10,... | collective-permute-start | bytes 798728 | tf_op jit(solution)/shard_map/ppermute | solution.py:373
  71.8 12.9 %collective-permute-start.15 = (s16[2064,128]{1,0:T(8,128)(2,1)S(1)}, s16[2064,128]{1,0:T(8,128)(2,1)S(1)}, u32[]{:S(2)}, u32[]{:S(2)}) collective-permute-start(s16[2064,128]{1,0:T(8,128)(2,1)S(1)} %get-tuple-element.96), channel_id=1, source_target_pairs={{1,0},{2,1},{3,2},{4,3},{5,4},{6,5},{7,6},{8,7},{9,8},{10,9},{11,1... | collective-permute-start | bytes 1585160 | tf_op jit(solution)/shard_map/ppermute | solution.py:351
  73.7 14.5 %collective-permute-start.13 = (s16[2064,128]{1,0:T(8,128)(2,1)S(1)}, s16[2064,128]{1,0:T(8,128)(2,1)S(1)}, u32[]{:S(2)}, u32[]{:S(2)}) collective-permute-start(s16[2064,128]{1,0:T(8,128)(2,1)S(1)} %get-tuple-element.93), channel_id=1, source_target_pairs={{0,1},{1,2},{2,3},{3,4},{4,5},{5,6},{6,7},{7,8},{8,9},{9,10},{10,1... | collective-permute-start | bytes 1585160 | tf_op jit(solution)/shard_map/ppermute | solution.py:351
  85.1 21.4 %collective-permute-start.16 = (s16[2064,128]{1,0:T(8,128)(2,1)S(1)}, s16[2064,128]{1,0:T(8,128)(2,1)S(1)}, u32[]{:S(2)}, u32[]{:S(2)}) collective-permute-start(s16[2064,128]{1,0:T(8,128)(2,1)S(1)} %join.5.own_ref), channel_id=1, source_target_pairs={{0,64},{64,0},{1,65},{65,1},{2,66},{66,2},{3,67},{67,3},{4,68},{68... | collective-permute-start | bytes 1585160 | tf_op jit(solution)/shard_map/ppermute | solution.py:359
  88.5 28.8 %collective-permute-start.14 = (s16[2064,128]{1,0:T(8,128)(2,1)S(1)}, s16[2064,128]{1,0:T(8,128)(2,1)S(1)}, u32[]{:S(2)}, u32[]{:S(2)}) collective-permute-start(s16[2064,128]{1,0:T(8,128)(2,1)S(1)} %join.4.own_ref), channel_id=1, source_target_pairs={{0,64},{64,0},{1,65},{65,1},{2,66},{66,2},{3,67},{67,3},{4,68},{68... | collective-permute-start | bytes 1585160 | tf_op jit(solution)/shard_map/ppermute | solution.py:359
  106.9 13.0 %collective-permute-start.17 = (bf16[16,128,128]{2,1,0:T(8,128)(2,1)S(1)}, bf16[16,128,128]{2,1,0:T(8,128)(2,1)S(1)}, u32[]{:S(2)}, u32[]{:S(2)}) collective-permute-start(bf16[16,128,128]{2,1,0:T(8,128)(2,1)S(1)} %get-tuple-element.98.refs_8_), channel_id=1, source_target_pairs={{0,1},{1,2},{2,3},{3,4},{4,5},{5,6},{6,7},{7,8},{8,9},{9,10},{10,1... | collective-permute-start | bytes 1572872 | tf_op jit(solution)/shard_map/ppermute | solution.py:351
  117.7 12.6 %collective-permute-start.18 = (bf16[16,128,128]{2,1,0:T(8,128)(2,1)S(1)}, bf16[16,128,128]{2,1,0:T(8,128)(2,1)S(1)}, u32[]{:S(2)}, u32[]{:S(2)}) collective-permute-start(bf16[16,128,128]{2,1,0:T(8,128)(2,1)S(1)} %get-tuple-element.99.refs_7_), channel_id=1, source_target_pairs={{1,0},{2,1},{3,2},{4,3},{5,4},{6,5},{7,6},{8,7},{9,8},{10,9},{11,1... | collective-permute-start | bytes 1572872 | tf_op jit(solution)/shard_map/ppermute | solution.py:351
  143.9 12.9 %collective-permute-start.21 = (s16[2064,128]{1,0:T(8,128)(2,1)S(1)}, s16[2064,128]{1,0:T(8,128)(2,1)S(1)}, u32[]{:S(2)}, u32[]{:S(2)}) collective-permute-start(s16[2064,128]{1,0:T(8,128)(2,1)S(1)} %get-tuple-element.104), channel_id=1, source_target_pairs={{1,0},{2,1},{3,2},{4,3},{5,4},{6,5},{7,6},{8,7},{9,8},{10,9},{11,1... | collective-permute-start | bytes 1585160 | tf_op jit(solution)/shard_map/ppermute | solution.py:351
  145.8 14.6 %collective-permute-start.19 = (s16[2064,128]{1,0:T(8,128)(2,1)S(1)}, s16[2064,128]{1,0:T(8,128)(2,1)S(1)}, u32[]{:S(2)}, u32[]{:S(2)}) collective-permute-start(s16[2064,128]{1,0:T(8,128)(2,1)S(1)} %get-tuple-element.102), channel_id=1, source_target_pairs={{0,1},{1,2},{2,3},{3,4},{4,5},{5,6},{6,7},{7,8},{8,9},{9,10},{10,1... | collective-permute-start | bytes 1585160 | tf_op jit(solution)/shard_map/ppermute | solution.py:351
  157.2 15.8 %collective-permute-start.22 = (s16[2064,128]{1,0:T(8,128)(2,1)S(1)}, s16[2064,128]{1,0:T(8,128)(2,1)S(1)}, u32[]{:S(2)}, u32[]{:S(2)}) collective-permute-start(s16[2064,128]{1,0:T(8,128)(2,1)S(1)} %join.7.refs_2_), channel_id=1, source_target_pairs={{0,64},{64,0},{1,65},{65,1},{2,66},{66,2},{3,67},{67,3},{4,68},{68... | collective-permute-start | bytes 1585160 | tf_op jit(solution)/shard_map/ppermute | solution.py:359
  160.7 20.2 %collective-permute-start.20 = (s16[2064,128]{1,0:T(8,128)(2,1)S(1)}, s16[2064,128]{1,0:T(8,128)(2,1)S(1)}, u32[]{:S(2)}, u32[]{:S(2)}) collective-permute-start(s16[2064,128]{1,0:T(8,128)(2,1)S(1)} %join.6.refs_0_), channel_id=1, source_target_pairs={{0,64},{64,0},{1,65},{65,1},{2,66},{66,2},{3,67},{67,3},{4,68},{68... | collective-permute-start | bytes 1585160 | tf_op jit(solution)/shard_map/ppermute | solution.py:359

commit v7 on v6

--- a/solution.py
+++ b/solution.py
@@ -11,6 +11,9 @@
 HALF = TAPS // 2
 BX = 32
 HX = 16
+CHUNKS = 4
+CX = BX // CHUNKS
+EDGES = HX // CX
 EX = BX + 2 * HX
 Y = 128
 Z = 128
@@ -173,13 +176,13 @@
 
 def write_payload(ref, planes, peak):
     shrink, power = column_codes(peak)
-    for p in range(HX):
+    for p in range(CX):
         ref[p * Y : (p + 1) * Y, :] = to_codes(planes[p] * shrink[p : p + 1])
-    ref[HX * Y :, :] = power.astype(jnp.int32).astype(I16)
+    ref[CX * Y :, :] = jnp.concatenate([power] * (16 // CX), axis=0).astype(jnp.int32).astype(I16)
 
 
 def payload_scales(ref):
-    return column_scales(from_codes(ref[HX * Y :, :]))
+    return column_scales(from_codes(ref[CX * Y :, :]))
 
 
 def payload_plane(ref, scales, p):
@@ -223,7 +226,7 @@
 
 
 def back_from(kx_ref, ky_ref, kz_ref, measured_ref, blurred_ref, half_ref, edge_ref, peak_ref, outs):
-    left_ref, low_ref, high_ref, right_ref = outs
+    owns = outs[EDGES : EDGES + CHUNKS]
 
     def along_zy(q, carry):
         v = q // (BX // TP)
@@ -251,16 +254,20 @@
             )
             got += [both[:, :Z], both[:, Z:]]
         planes = swapped(jnp.stack(got, axis=0))
-        for i, ref in enumerate((edge_ref.at[0], low_ref, high_ref, edge_ref.at[1])):
-            ref[:, pl.ds(y0, 8), :] = planes[i * HX : (i + 1) * HX]
+        for i, ref in enumerate(owns):
+            ref[:, pl.ds(y0, 8), :] = planes[HX + i * CX : HX + (i + 1) * CX]
+        edge_ref[0, :, pl.ds(y0, 8), :] = planes[:HX]
+        edge_ref[1, :, pl.ds(y0, 8), :] = planes[HX + BX :]
         for i, part in enumerate((planes[:HX], planes[HX + BX :])):
             peak_ref[i] = jnp.maximum(peak_ref[i], part)
         return carry
 
     peak_ref[...] = jnp.zeros(peak_ref.shape, F32)
     lax.fori_loop(0, Y // 8, along_x, 0, unroll=UNROLL)
-    for i, ref in enumerate((left_ref, right_ref)):
-        write_payload(ref, edge_ref.at[i], jnp.max(peak_ref[i], axis=1))
+    for i, refs in enumerate((outs[:EDGES], outs[EDGES + CHUNKS :])):
+        for c, ref in enumerate(refs):
+            part = pl.ds(c * CX, CX)
+            write_payload(ref, edge_ref.at[i, part], jnp.max(peak_ref[i, part], axis=1))
 
 
 def first_blur_kernel(kx_ref, ky_ref, kz_ref, *refs):
@@ -279,10 +286,8 @@
 
 
 def sweep_kernel(*refs):
-    fwd, back, parts = refs[0:3], refs[3:6], refs[6:10]
-    measured_ref = refs[10]
-    outs = refs[11:15]
-    half_ref, edge_ref, peak_ref, blurred_ref = refs[15:]
+    fwd, back, parts = refs[0:3], refs[3:6], refs[6 : 6 + EX // CX]
+    measured_ref, *outs, half_ref, edge_ref, peak_ref, blurred_ref = refs[6 + EX // CX :]
     blur_into(*fwd, parts, half_ref, blurred_ref)
     back_from(*back, measured_ref, blurred_ref, half_ref, edge_ref, peak_ref, outs)
 
@@ -290,7 +295,7 @@
 def join_kernel(own_ref, edge_ref, out_ref, sum_ref):
     scales = payload_scales(edge_ref)
     peaks = []
-    for p in range(HX):
+    for p in range(CX):
         plane = own_ref[p] + payload_plane(edge_ref, scales, p)
         sum_ref[p] = plane
         peaks.append(jnp.max(plane, axis=0, keepdims=True))
@@ -299,7 +304,7 @@
 
 def update_planes(view_count, before_ref, own_ref, other_ref, out_refs):
     own, other = payload_scales(own_ref), payload_scales(other_ref)
-    for p in range(HX):
+    for p in range(CX):
         total = payload_plane(own_ref, own, p) + payload_plane(other_ref, other, p)
         plane = before_ref[p] * total * (1.0 / view_count)
         for ref in out_refs:
@@ -310,19 +315,19 @@
     update_planes(view_count, before_ref, own_ref, other_ref, out_refs)
 
 
-def last_kernel(view_count, low_ref, high_ref, *refs):
-    *payloads, out_ref = refs
-    for i, before_ref in enumerate((low_ref, high_ref)):
-        own_ref, other_ref = payloads[2 * i : 2 * i + 2]
-        update_planes(view_count, before_ref, own_ref, other_ref, (out_ref.at[pl.ds(i * HX, HX)],))
+def last_kernel(view_count, *refs):
+    *refs, out_ref = refs
+    for i in range(CHUNKS):
+        own_ref, other_ref = refs[CHUNKS + 2 * i : CHUNKS + 2 * i + 2]
+        update_planes(view_count, refs[i], own_ref, other_ref, (out_ref.at[pl.ds(i * CX, CX)],))
 
 
 VM = pl.BlockSpec(memory_space=pltpu.VMEM)
 BLURRED = (VIEWS_DEV * BX // TP, TROWS, Z)
 HALF_SHAPE = (VIEWS_DEV * BX, Y, Z)
-PAYLOAD = jax.ShapeDtypeStruct((HX * Y + HX, Z), I16)
-OWN = jax.ShapeDtypeStruct((HX, Y, Z), F32)
-CONTRIB = [PAYLOAD, OWN, OWN, PAYLOAD]
+PAYLOAD = jax.ShapeDtypeStruct((CX * Y + 16, Z), I16)
+OWN = jax.ShapeDtypeStruct((CX, Y, Z), F32)
+CONTRIB = [*[PAYLOAD] * EDGES, *[OWN] * CHUNKS, *[PAYLOAD] * EDGES]
 BLUR_SCRATCH = [pltpu.VMEM(HALF_SHAPE, F32)]
 BACK_SCRATCH = [
     pltpu.VMEM(HALF_SHAPE, F32),
@@ -344,17 +349,24 @@
     )(*operands)
 
 
-def neighbours(low, high):
+def to_right(shard):
     size = lax.axis_size("block")
-    up = [(i, i + 1) for i in range(size - 1)]
-    down = [(j, i) for i, j in up]
-    return lax.ppermute(high, "block", up), lax.ppermute(low, "block", down)
+    return lax.ppermute(shard, "block", [(i, i + 1) for i in range(size - 1)])
+
+
+def to_left(shard):
+    size = lax.axis_size("block")
+    return lax.ppermute(shard, "block", [(i + 1, i) for i in range(size - 1)])
 
 
 def exchanged(contributions):
-    left, low, high, right = contributions
+    owns = contributions[EDGES : EDGES + CHUNKS]
+    arrived = [None] * CHUNKS
+    for c in range(EDGES):
+        arrived[c] = to_right(contributions[EDGES + CHUNKS + c])
+        arrived[CHUNKS - EDGES + c] = to_left(contributions[c])
     pairs = []
-    for own, edge in zip((low, high), neighbours(left, right)):
+    for own, edge in zip(owns, arrived):
         payload = call(join_kernel, "join", (own, edge), PAYLOAD, [pltpu.VMEM(OWN.shape, F32)], 1 << 20)
         pairs.append((payload, lax.ppermute(payload, "view", [(0, 1), (1, 0)])))
     return pairs
@@ -374,7 +386,7 @@
 
     planes = estimate.astype(BF16)
     low, high = planes[:HX], planes[HX:]
-    left, right = neighbours(low, high)
+    left, right = to_right(high), to_left(low)
     route(EARLY)
     fwd, back = blur_matrices(psf_taps)
     blurred = call(
@@ -397,24 +409,25 @@
         8 << 30,
         28,
     )
-    halves = []
+    chunks = []
     for i, (own, other) in enumerate(exchanged(contributions)):
-        halves.append(
+        chunks.append(
             call(
                 functools.partial(update_kernel, view_count),
                 "update",
-                (estimate[i * HX : (i + 1) * HX], own, other),
+                (estimate[i * CX : (i + 1) * CX], own, other),
                 [OWN, jax.ShapeDtypeStruct(OWN.shape, BF16)],
                 [],
                 1 << 20,
             )
         )
-    (low, low_planes), (high, high_planes) = halves
-    left, right = neighbours(low_planes, high_planes)
+    planes = [chunk[1] for chunk in chunks]
+    left = [to_right(part) for part in planes[CHUNKS - EDGES :]]
+    right = [to_left(part) for part in planes[:EDGES]]
     contributions = call(
         sweep_kernel,
         "sweep",
-        (*fwd, *back, left, low_planes, high_planes, right, measured),
+        (*fwd, *back, *left, *planes, *right, measured),
         CONTRIB,
         [*BACK_SCRATCH, pltpu.VMEM(BLURRED, F32)],
         14 << 30,
@@ -424,7 +437,7 @@
     return call(
         functools.partial(last_kernel, view_count),
         "last_update",
-        (low, high, *payloads),
+        (*[chunk[0] for chunk in chunks], *payloads),
         jax.ShapeDtypeStruct(estimate.shape, F32),
         [],
         1 << 20,

time: 183 us -> 190 us (1.038)
  starting transfers between devices: 58.4 us -> 77.6 us
  waiting for transfers between devices: 87.5 us -> 74.8 us
    ppermute x8 -> x14, starting transfers between devices: 23.9 us -> 37.6 us  [the longest x7 22.5 us: to_right(): return lax.ppermute(shard, 'block', [(i, i + 1) for i in range(size - 1)])]
    ppermute x8 -> x14, waiting for transfers between devices: 21 us -> 7.37 us  [the longest x7 7.35 us: to_left(): return lax.ppermute(shard, 'block', [(i + 1, i) for i in range(size - 1)])]
    ppermute x4 -> x8, starting transfers between devices: 7.95 us -> 13.4 us  [exchanged(): pairs.append((payload, lax.ppermute(payload, 'view', [(0, 1), (1, 0)])))]
    ppermute x4 -> x8, waiting for transfers between devices: 44.8 us -> 45.7 us  [exchanged(): pairs.append((payload, lax.ppermute(payload, 'view', [(0, 1), (1, 0)])))]
    pallas_call x11 -> x17, Pallas kernels: 32 us -> 32.1 us  [call(): pl.pallas_call(kernel, out_shape=out_shape, in_specs=[VM] * len(operands)...]
  transfers between devices with their start and end apart: 23 -> 33, of which waited for: 11 -> 14; matrix products, arithmetic and copies ran while one was open for 0% -> 0% of each run, Pallas kernels for 5% -> 5%
where the time goes in v7:
time: 190 us; the launch traced here: 189 us
  starting transfers between devices  77.6 us (41%)
  waiting for transfers between devices  74.8 us (39%)
  Pallas kernels  33.1 us (17%)
  local copies, waits for them, and re-layouts  3.39 us (2%)
    ppermute x8, waiting for transfers between devices, exchanged(): pairs.append((payload, lax.ppermute(payload, 'view', [(0, 1), (1, 0)])))  45.7 us
    pallas_call x17, Pallas kernels, call(): pl.pallas_call(kernel, out_shape=out_shape, in_specs=[VM] * len(operands)...  32.1 us
    ppermute x11, starting transfers between devices, route(): lax.ppermute(packed[by + SPAN // 2], 'block', perm)  26.6 us
    ppermute x7, starting transfers between devices, to_right(): return lax.ppermute(shard, 'block', [(i, i + 1) for i in range(size - 1)])  22.5 us
    ppermute x11, waiting for transfers between devices, route(): lax.ppermute(packed[by + SPAN // 2], 'block', perm)  21.7 us
    ppermute x7, starting transfers between devices, to_left(): return lax.ppermute(shard, 'block', [(i + 1, i) for i in range(size - 1)])  15 us
    ppermute x8, starting transfers between devices, exchanged(): pairs.append((payload, lax.ppermute(payload, 'view', [(0, 1), (1, 0)])))  13.4 us
    ppermute x7, waiting for transfers between devices, to_left(): return lax.ppermute(shard, 'block', [(i + 1, i) for i in range(size - 1)])  7.35 us
  transfers between devices with their start and end apart: 33, of which 14 were waited for; matrix products, arithmetic and copies ran while one was open for 0% of the time, Pallas kernels for 5%

profile of v7, /device:TPU:97, one launch (start us, length us, event | category | flops | bytes accessed | tf_op | source)
XLA Modules:
  0.0 189.3 jit_solution(2792037446352473366)
XLA Ops:
  0.0 0.8 copy.6
  0.8 1.9 copy-done
  2.7 1.1 pack_tiles.1
  3.7 0.5 copy-done.2
  4.2 0.2 convert_element_type.3
  4.5 2.3 %collective-permute-start = (bf16[16,128,128]{2,1,0:T(8,128)(2,1)S(1)}, bf16[16,128,128]{2,1,0:T(8,128)(2,1)S(1)}, u32[]{:S(2)}, u32[]{:S(2)}) collective-permute-start(bf16[16,128,128]{2,1,0:T(8,128)(2,1)S(1)} %get-tuple-element.134.refs_2_), channel_id=1, source_target_pairs={{0,1},{1,2},{2,3},{3,4},{4,5},{5,6},{6,7},{7,8},{8,9},{9,10},{10,1... | collective-permute-start | bytes 1572872 | tf_op jit(solution)/shard_map/ppermute | solution.py:354
  6.8 2.2 %collective-permute-start.1 = (bf16[16,128,128]{2,1,0:T(8,128)(2,1)S(1)}, bf16[16,128,128]{2,1,0:T(8,128)(2,1)S(1)}, u32[]{:S(2)}, u32[]{:S(2)}) collective-permute-start(bf16[16,128,128]{2,1,0:T(8,128)(2,1)S(1)} %get-tuple-element.133.refs_1_), channel_id=1, source_target_pairs={{1,0},{2,1},{3,2},{4,3},{5,4},{6,5},{7,6},{8,7},{9,8},{10,9},{11,1... | collective-permute-start | bytes 1572872 | tf_op jit(solution)/shard_map/ppermute | solution.py:359
  9.0 2.9 %collective-permute-start.10 = (bf16[1040,128]{1,0:T(8,128)(2,1)S(1)}, bf16[1040,128]{1,0:T(8,128)(2,1)S(1)}, u32[]{:S(2)}, u32[]{:S(2)}) collective-permute-start(bf16[1040,128]{1,0:T(8,128)(2,1)S(1)} %get-tuple-element.93), channel_id=1, source_target_pairs={{0,3},{1,4},{2,5},{3,6},{4,7},{5,8},{6,9},{7,10},{8,11},{9,12},{10... | collective-permute-start | bytes 798728 | tf_op jit(solution)/shard_map/ppermute | solution.py:385
  11.9 2.7 %collective-permute-start.11 = (bf16[1040,128]{1,0:T(8,128)(2,1)S(1)}, bf16[1040,128]{1,0:T(8,128)(2,1)S(1)}, u32[]{:S(2)}, u32[]{:S(2)}) collective-permute-start(bf16[1040,128]{1,0:T(8,128)(2,1)S(1)} %get-tuple-element.94), channel_id=1, source_target_pairs={{0,4},{1,5},{2,6},{3,7},{4,8},{5,9},{6,10},{7,11},{8,12},{9,13},{1... | collective-permute-start | bytes 798728 | tf_op jit(solution)/shard_map/ppermute | solution.py:385
  14.6 0.7 prepare.1
  15.3 12.6 %collective-permute-done.10.refs_9_ = bf16[1040,128]{1,0:T(8,128)(2,1)S(1)} collective-permute-done((bf16[1040,128]{1,0:T(8,128)(2,1)S(1)}, bf16[1040,128]{1,0:T(8,128)(2,1)S(1)}, u32[]{:S(2)}, u32[]{:S(2)}) %collective-permute-start.10) | collective-permute-done | bytes 266272 | tf_op jit(solution)/shard_map/ppermute | solution.py:385
  27.9 6.5 %collective-permute-start.3 = (bf16[1040,128]{1,0:T(8,128)(2,1)S(1)}, bf16[1040,128]{1,0:T(8,128)(2,1)S(1)}, u32[]{:S(2)}, u32[]{:S(2)}) collective-permute-start(bf16[1040,128]{1,0:T(8,128)(2,1)S(1)} %get-tuple-element.85), channel_id=1, source_target_pairs={{0,59},{1,60},{2,61},{3,62},{4,63},{5,0},{6,1},{7,2},{8,3},{9,4},{... | collective-permute-start | bytes 798728 | tf_op jit(solution)/shard_map/ppermute | solution.py:385
  34.4 1.6 collective-permute-start.4
  36.0 6.1 %first_blur.1.blurred_ref = f32[24,512,128]{2,1,0:T(8,128)S(1)} custom-call(bf16[96,64]{1,0:T(8,128)(2,1)S(1)} %get-tuple-element.96.kx_ref.refs_0_, bf16[3,128,128]{2,1,0:T(8,128)(2,1)S(1)} %get-tuple-element.97.ky_ref.refs_1_, bf16[3,128,128]{2,1,0:T(8,128)(2,1)S(1)} %get-tuple-element.98.kz_ref.refs_2_, ...), custom_call_target="tpu_custom_call" | custom-call | flops 6442450944 | bytes 12582912 | tf_op jit(solution)/shard_map/first_blur/pallas_call | solution.py:340
  42.2 9.0 %collective-permute-start.6 = (bf16[1040,128]{1,0:T(8,128)(2,1)S(1)}, bf16[1040,128]{1,0:T(8,128)(2,1)S(1)}, u32[]{:S(2)}, u32[]{:S(2)}) collective-permute-start(bf16[1040,128]{1,0:T(8,128)(2,1)S(1)} %get-tuple-element.100), channel_id=1, source_target_pairs={{0,62},{1,63},{2,0},{3,1},{4,2},{5,3},{6,4},{7,5},{8,6},{9,7},{10,... | collective-permute-start | bytes 798728 | tf_op jit(solution)/shard_map/ppermute | solution.py:385
  51.3 3.9 %collective-permute-start.8 = (bf16[1040,128]{1,0:T(8,128)(2,1)S(1)}, bf16[1040,128]{1,0:T(8,128)(2,1)S(1)}, u32[]{:S(2)}, u32[]{:S(2)}) collective-permute-start(bf16[1040,128]{1,0:T(8,128)(2,1)S(1)} %get-tuple-element.102), channel_id=1, source_target_pairs={{0,1},{1,2},{2,3},{3,4},{4,5},{5,6},{6,7},{7,8},{8,9},{9,10},{10,1... | collective-permute-start | bytes 798728 | tf_op jit(solution)/shard_map/ppermute | solution.py:385
  55.1 5.1 %collective-permute-done.6.refs_4_ = bf16[1040,128]{1,0:T(8,128)(2,1)S(1)} collective-permute-done((bf16[1040,128]{1,0:T(8,128)(2,1)S(1)}, bf16[1040,128]{1,0:T(8,128)(2,1)S(1)}, u32[]{:S(2)}, u32[]{:S(2)}) %collective-permute-start.6) | collective-permute-done | bytes 266272 | tf_op jit(solution)/shard_map/ppermute | solution.py:385
  60.2 1.7 collective-permute-done.7.refs_5_
  61.9 2.3 %collective-permute-done.9.refs_8_ = bf16[1040,128]{1,0:T(8,128)(2,1)S(1)} collective-permute-done((bf16[1040,128]{1,0:T(8,128)(2,1)S(1)}, bf16[1040,128]{1,0:T(8,128)(2,1)S(1)}, u32[]{:S(2)}, u32[]{:S(2)}) %collective-permute-start.9) | collective-permute-done | bytes 266272 | tf_op jit(solution)/shard_map/ppermute | solution.py:385
  64.2 7.6 %first_back.1 = (s16[1040,128]{1,0:T(8,128)(2,1)S(1)}, s16[1040,128]{1,0:T(8,128)(2,1)S(1)}, f32[8,128,128]{2,1,0:T(8,128)S(1)}, f32[8,128,128]{2,1,0:T(8,128)S(...) custom-call(bf16[64,192]{1,0:T(8,128)(2,1)S(1)} %get-tuple-element.8, ...), custom_call_target="tpu_custom_call" | custom-call | flops 8589934592 | bytes 12582912 | tf_op jit(solution)/shard_map/first_back/pallas_call | solution.py:340
  71.8 1.9 %collective-permute-start.19 = (s16[1040,128]{1,0:T(8,128)(2,1)S(1)}, s16[1040,128]{1,0:T(8,128)(2,1)S(1)}, u32[]{:S(2)}, u32[]{:S(2)}) collective-permute-start(s16[1040,128]{1,0:T(8,128)(2,1)S(1)} %get-tuple-element.114), channel_id=1, source_target_pairs={{1,0},{2,1},{3,2},{4,3},{5,4},{6,5},{7,6},{8,7},{9,8},{10,9},{11,1... | collective-permute-start | bytes 798728 | tf_op jit(solution)/shard_map/ppermute | solution.py:359
  73.7 1.9 %collective-permute-start.17 = (s16[1040,128]{1,0:T(8,128)(2,1)S(1)}, s16[1040,128]{1,0:T(8,128)(2,1)S(1)}, u32[]{:S(2)}, u32[]{:S(2)}) collective-permute-start(s16[1040,128]{1,0:T(8,128)(2,1)S(1)} %get-tuple-element.111), channel_id=1, source_target_pairs={{1,0},{2,1},{3,2},{4,3},{5,4},{6,5},{7,6},{8,7},{9,8},{10,9},{11,1... | collective-permute-start | bytes 798728 | tf_op jit(solution)/shard_map/ppermute | solution.py:359
  75.7 5.8 %collective-permute-start.15 = (s16[1040,128]{1,0:T(8,128)(2,1)S(1)}, s16[1040,128]{1,0:T(8,128)(2,1)S(1)}, u32[]{:S(2)}, u32[]{:S(2)}) collective-permute-start(s16[1040,128]{1,0:T(8,128)(2,1)S(1)} %get-tuple-element.108), channel_id=1, source_target_pairs={{0,1},{1,2},{2,3},{3,4},{4,5},{5,6},{6,7},{7,8},{8,9},{9,10},{10,1... | collective-permute-start | bytes 798728 | tf_op jit(solution)/shard_map/ppermute | solution.py:354
  81.4 2.5 %collective-permute-start.13 = (s16[1040,128]{1,0:T(8,128)(2,1)S(1)}, s16[1040,128]{1,0:T(8,128)(2,1)S(1)}, u32[]{:S(2)}, u32[]{:S(2)}) collective-permute-start(s16[1040,128]{1,0:T(8,128)(2,1)S(1)} %get-tuple-element.105), channel_id=1, source_target_pairs={{0,1},{1,2},{2,3},{3,4},{4,5},{5,6},{6,7},{7,8},{8,9},{9,10},{10,1... | collective-permute-start | bytes 798728 | tf_op jit(solution)/shard_map/ppermute | solution.py:354
  83.9 0.2 join.11.own_ref
  84.1 3.4 %collective-permute-start.20 = (s16[1040,128]{1,0:T(8,128)(2,1)S(1)}, s16[1040,128]{1,0:T(8,128)(2,1)S(1)}, u32[]{:S(2)}, u32[]{:S(2)}) collective-permute-start(s16[1040,128]{1,0:T(8,128)(2,1)S(1)} %join.11.own_ref), channel_id=1, source_target_pairs={{0,64},{64,0},{1,65},{65,1},{2,66},{66,2},{3,67},{67,3},{4,68},{68... | collective-permute-start | bytes 798728 | tf_op jit(solution)/shard_map/ppermute | solution.py:371
  87.5 0.2 join.10.own_ref
  87.7 0.4 collective-permute-start.18
  88.1 0.2 join.9.own_ref
  88.3 2.7 %collective-permute-start.16 = (s16[1040,128]{1,0:T(8,128)(2,1)S(1)}, s16[1040,128]{1,0:T(8,128)(2,1)S(1)}, u32[]{:S(2)}, u32[]{:S(2)}) collective-permute-start(s16[1040,128]{1,0:T(8,128)(2,1)S(1)} %join.9.own_ref), channel_id=1, source_target_pairs={{0,64},{64,0},{1,65},{65,1},{2,66},{66,2},{3,67},{67,3},{4,68},{68... | collective-permute-start | bytes 798728 | tf_op jit(solution)/shard_map/ppermute | solution.py:371
  91.0 0.2 join.8.own_ref
  91.2 0.4 collective-permute-start.14
  91.7 8.3 %collective-permute-done.20.other_ref = s16[1040,128]{1,0:T(8,128)(2,1)S(1)} collective-permute-done((s16[1040,128]{1,0:T(8,128)(2,1)S(1)}, s16[1040,128]{1,0:T(8,128)(2,1)S(1)}, u32[]{:S(2)}, u32[]{:S(2)}) %collective-permute-start.20) | collective-permute-done | bytes 266272 | tf_op jit(solution)/shard_map/ppermute | solution.py:371
  100.0 0.2 update.7
  100.2 1.9 %collective-permute-start.22 = (bf16[8,128,128]{2,1,0:T(8,128)(2,1)S(1)}, bf16[8,128,128]{2,1,0:T(8,128)(2,1)S(1)}, u32[]{:S(2)}, u32[]{:S(2)}) collective-permute-start(bf16[8,128,128]{2,1,0:T(8,128)(2,1)S(1)} %get-tuple-element.117.refs_11_), channel_id=1, source_target_pairs={{0,1},{1,2},{2,3},{3,4},{4,5},{5,6},{6,7},{7,8},{8,9},{9,10},{10,1... | collective-permute-start | bytes 786440 | tf_op jit(solution)/shard_map/ppermute | solution.py:354
  102.1 3.6 %collective-permute-done.18.other_ref = s16[1040,128]{1,0:T(8,128)(2,1)S(1)} collective-permute-done((s16[1040,128]{1,0:T(8,128)(2,1)S(1)}, s16[1040,128]{1,0:T(8,128)(2,1)S(1)}, u32[]{:S(2)}, u32[]{:S(2)}) %collective-permute-start.18) | collective-permute-done | bytes 266272 | tf_op jit(solution)/shard_map/ppermute | solution.py:371
  105.7 0.2 update.6
  105.9 1.9 %collective-permute-start.21 = (bf16[8,128,128]{2,1,0:T(8,128)(2,1)S(1)}, bf16[8,128,128]{2,1,0:T(8,128)(2,1)S(1)}, u32[]{:S(2)}, u32[]{:S(2)}) collective-permute-start(bf16[8,128,128]{2,1,0:T(8,128)(2,1)S(1)} %get-tuple-element.116.refs_10_), channel_id=1, source_target_pairs={{0,1},{1,2},{2,3},{3,4},{4,5},{5,6},{6,7},{7,8},{8,9},{9,10},{10,1... | collective-permute-start | bytes 786440 | tf_op jit(solution)/shard_map/ppermute | solution.py:354
  107.9 9.2 %collective-permute-done.16.other_ref = s16[1040,128]{1,0:T(8,128)(2,1)S(1)} collective-permute-done((s16[1040,128]{1,0:T(8,128)(2,1)S(1)}, s16[1040,128]{1,0:T(8,128)(2,1)S(1)}, u32[]{:S(2)}, u32[]{:S(2)}) %collective-permute-start.16) | collective-permute-done | bytes 266272 | tf_op jit(solution)/shard_map/ppermute | solution.py:371
  117.1 0.2 update.5
  117.2 2.7 %collective-permute-start.24 = (bf16[8,128,128]{2,1,0:T(8,128)(2,1)S(1)}, bf16[8,128,128]{2,1,0:T(8,128)(2,1)S(1)}, u32[]{:S(2)}, u32[]{:S(2)}) collective-permute-start(bf16[8,128,128]{2,1,0:T(8,128)(2,1)S(1)} %get-tuple-element.119.refs_9_), channel_id=1, source_target_pairs={{1,0},{2,1},{3,2},{4,3},{5,4},{6,5},{7,6},{8,7},{9,8},{10,9},{11,1... | collective-permute-start | bytes 786440 | tf_op jit(solution)/shard_map/ppermute | solution.py:359
  120.0 2.8 %collective-permute-done.14.other_ref = s16[1040,128]{1,0:T(8,128)(2,1)S(1)} collective-permute-done((s16[1040,128]{1,0:T(8,128)(2,1)S(1)}, s16[1040,128]{1,0:T(8,128)(2,1)S(1)}, u32[]{:S(2)}, u32[]{:S(2)}) %collective-permute-start.14) | collective-permute-done | bytes 266272 | tf_op jit(solution)/shard_map/ppermute | solution.py:371
  122.8 0.2 update.4
  122.9 2.4 %collective-permute-start.23 = (bf16[8,128,128]{2,1,0:T(8,128)(2,1)S(1)}, bf16[8,128,128]{2,1,0:T(8,128)(2,1)S(1)}, u32[]{:S(2)}, u32[]{:S(2)}) collective-permute-start(bf16[8,128,128]{2,1,0:T(8,128)(2,1)S(1)} %get-tuple-element.118.refs_8_), channel_id=1, source_target_pairs={{1,0},{2,1},{3,2},{4,3},{5,4},{6,5},{7,6},{8,7},{9,8},{10,9},{11,1... | collective-permute-start | bytes 786440 | tf_op jit(solution)/shard_map/ppermute | solution.py:359
  125.4 1.6 collective-permute-done.24.refs_13_
  127.0 5.7 %collective-permute-done.23.refs_12_ = bf16[8,128,128]{2,1,0:T(8,128)(2,1)S(1)} collective-permute-done((bf16[8,128,128]{2,1,0:T(8,128)(2,1)S(1)}, bf16[8,128,128]{2,1,0:T(8,128)(2,1)S(1)}, u32[]{:S(2)}, u32[]{:S(2)}) %collective-permute-start.23) | collective-permute-done | bytes 262176 | tf_op jit(solution)/shard_map/ppermute | solution.py:359
  132.7 13.4 %sweep.1 = (s16[1040,128]{1,0:T(8,128)(2,1)S(1)}, s16[1040,128]{1,0:T(8,128)(2,1)S(1)}, f32[8,128,128]{2,1,0:T(8,128)S(1)}, f32[8,128,128]{2,1,0:T(8,128)S(1)}, ...) custom-call(bf16[96,64]{1,0:T(8,128)(2,1)S(1)} %get-tuple-element.96, ...), custom_call_target="tpu_custom_call" | custom-call | flops 15032385536 | bytes 12582912 | tf_op jit(solution)/shard_map/sweep/pallas_call | solution.py:340
  146.2 1.9 %collective-permute-start.31 = (s16[1040,128]{1,0:T(8,128)(2,1)S(1)}, s16[1040,128]{1,0:T(8,128)(2,1)S(1)}, u32[]{:S(2)}, u32[]{:S(2)}) collective-permute-start(s16[1040,128]{1,0:T(8,128)(2,1)S(1)} %get-tuple-element.128), channel_id=1, source_target_pairs={{1,0},{2,1},{3,2},{4,3},{5,4},{6,5},{7,6},{8,7},{9,8},{10,9},{11,1... | collective-permute-start | bytes 798728 | tf_op jit(solution)/shard_map/ppermute | solution.py:359
  148.1 1.9 %collective-permute-start.29 = (s16[1040,128]{1,0:T(8,128)(2,1)S(1)}, s16[1040,128]{1,0:T(8,128)(2,1)S(1)}, u32[]{:S(2)}, u32[]{:S(2)}) collective-permute-start(s16[1040,128]{1,0:T(8,128)(2,1)S(1)} %get-tuple-element.126), channel_id=1, source_target_pairs={{1,0},{2,1},{3,2},{4,3},{5,4},{6,5},{7,6},{8,7},{9,8},{10,9},{11,1... | collective-permute-start | bytes 798728 | tf_op jit(solution)/shard_map/ppermute | solution.py:359
  150.0 5.8 %collective-permute-start.27 = (s16[1040,128]{1,0:T(8,128)(2,1)S(1)}, s16[1040,128]{1,0:T(8,128)(2,1)S(1)}, u32[]{:S(2)}, u32[]{:S(2)}) collective-permute-start(s16[1040,128]{1,0:T(8,128)(2,1)S(1)} %get-tuple-element.124), channel_id=1, source_target_pairs={{0,1},{1,2},{2,3},{3,4},{4,5},{5,6},{6,7},{7,8},{8,9},{9,10},{10,1... | collective-permute-start | bytes 798728 | tf_op jit(solution)/shard_map/ppermute | solution.py:354
  155.8 2.4 %collective-permute-start.25 = (s16[1040,128]{1,0:T(8,128)(2,1)S(1)}, s16[1040,128]{1,0:T(8,128)(2,1)S(1)}, u32[]{:S(2)}, u32[]{:S(2)}) collective-permute-start(s16[1040,128]{1,0:T(8,128)(2,1)S(1)} %get-tuple-element.122), channel_id=1, source_target_pairs={{0,1},{1,2},{2,3},{3,4},{4,5},{5,6},{6,7},{7,8},{8,9},{9,10},{10,1... | collective-permute-start | bytes 798728 | tf_op jit(solution)/shard_map/ppermute | solution.py:354
  158.2 0.2 join.15.refs_10_
  158.4 2.9 %collective-permute-start.32 = (s16[1040,128]{1,0:T(8,128)(2,1)S(1)}, s16[1040,128]{1,0:T(8,128)(2,1)S(1)}, u32[]{:S(2)}, u32[]{:S(2)}) collective-permute-start(s16[1040,128]{1,0:T(8,128)(2,1)S(1)} %join.15.refs_10_), channel_id=1, source_target_pairs={{0,64},{64,0},{1,65},{65,1},{2,66},{66,2},{3,67},{67,3},{4,68},{68... | collective-permute-start | bytes 798728 | tf_op jit(solution)/shard_map/ppermute | solution.py:371
  161.3 0.2 join.14.refs_8_
  161.4 0.5 collective-permute-start.30
  161.9 0.2 join.13.refs_6_
  162.1 2.6 %collective-permute-start.28 = (s16[1040,128]{1,0:T(8,128)(2,1)S(1)}, s16[1040,128]{1,0:T(8,128)(2,1)S(1)}, u32[]{:S(2)}, u32[]{:S(2)}) collective-permute-start(s16[1040,128]{1,0:T(8,128)(2,1)S(1)} %join.13.refs_6_), channel_id=1, source_target_pairs={{0,64},{64,0},{1,65},{65,1},{2,66},{66,2},{3,67},{67,3},{4,68},{68... | collective-permute-start | bytes 798728 | tf_op jit(solution)/shard_map/ppermute | solution.py:371
  164.8 0.2 join.12.refs_4_
  164.9 0.5 collective-permute-start.26
  165.4 4.8 %collective-permute-done.32.refs_11_ = s16[1040,128]{1,0:T(8,128)(2,1)S(1)} collective-permute-done((s16[1040,128]{1,0:T(8,128)(2,1)S(1)}, s16[1040,128]{1,0:T(8,128)(2,1)S(1)}, u32[]{:S(2)}, u32[]{:S(2)}) %collective-permute-start.32) | collective-permute-done | bytes 266272 | tf_op jit(solution)/shard_map/ppermute | solution.py:371
  170.2 5.7 %collective-permute-done.30.refs_9_ = s16[1040,128]{1,0:T(8,128)(2,1)S(1)} collective-permute-done((s16[1040,128]{1,0:T(8,128)(2,1)S(1)}, s16[1040,128]{1,0:T(8,128)(2,1)S(1)}, u32[]{:S(2)}, u32[]{:S(2)}) %collective-permute-start.30) | collective-permute-done | bytes 266272 | tf_op jit(solution)/shard_map/ppermute | solution.py:371
  175.9 5.7 %collective-permute-done.28.refs_7_ = s16[1040,128]{1,0:T(8,128)(2,1)S(1)} collective-permute-done((s16[1040,128]{1,0:T(8,128)(2,1)S(1)}, s16[1040,128]{1,0:T(8,128)(2,1)S(1)}, u32[]{:S(2)}, u32[]{:S(2)}) %collective-permute-start.28) | collective-permute-done | bytes 266272 | tf_op jit(solution)/shard_map/ppermute | solution.py:371
  181.6 5.7 %collective-permute-done.26.refs_5_ = s16[1040,128]{1,0:T(8,128)(2,1)S(1)} collective-permute-done((s16[1040,128]{1,0:T(8,128)(2,1)S(1)}, s16[1040,128]{1,0:T(8,128)(2,1)S(1)}, u32[]{:S(2)}, u32[]{:S(2)}) %collective-permute-start.26) | collective-permute-done | bytes 266272 | tf_op jit(solution)/shard_map/ppermute | solution.py:371
  187.3 2.0 %last_update.1 = f32[32,128,128]{2,1,0:T(8,128)} custom-call(f32[8,128,128]{2,1,0:T(8,128)S(1)} %get-tuple-element.106.refs_0_, f32[8,128,128]{2,1,0:T(8,128)S(1)} %get-tuple-element.109.refs_1_, f32[8,128,128]{2,1,0:T(8,128)S(1)} %get-tuple-element.112.refs_2_, f32[8,128,128]{2,1,0:T(8,128)S(1)} %get-tuple-element.115.refs_3_, ...), custom_call_target="tpu_custom_call" | custom-call | flops 1048576 | bytes 12582912 | tf_op jit(solution)/shard_map/last_update/pallas_call | solution.py:340
  (30 shorter events, 0.4 us)
Async XLA Ops:
  0.8 1.9 copy-start
  2.6 1.6 copy-start.2
  3.7 10.9 %copy-start.1 = (f32[3,3,31]{2,1,0:T(4,128)S(1)}, f32[3,3,31]{2,1,0:T(4,128)}, u32[]{:S(2)}) copy-start(f32[3,3,31]{2,1,0:T(4,128)} %psf_ref) | copy-start | bytes 3352
  4.5 23.4 %collective-permute-start = (bf16[16,128,128]{2,1,0:T(8,128)(2,1)S(1)}, bf16[16,128,128]{2,1,0:T(8,128)(2,1)S(1)}, u32[]{:S(2)}, u32[]{:S(2)}) collective-permute-start(bf16[16,128,128]{2,1,0:T(8,128)(2,1)S(1)} %get-tuple-element.134.refs_2_), channel_id=1, source_target_pairs={{0,1},{1,2},{2,3},{3,4},{4,5},{5,6},{6,7},{7,8},{8,9},{9,10},{10,1... | collective-permute-start | bytes 1572872 | tf_op jit(solution)/shard_map/ppermute | solution.py:354
  6.8 27.6 %collective-permute-start.1 = (bf16[16,128,128]{2,1,0:T(8,128)(2,1)S(1)}, bf16[16,128,128]{2,1,0:T(8,128)(2,1)S(1)}, u32[]{:S(2)}, u32[]{:S(2)}) collective-permute-start(bf16[16,128,128]{2,1,0:T(8,128)(2,1)S(1)} %get-tuple-element.133.refs_1_), channel_id=1, source_target_pairs={{1,0},{2,1},{3,2},{4,3},{5,4},{6,5},{7,6},{8,7},{9,8},{10,9},{11,1... | collective-permute-start | bytes 1572872 | tf_op jit(solution)/shard_map/ppermute | solution.py:359
  9.0 18.9 %collective-permute-start.10 = (bf16[1040,128]{1,0:T(8,128)(2,1)S(1)}, bf16[1040,128]{1,0:T(8,128)(2,1)S(1)}, u32[]{:S(2)}, u32[]{:S(2)}) collective-permute-start(bf16[1040,128]{1,0:T(8,128)(2,1)S(1)} %get-tuple-element.93), channel_id=1, source_target_pairs={{0,3},{1,4},{2,5},{3,6},{4,7},{5,8},{6,9},{7,10},{8,11},{9,12},{10... | collective-permute-start | bytes 798728 | tf_op jit(solution)/shard_map/ppermute | solution.py:385
  11.9 30.2 %collective-permute-start.11 = (bf16[1040,128]{1,0:T(8,128)(2,1)S(1)}, bf16[1040,128]{1,0:T(8,128)(2,1)S(1)}, u32[]{:S(2)}, u32[]{:S(2)}) collective-permute-start(bf16[1040,128]{1,0:T(8,128)(2,1)S(1)} %get-tuple-element.94), channel_id=1, source_target_pairs={{0,4},{1,5},{2,6},{3,7},{4,8},{5,9},{6,10},{7,11},{8,12},{9,13},{1... | collective-permute-start | bytes 798728 | tf_op jit(solution)/shard_map/ppermute | solution.py:385
  14.6 27.6 %collective-permute-start.12 = (bf16[1040,128]{1,0:T(8,128)(2,1)S(1)}, bf16[1040,128]{1,0:T(8,128)(2,1)S(1)}, u32[]{:S(2)}, u32[]{:S(2)}) collective-permute-start(bf16[1040,128]{1,0:T(8,128)(2,1)S(1)} %get-tuple-element.95), channel_id=1, source_target_pairs={{0,5},{1,6},{2,7},{3,8},{4,9},{5,10},{6,11},{7,12},{8,13},{9,14},{... | collective-permute-start | bytes 798728 | tf_op jit(solution)/shard_map/ppermute | solution.py:385
  27.9 23.3 %collective-permute-start.2 = (bf16[1040,128]{1,0:T(8,128)(2,1)S(1)}, bf16[1040,128]{1,0:T(8,128)(2,1)S(1)}, u32[]{:S(2)}, u32[]{:S(2)}) collective-permute-start(bf16[1040,128]{1,0:T(8,128)(2,1)S(1)} %get-tuple-element.84), channel_id=1, source_target_pairs={{0,58},{1,59},{2,60},{3,61},{4,62},{5,63},{6,0},{7,1},{8,2},{9,3},... | collective-permute-start | bytes 798728 | tf_op jit(solution)/shard_map/ppermute | solution.py:385
  27.9 23.3 %collective-permute-start.3 = (bf16[1040,128]{1,0:T(8,128)(2,1)S(1)}, bf16[1040,128]{1,0:T(8,128)(2,1)S(1)}, u32[]{:S(2)}, u32[]{:S(2)}) collective-permute-start(bf16[1040,128]{1,0:T(8,128)(2,1)S(1)} %get-tuple-element.85), channel_id=1, source_target_pairs={{0,59},{1,60},{2,61},{3,62},{4,63},{5,0},{6,1},{7,2},{8,3},{9,4},{... | collective-permute-start | bytes 798728 | tf_op jit(solution)/shard_map/ppermute | solution.py:385
  34.4 20.7 %collective-permute-start.4 = (bf16[1040,128]{1,0:T(8,128)(2,1)S(1)}, bf16[1040,128]{1,0:T(8,128)(2,1)S(1)}, u32[]{:S(2)}, u32[]{:S(2)}) collective-permute-start(bf16[1040,128]{1,0:T(8,128)(2,1)S(1)} %get-tuple-element.86), channel_id=1, source_target_pairs={{0,60},{1,61},{2,62},{3,63},{4,0},{5,1},{6,2},{7,3},{8,4},{9,5},{1... | collective-permute-start | bytes 798728 | tf_op jit(solution)/shard_map/ppermute | solution.py:385
  42.1 13.0 %collective-permute-start.5 = (bf16[1040,128]{1,0:T(8,128)(2,1)S(1)}, bf16[1040,128]{1,0:T(8,128)(2,1)S(1)}, u32[]{:S(2)}, u32[]{:S(2)}) collective-permute-start(bf16[1040,128]{1,0:T(8,128)(2,1)S(1)} %get-tuple-element.87), channel_id=1, source_target_pairs={{0,61},{1,62},{2,63},{3,0},{4,1},{5,2},{6,3},{7,4},{8,5},{9,6},{10... | collective-permute-start | bytes 798728 | tf_op jit(solution)/shard_map/ppermute | solution.py:385
  42.2 18.0 %collective-permute-start.6 = (bf16[1040,128]{1,0:T(8,128)(2,1)S(1)}, bf16[1040,128]{1,0:T(8,128)(2,1)S(1)}, u32[]{:S(2)}, u32[]{:S(2)}) collective-permute-start(bf16[1040,128]{1,0:T(8,128)(2,1)S(1)} %get-tuple-element.100), channel_id=1, source_target_pairs={{0,62},{1,63},{2,0},{3,1},{4,2},{5,3},{6,4},{7,5},{8,6},{9,7},{10,... | collective-permute-start | bytes 798728 | tf_op jit(solution)/shard_map/ppermute | solution.py:385
  51.3 10.6 %collective-permute-start.7 = (bf16[1040,128]{1,0:T(8,128)(2,1)S(1)}, bf16[1040,128]{1,0:T(8,128)(2,1)S(1)}, u32[]{:S(2)}, u32[]{:S(2)}) collective-permute-start(bf16[1040,128]{1,0:T(8,128)(2,1)S(1)} %get-tuple-element.101), channel_id=1, source_target_pairs={{0,63},{1,0},{2,1},{3,2},{4,3},{5,4},{6,5},{7,6},{8,7},{9,8},{10,9... | collective-permute-start | bytes 798728 | tf_op jit(solution)/shard_map/ppermute | solution.py:385
  51.3 10.6 %collective-permute-start.8 = (bf16[1040,128]{1,0:T(8,128)(2,1)S(1)}, bf16[1040,128]{1,0:T(8,128)(2,1)S(1)}, u32[]{:S(2)}, u32[]{:S(2)}) collective-permute-start(bf16[1040,128]{1,0:T(8,128)(2,1)S(1)} %get-tuple-element.102), channel_id=1, source_target_pairs={{0,1},{1,2},{2,3},{3,4},{4,5},{5,6},{6,7},{7,8},{8,9},{9,10},{10,1... | collective-permute-start | bytes 798728 | tf_op jit(solution)/shard_map/ppermute | solution.py:385
  55.1 9.1 %collective-permute-start.9 = (bf16[1040,128]{1,0:T(8,128)(2,1)S(1)}, bf16[1040,128]{1,0:T(8,128)(2,1)S(1)}, u32[]{:S(2)}, u32[]{:S(2)}) collective-permute-start(bf16[1040,128]{1,0:T(8,128)(2,1)S(1)} %get-tuple-element.103), channel_id=1, source_target_pairs={{0,2},{1,3},{2,4},{3,5},{4,6},{5,7},{6,8},{7,9},{8,10},{9,11},{10,... | collective-permute-start | bytes 798728 | tf_op jit(solution)/shard_map/ppermute | solution.py:385
  71.8 12.1 %collective-permute-start.19 = (s16[1040,128]{1,0:T(8,128)(2,1)S(1)}, s16[1040,128]{1,0:T(8,128)(2,1)S(1)}, u32[]{:S(2)}, u32[]{:S(2)}) collective-permute-start(s16[1040,128]{1,0:T(8,128)(2,1)S(1)} %get-tuple-element.114), channel_id=1, source_target_pairs={{1,0},{2,1},{3,2},{4,3},{5,4},{6,5},{7,6},{8,7},{9,8},{10,9},{11,1... | collective-permute-start | bytes 798728 | tf_op jit(solution)/shard_map/ppermute | solution.py:359
  73.7 13.8 %collective-permute-start.17 = (s16[1040,128]{1,0:T(8,128)(2,1)S(1)}, s16[1040,128]{1,0:T(8,128)(2,1)S(1)}, u32[]{:S(2)}, u32[]{:S(2)}) collective-permute-start(s16[1040,128]{1,0:T(8,128)(2,1)S(1)} %get-tuple-element.111), channel_id=1, source_target_pairs={{1,0},{2,1},{3,2},{4,3},{5,4},{6,5},{7,6},{8,7},{9,8},{10,9},{11,1... | collective-permute-start | bytes 798728 | tf_op jit(solution)/shard_map/ppermute | solution.py:359
  75.7 12.4 %collective-permute-start.15 = (s16[1040,128]{1,0:T(8,128)(2,1)S(1)}, s16[1040,128]{1,0:T(8,128)(2,1)S(1)}, u32[]{:S(2)}, u32[]{:S(2)}) collective-permute-start(s16[1040,128]{1,0:T(8,128)(2,1)S(1)} %get-tuple-element.108), channel_id=1, source_target_pairs={{0,1},{1,2},{2,3},{3,4},{4,5},{5,6},{6,7},{7,8},{8,9},{9,10},{10,1... | collective-permute-start | bytes 798728 | tf_op jit(solution)/shard_map/ppermute | solution.py:354
  81.4 9.6 %collective-permute-start.13 = (s16[1040,128]{1,0:T(8,128)(2,1)S(1)}, s16[1040,128]{1,0:T(8,128)(2,1)S(1)}, u32[]{:S(2)}, u32[]{:S(2)}) collective-permute-start(s16[1040,128]{1,0:T(8,128)(2,1)S(1)} %get-tuple-element.105), channel_id=1, source_target_pairs={{0,1},{1,2},{2,3},{3,4},{4,5},{5,6},{6,7},{7,8},{8,9},{9,10},{10,1... | collective-permute-start | bytes 798728 | tf_op jit(solution)/shard_map/ppermute | solution.py:354
  84.1 15.9 %collective-permute-start.20 = (s16[1040,128]{1,0:T(8,128)(2,1)S(1)}, s16[1040,128]{1,0:T(8,128)(2,1)S(1)}, u32[]{:S(2)}, u32[]{:S(2)}) collective-permute-start(s16[1040,128]{1,0:T(8,128)(2,1)S(1)} %join.11.own_ref), channel_id=1, source_target_pairs={{0,64},{64,0},{1,65},{65,1},{2,66},{66,2},{3,67},{67,3},{4,68},{68... | collective-permute-start | bytes 798728 | tf_op jit(solution)/shard_map/ppermute | solution.py:371
  87.7 18.1 %collective-permute-start.18 = (s16[1040,128]{1,0:T(8,128)(2,1)S(1)}, s16[1040,128]{1,0:T(8,128)(2,1)S(1)}, u32[]{:S(2)}, u32[]{:S(2)}) collective-permute-start(s16[1040,128]{1,0:T(8,128)(2,1)S(1)} %join.10.own_ref), channel_id=1, source_target_pairs={{0,64},{64,0},{1,65},{65,1},{2,66},{66,2},{3,67},{67,3},{4,68},{68... | collective-permute-start | bytes 798728 | tf_op jit(solution)/shard_map/ppermute | solution.py:371
  88.3 28.8 %collective-permute-start.16 = (s16[1040,128]{1,0:T(8,128)(2,1)S(1)}, s16[1040,128]{1,0:T(8,128)(2,1)S(1)}, u32[]{:S(2)}, u32[]{:S(2)}) collective-permute-start(s16[1040,128]{1,0:T(8,128)(2,1)S(1)} %join.9.own_ref), channel_id=1, source_target_pairs={{0,64},{64,0},{1,65},{65,1},{2,66},{66,2},{3,67},{67,3},{4,68},{68... | collective-permute-start | bytes 798728 | tf_op jit(solution)/shard_map/ppermute | solution.py:371
  91.2 31.6 %collective-permute-start.14 = (s16[1040,128]{1,0:T(8,128)(2,1)S(1)}, s16[1040,128]{1,0:T(8,128)(2,1)S(1)}, u32[]{:S(2)}, u32[]{:S(2)}) collective-permute-start(s16[1040,128]{1,0:T(8,128)(2,1)S(1)} %join.8.own_ref), channel_id=1, source_target_pairs={{0,64},{64,0},{1,65},{65,1},{2,66},{66,2},{3,67},{67,3},{4,68},{68... | collective-permute-start | bytes 798728 | tf_op jit(solution)/shard_map/ppermute | solution.py:371
  100.2 25.2 %collective-permute-start.22 = (bf16[8,128,128]{2,1,0:T(8,128)(2,1)S(1)}, bf16[8,128,128]{2,1,0:T(8,128)(2,1)S(1)}, u32[]{:S(2)}, u32[]{:S(2)}) collective-permute-start(bf16[8,128,128]{2,1,0:T(8,128)(2,1)S(1)} %get-tuple-element.117.refs_11_), channel_id=1, source_target_pairs={{0,1},{1,2},{2,3},{3,4},{4,5},{5,6},{6,7},{7,8},{8,9},{9,10},{10,1... | collective-permute-start | bytes 786440 | tf_op jit(solution)/shard_map/ppermute | solution.py:354
  105.9 19.5 %collective-permute-start.21 = (bf16[8,128,128]{2,1,0:T(8,128)(2,1)S(1)}, bf16[8,128,128]{2,1,0:T(8,128)(2,1)S(1)}, u32[]{:S(2)}, u32[]{:S(2)}) collective-permute-start(bf16[8,128,128]{2,1,0:T(8,128)(2,1)S(1)} %get-tuple-element.116.refs_10_), channel_id=1, source_target_pairs={{0,1},{1,2},{2,3},{3,4},{4,5},{5,6},{6,7},{7,8},{8,9},{9,10},{10,1... | collective-permute-start | bytes 786440 | tf_op jit(solution)/shard_map/ppermute | solution.py:354
  117.2 9.8 %collective-permute-start.24 = (bf16[8,128,128]{2,1,0:T(8,128)(2,1)S(1)}, bf16[8,128,128]{2,1,0:T(8,128)(2,1)S(1)}, u32[]{:S(2)}, u32[]{:S(2)}) collective-permute-start(bf16[8,128,128]{2,1,0:T(8,128)(2,1)S(1)} %get-tuple-element.119.refs_9_), channel_id=1, source_target_pairs={{1,0},{2,1},{3,2},{4,3},{5,4},{6,5},{7,6},{8,7},{9,8},{10,9},{11,1... | collective-permute-start | bytes 786440 | tf_op jit(solution)/shard_map/ppermute | solution.py:359
  122.9 9.8 %collective-permute-start.23 = (bf16[8,128,128]{2,1,0:T(8,128)(2,1)S(1)}, bf16[8,128,128]{2,1,0:T(8,128)(2,1)S(1)}, u32[]{:S(2)}, u32[]{:S(2)}) collective-permute-start(bf16[8,128,128]{2,1,0:T(8,128)(2,1)S(1)} %get-tuple-element.118.refs_8_), channel_id=1, source_target_pairs={{1,0},{2,1},{3,2},{4,3},{5,4},{6,5},{7,6},{8,7},{9,8},{10,9},{11,1... | collective-permute-start | bytes 786440 | tf_op jit(solution)/shard_map/ppermute | solution.py:359
  146.2 12.0 %collective-permute-start.31 = (s16[1040,128]{1,0:T(8,128)(2,1)S(1)}, s16[1040,128]{1,0:T(8,128)(2,1)S(1)}, u32[]{:S(2)}, u32[]{:S(2)}) collective-permute-start(s16[1040,128]{1,0:T(8,128)(2,1)S(1)} %get-tuple-element.128), channel_id=1, source_target_pairs={{1,0},{2,1},{3,2},{4,3},{5,4},{6,5},{7,6},{8,7},{9,8},{10,9},{11,1... | collective-permute-start | bytes 798728 | tf_op jit(solution)/shard_map/ppermute | solution.py:359
  148.1 13.2 %collective-permute-start.29 = (s16[1040,128]{1,0:T(8,128)(2,1)S(1)}, s16[1040,128]{1,0:T(8,128)(2,1)S(1)}, u32[]{:S(2)}, u32[]{:S(2)}) collective-permute-start(s16[1040,128]{1,0:T(8,128)(2,1)S(1)} %get-tuple-element.126), channel_id=1, source_target_pairs={{1,0},{2,1},{3,2},{4,3},{5,4},{6,5},{7,6},{8,7},{9,8},{10,9},{11,1... | collective-permute-start | bytes 798728 | tf_op jit(solution)/shard_map/ppermute | solution.py:359
  150.0 11.9 %collective-permute-start.27 = (s16[1040,128]{1,0:T(8,128)(2,1)S(1)}, s16[1040,128]{1,0:T(8,128)(2,1)S(1)}, u32[]{:S(2)}, u32[]{:S(2)}) collective-permute-start(s16[1040,128]{1,0:T(8,128)(2,1)S(1)} %get-tuple-element.124), channel_id=1, source_target_pairs={{0,1},{1,2},{2,3},{3,4},{4,5},{5,6},{6,7},{7,8},{8,9},{9,10},{10,1... | collective-permute-start | bytes 798728 | tf_op jit(solution)/shard_map/ppermute | solution.py:354
  155.8 9.0 %collective-permute-start.25 = (s16[1040,128]{1,0:T(8,128)(2,1)S(1)}, s16[1040,128]{1,0:T(8,128)(2,1)S(1)}, u32[]{:S(2)}, u32[]{:S(2)}) collective-permute-start(s16[1040,128]{1,0:T(8,128)(2,1)S(1)} %get-tuple-element.122), channel_id=1, source_target_pairs={{0,1},{1,2},{2,3},{3,4},{4,5},{5,6},{6,7},{7,8},{8,9},{9,10},{10,1... | collective-permute-start | bytes 798728 | tf_op jit(solution)/shard_map/ppermute | solution.py:354
  158.4 11.8 %collective-permute-start.32 = (s16[1040,128]{1,0:T(8,128)(2,1)S(1)}, s16[1040,128]{1,0:T(8,128)(2,1)S(1)}, u32[]{:S(2)}, u32[]{:S(2)}) collective-permute-start(s16[1040,128]{1,0:T(8,128)(2,1)S(1)} %join.15.refs_10_), channel_id=1, source_target_pairs={{0,64},{64,0},{1,65},{65,1},{2,66},{66,2},{3,67},{67,3},{4,68},{68... | collective-permute-start | bytes 798728 | tf_op jit(solution)/shard_map/ppermute | solution.py:371
  161.4 14.5 %collective-permute-start.30 = (s16[1040,128]{1,0:T(8,128)(2,1)S(1)}, s16[1040,128]{1,0:T(8,128)(2,1)S(1)}, u32[]{:S(2)}, u32[]{:S(2)}) collective-permute-start(s16[1040,128]{1,0:T(8,128)(2,1)S(1)} %join.14.refs_8_), channel_id=1, source_target_pairs={{0,64},{64,0},{1,65},{65,1},{2,66},{66,2},{3,67},{67,3},{4,68},{68... | collective-permute-start | bytes 798728 | tf_op jit(solution)/shard_map/ppermute | solution.py:371
  162.1 19.5 %collective-permute-start.28 = (s16[1040,128]{1,0:T(8,128)(2,1)S(1)}, s16[1040,128]{1,0:T(8,128)(2,1)S(1)}, u32[]{:S(2)}, u32[]{:S(2)}) collective-permute-start(s16[1040,128]{1,0:T(8,128)(2,1)S(1)} %join.13.refs_6_), channel_id=1, source_target_pairs={{0,64},{64,0},{1,65},{65,1},{2,66},{66,2},{3,67},{67,3},{4,68},{68... | collective-permute-start | bytes 798728 | tf_op jit(solution)/shard_map/ppermute | solution.py:371
  164.9 22.4 %collective-permute-start.26 = (s16[1040,128]{1,0:T(8,128)(2,1)S(1)}, s16[1040,128]{1,0:T(8,128)(2,1)S(1)}, u32[]{:S(2)}, u32[]{:S(2)}) collective-permute-start(s16[1040,128]{1,0:T(8,128)(2,1)S(1)} %join.12.refs_4_), channel_id=1, source_target_pairs={{0,64},{64,0},{1,65},{65,1},{2,66},{66,2},{3,67},{67,3},{4,68},{68... | collective-permute-start | bytes 798728 | tf_op jit(solution)/shard_map/ppermute | solution.py:371

commit v8 on v6

--- a/solution.py
+++ b/solution.py
@@ -28,7 +28,7 @@
 BF16 = jnp.bfloat16
 I16 = jnp.int16
 MIB = 1 << 20
-UNROLL = 4
+UNROLL = 12
 EARLY = (-6, 5, -5, 4, -4, 3, -3)
 LATE = (2, -2, 1, -1)
 
@@ -69,13 +69,13 @@
         ahead = [taps_ref[v * dims + d : v * dims + d + 1, :] for d in range(dims)]
         behind = [turned_ref[v * dims + d : v * dims + d + 1, :] for d in range(dims)]
         wide.append(toeplitz(ahead[0], BX, 1, 1, TAPS))
-        for ref, row in (
-            (fwd_y_ref, ahead[1]),
-            (back_y_ref, behind[1]),
-            (fwd_z_ref, behind[2]),
-            (back_z_ref, ahead[2]),
-        ):
+        for ref, row in ((fwd_y_ref, ahead[1]), (back_y_ref, behind[1])):
             ref[v] = toeplitz(row, LANES, -HALF, -HALF, HALF).astype(BF16)
+        for ref, row in ((fwd_z_ref, behind[2]), (back_z_ref, ahead[2])):
+            block = toeplitz(row, LANES, -HALF, -HALF, HALF).astype(BF16)
+            ref[v] = jnp.zeros(ref.shape[1:], BF16)
+            ref[v, :LANES, :LANES] = block
+            ref[v, LANES:, LANES:] = block
     along = jnp.concatenate(wide, axis=0)
     fwd_x_ref[...] = along[:, :EX].astype(BF16)
     full = jnp.concatenate([along, jnp.zeros((LANES - VIEWS_DEV * BX, LANES), F32)], axis=0)
@@ -85,13 +85,14 @@
 
 def blur_matrices(psf_taps):
     square = jax.ShapeDtypeStruct((VIEWS_DEV, LANES, LANES), BF16)
+    double = jax.ShapeDtypeStruct((VIEWS_DEV, 2 * LANES, 2 * LANES), BF16)
     shapes = [
         jax.ShapeDtypeStruct((VIEWS_DEV * BX, EX), BF16),
         square,
-        square,
+        double,
         jax.ShapeDtypeStruct((EX, 2 * VIEWS_DEV * BX), BF16),
         square,
-        square,
+        double,
     ]
     scratch = [pltpu.VMEM((LANES, LANES), F32)] * 2
     matrices = call(prepare_kernel, "prepare", (psf_taps,), shapes, scratch, 1 << 20)
@@ -194,6 +195,7 @@
     def along_x(t, carry):
         y0 = pl.multiple_of(t * SUB, SUB)
         data = jnp.concatenate([ref[:, pl.ds(y0, SUB), :] for ref in parts], axis=0).astype(F32)
+        planes = []
         for h in range(0, SUB, 8):
             rows = swapped(data[:, h : h + 8]).astype(BF16)
             outs = []
@@ -201,7 +203,8 @@
                 pair = jnp.concatenate([rows[j], rows[j + 1]], axis=1)
                 got = jnp.dot(kx_ref[...], pair, preferred_element_type=F32)
                 outs += [got[:, :Z], got[:, Z:]]
-            half_ref[:, pl.ds(y0 + h, 8), :] = swapped(jnp.stack(outs, axis=0))
+            planes.append(swapped(jnp.stack(outs, axis=0)))
+        half_ref[:, pl.ds(y0, SUB), :] = jnp.concatenate(planes, axis=1).astype(half_ref.dtype)
         return carry
 
     lax.fori_loop(0, Y // SUB, along_x, 0, unroll=2)
@@ -210,13 +213,12 @@
         v = q // (BX // TP)
         outs = []
         for i in range(0, TP, 2):
-            pair = jnp.concatenate(
-                [half_ref[q * TP + i + j].astype(BF16) for j in range(2)], axis=1
-            )
-            got = jnp.dot(ky_ref[v], pair, preferred_element_type=F32).astype(BF16)
-            outs += [got[:, :Z], got[:, Z:]]
-        rows = jnp.concatenate(outs, axis=0)
-        out_ref[q] = jnp.dot(rows, kz_ref[v], preferred_element_type=F32)
+            pair = jnp.concatenate([half_ref[q * TP + i + j].astype(BF16) for j in range(2)], axis=1)
+            outs.append(jnp.dot(ky_ref[v], pair, preferred_element_type=F32).astype(BF16))
+        got = jnp.dot(jnp.concatenate(outs, axis=0), kz_ref[v], preferred_element_type=F32)
+        for i in range(TP):
+            rows, lanes = i // 2 * Y, i % 2 * Z
+            out_ref[q, i * Y : (i + 1) * Y, :] = got[rows : rows + Y, lanes : lanes + Z]
         return carry
 
     lax.fori_loop(0, VIEWS_DEV * BX // TP, along_yz, 0, unroll=UNROLL)
@@ -228,9 +230,15 @@
     def along_zy(q, carry):
         v = q // (BX // TP)
         ratio = (measured_ref[q].astype(F32) / blurred_ref[q]).astype(BF16)
-        rows = jnp.dot(ratio, kz_ref[v], preferred_element_type=F32).astype(BF16)
+        pairs = [
+            jnp.concatenate([ratio[(i + j) * Y : (i + j + 1) * Y] for j in range(2)], axis=1)
+            for i in range(0, TP, 2)
+        ]
+        rows = jnp.dot(
+            jnp.concatenate(pairs, axis=0), kz_ref[v], preferred_element_type=F32
+        ).astype(BF16)
         for i in range(0, TP, 2):
-            pair = jnp.concatenate([rows[(i + j) * Y : (i + j + 1) * Y] for j in range(2)], axis=1)
+            pair = rows[i // 2 * Y : (i // 2 + 1) * Y]
             got = jnp.dot(ky_ref[v], pair, preferred_element_type=F32)
             for j in range(2):
                 half_ref[q * TP + i + j] = got[:, j * Z : (j + 1) * Z]
@@ -258,7 +266,7 @@
         return carry
 
     peak_ref[...] = jnp.zeros(peak_ref.shape, F32)
-    lax.fori_loop(0, Y // 8, along_x, 0, unroll=UNROLL)
+    lax.fori_loop(0, Y // 8, along_x, 0, unroll=8)
     for i, ref in enumerate((left_ref, right_ref)):
         write_payload(ref, edge_ref.at[i], jnp.max(peak_ref[i], axis=1))
 
@@ -323,7 +331,7 @@
 PAYLOAD = jax.ShapeDtypeStruct((HX * Y + HX, Z), I16)
 OWN = jax.ShapeDtypeStruct((HX, Y, Z), F32)
 CONTRIB = [PAYLOAD, OWN, OWN, PAYLOAD]
-BLUR_SCRATCH = [pltpu.VMEM(HALF_SHAPE, F32)]
+BLUR_SCRATCH = [pltpu.VMEM(HALF_SHAPE, BF16)]
 BACK_SCRATCH = [
     pltpu.VMEM(HALF_SHAPE, F32),
     pltpu.VMEM((2, HX, Y, Z), F32),
@@ -364,7 +372,6 @@
     view_count = psf_taps.shape[0] * lax.axis_size("view")
     blocks = lax.axis_size("block")
     packed = pack_tiles(view_tiles, tile_dest)
-    estimate, psf_taps, packed = lax.optimization_barrier((estimate, psf_taps, packed))
     arrived = list(packed)
 
     def route(steps):

time: 183 us -> 178 us (0.973)
  the two profiles are of different devices: /device:TPU:97 before, /device:TPU:15 now
where the time goes in v8:
time: 178 us
  waiting for transfers between devices  94 us (53%)
  starting transfers between devices  49.4 us (28%)
  Pallas kernels  31.2 us (18%)
  other arithmetic  1.9 us (1%)
    ppermute x4, waiting for transfers between devices, exchanged(): pairs.append((payload, lax.ppermute(payload, 'view', [(0, 1), (1, 0)])))  47.7 us
    pallas_call x11, Pallas kernels, call(): pl.pallas_call(kernel, out_shape=out_shape, in_specs=[VM] * len(operands)...  30.1 us
    ppermute x11, waiting for transfers between devices, route(): lax.ppermute(packed[by + SPAN // 2], 'block', perm)  27.8 us
    ppermute x11, starting transfers between devices, route(): lax.ppermute(packed[by + SPAN // 2], 'block', perm)  21.7 us
    ppermute x8, starting transfers between devices, neighbours(): return (lax.ppermute(high, 'block', up), lax.ppermute(low, 'block', down))  21.4 us
    ppermute x8, waiting for transfers between devices, neighbours(): return (lax.ppermute(high, 'block', up), lax.ppermute(low, 'block', down))  18.6 us
    ppermute x4, starting transfers between devices, exchanged(): pairs.append((payload, lax.ppermute(payload, 'view', [(0, 1), (1, 0)])))  6.34 us
  transfers between devices with their start and end apart: 23, of which 14 were waited for; matrix products, arithmetic and copies ran while one was open for 0% of the time, Pallas kernels for 6%

profile of v8, /device:TPU:15, one launch (start us, length us, event | category | flops | bytes accessed | tf_op | source)
XLA Modules:
  0.0 178.0 jit_solution(16136623792765793584)
XLA Ops:
  0.0 1.9 %convert_element_type.3 = bf16[32,128,128]{2,1,0:T(8,128)(2,1)S(1)} convert(f32[32,128,128]{2,1,0:T(8,128)} %param.4) | non-fusion elementwise | flops 524288 | bytes 3145728 | tf_op jit(solution)/shard_map/convert_element_type | solution.py:382
  1.9 0.0 copy-start.1
  1.9 1.0 fusion.1
  3.0 4.1 %collective-permute-start = (bf16[16,128,128]{2,1,0:T(8,128)(2,1)}, bf16[16,128,128]{2,1,0:T(8,128)(2,1)}, u32[]{:S(2)}, u32[]{:S(2)}) collective-permute-start(bf16[16,128,128]{2,1,0:T(8,128)(2,1)} %get-tuple-element.80.refs_2_), channel_id=1, source_target_pairs={{0,1},{1,2},{2,3},{3,4},{4,5},{5,6},{6,7},{7,8},{8,9},{9,10},{10,1... | collective-permute-start | bytes 1572872 | tf_op jit(solution)/shard_map/ppermute | solution.py:359
  7.1 1.9 %collective-permute-start.1 = (bf16[16,128,128]{2,1,0:T(8,128)(2,1)}, bf16[16,128,128]{2,1,0:T(8,128)(2,1)}, u32[]{:S(2)}, u32[]{:S(2)}) collective-permute-start(bf16[16,128,128]{2,1,0:T(8,128)(2,1)} %get-tuple-element.79.refs_1_), channel_id=1, source_target_pairs={{1,0},{2,1},{3,2},{4,3},{5,4},{6,5},{7,6},{8,7},{9,8},{10,9},{11,1... | collective-permute-start | bytes 1572872 | tf_op jit(solution)/shard_map/ppermute | solution.py:359
  9.0 0.1 copy.6
  9.1 1.1 pack_tiles.1
  10.2 3.8 %collective-permute-start.10 = (bf16[1040,128]{1,0:T(8,128)(2,1)S(1)}, bf16[1040,128]{1,0:T(8,128)(2,1)S(1)}, u32[]{:S(2)}, u32[]{:S(2)}) collective-permute-start(bf16[1040,128]{1,0:T(8,128)(2,1)S(1)} %get-tuple-element.53), channel_id=1, source_target_pairs={{0,3},{1,4},{2,5},{3,6},{4,7},{5,8},{6,9},{7,10},{8,11},{9,12},{10... | collective-permute-start | bytes 798728 | tf_op jit(solution)/shard_map/ppermute | solution.py:380
  13.9 0.0 collective-permute-start.11
  13.9 2.0 %collective-permute-start.12 = (bf16[1040,128]{1,0:T(8,128)(2,1)S(1)}, bf16[1040,128]{1,0:T(8,128)(2,1)S(1)}, u32[]{:S(2)}, u32[]{:S(2)}) collective-permute-start(bf16[1040,128]{1,0:T(8,128)(2,1)S(1)} %get-tuple-element.55), channel_id=1, source_target_pairs={{0,5},{1,6},{2,7},{3,8},{4,9},{5,10},{6,11},{7,12},{8,13},{9,14},{... | collective-permute-start | bytes 798728 | tf_op jit(solution)/shard_map/ppermute | solution.py:380
  16.0 0.7 prepare.1
  16.7 5.5 %collective-permute-done.10.refs_9_ = bf16[1040,128]{1,0:T(8,128)(2,1)S(1)} collective-permute-done((bf16[1040,128]{1,0:T(8,128)(2,1)S(1)}, bf16[1040,128]{1,0:T(8,128)(2,1)S(1)}, u32[]{:S(2)}, u32[]{:S(2)}) %collective-permute-start.10) | collective-permute-done | bytes 266272 | tf_op jit(solution)/shard_map/ppermute | solution.py:380
  22.2 1.9 %collective-permute-start.2 = (bf16[1040,128]{1,0:T(8,128)(2,1)S(1)}, bf16[1040,128]{1,0:T(8,128)(2,1)S(1)}, u32[]{:S(2)}, u32[]{:S(2)}) collective-permute-start(bf16[1040,128]{1,0:T(8,128)(2,1)S(1)} %get-tuple-element.44), channel_id=1, source_target_pairs={{0,58},{1,59},{2,60},{3,61},{4,62},{5,63},{6,0},{7,1},{8,2},{9,3},... | collective-permute-start | bytes 798728 | tf_op jit(solution)/shard_map/ppermute | solution.py:380
  24.1 0.0 collective-permute-done.refs_0_
  24.1 7.5 %collective-permute-start.3 = (bf16[1040,128]{1,0:T(8,128)(2,1)S(1)}, bf16[1040,128]{1,0:T(8,128)(2,1)S(1)}, u32[]{:S(2)}, u32[]{:S(2)}) collective-permute-start(bf16[1040,128]{1,0:T(8,128)(2,1)S(1)} %get-tuple-element.45), channel_id=1, source_target_pairs={{0,59},{1,60},{2,61},{3,62},{4,63},{5,0},{6,1},{7,2},{8,3},{9,4},{... | collective-permute-start | bytes 798728 | tf_op jit(solution)/shard_map/ppermute | solution.py:380
  31.5 0.0 collective-permute-done.1.refs_3_
  31.5 4.4 %collective-permute-start.4 = (bf16[1040,128]{1,0:T(8,128)(2,1)S(1)}, bf16[1040,128]{1,0:T(8,128)(2,1)S(1)}, u32[]{:S(2)}, u32[]{:S(2)}) collective-permute-start(bf16[1040,128]{1,0:T(8,128)(2,1)S(1)} %get-tuple-element.46), channel_id=1, source_target_pairs={{0,60},{1,61},{2,62},{3,63},{4,0},{5,1},{6,2},{7,3},{8,4},{9,5},{1... | collective-permute-start | bytes 798728 | tf_op jit(solution)/shard_map/ppermute | solution.py:380
  35.9 6.7 %first_blur.1.blurred_ref = f32[24,512,128]{2,1,0:T(8,128)S(1)} custom-call(bf16[96,64]{1,0:T(8,128)(2,1)S(1)} %get-tuple-element.56.kx_ref.refs_0_, bf16[3,128,128]{2,1,0:T(8,128)(2,1)S(1)} %get-tuple-element.57.ky_ref.refs_1_, bf16[3,256,256]{2,1,0:T(8,128)(2,1)S(1)} %get-tuple-element.58.kz_ref.refs_2_, ...), custom_call_target="tpu_custom_call" | custom-call | flops 6442450944 | bytes 12582912 | tf_op jit(solution)/shard_map/first_blur/pallas_call | solution.py:343
  42.6 0.0 collective-permute-done.11.refs_10_
  42.6 0.1 collective-permute-start.5
  42.7 0.0 collective-permute-done.12.refs_11_
  42.7 0.1 collective-permute-start.6
  42.8 0.0 collective-permute-done.2.refs_0_
  42.8 0.5 collective-permute-start.7
  43.3 0.0 collective-permute-done.3.refs_1_
  43.3 1.5 collective-permute-start.8
  44.8 8.0 %collective-permute-done.4.refs_2_ = bf16[1040,128]{1,0:T(8,128)(2,1)S(1)} collective-permute-done((bf16[1040,128]{1,0:T(8,128)(2,1)S(1)}, bf16[1040,128]{1,0:T(8,128)(2,1)S(1)}, u32[]{:S(2)}, u32[]{:S(2)}) %collective-permute-start.4) | collective-permute-done | bytes 266272 | tf_op jit(solution)/shard_map/ppermute | solution.py:380
  52.8 0.0 collective-permute-start.9
  52.8 0.4 collective-permute-done.5.refs_3_
  53.3 11.8 %collective-permute-done.6.refs_4_ = bf16[1040,128]{1,0:T(8,128)(2,1)S(1)} collective-permute-done((bf16[1040,128]{1,0:T(8,128)(2,1)S(1)}, bf16[1040,128]{1,0:T(8,128)(2,1)S(1)}, u32[]{:S(2)}, u32[]{:S(2)}) %collective-permute-start.6) | collective-permute-done | bytes 266272 | tf_op jit(solution)/shard_map/ppermute | solution.py:380
  65.0 0.9 collective-permute-done.7.refs_5_
  65.9 0.0 collective-permute-done.8.refs_7_
  65.9 1.2 collective-permute-done.9.refs_8_
  67.1 6.8 %first_back.1 = (s16[2064,128]{1,0:T(8,128)(2,1)S(1)}, f32[16,128,128]{2,1,0:T(8,128)S(1)}, f32[16,128,128]{2,1,0:T(8,128)S(1)}, s16[2064,128]{1,0:T(8,128)(2,1)S(1)}, bf16[24,512,128]{2,1,0:T(8,128)(2,1)S(1)}) custom-call(bf16[64,192]{1,0:T(8,128)(2,1)S(1)} %get-tuple-element.41.kx_ref.refs_3_, bf16[3,128,128]{2,1,0:T(8,128)(2,1)S(1)} %get-tuple-element.42.ky_ref.refs_4_, ...), custom_call_target="tpu_custom_call" | custom-call | flops 8589934592 | bytes 12582912 | tf_op jit(solution)/shard_map/first_back/pallas_call | solution.py:343
  73.9 0.0 copy-start.2
  73.9 2.1 %collective-permute-start.15 = (s16[2064,128]{1,0:T(8,128)(2,1)S(1)}, s16[2064,128]{1,0:T(8,128)(2,1)S(1)}, u32[]{:S(2)}, u32[]{:S(2)}) collective-permute-start(s16[2064,128]{1,0:T(8,128)(2,1)S(1)} %get-tuple-element.68), channel_id=1, source_target_pairs={{1,0},{2,1},{3,2},{4,3},{5,4},{6,5},{7,6},{8,7},{9,8},{10,9},{11,1... | collective-permute-start | bytes 1585160 | tf_op jit(solution)/shard_map/ppermute | solution.py:359
  75.9 3.6 %collective-permute-start.13 = (s16[2064,128]{1,0:T(8,128)(2,1)S(1)}, s16[2064,128]{1,0:T(8,128)(2,1)S(1)}, u32[]{:S(2)}, u32[]{:S(2)}) collective-permute-start(s16[2064,128]{1,0:T(8,128)(2,1)S(1)} %get-tuple-element.65), channel_id=1, source_target_pairs={{0,1},{1,2},{2,3},{3,4},{4,5},{5,6},{6,7},{7,8},{8,9},{9,10},{10,1... | collective-permute-start | bytes 1585160 | tf_op jit(solution)/shard_map/ppermute | solution.py:359
  79.6 5.3 %collective-permute-done.15.edge_ref = s16[2064,128]{1,0:T(8,128)(2,1)S(1)} collective-permute-done((s16[2064,128]{1,0:T(8,128)(2,1)S(1)}, s16[2064,128]{1,0:T(8,128)(2,1)S(1)}, u32[]{:S(2)}, u32[]{:S(2)}) %collective-permute-start.15) | collective-permute-done | bytes 528416 | tf_op jit(solution)/shard_map/ppermute | solution.py:359
  84.8 0.3 join.5.own_ref
  85.2 2.1 %collective-permute-start.16 = (s16[2064,128]{1,0:T(8,128)(2,1)S(1)}, s16[2064,128]{1,0:T(8,128)(2,1)S(1)}, u32[]{:S(2)}, u32[]{:S(2)}) collective-permute-start(s16[2064,128]{1,0:T(8,128)(2,1)S(1)} %join.5.own_ref), channel_id=1, source_target_pairs={{0,64},{64,0},{1,65},{65,1},{2,66},{66,2},{3,67},{67,3},{4,68},{68... | collective-permute-start | bytes 1585160 | tf_op jit(solution)/shard_map/ppermute | solution.py:367
  87.3 0.0 collective-permute-done.13.edge_ref
  87.3 0.3 join.4.own_ref
  87.6 1.2 collective-permute-start.14
  88.8 0.1 fusion
  89.0 14.4 %collective-permute-done.16.other_ref = s16[2064,128]{1,0:T(8,128)(2,1)S(1)} collective-permute-done((s16[2064,128]{1,0:T(8,128)(2,1)S(1)}, s16[2064,128]{1,0:T(8,128)(2,1)S(1)}, u32[]{:S(2)}, u32[]{:S(2)}) %collective-permute-start.16) | collective-permute-done | bytes 528416 | tf_op jit(solution)/shard_map/ppermute | solution.py:367
  103.4 0.4 update.3
  103.7 1.9 %collective-permute-start.17 = (bf16[16,128,128]{2,1,0:T(8,128)(2,1)S(1)}, bf16[16,128,128]{2,1,0:T(8,128)(2,1)S(1)}, u32[]{:S(2)}, u32[]{:S(2)}) collective-permute-start(bf16[16,128,128]{2,1,0:T(8,128)(2,1)S(1)} %get-tuple-element.70.refs_8_), channel_id=1, source_target_pairs={{0,1},{1,2},{2,3},{3,4},{4,5},{5,6},{6,7},{7,8},{8,9},{9,10},{10,1... | collective-permute-start | bytes 1572872 | tf_op jit(solution)/shard_map/ppermute | solution.py:359
  105.7 8.9 %collective-permute-done.14.other_ref = s16[2064,128]{1,0:T(8,128)(2,1)S(1)} collective-permute-done((s16[2064,128]{1,0:T(8,128)(2,1)S(1)}, s16[2064,128]{1,0:T(8,128)(2,1)S(1)}, u32[]{:S(2)}, u32[]{:S(2)}) %collective-permute-start.14) | collective-permute-done | bytes 528416 | tf_op jit(solution)/shard_map/ppermute | solution.py:367
  114.6 0.4 update.2
  115.0 2.2 %collective-permute-start.18 = (bf16[16,128,128]{2,1,0:T(8,128)(2,1)S(1)}, bf16[16,128,128]{2,1,0:T(8,128)(2,1)S(1)}, u32[]{:S(2)}, u32[]{:S(2)}) collective-permute-start(bf16[16,128,128]{2,1,0:T(8,128)(2,1)S(1)} %get-tuple-element.71.refs_7_), channel_id=1, source_target_pairs={{1,0},{2,1},{3,2},{4,3},{5,4},{6,5},{7,6},{8,7},{9,8},{10,9},{11,1... | collective-permute-start | bytes 1572872 | tf_op jit(solution)/shard_map/ppermute | solution.py:359
  117.2 0.0 collective-permute-done.17.refs_6_
  117.2 8.3 %collective-permute-done.18.refs_9_ = bf16[16,128,128]{2,1,0:T(8,128)(2,1)S(1)} collective-permute-done((bf16[16,128,128]{2,1,0:T(8,128)(2,1)S(1)}, bf16[16,128,128]{2,1,0:T(8,128)(2,1)S(1)}, u32[]{:S(2)}, u32[]{:S(2)}) %collective-permute-start.18) | collective-permute-done | bytes 524320 | tf_op jit(solution)/shard_map/ppermute | solution.py:359
  125.5 11.8 %sweep.1 = (s16[2064,128]{1,0:T(8,128)(2,1)S(1)}, f32[16,128,128]{2,1,0:T(8,128)S(1)}, f32[16,128,128]{2,1,0:T(8,128)S(1)}, s16[2064,128]{1,0:T(8,128)(2,1)S(1)}) custom-call(bf16[96,64]{1,0:T(8,128)(2,1)S(1)} %get-tuple-element.56.kx_ref.refs_0_, bf16[3,128,128]{2,1,0:T(8,128)(2,1)S(1)} %get-tuple-element.57.ky_ref.refs_1_, ...), custom_call_target="tpu_custom_call" | custom-call | flops 15032385536 | bytes 12582912 | tf_op jit(solution)/shard_map/sweep/pallas_call | solution.py:343
  137.3 1.9 %collective-permute-start.21 = (s16[2064,128]{1,0:T(8,128)(2,1)S(1)}, s16[2064,128]{1,0:T(8,128)(2,1)S(1)}, u32[]{:S(2)}, u32[]{:S(2)}) collective-permute-start(s16[2064,128]{1,0:T(8,128)(2,1)S(1)} %get-tuple-element.76), channel_id=1, source_target_pairs={{1,0},{2,1},{3,2},{4,3},{5,4},{6,5},{7,6},{8,7},{9,8},{10,9},{11,1... | collective-permute-start | bytes 1585160 | tf_op jit(solution)/shard_map/ppermute | solution.py:359
  139.2 3.6 %collective-permute-start.19 = (s16[2064,128]{1,0:T(8,128)(2,1)S(1)}, s16[2064,128]{1,0:T(8,128)(2,1)S(1)}, u32[]{:S(2)}, u32[]{:S(2)}) collective-permute-start(s16[2064,128]{1,0:T(8,128)(2,1)S(1)} %get-tuple-element.74), channel_id=1, source_target_pairs={{0,1},{1,2},{2,3},{3,4},{4,5},{5,6},{6,7},{7,8},{8,9},{9,10},{10,1... | collective-permute-start | bytes 1585160 | tf_op jit(solution)/shard_map/ppermute | solution.py:359
  142.9 5.0 %collective-permute-done.21.edge_ref = s16[2064,128]{1,0:T(8,128)(2,1)S(1)} collective-permute-done((s16[2064,128]{1,0:T(8,128)(2,1)S(1)}, s16[2064,128]{1,0:T(8,128)(2,1)S(1)}, u32[]{:S(2)}, u32[]{:S(2)}) %collective-permute-start.21) | collective-permute-done | bytes 528416 | tf_op jit(solution)/shard_map/ppermute | solution.py:359
  147.8 0.3 join.7.refs_2_
  148.2 0.7 collective-permute-start.22
  148.9 0.1 collective-permute-done.19.edge_ref
  149.0 0.3 join.6.refs_0_
  149.4 2.3 %collective-permute-start.20 = (s16[2064,128]{1,0:T(8,128)(2,1)S(1)}, s16[2064,128]{1,0:T(8,128)(2,1)S(1)}, u32[]{:S(2)}, u32[]{:S(2)}) collective-permute-start(s16[2064,128]{1,0:T(8,128)(2,1)S(1)} %join.6.refs_0_), channel_id=1, source_target_pairs={{0,64},{64,0},{1,65},{65,1},{2,66},{66,2},{3,67},{67,3},{4,68},{68... | collective-permute-start | bytes 1585160 | tf_op jit(solution)/shard_map/ppermute | solution.py:367
  151.7 13.0 %collective-permute-done.22.refs_3_ = s16[2064,128]{1,0:T(8,128)(2,1)S(1)} collective-permute-done((s16[2064,128]{1,0:T(8,128)(2,1)S(1)}, s16[2064,128]{1,0:T(8,128)(2,1)S(1)}, u32[]{:S(2)}, u32[]{:S(2)}) %collective-permute-start.22) | collective-permute-done | bytes 528416 | tf_op jit(solution)/shard_map/ppermute | solution.py:367
  164.7 11.3 %collective-permute-done.20.refs_1_ = s16[2064,128]{1,0:T(8,128)(2,1)S(1)} collective-permute-done((s16[2064,128]{1,0:T(8,128)(2,1)S(1)}, s16[2064,128]{1,0:T(8,128)(2,1)S(1)}, u32[]{:S(2)}, u32[]{:S(2)}) %collective-permute-start.20) | collective-permute-done | bytes 528416 | tf_op jit(solution)/shard_map/ppermute | solution.py:367
  176.0 2.0 %last_update.1 = f32[32,128,128]{2,1,0:T(8,128)} custom-call(f32[16,128,128]{2,1,0:T(8,128)S(1)} %get-tuple-element.66.low_ref, f32[16,128,128]{2,1,0:T(8,128)S(1)} %get-tuple-element.69.high_ref, s16[2064,128]{1,0:T(8,128)(2,1)S(1)} %join.6.refs_0_, s16[2064,128]{1,0:T(8,128)(2,1)S(1)} %collective-permute-done.20.refs_1_, ...), custom_call_target="tpu_custom_call" | custom-call | flops 1048576 | bytes 12582912 | tf_op jit(solution)/shard_map/last_update/pallas_call | solution.py:343
  (6 shorter events, 0.0 us)
Async XLA Ops:
  0.0 9.0 %copy-start.3 = (s32[1,24,3]{1,0,2:T(1,128)S(1)}, s32[1,24,3]{1,0,2:T(1,128)}, u32[]{:S(2)}) copy-start(s32[1,24,3]{1,0,2:T(1,128)} %param.6) | copy-start | bytes 868
  0.0 9.1 %copy-start = (bf16[1,24,4,128,128]{4,3,2,1,0:T(8,128)(2,1)S(1)}, bf16[1,24,4,128,128]{4,3,2,1,0:T(8,128)(2,1)}, u32[]{:S(2)}) copy-start(bf16[1,24,4,128,128]{4,3,2,1,0:T(8,128)(2,1)} %param.5) | copy-start | bytes 9437188
  1.9 14.1 %copy-start.1 = (f32[3,3,31]{2,1,0:T(4,128)S(1)}, f32[3,3,31]{2,1,0:T(4,128)}, u32[]{:S(2)}) copy-start(f32[3,3,31]{2,1,0:T(4,128)} %psf_ref.1) | copy-start | bytes 3352
  3.0 21.1 %collective-permute-start = (bf16[16,128,128]{2,1,0:T(8,128)(2,1)}, bf16[16,128,128]{2,1,0:T(8,128)(2,1)}, u32[]{:S(2)}, u32[]{:S(2)}) collective-permute-start(bf16[16,128,128]{2,1,0:T(8,128)(2,1)} %get-tuple-element.80.refs_2_), channel_id=1, source_target_pairs={{0,1},{1,2},{2,3},{3,4},{4,5},{5,6},{6,7},{7,8},{8,9},{9,10},{10,1... | collective-permute-start | bytes 1572872 | tf_op jit(solution)/shard_map/ppermute | solution.py:359
  7.1 24.5 %collective-permute-start.1 = (bf16[16,128,128]{2,1,0:T(8,128)(2,1)}, bf16[16,128,128]{2,1,0:T(8,128)(2,1)}, u32[]{:S(2)}, u32[]{:S(2)}) collective-permute-start(bf16[16,128,128]{2,1,0:T(8,128)(2,1)} %get-tuple-element.79.refs_1_), channel_id=1, source_target_pairs={{1,0},{2,1},{3,2},{4,3},{5,4},{6,5},{7,6},{8,7},{9,8},{10,9},{11,1... | collective-permute-start | bytes 1572872 | tf_op jit(solution)/shard_map/ppermute | solution.py:359
  10.2 12.0 %collective-permute-start.10 = (bf16[1040,128]{1,0:T(8,128)(2,1)S(1)}, bf16[1040,128]{1,0:T(8,128)(2,1)S(1)}, u32[]{:S(2)}, u32[]{:S(2)}) collective-permute-start(bf16[1040,128]{1,0:T(8,128)(2,1)S(1)} %get-tuple-element.53), channel_id=1, source_target_pairs={{0,3},{1,4},{2,5},{3,6},{4,7},{5,8},{6,9},{7,10},{8,11},{9,12},{10... | collective-permute-start | bytes 798728 | tf_op jit(solution)/shard_map/ppermute | solution.py:380
  13.9 28.7 %collective-permute-start.11 = (bf16[1040,128]{1,0:T(8,128)(2,1)S(1)}, bf16[1040,128]{1,0:T(8,128)(2,1)S(1)}, u32[]{:S(2)}, u32[]{:S(2)}) collective-permute-start(bf16[1040,128]{1,0:T(8,128)(2,1)S(1)} %get-tuple-element.54), channel_id=1, source_target_pairs={{0,4},{1,5},{2,6},{3,7},{4,8},{5,9},{6,10},{7,11},{8,12},{9,13},{1... | collective-permute-start | bytes 798728 | tf_op jit(solution)/shard_map/ppermute | solution.py:380
  13.9 28.8 %collective-permute-start.12 = (bf16[1040,128]{1,0:T(8,128)(2,1)S(1)}, bf16[1040,128]{1,0:T(8,128)(2,1)S(1)}, u32[]{:S(2)}, u32[]{:S(2)}) collective-permute-start(bf16[1040,128]{1,0:T(8,128)(2,1)S(1)} %get-tuple-element.55), channel_id=1, source_target_pairs={{0,5},{1,6},{2,7},{3,8},{4,9},{5,10},{6,11},{7,12},{8,13},{9,14},{... | collective-permute-start | bytes 798728 | tf_op jit(solution)/shard_map/ppermute | solution.py:380
  22.2 20.6 %collective-permute-start.2 = (bf16[1040,128]{1,0:T(8,128)(2,1)S(1)}, bf16[1040,128]{1,0:T(8,128)(2,1)S(1)}, u32[]{:S(2)}, u32[]{:S(2)}) collective-permute-start(bf16[1040,128]{1,0:T(8,128)(2,1)S(1)} %get-tuple-element.44), channel_id=1, source_target_pairs={{0,58},{1,59},{2,60},{3,61},{4,62},{5,63},{6,0},{7,1},{8,2},{9,3},... | collective-permute-start | bytes 798728 | tf_op jit(solution)/shard_map/ppermute | solution.py:380
  24.1 19.2 %collective-permute-start.3 = (bf16[1040,128]{1,0:T(8,128)(2,1)S(1)}, bf16[1040,128]{1,0:T(8,128)(2,1)S(1)}, u32[]{:S(2)}, u32[]{:S(2)}) collective-permute-start(bf16[1040,128]{1,0:T(8,128)(2,1)S(1)} %get-tuple-element.45), channel_id=1, source_target_pairs={{0,59},{1,60},{2,61},{3,62},{4,63},{5,0},{6,1},{7,2},{8,3},{9,4},{... | collective-permute-start | bytes 798728 | tf_op jit(solution)/shard_map/ppermute | solution.py:380
  31.5 21.3 %collective-permute-start.4 = (bf16[1040,128]{1,0:T(8,128)(2,1)S(1)}, bf16[1040,128]{1,0:T(8,128)(2,1)S(1)}, u32[]{:S(2)}, u32[]{:S(2)}) collective-permute-start(bf16[1040,128]{1,0:T(8,128)(2,1)S(1)} %get-tuple-element.46), channel_id=1, source_target_pairs={{0,60},{1,61},{2,62},{3,63},{4,0},{5,1},{6,2},{7,3},{8,4},{9,5},{1... | collective-permute-start | bytes 798728 | tf_op jit(solution)/shard_map/ppermute | solution.py:380
  42.6 10.6 %collective-permute-start.5 = (bf16[1040,128]{1,0:T(8,128)(2,1)S(1)}, bf16[1040,128]{1,0:T(8,128)(2,1)S(1)}, u32[]{:S(2)}, u32[]{:S(2)}) collective-permute-start(bf16[1040,128]{1,0:T(8,128)(2,1)S(1)} %get-tuple-element.47), channel_id=1, source_target_pairs={{0,61},{1,62},{2,63},{3,0},{4,1},{5,2},{6,3},{7,4},{8,5},{9,6},{10... | collective-permute-start | bytes 798728 | tf_op jit(solution)/shard_map/ppermute | solution.py:380
  42.7 22.3 %collective-permute-start.6 = (bf16[1040,128]{1,0:T(8,128)(2,1)S(1)}, bf16[1040,128]{1,0:T(8,128)(2,1)S(1)}, u32[]{:S(2)}, u32[]{:S(2)}) collective-permute-start(bf16[1040,128]{1,0:T(8,128)(2,1)S(1)} %get-tuple-element.60), channel_id=1, source_target_pairs={{0,62},{1,63},{2,0},{3,1},{4,2},{5,3},{6,4},{7,5},{8,6},{9,7},{10,... | collective-permute-start | bytes 798728 | tf_op jit(solution)/shard_map/ppermute | solution.py:380
  42.8 23.1 %collective-permute-start.7 = (bf16[1040,128]{1,0:T(8,128)(2,1)S(1)}, bf16[1040,128]{1,0:T(8,128)(2,1)S(1)}, u32[]{:S(2)}, u32[]{:S(2)}) collective-permute-start(bf16[1040,128]{1,0:T(8,128)(2,1)S(1)} %get-tuple-element.61), channel_id=1, source_target_pairs={{0,63},{1,0},{2,1},{3,2},{4,3},{5,4},{6,5},{7,6},{8,7},{9,8},{10,9... | collective-permute-start | bytes 798728 | tf_op jit(solution)/shard_map/ppermute | solution.py:380
  43.3 22.6 %collective-permute-start.8 = (bf16[1040,128]{1,0:T(8,128)(2,1)S(1)}, bf16[1040,128]{1,0:T(8,128)(2,1)S(1)}, u32[]{:S(2)}, u32[]{:S(2)}) collective-permute-start(bf16[1040,128]{1,0:T(8,128)(2,1)S(1)} %get-tuple-element.62), channel_id=1, source_target_pairs={{0,1},{1,2},{2,3},{3,4},{4,5},{5,6},{6,7},{7,8},{8,9},{9,10},{10,1... | collective-permute-start | bytes 798728 | tf_op jit(solution)/shard_map/ppermute | solution.py:380
  52.8 14.2 %collective-permute-start.9 = (bf16[1040,128]{1,0:T(8,128)(2,1)S(1)}, bf16[1040,128]{1,0:T(8,128)(2,1)S(1)}, u32[]{:S(2)}, u32[]{:S(2)}) collective-permute-start(bf16[1040,128]{1,0:T(8,128)(2,1)S(1)} %get-tuple-element.63), channel_id=1, source_target_pairs={{0,2},{1,3},{2,4},{3,5},{4,6},{5,7},{6,8},{7,9},{8,10},{9,11},{10,... | collective-permute-start | bytes 798728 | tf_op jit(solution)/shard_map/ppermute | solution.py:380
  73.9 15.0 %copy-start.2 = (f32[32,128,128]{2,1,0:T(8,128)S(1)}, f32[32,128,128]{2,1,0:T(8,128)}, u32[]{:S(2)}) copy-start(f32[32,128,128]{2,1,0:T(8,128)} %param.4) | copy-start | bytes 6291460
  73.9 11.0 %collective-permute-start.15 = (s16[2064,128]{1,0:T(8,128)(2,1)S(1)}, s16[2064,128]{1,0:T(8,128)(2,1)S(1)}, u32[]{:S(2)}, u32[]{:S(2)}) collective-permute-start(s16[2064,128]{1,0:T(8,128)(2,1)S(1)} %get-tuple-element.68), channel_id=1, source_target_pairs={{1,0},{2,1},{3,2},{4,3},{5,4},{6,5},{7,6},{8,7},{9,8},{10,9},{11,1... | collective-permute-start | bytes 1585160 | tf_op jit(solution)/shard_map/ppermute | solution.py:359
  75.9 11.4 %collective-permute-start.13 = (s16[2064,128]{1,0:T(8,128)(2,1)S(1)}, s16[2064,128]{1,0:T(8,128)(2,1)S(1)}, u32[]{:S(2)}, u32[]{:S(2)}) collective-permute-start(s16[2064,128]{1,0:T(8,128)(2,1)S(1)} %get-tuple-element.65), channel_id=1, source_target_pairs={{0,1},{1,2},{2,3},{3,4},{4,5},{5,6},{6,7},{7,8},{8,9},{9,10},{10,1... | collective-permute-start | bytes 1585160 | tf_op jit(solution)/shard_map/ppermute | solution.py:359
  85.2 18.2 %collective-permute-start.16 = (s16[2064,128]{1,0:T(8,128)(2,1)S(1)}, s16[2064,128]{1,0:T(8,128)(2,1)S(1)}, u32[]{:S(2)}, u32[]{:S(2)}) collective-permute-start(s16[2064,128]{1,0:T(8,128)(2,1)S(1)} %join.5.own_ref), channel_id=1, source_target_pairs={{0,64},{64,0},{1,65},{65,1},{2,66},{66,2},{3,67},{67,3},{4,68},{68... | collective-permute-start | bytes 1585160 | tf_op jit(solution)/shard_map/ppermute | solution.py:367
  87.6 27.0 %collective-permute-start.14 = (s16[2064,128]{1,0:T(8,128)(2,1)S(1)}, s16[2064,128]{1,0:T(8,128)(2,1)S(1)}, u32[]{:S(2)}, u32[]{:S(2)}) collective-permute-start(s16[2064,128]{1,0:T(8,128)(2,1)S(1)} %join.4.own_ref), channel_id=1, source_target_pairs={{0,64},{64,0},{1,65},{65,1},{2,66},{66,2},{3,67},{67,3},{4,68},{68... | collective-permute-start | bytes 1585160 | tf_op jit(solution)/shard_map/ppermute | solution.py:367
  103.7 13.4 %collective-permute-start.17 = (bf16[16,128,128]{2,1,0:T(8,128)(2,1)S(1)}, bf16[16,128,128]{2,1,0:T(8,128)(2,1)S(1)}, u32[]{:S(2)}, u32[]{:S(2)}) collective-permute-start(bf16[16,128,128]{2,1,0:T(8,128)(2,1)S(1)} %get-tuple-element.70.refs_8_), channel_id=1, source_target_pairs={{0,1},{1,2},{2,3},{3,4},{4,5},{5,6},{6,7},{7,8},{8,9},{9,10},{10,1... | collective-permute-start | bytes 1572872 | tf_op jit(solution)/shard_map/ppermute | solution.py:359
  115.0 10.5 %collective-permute-start.18 = (bf16[16,128,128]{2,1,0:T(8,128)(2,1)S(1)}, bf16[16,128,128]{2,1,0:T(8,128)(2,1)S(1)}, u32[]{:S(2)}, u32[]{:S(2)}) collective-permute-start(bf16[16,128,128]{2,1,0:T(8,128)(2,1)S(1)} %get-tuple-element.71.refs_7_), channel_id=1, source_target_pairs={{1,0},{2,1},{3,2},{4,3},{5,4},{6,5},{7,6},{8,7},{9,8},{10,9},{11,1... | collective-permute-start | bytes 1572872 | tf_op jit(solution)/shard_map/ppermute | solution.py:359
  137.3 10.5 %collective-permute-start.21 = (s16[2064,128]{1,0:T(8,128)(2,1)S(1)}, s16[2064,128]{1,0:T(8,128)(2,1)S(1)}, u32[]{:S(2)}, u32[]{:S(2)}) collective-permute-start(s16[2064,128]{1,0:T(8,128)(2,1)S(1)} %get-tuple-element.76), channel_id=1, source_target_pairs={{1,0},{2,1},{3,2},{4,3},{5,4},{6,5},{7,6},{8,7},{9,8},{10,9},{11,1... | collective-permute-start | bytes 1585160 | tf_op jit(solution)/shard_map/ppermute | solution.py:359
  139.2 9.8 %collective-permute-start.19 = (s16[2064,128]{1,0:T(8,128)(2,1)S(1)}, s16[2064,128]{1,0:T(8,128)(2,1)S(1)}, u32[]{:S(2)}, u32[]{:S(2)}) collective-permute-start(s16[2064,128]{1,0:T(8,128)(2,1)S(1)} %get-tuple-element.74), channel_id=1, source_target_pairs={{0,1},{1,2},{2,3},{3,4},{4,5},{5,6},{6,7},{7,8},{8,9},{9,10},{10,1... | collective-permute-start | bytes 1585160 | tf_op jit(solution)/shard_map/ppermute | solution.py:359
  148.2 16.5 %collective-permute-start.22 = (s16[2064,128]{1,0:T(8,128)(2,1)S(1)}, s16[2064,128]{1,0:T(8,128)(2,1)S(1)}, u32[]{:S(2)}, u32[]{:S(2)}) collective-permute-start(s16[2064,128]{1,0:T(8,128)(2,1)S(1)} %join.7.refs_2_), channel_id=1, source_target_pairs={{0,64},{64,0},{1,65},{65,1},{2,66},{66,2},{3,67},{67,3},{4,68},{68... | collective-permute-start | bytes 1585160 | tf_op jit(solution)/shard_map/ppermute | solution.py:367
  149.4 26.7 %collective-permute-start.20 = (s16[2064,128]{1,0:T(8,128)(2,1)S(1)}, s16[2064,128]{1,0:T(8,128)(2,1)S(1)}, u32[]{:S(2)}, u32[]{:S(2)}) collective-permute-start(s16[2064,128]{1,0:T(8,128)(2,1)S(1)} %join.6.refs_0_), channel_id=1, source_target_pairs={{0,64},{64,0},{1,65},{65,1},{2,66},{66,2},{3,67},{67,3},{4,68},{68... | collective-permute-start | bytes 1585160 | tf_op jit(solution)/shard_map/ppermute | solution.py:367

commit v9 on v8

--- a/solution.py
+++ b/solution.py
@@ -224,8 +224,31 @@
     lax.fori_loop(0, VIEWS_DEV * BX // TP, along_yz, 0, unroll=UNROLL)
 
 
+def times_rows(taps, rows):
+    got = []
+    for j in range(0, 8, 2):
+        pair = jnp.concatenate([rows[j], rows[j + 1]], axis=1)
+        both = jnp.dot(taps, pair, preferred_element_type=F32)
+        got += [both[:, :Z], both[:, Z:]]
+    return got
+
+
+def own_kernel(kx_ref, turned_ref, low_ref, high_ref):
+    taps = kx_ref[HX : HX + BX]
+
+    def along_x(t, carry):
+        y0 = pl.multiple_of(t * 8, 8)
+        planes = swapped(jnp.stack(times_rows(taps, turned_ref[pl.ds(y0, 8)]), axis=0))
+        low_ref[:, pl.ds(y0, 8), :] = planes[:HX]
+        high_ref[:, pl.ds(y0, 8), :] = planes[HX:]
+        return carry
+
+    lax.fori_loop(0, Y // 8, along_x, 0, unroll=8)
+
+
 def back_from(kx_ref, ky_ref, kz_ref, measured_ref, blurred_ref, half_ref, edge_ref, peak_ref, outs):
-    left_ref, low_ref, high_ref, right_ref = outs
+    left_ref, right_ref, turned_ref = outs
+    taps = jnp.concatenate([kx_ref[:HX], kx_ref[HX + BX :]], axis=0)
 
     def along_zy(q, carry):
         v = q // (BX // TP)
@@ -251,17 +274,12 @@
         data = swapped(half_ref[:, pl.ds(y0, 8), :])
         high = data.astype(BF16)
         low = (data - high.astype(F32)).astype(BF16)
-        got = []
-        for j in range(0, 8, 2):
-            pair = [jnp.concatenate([part[j], part[j + 1]], axis=1) for part in (high, low)]
-            both = jnp.dot(
-                kx_ref[...], jnp.concatenate(pair, axis=0), preferred_element_type=F32
-            )
-            got += [both[:, :Z], both[:, Z:]]
-        planes = swapped(jnp.stack(got, axis=0))
-        for i, ref in enumerate((edge_ref.at[0], low_ref, high_ref, edge_ref.at[1])):
-            ref[:, pl.ds(y0, 8), :] = planes[i * HX : (i + 1) * HX]
-        for i, part in enumerate((planes[:HX], planes[HX + BX :])):
+        both = jnp.concatenate([high, low], axis=1)
+        turned_ref[pl.ds(y0, 8)] = both
+        planes = swapped(jnp.stack(times_rows(taps, both), axis=0))
+        for i in range(2):
+            part = planes[i * HX : (i + 1) * HX]
+            edge_ref[i, :, pl.ds(y0, 8), :] = part
             peak_ref[i] = jnp.maximum(peak_ref[i], part)
         return carry
 
@@ -289,8 +307,8 @@
 def sweep_kernel(*refs):
     fwd, back, parts = refs[0:3], refs[3:6], refs[6:10]
     measured_ref = refs[10]
-    outs = refs[11:15]
-    half_ref, edge_ref, peak_ref, blurred_ref = refs[15:]
+    outs = refs[11:14]
+    half_ref, edge_ref, peak_ref, blurred_ref = refs[14:]
     blur_into(*fwd, parts, half_ref, blurred_ref)
     back_from(*back, measured_ref, blurred_ref, half_ref, edge_ref, peak_ref, outs)
 
@@ -319,10 +337,16 @@
 
 
 def last_kernel(view_count, low_ref, high_ref, *refs):
-    *payloads, out_ref = refs
+    *payloads, out_ref, plane_ref, sems = refs
+    copies = []
     for i, before_ref in enumerate((low_ref, high_ref)):
         own_ref, other_ref = payloads[2 * i : 2 * i + 2]
-        update_planes(view_count, before_ref, own_ref, other_ref, (out_ref.at[pl.ds(i * HX, HX)],))
+        part = pl.ds(i * HX, HX)
+        update_planes(view_count, before_ref, own_ref, other_ref, (plane_ref.at[part],))
+        copies.append(pltpu.make_async_copy(plane_ref.at[part], out_ref.at[part], sems.at[i]))
+        copies[-1].start()
+    for copy in copies:
+        copy.wait()
 
 
 VM = pl.BlockSpec(memory_space=pltpu.VMEM)
@@ -330,7 +354,7 @@
 HALF_SHAPE = (VIEWS_DEV * BX, Y, Z)
 PAYLOAD = jax.ShapeDtypeStruct((HX * Y + HX, Z), I16)
 OWN = jax.ShapeDtypeStruct((HX, Y, Z), F32)
-CONTRIB = [PAYLOAD, OWN, OWN, PAYLOAD]
+CONTRIB = [PAYLOAD, PAYLOAD, jax.ShapeDtypeStruct((Y, 2 * VIEWS_DEV * BX, Z), BF16)]
 BLUR_SCRATCH = [pltpu.VMEM(HALF_SHAPE, BF16)]
 BACK_SCRATCH = [
     pltpu.VMEM(HALF_SHAPE, F32),
@@ -339,12 +363,12 @@
 ]
 
 
-def call(kernel, name, operands, out_shape, scratch, flops, vmem=6):
+def call(kernel, name, operands, out_shape, scratch, flops, vmem=6, out=VM):
     return pl.pallas_call(
         kernel,
         out_shape=out_shape,
         in_specs=[VM] * len(operands),
-        out_specs=jax.tree.map(lambda _: VM, out_shape),
+        out_specs=jax.tree.map(lambda _: out, out_shape),
         scratch_shapes=scratch,
         compiler_params=pltpu.CompilerParams(vmem_limit_bytes=vmem * MIB),
         cost_estimate=pl.CostEstimate(flops=flops, bytes_accessed=12 << 20, transcendentals=0),
@@ -359,10 +383,12 @@
     return lax.ppermute(high, "block", up), lax.ppermute(low, "block", down)
 
 
-def exchanged(contributions):
-    left, low, high, right = contributions
+def exchanged(contributions, back_x):
+    left, right, turned = contributions
+    arrived = neighbours(left, right)
+    owns = call(own_kernel, "own", (back_x, turned), [OWN, OWN], [], 1 << 30, 12)
     pairs = []
-    for own, edge in zip((low, high), neighbours(left, right)):
+    for own, edge in zip(owns, arrived):
         payload = call(join_kernel, "join", (own, edge), PAYLOAD, [pltpu.VMEM(OWN.shape, F32)], 1 << 20)
         pairs.append((payload, lax.ppermute(payload, "view", [(0, 1), (1, 0)])))
     return pairs
@@ -402,10 +428,10 @@
         [*CONTRIB, jax.ShapeDtypeStruct((VIEWS_DEV * BX // TP, TROWS, Z), BF16)],
         BACK_SCRATCH,
         8 << 30,
-        28,
+        32,
     )
     halves = []
-    for i, (own, other) in enumerate(exchanged(contributions)):
+    for i, (own, other) in enumerate(exchanged(contributions, back[0])):
         halves.append(
             call(
                 functools.partial(update_kernel, view_count),
@@ -425,17 +451,18 @@
         CONTRIB,
         [*BACK_SCRATCH, pltpu.VMEM(BLURRED, F32)],
         14 << 30,
-        28,
-    )
-    payloads = [payload for pair in exchanged(contributions) for payload in pair]
+        34,
+    )
+    payloads = [payload for pair in exchanged(contributions, back[0]) for payload in pair]
     return call(
         functools.partial(last_kernel, view_count),
         "last_update",
         (low, high, *payloads),
         jax.ShapeDtypeStruct(estimate.shape, F32),
-        [],
+        [pltpu.VMEM(estimate.shape, F32), pltpu.SemaphoreType.DMA((2,))],
         1 << 20,
         10,
+        pl.BlockSpec(memory_space=pl.ANY),
     )
 
 

time: 178 us -> 178 us (level)
  waiting for transfers between devices: 94 us -> 91.3 us
  Pallas kernels: 31.2 us -> 33.1 us
    ppermute x8, waiting for transfers between devices: 18.6 us -> 15.7 us  [neighbours(): return (lax.ppermute(high, 'block', up), lax.ppermute(low, 'block', down))]
    pallas_call x11 -> x13, Pallas kernels: 30.1 us -> 32.1 us  [call(): pl.pallas_call(kernel, out_shape=out_shape, in_specs=[VM] * len(operands)...]
  transfers between devices with their start and end apart: 23 -> 23, of which waited for: 14 -> 14; matrix products, arithmetic and copies ran while one was open for 0% -> 0% of each run, Pallas kernels for 6% -> 8%
where the time goes in v9:
time: 178 us; the launch traced here: 177 us
  waiting for transfers between devices  91.3 us (51%)
  starting transfers between devices  49.3 us (28%)
  Pallas kernels  33.1 us (19%)
  other arithmetic  1.9 us (1%)
    ppermute x4, waiting for transfers between devices, exchanged(): pairs.append((payload, lax.ppermute(payload, 'view', [(0, 1), (1, 0)])))  47.8 us
    pallas_call x13, Pallas kernels, call(): pl.pallas_call(kernel, out_shape=out_shape, in_specs=[VM] * len(operands)...  32.1 us
    ppermute x11, waiting for transfers between devices, route(): lax.ppermute(packed[by + SPAN // 2], 'block', perm)  27.7 us
    ppermute x11, starting transfers between devices, route(): lax.ppermute(packed[by + SPAN // 2], 'block', perm)  21.7 us
    ppermute x8, starting transfers between devices, neighbours(): return (lax.ppermute(high, 'block', up), lax.ppermute(low, 'block', down))  21.3 us
    ppermute x8, waiting for transfers between devices, neighbours(): return (lax.ppermute(high, 'block', up), lax.ppermute(low, 'block', down))  15.7 us
    ppermute x4, starting transfers between devices, exchanged(): pairs.append((payload, lax.ppermute(payload, 'view', [(0, 1), (1, 0)])))  6.34 us
  transfers between devices with their start and end apart: 23, of which 14 were waited for; matrix products, arithmetic and copies ran while one was open for 0% of the time, Pallas kernels for 8%

profile of v9, /device:TPU:15, one launch (start us, length us, event | category | flops | bytes accessed | tf_op | source)
XLA Modules:
  0.0 177.3 jit_solution(3863589912485245723)
XLA Ops:
  0.0 1.9 %convert_element_type.3 = bf16[32,128,128]{2,1,0:T(8,128)(2,1)S(1)} convert(f32[32,128,128]{2,1,0:T(8,128)} %param.4) | non-fusion elementwise | flops 524288 | bytes 3145728 | tf_op jit(solution)/shard_map/convert_element_type | solution.py:408
  1.9 0.0 copy-start.1
  1.9 1.0 fusion.1
  3.0 4.1 %collective-permute-start = (bf16[16,128,128]{2,1,0:T(8,128)(2,1)}, bf16[16,128,128]{2,1,0:T(8,128)(2,1)}, u32[]{:S(2)}, u32[]{:S(2)}) collective-permute-start(bf16[16,128,128]{2,1,0:T(8,128)(2,1)} %get-tuple-element.84.refs_2_), channel_id=1, source_target_pairs={{0,1},{1,2},{2,3},{3,4},{4,5},{5,6},{6,7},{7,8},{8,9},{9,10},{10,1... | collective-permute-start | bytes 1572872 | tf_op jit(solution)/shard_map/ppermute | solution.py:383
  7.1 1.9 %collective-permute-start.1 = (bf16[16,128,128]{2,1,0:T(8,128)(2,1)}, bf16[16,128,128]{2,1,0:T(8,128)(2,1)}, u32[]{:S(2)}, u32[]{:S(2)}) collective-permute-start(bf16[16,128,128]{2,1,0:T(8,128)(2,1)} %get-tuple-element.83.refs_1_), channel_id=1, source_target_pairs={{1,0},{2,1},{3,2},{4,3},{5,4},{6,5},{7,6},{8,7},{9,8},{10,9},{11,1... | collective-permute-start | bytes 1572872 | tf_op jit(solution)/shard_map/ppermute | solution.py:383
  9.0 0.1 copy.6
  9.1 1.1 pack_tiles.1
  10.2 3.8 %collective-permute-start.10 = (bf16[1040,128]{1,0:T(8,128)(2,1)S(1)}, bf16[1040,128]{1,0:T(8,128)(2,1)S(1)}, u32[]{:S(2)}, u32[]{:S(2)}) collective-permute-start(bf16[1040,128]{1,0:T(8,128)(2,1)S(1)} %get-tuple-element.55), channel_id=1, source_target_pairs={{0,3},{1,4},{2,5},{3,6},{4,7},{5,8},{6,9},{7,10},{8,11},{9,12},{10... | collective-permute-start | bytes 798728 | tf_op jit(solution)/shard_map/ppermute | solution.py:406
  13.9 0.0 collective-permute-start.11
  13.9 2.0 %collective-permute-start.12 = (bf16[1040,128]{1,0:T(8,128)(2,1)S(1)}, bf16[1040,128]{1,0:T(8,128)(2,1)S(1)}, u32[]{:S(2)}, u32[]{:S(2)}) collective-permute-start(bf16[1040,128]{1,0:T(8,128)(2,1)S(1)} %get-tuple-element.57), channel_id=1, source_target_pairs={{0,5},{1,6},{2,7},{3,8},{4,9},{5,10},{6,11},{7,12},{8,13},{9,14},{... | collective-permute-start | bytes 798728 | tf_op jit(solution)/shard_map/ppermute | solution.py:406
  16.0 0.7 prepare.1
  16.7 5.5 %collective-permute-done.10.refs_9_ = bf16[1040,128]{1,0:T(8,128)(2,1)S(1)} collective-permute-done((bf16[1040,128]{1,0:T(8,128)(2,1)S(1)}, bf16[1040,128]{1,0:T(8,128)(2,1)S(1)}, u32[]{:S(2)}, u32[]{:S(2)}) %collective-permute-start.10) | collective-permute-done | bytes 266272 | tf_op jit(solution)/shard_map/ppermute | solution.py:406
  22.2 1.9 %collective-permute-start.2 = (bf16[1040,128]{1,0:T(8,128)(2,1)S(1)}, bf16[1040,128]{1,0:T(8,128)(2,1)S(1)}, u32[]{:S(2)}, u32[]{:S(2)}) collective-permute-start(bf16[1040,128]{1,0:T(8,128)(2,1)S(1)} %get-tuple-element.46), channel_id=1, source_target_pairs={{0,58},{1,59},{2,60},{3,61},{4,62},{5,63},{6,0},{7,1},{8,2},{9,3},... | collective-permute-start | bytes 798728 | tf_op jit(solution)/shard_map/ppermute | solution.py:406
  24.1 0.0 collective-permute-done.refs_0_
  24.1 7.5 %collective-permute-start.3 = (bf16[1040,128]{1,0:T(8,128)(2,1)S(1)}, bf16[1040,128]{1,0:T(8,128)(2,1)S(1)}, u32[]{:S(2)}, u32[]{:S(2)}) collective-permute-start(bf16[1040,128]{1,0:T(8,128)(2,1)S(1)} %get-tuple-element.47), channel_id=1, source_target_pairs={{0,59},{1,60},{2,61},{3,62},{4,63},{5,0},{6,1},{7,2},{8,3},{9,4},{... | collective-permute-start | bytes 798728 | tf_op jit(solution)/shard_map/ppermute | solution.py:406
  31.5 0.0 collective-permute-done.1.refs_3_
  31.5 4.4 %collective-permute-start.4 = (bf16[1040,128]{1,0:T(8,128)(2,1)S(1)}, bf16[1040,128]{1,0:T(8,128)(2,1)S(1)}, u32[]{:S(2)}, u32[]{:S(2)}) collective-permute-start(bf16[1040,128]{1,0:T(8,128)(2,1)S(1)} %get-tuple-element.48), channel_id=1, source_target_pairs={{0,60},{1,61},{2,62},{3,63},{4,0},{5,1},{6,2},{7,3},{8,4},{9,5},{1... | collective-permute-start | bytes 798728 | tf_op jit(solution)/shard_map/ppermute | solution.py:406
  35.9 6.7 %first_blur.1.blurred_ref = f32[24,512,128]{2,1,0:T(8,128)S(1)} custom-call(bf16[96,64]{1,0:T(8,128)(2,1)S(1)} %get-tuple-element.58.kx_ref.refs_0_, bf16[3,128,128]{2,1,0:T(8,128)(2,1)S(1)} %get-tuple-element.59.ky_ref.refs_1_, bf16[3,256,256]{2,1,0:T(8,128)(2,1)S(1)} %get-tuple-element.60.kz_ref.refs_2_, ...), custom_call_target="tpu_custom_call" | custom-call | flops 6442450944 | bytes 12582912 | tf_op jit(solution)/shard_map/first_blur/pallas_call | solution.py:367
  42.6 0.0 collective-permute-done.11.refs_10_
  42.6 0.1 collective-permute-start.5
  42.7 0.0 collective-permute-done.12.refs_11_
  42.7 0.1 collective-permute-start.6
  42.8 0.0 collective-permute-done.2.refs_0_
  42.8 0.5 collective-permute-start.7
  43.3 1.5 collective-permute-start.8
  44.8 8.0 %collective-permute-done.4.refs_2_ = bf16[1040,128]{1,0:T(8,128)(2,1)S(1)} collective-permute-done((bf16[1040,128]{1,0:T(8,128)(2,1)S(1)}, bf16[1040,128]{1,0:T(8,128)(2,1)S(1)}, u32[]{:S(2)}, u32[]{:S(2)}) %collective-permute-start.4) | collective-permute-done | bytes 266272 | tf_op jit(solution)/shard_map/ppermute | solution.py:406
  52.8 0.0 collective-permute-start.9
  52.8 0.4 collective-permute-done.5.refs_3_
  53.3 11.8 %collective-permute-done.6.refs_4_ = bf16[1040,128]{1,0:T(8,128)(2,1)S(1)} collective-permute-done((bf16[1040,128]{1,0:T(8,128)(2,1)S(1)}, bf16[1040,128]{1,0:T(8,128)(2,1)S(1)}, u32[]{:S(2)}, u32[]{:S(2)}) %collective-permute-start.6) | collective-permute-done | bytes 266272 | tf_op jit(solution)/shard_map/ppermute | solution.py:406
  65.0 0.9 collective-permute-done.7.refs_5_
  65.9 0.0 collective-permute-done.8.refs_7_
  65.9 1.2 collective-permute-done.9.refs_8_
  67.1 6.4 %first_back.1 = (s16[2064,128]{1,0:T(8,128)(2,1)S(1)}, s16[2064,128]{1,0:T(8,128)(2,1)S(1)}, bf16[128,192,128]{2,1,0:T(8,128)(2,1)S(1)}, bf16[24,512,128]{2,1,0:T(8,128)(2,1)S(1)}) custom-call(bf16[64,192]{1,0:T(8,128)(2,1)S(1)} %get-tuple-element.43.kx_ref.refs_3_, bf16[3,128,128]{2,1,0:T(8,128)(2,1)S(1)} %get-tuple-element.44.ky_ref.refs_4_, ...), custom_call_target="tpu_custom_call" | custom-call | flops 8589934592 | bytes 12582912 | tf_op jit(solution)/shard_map/first_back/pallas_call | solution.py:367
  73.5 1.9 %collective-permute-start.15 = (s16[2064,128]{1,0:T(8,128)(2,1)S(1)}, s16[2064,128]{1,0:T(8,128)(2,1)S(1)}, u32[]{:S(2)}, u32[]{:S(2)}) collective-permute-start(s16[2064,128]{1,0:T(8,128)(2,1)S(1)} %get-tuple-element.71), channel_id=1, source_target_pairs={{1,0},{2,1},{3,2},{4,3},{5,4},{6,5},{7,6},{8,7},{9,8},{10,9},{11,1... | collective-permute-start | bytes 1585160 | tf_op jit(solution)/shard_map/ppermute | solution.py:383
  75.5 3.6 %collective-permute-start.13 = (s16[2064,128]{1,0:T(8,128)(2,1)S(1)}, s16[2064,128]{1,0:T(8,128)(2,1)S(1)}, u32[]{:S(2)}, u32[]{:S(2)}) collective-permute-start(s16[2064,128]{1,0:T(8,128)(2,1)S(1)} %get-tuple-element.68), channel_id=1, source_target_pairs={{0,1},{1,2},{2,3},{3,4},{4,5},{5,6},{6,7},{7,8},{8,9},{9,10},{10,1... | collective-permute-start | bytes 1585160 | tf_op jit(solution)/shard_map/ppermute | solution.py:383
  79.1 1.5 own.2
  80.6 0.0 copy-start.2
  80.6 3.8 %collective-permute-done.15.edge_ref = s16[2064,128]{1,0:T(8,128)(2,1)S(1)} collective-permute-done((s16[2064,128]{1,0:T(8,128)(2,1)S(1)}, s16[2064,128]{1,0:T(8,128)(2,1)S(1)}, u32[]{:S(2)}, u32[]{:S(2)}) %collective-permute-start.15) | collective-permute-done | bytes 528416 | tf_op jit(solution)/shard_map/ppermute | solution.py:383
  84.4 0.3 join.5.own_ref
  84.7 2.3 %collective-permute-start.16 = (s16[2064,128]{1,0:T(8,128)(2,1)S(1)}, s16[2064,128]{1,0:T(8,128)(2,1)S(1)}, u32[]{:S(2)}, u32[]{:S(2)}) collective-permute-start(s16[2064,128]{1,0:T(8,128)(2,1)S(1)} %join.5.own_ref), channel_id=1, source_target_pairs={{0,64},{64,0},{1,65},{65,1},{2,66},{66,2},{3,67},{67,3},{4,68},{68... | collective-permute-start | bytes 1585160 | tf_op jit(solution)/shard_map/ppermute | solution.py:393
  87.0 0.3 join.4.own_ref
  87.3 1.0 collective-permute-start.14
  88.4 0.1 fusion
  88.5 14.4 %collective-permute-done.16.other_ref = s16[2064,128]{1,0:T(8,128)(2,1)S(1)} collective-permute-done((s16[2064,128]{1,0:T(8,128)(2,1)S(1)}, s16[2064,128]{1,0:T(8,128)(2,1)S(1)}, u32[]{:S(2)}, u32[]{:S(2)}) %collective-permute-start.16) | collective-permute-done | bytes 528416 | tf_op jit(solution)/shard_map/ppermute | solution.py:393
  102.9 0.4 update.3
  103.3 1.9 %collective-permute-start.17 = (bf16[16,128,128]{2,1,0:T(8,128)(2,1)S(1)}, bf16[16,128,128]{2,1,0:T(8,128)(2,1)S(1)}, u32[]{:S(2)}, u32[]{:S(2)}) collective-permute-start(bf16[16,128,128]{2,1,0:T(8,128)(2,1)S(1)} %get-tuple-element.73.refs_8_), channel_id=1, source_target_pairs={{0,1},{1,2},{2,3},{3,4},{4,5},{5,6},{6,7},{7,8},{8,9},{9,10},{10,1... | collective-permute-start | bytes 1572872 | tf_op jit(solution)/shard_map/ppermute | solution.py:383
  105.2 8.9 %collective-permute-done.14.other_ref = s16[2064,128]{1,0:T(8,128)(2,1)S(1)} collective-permute-done((s16[2064,128]{1,0:T(8,128)(2,1)S(1)}, s16[2064,128]{1,0:T(8,128)(2,1)S(1)}, u32[]{:S(2)}, u32[]{:S(2)}) %collective-permute-start.14) | collective-permute-done | bytes 528416 | tf_op jit(solution)/shard_map/ppermute | solution.py:393
  114.1 0.4 update.2
  114.5 2.2 %collective-permute-start.18 = (bf16[16,128,128]{2,1,0:T(8,128)(2,1)S(1)}, bf16[16,128,128]{2,1,0:T(8,128)(2,1)S(1)}, u32[]{:S(2)}, u32[]{:S(2)}) collective-permute-start(bf16[16,128,128]{2,1,0:T(8,128)(2,1)S(1)} %get-tuple-element.74.refs_7_), channel_id=1, source_target_pairs={{1,0},{2,1},{3,2},{4,3},{5,4},{6,5},{7,6},{8,7},{9,8},{10,9},{11,1... | collective-permute-start | bytes 1572872 | tf_op jit(solution)/shard_map/ppermute | solution.py:383
  116.7 0.0 collective-permute-done.17.refs_6_
  116.7 8.3 %collective-permute-done.18.refs_9_ = bf16[16,128,128]{2,1,0:T(8,128)(2,1)S(1)} collective-permute-done((bf16[16,128,128]{2,1,0:T(8,128)(2,1)S(1)}, bf16[16,128,128]{2,1,0:T(8,128)(2,1)S(1)}, u32[]{:S(2)}, u32[]{:S(2)}) %collective-permute-start.18) | collective-permute-done | bytes 524320 | tf_op jit(solution)/shard_map/ppermute | solution.py:383
  125.0 11.5 %sweep.1 = (s16[2064,128]{1,0:T(8,128)(2,1)S(1)}, s16[2064,128]{1,0:T(8,128)(2,1)S(1)}, bf16[128,192,128]{2,1,0:T(8,128)(2,1)S(1)}) custom-call(bf16[96,64]{1,0:T(8,128)(2,1)S(1)} %get-tuple-element.58.kx_ref.refs_0_, bf16[3,128,128]{2,1,0:T(8,128)(2,1)S(1)} %get-tuple-element.59.ky_ref.refs_1_, bf16[3,256,256]{2,1,0:T(8,128)(2,1)S(1)} %get-tuple-element.60.kz_ref.refs_2_, ...), custom_call_target="tpu_custom_call" | custom-call | flops 15032385536 | bytes 12582912 | tf_op jit(solution)/shard_map/sweep/pallas_call | solution.py:367
  136.5 1.9 %collective-permute-start.21 = (s16[2064,128]{1,0:T(8,128)(2,1)S(1)}, s16[2064,128]{1,0:T(8,128)(2,1)S(1)}, u32[]{:S(2)}, u32[]{:S(2)}) collective-permute-start(s16[2064,128]{1,0:T(8,128)(2,1)S(1)} %get-tuple-element.80), channel_id=1, source_target_pairs={{1,0},{2,1},{3,2},{4,3},{5,4},{6,5},{7,6},{8,7},{9,8},{10,9},{11,1... | collective-permute-start | bytes 1585160 | tf_op jit(solution)/shard_map/ppermute | solution.py:383
  138.5 3.6 %collective-permute-start.19 = (s16[2064,128]{1,0:T(8,128)(2,1)S(1)}, s16[2064,128]{1,0:T(8,128)(2,1)S(1)}, u32[]{:S(2)}, u32[]{:S(2)}) collective-permute-start(s16[2064,128]{1,0:T(8,128)(2,1)S(1)} %get-tuple-element.78), channel_id=1, source_target_pairs={{0,1},{1,2},{2,3},{3,4},{4,5},{5,6},{6,7},{7,8},{8,9},{9,10},{10,1... | collective-permute-start | bytes 1585160 | tf_op jit(solution)/shard_map/ppermute | solution.py:383
  142.1 1.4 own.3
  143.6 3.5 %collective-permute-done.21.edge_ref = s16[2064,128]{1,0:T(8,128)(2,1)S(1)} collective-permute-done((s16[2064,128]{1,0:T(8,128)(2,1)S(1)}, s16[2064,128]{1,0:T(8,128)(2,1)S(1)}, u32[]{:S(2)}, u32[]{:S(2)}) %collective-permute-start.21) | collective-permute-done | bytes 528416 | tf_op jit(solution)/shard_map/ppermute | solution.py:383
  147.1 0.3 join.7.refs_2_
  147.4 0.7 collective-permute-start.22
  148.2 0.1 collective-permute-done.19.edge_ref
  148.3 0.3 join.6.refs_0_
  148.6 2.3 %collective-permute-start.20 = (s16[2064,128]{1,0:T(8,128)(2,1)S(1)}, s16[2064,128]{1,0:T(8,128)(2,1)S(1)}, u32[]{:S(2)}, u32[]{:S(2)}) collective-permute-start(s16[2064,128]{1,0:T(8,128)(2,1)S(1)} %join.6.refs_0_), channel_id=1, source_target_pairs={{0,64},{64,0},{1,65},{65,1},{2,66},{66,2},{3,67},{67,3},{4,68},{68... | collective-permute-start | bytes 1585160 | tf_op jit(solution)/shard_map/ppermute | solution.py:393
  150.9 13.2 %collective-permute-done.22.refs_3_ = s16[2064,128]{1,0:T(8,128)(2,1)S(1)} collective-permute-done((s16[2064,128]{1,0:T(8,128)(2,1)S(1)}, s16[2064,128]{1,0:T(8,128)(2,1)S(1)}, u32[]{:S(2)}, u32[]{:S(2)}) %collective-permute-start.22) | collective-permute-done | bytes 528416 | tf_op jit(solution)/shard_map/ppermute | solution.py:393
  164.1 11.3 %collective-permute-done.20.refs_1_ = s16[2064,128]{1,0:T(8,128)(2,1)S(1)} collective-permute-done((s16[2064,128]{1,0:T(8,128)(2,1)S(1)}, s16[2064,128]{1,0:T(8,128)(2,1)S(1)}, u32[]{:S(2)}, u32[]{:S(2)}) %collective-permute-start.20) | collective-permute-done | bytes 528416 | tf_op jit(solution)/shard_map/ppermute | solution.py:393
  175.4 1.7 last_update.1
  (8 shorter events, 0.0 us)
Async XLA Ops:
  0.0 9.0 %copy-start.3 = (s32[1,24,3]{1,0,2:T(1,128)S(1)}, s32[1,24,3]{1,0,2:T(1,128)}, u32[]{:S(2)}) copy-start(s32[1,24,3]{1,0,2:T(1,128)} %param.6) | copy-start | bytes 868
  0.0 9.1 %copy-start = (bf16[1,24,4,128,128]{4,3,2,1,0:T(8,128)(2,1)S(1)}, bf16[1,24,4,128,128]{4,3,2,1,0:T(8,128)(2,1)}, u32[]{:S(2)}) copy-start(bf16[1,24,4,128,128]{4,3,2,1,0:T(8,128)(2,1)} %param.5) | copy-start | bytes 9437188
  1.9 14.1 %copy-start.1 = (f32[3,3,31]{2,1,0:T(4,128)S(1)}, f32[3,3,31]{2,1,0:T(4,128)}, u32[]{:S(2)}) copy-start(f32[3,3,31]{2,1,0:T(4,128)} %psf_ref.1) | copy-start | bytes 3352
  3.0 21.1 %collective-permute-start = (bf16[16,128,128]{2,1,0:T(8,128)(2,1)}, bf16[16,128,128]{2,1,0:T(8,128)(2,1)}, u32[]{:S(2)}, u32[]{:S(2)}) collective-permute-start(bf16[16,128,128]{2,1,0:T(8,128)(2,1)} %get-tuple-element.84.refs_2_), channel_id=1, source_target_pairs={{0,1},{1,2},{2,3},{3,4},{4,5},{5,6},{6,7},{7,8},{8,9},{9,10},{10,1... | collective-permute-start | bytes 1572872 | tf_op jit(solution)/shard_map/ppermute | solution.py:383
  7.1 24.5 %collective-permute-start.1 = (bf16[16,128,128]{2,1,0:T(8,128)(2,1)}, bf16[16,128,128]{2,1,0:T(8,128)(2,1)}, u32[]{:S(2)}, u32[]{:S(2)}) collective-permute-start(bf16[16,128,128]{2,1,0:T(8,128)(2,1)} %get-tuple-element.83.refs_1_), channel_id=1, source_target_pairs={{1,0},{2,1},{3,2},{4,3},{5,4},{6,5},{7,6},{8,7},{9,8},{10,9},{11,1... | collective-permute-start | bytes 1572872 | tf_op jit(solution)/shard_map/ppermute | solution.py:383
  10.2 12.0 %collective-permute-start.10 = (bf16[1040,128]{1,0:T(8,128)(2,1)S(1)}, bf16[1040,128]{1,0:T(8,128)(2,1)S(1)}, u32[]{:S(2)}, u32[]{:S(2)}) collective-permute-start(bf16[1040,128]{1,0:T(8,128)(2,1)S(1)} %get-tuple-element.55), channel_id=1, source_target_pairs={{0,3},{1,4},{2,5},{3,6},{4,7},{5,8},{6,9},{7,10},{8,11},{9,12},{10... | collective-permute-start | bytes 798728 | tf_op jit(solution)/shard_map/ppermute | solution.py:406
  13.9 28.7 %collective-permute-start.11 = (bf16[1040,128]{1,0:T(8,128)(2,1)S(1)}, bf16[1040,128]{1,0:T(8,128)(2,1)S(1)}, u32[]{:S(2)}, u32[]{:S(2)}) collective-permute-start(bf16[1040,128]{1,0:T(8,128)(2,1)S(1)} %get-tuple-element.56), channel_id=1, source_target_pairs={{0,4},{1,5},{2,6},{3,7},{4,8},{5,9},{6,10},{7,11},{8,12},{9,13},{1... | collective-permute-start | bytes 798728 | tf_op jit(solution)/shard_map/ppermute | solution.py:406
  13.9 28.8 %collective-permute-start.12 = (bf16[1040,128]{1,0:T(8,128)(2,1)S(1)}, bf16[1040,128]{1,0:T(8,128)(2,1)S(1)}, u32[]{:S(2)}, u32[]{:S(2)}) collective-permute-start(bf16[1040,128]{1,0:T(8,128)(2,1)S(1)} %get-tuple-element.57), channel_id=1, source_target_pairs={{0,5},{1,6},{2,7},{3,8},{4,9},{5,10},{6,11},{7,12},{8,13},{9,14},{... | collective-permute-start | bytes 798728 | tf_op jit(solution)/shard_map/ppermute | solution.py:406
  22.2 20.6 %collective-permute-start.2 = (bf16[1040,128]{1,0:T(8,128)(2,1)S(1)}, bf16[1040,128]{1,0:T(8,128)(2,1)S(1)}, u32[]{:S(2)}, u32[]{:S(2)}) collective-permute-start(bf16[1040,128]{1,0:T(8,128)(2,1)S(1)} %get-tuple-element.46), channel_id=1, source_target_pairs={{0,58},{1,59},{2,60},{3,61},{4,62},{5,63},{6,0},{7,1},{8,2},{9,3},... | collective-permute-start | bytes 798728 | tf_op jit(solution)/shard_map/ppermute | solution.py:406
  24.1 19.2 %collective-permute-start.3 = (bf16[1040,128]{1,0:T(8,128)(2,1)S(1)}, bf16[1040,128]{1,0:T(8,128)(2,1)S(1)}, u32[]{:S(2)}, u32[]{:S(2)}) collective-permute-start(bf16[1040,128]{1,0:T(8,128)(2,1)S(1)} %get-tuple-element.47), channel_id=1, source_target_pairs={{0,59},{1,60},{2,61},{3,62},{4,63},{5,0},{6,1},{7,2},{8,3},{9,4},{... | collective-permute-start | bytes 798728 | tf_op jit(solution)/shard_map/ppermute | solution.py:406
  31.5 21.3 %collective-permute-start.4 = (bf16[1040,128]{1,0:T(8,128)(2,1)S(1)}, bf16[1040,128]{1,0:T(8,128)(2,1)S(1)}, u32[]{:S(2)}, u32[]{:S(2)}) collective-permute-start(bf16[1040,128]{1,0:T(8,128)(2,1)S(1)} %get-tuple-element.48), channel_id=1, source_target_pairs={{0,60},{1,61},{2,62},{3,63},{4,0},{5,1},{6,2},{7,3},{8,4},{9,5},{1... | collective-permute-start | bytes 798728 | tf_op jit(solution)/shard_map/ppermute | solution.py:406
  42.6 10.6 %collective-permute-start.5 = (bf16[1040,128]{1,0:T(8,128)(2,1)S(1)}, bf16[1040,128]{1,0:T(8,128)(2,1)S(1)}, u32[]{:S(2)}, u32[]{:S(2)}) collective-permute-start(bf16[1040,128]{1,0:T(8,128)(2,1)S(1)} %get-tuple-element.49), channel_id=1, source_target_pairs={{0,61},{1,62},{2,63},{3,0},{4,1},{5,2},{6,3},{7,4},{8,5},{9,6},{10... | collective-permute-start | bytes 798728 | tf_op jit(solution)/shard_map/ppermute | solution.py:406
  42.7 22.3 %collective-permute-start.6 = (bf16[1040,128]{1,0:T(8,128)(2,1)S(1)}, bf16[1040,128]{1,0:T(8,128)(2,1)S(1)}, u32[]{:S(2)}, u32[]{:S(2)}) collective-permute-start(bf16[1040,128]{1,0:T(8,128)(2,1)S(1)} %get-tuple-element.62), channel_id=1, source_target_pairs={{0,62},{1,63},{2,0},{3,1},{4,2},{5,3},{6,4},{7,5},{8,6},{9,7},{10,... | collective-permute-start | bytes 798728 | tf_op jit(solution)/shard_map/ppermute | solution.py:406
  42.8 23.1 %collective-permute-start.7 = (bf16[1040,128]{1,0:T(8,128)(2,1)S(1)}, bf16[1040,128]{1,0:T(8,128)(2,1)S(1)}, u32[]{:S(2)}, u32[]{:S(2)}) collective-permute-start(bf16[1040,128]{1,0:T(8,128)(2,1)S(1)} %get-tuple-element.63), channel_id=1, source_target_pairs={{0,63},{1,0},{2,1},{3,2},{4,3},{5,4},{6,5},{7,6},{8,7},{9,8},{10,9... | collective-permute-start | bytes 798728 | tf_op jit(solution)/shard_map/ppermute | solution.py:406
  43.3 22.6 %collective-permute-start.8 = (bf16[1040,128]{1,0:T(8,128)(2,1)S(1)}, bf16[1040,128]{1,0:T(8,128)(2,1)S(1)}, u32[]{:S(2)}, u32[]{:S(2)}) collective-permute-start(bf16[1040,128]{1,0:T(8,128)(2,1)S(1)} %get-tuple-element.64), channel_id=1, source_target_pairs={{0,1},{1,2},{2,3},{3,4},{4,5},{5,6},{6,7},{7,8},{8,9},{9,10},{10,1... | collective-permute-start | bytes 798728 | tf_op jit(solution)/shard_map/ppermute | solution.py:406
  52.8 14.2 %collective-permute-start.9 = (bf16[1040,128]{1,0:T(8,128)(2,1)S(1)}, bf16[1040,128]{1,0:T(8,128)(2,1)S(1)}, u32[]{:S(2)}, u32[]{:S(2)}) collective-permute-start(bf16[1040,128]{1,0:T(8,128)(2,1)S(1)} %get-tuple-element.65), channel_id=1, source_target_pairs={{0,2},{1,3},{2,4},{3,5},{4,6},{5,7},{6,8},{7,9},{8,10},{9,11},{10,... | collective-permute-start | bytes 798728 | tf_op jit(solution)/shard_map/ppermute | solution.py:406
  73.5 10.8 %collective-permute-start.15 = (s16[2064,128]{1,0:T(8,128)(2,1)S(1)}, s16[2064,128]{1,0:T(8,128)(2,1)S(1)}, u32[]{:S(2)}, u32[]{:S(2)}) collective-permute-start(s16[2064,128]{1,0:T(8,128)(2,1)S(1)} %get-tuple-element.71), channel_id=1, source_target_pairs={{1,0},{2,1},{3,2},{4,3},{5,4},{6,5},{7,6},{8,7},{9,8},{10,9},{11,1... | collective-permute-start | bytes 1585160 | tf_op jit(solution)/shard_map/ppermute | solution.py:383
  75.5 11.5 %collective-permute-start.13 = (s16[2064,128]{1,0:T(8,128)(2,1)S(1)}, s16[2064,128]{1,0:T(8,128)(2,1)S(1)}, u32[]{:S(2)}, u32[]{:S(2)}) collective-permute-start(s16[2064,128]{1,0:T(8,128)(2,1)S(1)} %get-tuple-element.68), channel_id=1, source_target_pairs={{0,1},{1,2},{2,3},{3,4},{4,5},{5,6},{6,7},{7,8},{8,9},{9,10},{10,1... | collective-permute-start | bytes 1585160 | tf_op jit(solution)/shard_map/ppermute | solution.py:383
  80.6 7.8 %copy-start.2 = (f32[32,128,128]{2,1,0:T(8,128)S(1)}, f32[32,128,128]{2,1,0:T(8,128)}, u32[]{:S(2)}) copy-start(f32[32,128,128]{2,1,0:T(8,128)} %param.4) | copy-start | bytes 6291460
  84.7 18.2 %collective-permute-start.16 = (s16[2064,128]{1,0:T(8,128)(2,1)S(1)}, s16[2064,128]{1,0:T(8,128)(2,1)S(1)}, u32[]{:S(2)}, u32[]{:S(2)}) collective-permute-start(s16[2064,128]{1,0:T(8,128)(2,1)S(1)} %join.5.own_ref), channel_id=1, source_target_pairs={{0,64},{64,0},{1,65},{65,1},{2,66},{66,2},{3,67},{67,3},{4,68},{68... | collective-permute-start | bytes 1585160 | tf_op jit(solution)/shard_map/ppermute | solution.py:393
  87.3 26.8 %collective-permute-start.14 = (s16[2064,128]{1,0:T(8,128)(2,1)S(1)}, s16[2064,128]{1,0:T(8,128)(2,1)S(1)}, u32[]{:S(2)}, u32[]{:S(2)}) collective-permute-start(s16[2064,128]{1,0:T(8,128)(2,1)S(1)} %join.4.own_ref), channel_id=1, source_target_pairs={{0,64},{64,0},{1,65},{65,1},{2,66},{66,2},{3,67},{67,3},{4,68},{68... | collective-permute-start | bytes 1585160 | tf_op jit(solution)/shard_map/ppermute | solution.py:393
  103.3 13.4 %collective-permute-start.17 = (bf16[16,128,128]{2,1,0:T(8,128)(2,1)S(1)}, bf16[16,128,128]{2,1,0:T(8,128)(2,1)S(1)}, u32[]{:S(2)}, u32[]{:S(2)}) collective-permute-start(bf16[16,128,128]{2,1,0:T(8,128)(2,1)S(1)} %get-tuple-element.73.refs_8_), channel_id=1, source_target_pairs={{0,1},{1,2},{2,3},{3,4},{4,5},{5,6},{6,7},{7,8},{8,9},{9,10},{10,1... | collective-permute-start | bytes 1572872 | tf_op jit(solution)/shard_map/ppermute | solution.py:383
  114.5 10.5 %collective-permute-start.18 = (bf16[16,128,128]{2,1,0:T(8,128)(2,1)S(1)}, bf16[16,128,128]{2,1,0:T(8,128)(2,1)S(1)}, u32[]{:S(2)}, u32[]{:S(2)}) collective-permute-start(bf16[16,128,128]{2,1,0:T(8,128)(2,1)S(1)} %get-tuple-element.74.refs_7_), channel_id=1, source_target_pairs={{1,0},{2,1},{3,2},{4,3},{5,4},{6,5},{7,6},{8,7},{9,8},{10,9},{11,1... | collective-permute-start | bytes 1572872 | tf_op jit(solution)/shard_map/ppermute | solution.py:383
  136.5 10.5 %collective-permute-start.21 = (s16[2064,128]{1,0:T(8,128)(2,1)S(1)}, s16[2064,128]{1,0:T(8,128)(2,1)S(1)}, u32[]{:S(2)}, u32[]{:S(2)}) collective-permute-start(s16[2064,128]{1,0:T(8,128)(2,1)S(1)} %get-tuple-element.80), channel_id=1, source_target_pairs={{1,0},{2,1},{3,2},{4,3},{5,4},{6,5},{7,6},{8,7},{9,8},{10,9},{11,1... | collective-permute-start | bytes 1585160 | tf_op jit(solution)/shard_map/ppermute | solution.py:383
  138.5 9.8 %collective-permute-start.19 = (s16[2064,128]{1,0:T(8,128)(2,1)S(1)}, s16[2064,128]{1,0:T(8,128)(2,1)S(1)}, u32[]{:S(2)}, u32[]{:S(2)}) collective-permute-start(s16[2064,128]{1,0:T(8,128)(2,1)S(1)} %get-tuple-element.78), channel_id=1, source_target_pairs={{0,1},{1,2},{2,3},{3,4},{4,5},{5,6},{6,7},{7,8},{8,9},{9,10},{10,1... | collective-permute-start | bytes 1585160 | tf_op jit(solution)/shard_map/ppermute | solution.py:383
  147.4 16.7 %collective-permute-start.22 = (s16[2064,128]{1,0:T(8,128)(2,1)S(1)}, s16[2064,128]{1,0:T(8,128)(2,1)S(1)}, u32[]{:S(2)}, u32[]{:S(2)}) collective-permute-start(s16[2064,128]{1,0:T(8,128)(2,1)S(1)} %join.7.refs_2_), channel_id=1, source_target_pairs={{0,64},{64,0},{1,65},{65,1},{2,66},{66,2},{3,67},{67,3},{4,68},{68... | collective-permute-start | bytes 1585160 | tf_op jit(solution)/shard_map/ppermute | solution.py:393
  148.6 26.8 %collective-permute-start.20 = (s16[2064,128]{1,0:T(8,128)(2,1)S(1)}, s16[2064,128]{1,0:T(8,128)(2,1)S(1)}, u32[]{:S(2)}, u32[]{:S(2)}) collective-permute-start(s16[2064,128]{1,0:T(8,128)(2,1)S(1)} %join.6.refs_0_), channel_id=1, source_target_pairs={{0,64},{64,0},{1,65},{65,1},{2,66},{66,2},{3,67},{67,3},{4,68},{68... | collective-permute-start | bytes 1585160 | tf_op jit(solution)/shard_map/ppermute | solution.py:393

commit v10 on v9

--- a/solution.py
+++ b/solution.py
@@ -336,15 +336,18 @@
     update_planes(view_count, before_ref, own_ref, other_ref, out_refs)
 
 
-def last_kernel(view_count, low_ref, high_ref, *refs):
-    *payloads, out_ref, plane_ref, sems = refs
-    copies = []
-    for i, before_ref in enumerate((low_ref, high_ref)):
-        own_ref, other_ref = payloads[2 * i : 2 * i + 2]
-        part = pl.ds(i * HX, HX)
-        update_planes(view_count, before_ref, own_ref, other_ref, (plane_ref.at[part],))
-        copies.append(pltpu.make_async_copy(plane_ref.at[part], out_ref.at[part], sems.at[i]))
-        copies[-1].start()
+def low_kernel(view_count, before_ref, own_ref, other_ref, out_ref):
+    update_planes(view_count, before_ref, own_ref, other_ref, (out_ref,))
+
+
+def last_kernel(view_count, low_ref, before_ref, own_ref, other_ref, out_ref, high_ref, sems):
+    copies = [
+        pltpu.make_async_copy(ref, out_ref.at[pl.ds(i * HX, HX)], sems.at[i])
+        for i, ref in enumerate((low_ref, high_ref))
+    ]
+    copies[0].start()
+    update_planes(view_count, before_ref, own_ref, other_ref, (high_ref,))
+    copies[1].start()
     for copy in copies:
         copy.wait()
 
@@ -453,13 +456,16 @@
         14 << 30,
         34,
     )
-    payloads = [payload for pair in exchanged(contributions, back[0]) for payload in pair]
+    low_pair, high_pair = exchanged(contributions, back[0])
+    low = call(
+        functools.partial(low_kernel, view_count), "low_update", (low, *low_pair), OWN, [], 1 << 20
+    )
     return call(
         functools.partial(last_kernel, view_count),
         "last_update",
-        (low, high, *payloads),
+        (low, high, *high_pair),
         jax.ShapeDtypeStruct(estimate.shape, F32),
-        [pltpu.VMEM(estimate.shape, F32), pltpu.SemaphoreType.DMA((2,))],
+        [pltpu.VMEM(OWN.shape, F32), pltpu.SemaphoreType.DMA((2,))],
         1 << 20,
         10,
         pl.BlockSpec(memory_space=pl.ANY),

time: 178 us -> 179 us (level)
  waiting for transfers between devices: 91.3 us -> 95.6 us
  starting transfers between devices: 49.3 us -> 46.5 us
    ppermute x4, waiting for transfers between devices: 47.8 us -> 50.2 us  [exchanged(): pairs.append((payload, lax.ppermute(payload, 'view', [(0, 1), (1, 0)])))]
    ppermute x8, waiting for transfers between devices: 15.7 us -> 17.7 us  [neighbours(): return (lax.ppermute(high, 'block', up), lax.ppermute(low, 'block', down))]
    pallas_call x13 -> x14, Pallas kernels: 32.1 us -> 32 us  [call(): pl.pallas_call(kernel, out_shape=out_shape, in_specs=[VM] * len(operands)...]
where the time goes in v10:
time: 179 us
  waiting for transfers between devices  95.6 us (53%)
  starting transfers between devices  46.5 us (26%)
  Pallas kernels  33.1 us (18%)
  other arithmetic  1.9 us (1%)
    ppermute x4, waiting for transfers between devices, exchanged(): pairs.append((payload, lax.ppermute(payload, 'view', [(0, 1), (1, 0)])))  50.2 us
    pallas_call x14, Pallas kernels, call(): pl.pallas_call(kernel, out_shape=out_shape, in_specs=[VM] * len(operands)...  32 us
    ppermute x11, waiting for transfers between devices, route(): lax.ppermute(packed[by + SPAN // 2], 'block', perm)  27.7 us
    ppermute x11, starting transfers between devices, route(): lax.ppermute(packed[by + SPAN // 2], 'block', perm)  21.7 us
    ppermute x8, starting transfers between devices, neighbours(): return (lax.ppermute(high, 'block', up), lax.ppermute(low, 'block', down))  20 us
    ppermute x8, waiting for transfers between devices, neighbours(): return (lax.ppermute(high, 'block', up), lax.ppermute(low, 'block', down))  17.7 us
    ppermute x4, starting transfers between devices, exchanged(): pairs.append((payload, lax.ppermute(payload, 'view', [(0, 1), (1, 0)])))  4.79 us
  transfers between devices with their start and end apart: 23, of which 14 were waited for; matrix products, arithmetic and copies ran while one was open for 0% of the time, Pallas kernels for 8%

profile of v10, /device:TPU:15, one launch (start us, length us, event | category | flops | bytes accessed | tf_op | source)
XLA Modules:
  0.0 178.8 jit_solution(4254340814172185879)
XLA Ops:
  0.0 1.9 %convert_element_type.3 = bf16[32,128,128]{2,1,0:T(8,128)(2,1)S(1)} convert(f32[32,128,128]{2,1,0:T(8,128)} %param.4) | non-fusion elementwise | flops 524288 | bytes 3145728 | tf_op jit(solution)/shard_map/convert_element_type | solution.py:411
  1.9 0.0 copy-start.1
  1.9 1.0 fusion.1
  3.0 4.1 %collective-permute-start = (bf16[16,128,128]{2,1,0:T(8,128)(2,1)}, bf16[16,128,128]{2,1,0:T(8,128)(2,1)}, u32[]{:S(2)}, u32[]{:S(2)}) collective-permute-start(bf16[16,128,128]{2,1,0:T(8,128)(2,1)} %get-tuple-element.84.refs_2_), channel_id=1, source_target_pairs={{0,1},{1,2},{2,3},{3,4},{4,5},{5,6},{6,7},{7,8},{8,9},{9,10},{10,1... | collective-permute-start | bytes 1572872 | tf_op jit(solution)/shard_map/ppermute | solution.py:386
  7.1 1.9 %collective-permute-start.1 = (bf16[16,128,128]{2,1,0:T(8,128)(2,1)}, bf16[16,128,128]{2,1,0:T(8,128)(2,1)}, u32[]{:S(2)}, u32[]{:S(2)}) collective-permute-start(bf16[16,128,128]{2,1,0:T(8,128)(2,1)} %get-tuple-element.83.refs_1_), channel_id=1, source_target_pairs={{1,0},{2,1},{3,2},{4,3},{5,4},{6,5},{7,6},{8,7},{9,8},{10,9},{11,1... | collective-permute-start | bytes 1572872 | tf_op jit(solution)/shard_map/ppermute | solution.py:386
  9.0 0.1 copy.6
  9.1 1.1 pack_tiles.1
  10.2 3.8 %collective-permute-start.10 = (bf16[1040,128]{1,0:T(8,128)(2,1)S(1)}, bf16[1040,128]{1,0:T(8,128)(2,1)S(1)}, u32[]{:S(2)}, u32[]{:S(2)}) collective-permute-start(bf16[1040,128]{1,0:T(8,128)(2,1)S(1)} %get-tuple-element.55), channel_id=1, source_target_pairs={{0,3},{1,4},{2,5},{3,6},{4,7},{5,8},{6,9},{7,10},{8,11},{9,12},{10... | collective-permute-start | bytes 798728 | tf_op jit(solution)/shard_map/ppermute | solution.py:409
  13.9 0.0 collective-permute-start.11
  13.9 2.0 %collective-permute-start.12 = (bf16[1040,128]{1,0:T(8,128)(2,1)S(1)}, bf16[1040,128]{1,0:T(8,128)(2,1)S(1)}, u32[]{:S(2)}, u32[]{:S(2)}) collective-permute-start(bf16[1040,128]{1,0:T(8,128)(2,1)S(1)} %get-tuple-element.57), channel_id=1, source_target_pairs={{0,5},{1,6},{2,7},{3,8},{4,9},{5,10},{6,11},{7,12},{8,13},{9,14},{... | collective-permute-start | bytes 798728 | tf_op jit(solution)/shard_map/ppermute | solution.py:409
  16.0 0.7 prepare.1
  16.7 5.5 %collective-permute-done.10.refs_9_ = bf16[1040,128]{1,0:T(8,128)(2,1)S(1)} collective-permute-done((bf16[1040,128]{1,0:T(8,128)(2,1)S(1)}, bf16[1040,128]{1,0:T(8,128)(2,1)S(1)}, u32[]{:S(2)}, u32[]{:S(2)}) %collective-permute-start.10) | collective-permute-done | bytes 266272 | tf_op jit(solution)/shard_map/ppermute | solution.py:409
  22.2 1.9 %collective-permute-start.2 = (bf16[1040,128]{1,0:T(8,128)(2,1)S(1)}, bf16[1040,128]{1,0:T(8,128)(2,1)S(1)}, u32[]{:S(2)}, u32[]{:S(2)}) collective-permute-start(bf16[1040,128]{1,0:T(8,128)(2,1)S(1)} %get-tuple-element.46), channel_id=1, source_target_pairs={{0,58},{1,59},{2,60},{3,61},{4,62},{5,63},{6,0},{7,1},{8,2},{9,3},... | collective-permute-start | bytes 798728 | tf_op jit(solution)/shard_map/ppermute | solution.py:409
  24.1 0.0 collective-permute-done.refs_0_
  24.1 7.5 %collective-permute-start.3 = (bf16[1040,128]{1,0:T(8,128)(2,1)S(1)}, bf16[1040,128]{1,0:T(8,128)(2,1)S(1)}, u32[]{:S(2)}, u32[]{:S(2)}) collective-permute-start(bf16[1040,128]{1,0:T(8,128)(2,1)S(1)} %get-tuple-element.47), channel_id=1, source_target_pairs={{0,59},{1,60},{2,61},{3,62},{4,63},{5,0},{6,1},{7,2},{8,3},{9,4},{... | collective-permute-start | bytes 798728 | tf_op jit(solution)/shard_map/ppermute | solution.py:409
  31.5 0.0 collective-permute-done.1.refs_3_
  31.5 4.4 %collective-permute-start.4 = (bf16[1040,128]{1,0:T(8,128)(2,1)S(1)}, bf16[1040,128]{1,0:T(8,128)(2,1)S(1)}, u32[]{:S(2)}, u32[]{:S(2)}) collective-permute-start(bf16[1040,128]{1,0:T(8,128)(2,1)S(1)} %get-tuple-element.48), channel_id=1, source_target_pairs={{0,60},{1,61},{2,62},{3,63},{4,0},{5,1},{6,2},{7,3},{8,4},{9,5},{1... | collective-permute-start | bytes 798728 | tf_op jit(solution)/shard_map/ppermute | solution.py:409
  35.9 6.7 %first_blur.1.blurred_ref = f32[24,512,128]{2,1,0:T(8,128)S(1)} custom-call(bf16[96,64]{1,0:T(8,128)(2,1)S(1)} %get-tuple-element.58.kx_ref.refs_0_, bf16[3,128,128]{2,1,0:T(8,128)(2,1)S(1)} %get-tuple-element.59.ky_ref.refs_1_, bf16[3,256,256]{2,1,0:T(8,128)(2,1)S(1)} %get-tuple-element.60.kz_ref.refs_2_, ...), custom_call_target="tpu_custom_call" | custom-call | flops 6442450944 | bytes 12582912 | tf_op jit(solution)/shard_map/first_blur/pallas_call | solution.py:370
  42.6 0.0 collective-permute-done.11.refs_10_
  42.6 0.1 collective-permute-start.5
  42.7 0.0 collective-permute-done.12.refs_11_
  42.7 0.1 collective-permute-start.6
  42.8 0.0 collective-permute-done.2.refs_0_
  42.8 0.5 collective-permute-start.7
  43.3 0.0 collective-permute-done.3.refs_1_
  43.3 1.5 collective-permute-start.8
  44.8 8.0 %collective-permute-done.4.refs_2_ = bf16[1040,128]{1,0:T(8,128)(2,1)S(1)} collective-permute-done((bf16[1040,128]{1,0:T(8,128)(2,1)S(1)}, bf16[1040,128]{1,0:T(8,128)(2,1)S(1)}, u32[]{:S(2)}, u32[]{:S(2)}) %collective-permute-start.4) | collective-permute-done | bytes 266272 | tf_op jit(solution)/shard_map/ppermute | solution.py:409
  52.8 0.4 collective-permute-done.5.refs_3_
  53.3 11.8 %collective-permute-done.6.refs_4_ = bf16[1040,128]{1,0:T(8,128)(2,1)S(1)} collective-permute-done((bf16[1040,128]{1,0:T(8,128)(2,1)S(1)}, bf16[1040,128]{1,0:T(8,128)(2,1)S(1)}, u32[]{:S(2)}, u32[]{:S(2)}) %collective-permute-start.6) | collective-permute-done | bytes 266272 | tf_op jit(solution)/shard_map/ppermute | solution.py:409
  65.0 0.9 collective-permute-done.7.refs_5_
  65.9 0.0 collective-permute-done.8.refs_7_
  65.9 1.2 collective-permute-done.9.refs_8_
  67.1 6.4 %first_back.1 = (s16[2064,128]{1,0:T(8,128)(2,1)S(1)}, s16[2064,128]{1,0:T(8,128)(2,1)S(1)}, bf16[128,192,128]{2,1,0:T(8,128)(2,1)S(1)}, bf16[24,512,128]{2,1,0:T(8,128)(2,1)S(1)}) custom-call(bf16[64,192]{1,0:T(8,128)(2,1)S(1)} %get-tuple-element.43.kx_ref.refs_3_, bf16[3,128,128]{2,1,0:T(8,128)(2,1)S(1)} %get-tuple-element.44.ky_ref.refs_4_, ...), custom_call_target="tpu_custom_call" | custom-call | flops 8589934592 | bytes 12582912 | tf_op jit(solution)/shard_map/first_back/pallas_call | solution.py:370
  73.5 1.9 %collective-permute-start.15 = (s16[2064,128]{1,0:T(8,128)(2,1)S(1)}, s16[2064,128]{1,0:T(8,128)(2,1)S(1)}, u32[]{:S(2)}, u32[]{:S(2)}) collective-permute-start(s16[2064,128]{1,0:T(8,128)(2,1)S(1)} %get-tuple-element.71), channel_id=1, source_target_pairs={{1,0},{2,1},{3,2},{4,3},{5,4},{6,5},{7,6},{8,7},{9,8},{10,9},{11,1... | collective-permute-start | bytes 1585160 | tf_op jit(solution)/shard_map/ppermute | solution.py:386
  75.5 3.6 %collective-permute-start.13 = (s16[2064,128]{1,0:T(8,128)(2,1)S(1)}, s16[2064,128]{1,0:T(8,128)(2,1)S(1)}, u32[]{:S(2)}, u32[]{:S(2)}) collective-permute-start(s16[2064,128]{1,0:T(8,128)(2,1)S(1)} %get-tuple-element.68), channel_id=1, source_target_pairs={{0,1},{1,2},{2,3},{3,4},{4,5},{5,6},{6,7},{7,8},{8,9},{9,10},{10,1... | collective-permute-start | bytes 1585160 | tf_op jit(solution)/shard_map/ppermute | solution.py:386
  79.1 1.5 own.2
  80.6 0.0 copy-start.2
  80.6 3.8 %collective-permute-done.15.edge_ref = s16[2064,128]{1,0:T(8,128)(2,1)S(1)} collective-permute-done((s16[2064,128]{1,0:T(8,128)(2,1)S(1)}, s16[2064,128]{1,0:T(8,128)(2,1)S(1)}, u32[]{:S(2)}, u32[]{:S(2)}) %collective-permute-start.15) | collective-permute-done | bytes 528416 | tf_op jit(solution)/shard_map/ppermute | solution.py:386
  84.4 0.3 join.5.own_ref
  84.7 2.3 %collective-permute-start.16 = (s16[2064,128]{1,0:T(8,128)(2,1)S(1)}, s16[2064,128]{1,0:T(8,128)(2,1)S(1)}, u32[]{:S(2)}, u32[]{:S(2)}) collective-permute-start(s16[2064,128]{1,0:T(8,128)(2,1)S(1)} %join.5.own_ref), channel_id=1, source_target_pairs={{0,64},{64,0},{1,65},{65,1},{2,66},{66,2},{3,67},{67,3},{4,68},{68... | collective-permute-start | bytes 1585160 | tf_op jit(solution)/shard_map/ppermute | solution.py:396
  87.0 0.3 join.4.own_ref
  87.3 1.0 collective-permute-start.14
  88.4 0.1 fusion
  88.5 14.4 %collective-permute-done.16.other_ref = s16[2064,128]{1,0:T(8,128)(2,1)S(1)} collective-permute-done((s16[2064,128]{1,0:T(8,128)(2,1)S(1)}, s16[2064,128]{1,0:T(8,128)(2,1)S(1)}, u32[]{:S(2)}, u32[]{:S(2)}) %collective-permute-start.16) | collective-permute-done | bytes 528416 | tf_op jit(solution)/shard_map/ppermute | solution.py:396
  102.9 0.4 update.3
  103.3 1.9 %collective-permute-start.17 = (bf16[16,128,128]{2,1,0:T(8,128)(2,1)S(1)}, bf16[16,128,128]{2,1,0:T(8,128)(2,1)S(1)}, u32[]{:S(2)}, u32[]{:S(2)}) collective-permute-start(bf16[16,128,128]{2,1,0:T(8,128)(2,1)S(1)} %get-tuple-element.72.refs_8_), channel_id=1, source_target_pairs={{0,1},{1,2},{2,3},{3,4},{4,5},{5,6},{6,7},{7,8},{8,9},{9,10},{10,1... | collective-permute-start | bytes 1572872 | tf_op jit(solution)/shard_map/ppermute | solution.py:386
  105.2 8.9 %collective-permute-done.14.other_ref = s16[2064,128]{1,0:T(8,128)(2,1)S(1)} collective-permute-done((s16[2064,128]{1,0:T(8,128)(2,1)S(1)}, s16[2064,128]{1,0:T(8,128)(2,1)S(1)}, u32[]{:S(2)}, u32[]{:S(2)}) %collective-permute-start.14) | collective-permute-done | bytes 528416 | tf_op jit(solution)/shard_map/ppermute | solution.py:396
  114.1 0.4 update.2
  114.5 2.2 %collective-permute-start.18 = (bf16[16,128,128]{2,1,0:T(8,128)(2,1)S(1)}, bf16[16,128,128]{2,1,0:T(8,128)(2,1)S(1)}, u32[]{:S(2)}, u32[]{:S(2)}) collective-permute-start(bf16[16,128,128]{2,1,0:T(8,128)(2,1)S(1)} %get-tuple-element.73.refs_7_), channel_id=1, source_target_pairs={{1,0},{2,1},{3,2},{4,3},{5,4},{6,5},{7,6},{8,7},{9,8},{10,9},{11,1... | collective-permute-start | bytes 1572872 | tf_op jit(solution)/shard_map/ppermute | solution.py:386
  116.7 8.3 %collective-permute-done.18.refs_9_ = bf16[16,128,128]{2,1,0:T(8,128)(2,1)S(1)} collective-permute-done((bf16[16,128,128]{2,1,0:T(8,128)(2,1)S(1)}, bf16[16,128,128]{2,1,0:T(8,128)(2,1)S(1)}, u32[]{:S(2)}, u32[]{:S(2)}) %collective-permute-start.18) | collective-permute-done | bytes 524320 | tf_op jit(solution)/shard_map/ppermute | solution.py:386
  125.0 11.5 %sweep.1 = (s16[2064,128]{1,0:T(8,128)(2,1)S(1)}, s16[2064,128]{1,0:T(8,128)(2,1)S(1)}, bf16[128,192,128]{2,1,0:T(8,128)(2,1)S(1)}) custom-call(bf16[96,64]{1,0:T(8,128)(2,1)S(1)} %get-tuple-element.58.kx_ref.refs_0_, bf16[3,128,128]{2,1,0:T(8,128)(2,1)S(1)} %get-tuple-element.59.ky_ref.refs_1_, bf16[3,256,256]{2,1,0:T(8,128)(2,1)S(1)} %get-tuple-element.60.kz_ref.refs_2_, ...), custom_call_target="tpu_custom_call" | custom-call | flops 15032385536 | bytes 12582912 | tf_op jit(solution)/shard_map/sweep/pallas_call | solution.py:370
  136.5 1.9 %collective-permute-start.19 = (s16[2064,128]{1,0:T(8,128)(2,1)S(1)}, s16[2064,128]{1,0:T(8,128)(2,1)S(1)}, u32[]{:S(2)}, u32[]{:S(2)}) collective-permute-start(s16[2064,128]{1,0:T(8,128)(2,1)S(1)} %get-tuple-element.77), channel_id=1, source_target_pairs={{0,1},{1,2},{2,3},{3,4},{4,5},{5,6},{6,7},{7,8},{8,9},{9,10},{10,1... | collective-permute-start | bytes 1585160 | tf_op jit(solution)/shard_map/ppermute | solution.py:386
  138.5 2.4 %collective-permute-start.21 = (s16[2064,128]{1,0:T(8,128)(2,1)S(1)}, s16[2064,128]{1,0:T(8,128)(2,1)S(1)}, u32[]{:S(2)}, u32[]{:S(2)}) collective-permute-start(s16[2064,128]{1,0:T(8,128)(2,1)S(1)} %get-tuple-element.80), channel_id=1, source_target_pairs={{1,0},{2,1},{3,2},{4,3},{5,4},{6,5},{7,6},{8,7},{9,8},{10,9},{11,1... | collective-permute-start | bytes 1585160 | tf_op jit(solution)/shard_map/ppermute | solution.py:386
  140.9 1.4 own.3
  142.3 2.3 %collective-permute-done.19.edge_ref = s16[2064,128]{1,0:T(8,128)(2,1)S(1)} collective-permute-done((s16[2064,128]{1,0:T(8,128)(2,1)S(1)}, s16[2064,128]{1,0:T(8,128)(2,1)S(1)}, u32[]{:S(2)}, u32[]{:S(2)}) %collective-permute-start.19) | collective-permute-done | bytes 528416 | tf_op jit(solution)/shard_map/ppermute | solution.py:386
  144.6 0.3 join.6.own_ref
  144.9 0.7 collective-permute-start.20
  145.7 3.3 %collective-permute-done.21.edge_ref = s16[2064,128]{1,0:T(8,128)(2,1)S(1)} collective-permute-done((s16[2064,128]{1,0:T(8,128)(2,1)S(1)}, s16[2064,128]{1,0:T(8,128)(2,1)S(1)}, u32[]{:S(2)}, u32[]{:S(2)}) %collective-permute-start.21) | collective-permute-done | bytes 528416 | tf_op jit(solution)/shard_map/ppermute | solution.py:386
  149.0 0.3 join.7.own_ref
  149.3 0.7 collective-permute-start.22
  150.1 15.9 %collective-permute-done.20.other_ref = s16[2064,128]{1,0:T(8,128)(2,1)S(1)} collective-permute-done((s16[2064,128]{1,0:T(8,128)(2,1)S(1)}, s16[2064,128]{1,0:T(8,128)(2,1)S(1)}, u32[]{:S(2)}, u32[]{:S(2)}) %collective-permute-start.20) | collective-permute-done | bytes 528416 | tf_op jit(solution)/shard_map/ppermute | solution.py:396
  166.0 0.3 low_update.1.low_ref
  166.4 11.0 %collective-permute-done.22.other_ref = s16[2064,128]{1,0:T(8,128)(2,1)S(1)} collective-permute-done((s16[2064,128]{1,0:T(8,128)(2,1)S(1)}, s16[2064,128]{1,0:T(8,128)(2,1)S(1)}, u32[]{:S(2)}, u32[]{:S(2)}) %collective-permute-start.22) | collective-permute-done | bytes 528416 | tf_op jit(solution)/shard_map/ppermute | solution.py:396
  177.4 1.3 last_update.1
  (9 shorter events, 0.0 us)
Async XLA Ops:
  0.0 9.0 %copy-start.3 = (s32[1,24,3]{1,0,2:T(1,128)S(1)}, s32[1,24,3]{1,0,2:T(1,128)}, u32[]{:S(2)}) copy-start(s32[1,24,3]{1,0,2:T(1,128)} %param.6) | copy-start | bytes 868
  0.0 9.1 %copy-start = (bf16[1,24,4,128,128]{4,3,2,1,0:T(8,128)(2,1)S(1)}, bf16[1,24,4,128,128]{4,3,2,1,0:T(8,128)(2,1)}, u32[]{:S(2)}) copy-start(bf16[1,24,4,128,128]{4,3,2,1,0:T(8,128)(2,1)} %param.5) | copy-start | bytes 9437188
  1.9 14.1 %copy-start.1 = (f32[3,3,31]{2,1,0:T(4,128)S(1)}, f32[3,3,31]{2,1,0:T(4,128)}, u32[]{:S(2)}) copy-start(f32[3,3,31]{2,1,0:T(4,128)} %psf_ref.1) | copy-start | bytes 3352
  3.0 21.1 %collective-permute-start = (bf16[16,128,128]{2,1,0:T(8,128)(2,1)}, bf16[16,128,128]{2,1,0:T(8,128)(2,1)}, u32[]{:S(2)}, u32[]{:S(2)}) collective-permute-start(bf16[16,128,128]{2,1,0:T(8,128)(2,1)} %get-tuple-element.84.refs_2_), channel_id=1, source_target_pairs={{0,1},{1,2},{2,3},{3,4},{4,5},{5,6},{6,7},{7,8},{8,9},{9,10},{10,1... | collective-permute-start | bytes 1572872 | tf_op jit(solution)/shard_map/ppermute | solution.py:386
  7.1 24.5 %collective-permute-start.1 = (bf16[16,128,128]{2,1,0:T(8,128)(2,1)}, bf16[16,128,128]{2,1,0:T(8,128)(2,1)}, u32[]{:S(2)}, u32[]{:S(2)}) collective-permute-start(bf16[16,128,128]{2,1,0:T(8,128)(2,1)} %get-tuple-element.83.refs_1_), channel_id=1, source_target_pairs={{1,0},{2,1},{3,2},{4,3},{5,4},{6,5},{7,6},{8,7},{9,8},{10,9},{11,1... | collective-permute-start | bytes 1572872 | tf_op jit(solution)/shard_map/ppermute | solution.py:386
  10.2 12.0 %collective-permute-start.10 = (bf16[1040,128]{1,0:T(8,128)(2,1)S(1)}, bf16[1040,128]{1,0:T(8,128)(2,1)S(1)}, u32[]{:S(2)}, u32[]{:S(2)}) collective-permute-start(bf16[1040,128]{1,0:T(8,128)(2,1)S(1)} %get-tuple-element.55), channel_id=1, source_target_pairs={{0,3},{1,4},{2,5},{3,6},{4,7},{5,8},{6,9},{7,10},{8,11},{9,12},{10... | collective-permute-start | bytes 798728 | tf_op jit(solution)/shard_map/ppermute | solution.py:409
  13.9 28.7 %collective-permute-start.11 = (bf16[1040,128]{1,0:T(8,128)(2,1)S(1)}, bf16[1040,128]{1,0:T(8,128)(2,1)S(1)}, u32[]{:S(2)}, u32[]{:S(2)}) collective-permute-start(bf16[1040,128]{1,0:T(8,128)(2,1)S(1)} %get-tuple-element.56), channel_id=1, source_target_pairs={{0,4},{1,5},{2,6},{3,7},{4,8},{5,9},{6,10},{7,11},{8,12},{9,13},{1... | collective-permute-start | bytes 798728 | tf_op jit(solution)/shard_map/ppermute | solution.py:409
  13.9 28.8 %collective-permute-start.12 = (bf16[1040,128]{1,0:T(8,128)(2,1)S(1)}, bf16[1040,128]{1,0:T(8,128)(2,1)S(1)}, u32[]{:S(2)}, u32[]{:S(2)}) collective-permute-start(bf16[1040,128]{1,0:T(8,128)(2,1)S(1)} %get-tuple-element.57), channel_id=1, source_target_pairs={{0,5},{1,6},{2,7},{3,8},{4,9},{5,10},{6,11},{7,12},{8,13},{9,14},{... | collective-permute-start | bytes 798728 | tf_op jit(solution)/shard_map/ppermute | solution.py:409
  22.2 20.6 %collective-permute-start.2 = (bf16[1040,128]{1,0:T(8,128)(2,1)S(1)}, bf16[1040,128]{1,0:T(8,128)(2,1)S(1)}, u32[]{:S(2)}, u32[]{:S(2)}) collective-permute-start(bf16[1040,128]{1,0:T(8,128)(2,1)S(1)} %get-tuple-element.46), channel_id=1, source_target_pairs={{0,58},{1,59},{2,60},{3,61},{4,62},{5,63},{6,0},{7,1},{8,2},{9,3},... | collective-permute-start | bytes 798728 | tf_op jit(solution)/shard_map/ppermute | solution.py:409
  24.1 19.2 %collective-permute-start.3 = (bf16[1040,128]{1,0:T(8,128)(2,1)S(1)}, bf16[1040,128]{1,0:T(8,128)(2,1)S(1)}, u32[]{:S(2)}, u32[]{:S(2)}) collective-permute-start(bf16[1040,128]{1,0:T(8,128)(2,1)S(1)} %get-tuple-element.47), channel_id=1, source_target_pairs={{0,59},{1,60},{2,61},{3,62},{4,63},{5,0},{6,1},{7,2},{8,3},{9,4},{... | collective-permute-start | bytes 798728 | tf_op jit(solution)/shard_map/ppermute | solution.py:409
  31.5 21.3 %collective-permute-start.4 = (bf16[1040,128]{1,0:T(8,128)(2,1)S(1)}, bf16[1040,128]{1,0:T(8,128)(2,1)S(1)}, u32[]{:S(2)}, u32[]{:S(2)}) collective-permute-start(bf16[1040,128]{1,0:T(8,128)(2,1)S(1)} %get-tuple-element.48), channel_id=1, source_target_pairs={{0,60},{1,61},{2,62},{3,63},{4,0},{5,1},{6,2},{7,3},{8,4},{9,5},{1... | collective-permute-start | bytes 798728 | tf_op jit(solution)/shard_map/ppermute | solution.py:409
  42.6 10.6 %collective-permute-start.5 = (bf16[1040,128]{1,0:T(8,128)(2,1)S(1)}, bf16[1040,128]{1,0:T(8,128)(2,1)S(1)}, u32[]{:S(2)}, u32[]{:S(2)}) collective-permute-start(bf16[1040,128]{1,0:T(8,128)(2,1)S(1)} %get-tuple-element.49), channel_id=1, source_target_pairs={{0,61},{1,62},{2,63},{3,0},{4,1},{5,2},{6,3},{7,4},{8,5},{9,6},{10... | collective-permute-start | bytes 798728 | tf_op jit(solution)/shard_map/ppermute | solution.py:409
  42.7 22.3 %collective-permute-start.6 = (bf16[1040,128]{1,0:T(8,128)(2,1)S(1)}, bf16[1040,128]{1,0:T(8,128)(2,1)S(1)}, u32[]{:S(2)}, u32[]{:S(2)}) collective-permute-start(bf16[1040,128]{1,0:T(8,128)(2,1)S(1)} %get-tuple-element.62), channel_id=1, source_target_pairs={{0,62},{1,63},{2,0},{3,1},{4,2},{5,3},{6,4},{7,5},{8,6},{9,7},{10,... | collective-permute-start | bytes 798728 | tf_op jit(solution)/shard_map/ppermute | solution.py:409
  42.8 23.1 %collective-permute-start.7 = (bf16[1040,128]{1,0:T(8,128)(2,1)S(1)}, bf16[1040,128]{1,0:T(8,128)(2,1)S(1)}, u32[]{:S(2)}, u32[]{:S(2)}) collective-permute-start(bf16[1040,128]{1,0:T(8,128)(2,1)S(1)} %get-tuple-element.63), channel_id=1, source_target_pairs={{0,63},{1,0},{2,1},{3,2},{4,3},{5,4},{6,5},{7,6},{8,7},{9,8},{10,9... | collective-permute-start | bytes 798728 | tf_op jit(solution)/shard_map/ppermute | solution.py:409
  43.3 22.6 %collective-permute-start.8 = (bf16[1040,128]{1,0:T(8,128)(2,1)S(1)}, bf16[1040,128]{1,0:T(8,128)(2,1)S(1)}, u32[]{:S(2)}, u32[]{:S(2)}) collective-permute-start(bf16[1040,128]{1,0:T(8,128)(2,1)S(1)} %get-tuple-element.64), channel_id=1, source_target_pairs={{0,1},{1,2},{2,3},{3,4},{4,5},{5,6},{6,7},{7,8},{8,9},{9,10},{10,1... | collective-permute-start | bytes 798728 | tf_op jit(solution)/shard_map/ppermute | solution.py:409
  52.8 14.2 %collective-permute-start.9 = (bf16[1040,128]{1,0:T(8,128)(2,1)S(1)}, bf16[1040,128]{1,0:T(8,128)(2,1)S(1)}, u32[]{:S(2)}, u32[]{:S(2)}) collective-permute-start(bf16[1040,128]{1,0:T(8,128)(2,1)S(1)} %get-tuple-element.65), channel_id=1, source_target_pairs={{0,2},{1,3},{2,4},{3,5},{4,6},{5,7},{6,8},{7,9},{8,10},{9,11},{10,... | collective-permute-start | bytes 798728 | tf_op jit(solution)/shard_map/ppermute | solution.py:409
  73.5 10.8 %collective-permute-start.15 = (s16[2064,128]{1,0:T(8,128)(2,1)S(1)}, s16[2064,128]{1,0:T(8,128)(2,1)S(1)}, u32[]{:S(2)}, u32[]{:S(2)}) collective-permute-start(s16[2064,128]{1,0:T(8,128)(2,1)S(1)} %get-tuple-element.71), channel_id=1, source_target_pairs={{1,0},{2,1},{3,2},{4,3},{5,4},{6,5},{7,6},{8,7},{9,8},{10,9},{11,1... | collective-permute-start | bytes 1585160 | tf_op jit(solution)/shard_map/ppermute | solution.py:386
  75.5 11.5 %collective-permute-start.13 = (s16[2064,128]{1,0:T(8,128)(2,1)S(1)}, s16[2064,128]{1,0:T(8,128)(2,1)S(1)}, u32[]{:S(2)}, u32[]{:S(2)}) collective-permute-start(s16[2064,128]{1,0:T(8,128)(2,1)S(1)} %get-tuple-element.68), channel_id=1, source_target_pairs={{0,1},{1,2},{2,3},{3,4},{4,5},{5,6},{6,7},{7,8},{8,9},{9,10},{10,1... | collective-permute-start | bytes 1585160 | tf_op jit(solution)/shard_map/ppermute | solution.py:386
  80.6 7.8 %copy-start.2 = (f32[32,128,128]{2,1,0:T(8,128)S(1)}, f32[32,128,128]{2,1,0:T(8,128)}, u32[]{:S(2)}) copy-start(f32[32,128,128]{2,1,0:T(8,128)} %param.4) | copy-start | bytes 6291460
  84.7 18.2 %collective-permute-start.16 = (s16[2064,128]{1,0:T(8,128)(2,1)S(1)}, s16[2064,128]{1,0:T(8,128)(2,1)S(1)}, u32[]{:S(2)}, u32[]{:S(2)}) collective-permute-start(s16[2064,128]{1,0:T(8,128)(2,1)S(1)} %join.5.own_ref), channel_id=1, source_target_pairs={{0,64},{64,0},{1,65},{65,1},{2,66},{66,2},{3,67},{67,3},{4,68},{68... | collective-permute-start | bytes 1585160 | tf_op jit(solution)/shard_map/ppermute | solution.py:396
  87.3 26.8 %collective-permute-start.14 = (s16[2064,128]{1,0:T(8,128)(2,1)S(1)}, s16[2064,128]{1,0:T(8,128)(2,1)S(1)}, u32[]{:S(2)}, u32[]{:S(2)}) collective-permute-start(s16[2064,128]{1,0:T(8,128)(2,1)S(1)} %join.4.own_ref), channel_id=1, source_target_pairs={{0,64},{64,0},{1,65},{65,1},{2,66},{66,2},{3,67},{67,3},{4,68},{68... | collective-permute-start | bytes 1585160 | tf_op jit(solution)/shard_map/ppermute | solution.py:396
  103.3 13.4 %collective-permute-start.17 = (bf16[16,128,128]{2,1,0:T(8,128)(2,1)S(1)}, bf16[16,128,128]{2,1,0:T(8,128)(2,1)S(1)}, u32[]{:S(2)}, u32[]{:S(2)}) collective-permute-start(bf16[16,128,128]{2,1,0:T(8,128)(2,1)S(1)} %get-tuple-element.72.refs_8_), channel_id=1, source_target_pairs={{0,1},{1,2},{2,3},{3,4},{4,5},{5,6},{6,7},{7,8},{8,9},{9,10},{10,1... | collective-permute-start | bytes 1572872 | tf_op jit(solution)/shard_map/ppermute | solution.py:386
  114.5 10.5 %collective-permute-start.18 = (bf16[16,128,128]{2,1,0:T(8,128)(2,1)S(1)}, bf16[16,128,128]{2,1,0:T(8,128)(2,1)S(1)}, u32[]{:S(2)}, u32[]{:S(2)}) collective-permute-start(bf16[16,128,128]{2,1,0:T(8,128)(2,1)S(1)} %get-tuple-element.73.refs_7_), channel_id=1, source_target_pairs={{1,0},{2,1},{3,2},{4,3},{5,4},{6,5},{7,6},{8,7},{9,8},{10,9},{11,1... | collective-permute-start | bytes 1572872 | tf_op jit(solution)/shard_map/ppermute | solution.py:386
  136.5 8.1 %collective-permute-start.19 = (s16[2064,128]{1,0:T(8,128)(2,1)S(1)}, s16[2064,128]{1,0:T(8,128)(2,1)S(1)}, u32[]{:S(2)}, u32[]{:S(2)}) collective-permute-start(s16[2064,128]{1,0:T(8,128)(2,1)S(1)} %get-tuple-element.77), channel_id=1, source_target_pairs={{0,1},{1,2},{2,3},{3,4},{4,5},{5,6},{6,7},{7,8},{8,9},{9,10},{10,1... | collective-permute-start | bytes 1585160 | tf_op jit(solution)/shard_map/ppermute | solution.py:386
  138.5 10.5 %collective-permute-start.21 = (s16[2064,128]{1,0:T(8,128)(2,1)S(1)}, s16[2064,128]{1,0:T(8,128)(2,1)S(1)}, u32[]{:S(2)}, u32[]{:S(2)}) collective-permute-start(s16[2064,128]{1,0:T(8,128)(2,1)S(1)} %get-tuple-element.80), channel_id=1, source_target_pairs={{1,0},{2,1},{3,2},{4,3},{5,4},{6,5},{7,6},{8,7},{9,8},{10,9},{11,1... | collective-permute-start | bytes 1585160 | tf_op jit(solution)/shard_map/ppermute | solution.py:386
  144.9 21.1 %collective-permute-start.20 = (s16[2064,128]{1,0:T(8,128)(2,1)S(1)}, s16[2064,128]{1,0:T(8,128)(2,1)S(1)}, u32[]{:S(2)}, u32[]{:S(2)}) collective-permute-start(s16[2064,128]{1,0:T(8,128)(2,1)S(1)} %join.6.own_ref), channel_id=1, source_target_pairs={{0,64},{64,0},{1,65},{65,1},{2,66},{66,2},{3,67},{67,3},{4,68},{68... | collective-permute-start | bytes 1585160 | tf_op jit(solution)/shard_map/ppermute | solution.py:396
  149.3 28.0 %collective-permute-start.22 = (s16[2064,128]{1,0:T(8,128)(2,1)S(1)}, s16[2064,128]{1,0:T(8,128)(2,1)S(1)}, u32[]{:S(2)}, u32[]{:S(2)}) collective-permute-start(s16[2064,128]{1,0:T(8,128)(2,1)S(1)} %join.7.own_ref), channel_id=1, source_target_pairs={{0,64},{64,0},{1,65},{65,1},{2,66},{66,2},{3,67},{67,3},{4,68},{68... | collective-permute-start | bytes 1585160 | tf_op jit(solution)/shard_map/ppermute | solution.py:396
